TPU v7x, 128 devices: a whole 4x4x4 slice. The times are simulated.
128 devices in a mesh: rows: 16 (over y, x_lo, core), cols: 8 (over z, x_hi).
Axes of the slice: x: 4 (x_hi: 2, x_lo: 2; x = x_hi * 2 + x_lo), y: 4, z: 4, core: 2. Of those that a mesh axis runs over, the one named last changes fastest.
Arguments:
- feat_left: bfloat16 [256, 2048, 256], P('rows', 'cols'), may hold values from -6 to 6
- feat_right: bfloat16 [256, 2048, 256], P('rows', 'cols'), may hold values from -6 to 6
- hidden: bfloat16 [256, 2048, 128], P('rows', 'cols'), may hold values from -1 to 1
- disparity: int32 [256, 2048], P('rows', 'cols'), may hold values from 0 to 127
- motion_weight: bfloat16 [9, 128], replicated, may hold values from -2 to 2
- gate_weight: bfloat16 [3, 3, 256, 256], replicated, may hold values from -0.125 to 0.125
- cand_weight: bfloat16 [3, 3, 256, 128], replicated, may hold values from -0.125 to 0.125
- grad_hidden: bfloat16 [256, 2048, 128], P('rows', 'cols'), may hold values from -6 to 6
Outputs:
- new_hidden: bfloat16 [256, 2048, 128], P('rows', 'cols')
- grad_left: bfloat16 [256, 2048, 256], P('rows', 'cols')
- grad_right: bfloat16 [256, 2048, 256], P('rows', 'cols')
Inputs may be any that keep to these rules, and one draw needn't show every extreme that they name: Whole disparity levels.
All inputs are finite; a program needn't handle non-finite values.
Results may differ from a plain program's by a relative error of at most 0.0075.
Values may be sent and summed in bfloat16 or wider, within the bound.
No kernel may reach another device: no remote copies, remote signals or barrier semaphores. Data moves between devices by JAX's collectives and lax.ppermute only.
A program may use at most 192 MiB of HBM per device.

v0:
```python
import math

import jax
import jax.numpy as jnp
from jax import lax
from jax.sharding import PartitionSpec as P

DISP = 128


def from_behind(array, axis, by):
    size = lax.axis_size(axis)
    pairs = [(i, i + by) for i in range(size) if 0 <= i + by < size]
    return lax.ppermute(array, axis, pairs)


def padded_2(block, sides, width):
    for axis, dim in sides:
        count = lax.axis_size(axis)
        forward = [(i, i + 1) for i in range(count - 1)]
        backward = [(target, source) for source, target in forward]
        low = lax.ppermute(
            lax.slice_in_dim(block, block.shape[dim] - width, None, axis=dim), axis, forward
        )
        high = lax.ppermute(lax.slice_in_dim(block, 0, width, axis=dim), axis, backward)
        block = jnp.concatenate([low, block, high], axis=dim)
    return block


def band_windows(own_right, before):
    row_count, col_count, chan_count = own_right.shape
    band_size = before.shape[1]
    extended = jnp.concatenate([before, own_right], axis=1)
    blocks = extended.reshape(row_count, col_count // band_size + 1, band_size, chan_count)
    return jnp.concatenate([blocks[:, :-1], blocks[:, 1:]], axis=2)


def tap_index(disparity, band_size, radius):
    col_count = disparity.shape[1]
    inner = jnp.arange(col_count, dtype=jnp.int32) % band_size
    offsets = jnp.arange(2 * radius + 1, dtype=jnp.int32) - radius
    levels = disparity[:, :, None] + offsets[None, None, :]
    usable = (levels >= 0) & (levels < band_size)
    columns = jnp.clip(inner[None, :, None] + band_size - levels, 0, 2 * band_size - 1)
    return (columns, usable)


def conv_local(padded, weight, row_count, col_count):
    result = None
    for row_off in range(3):
        for col_off in range(3):
            product_term = jnp.einsum(
                "hwi,io->hwo",
                padded[row_off : row_off + row_count, col_off : col_off + col_count],
                weight[row_off, col_off],
                preferred_element_type=jnp.float32,
            )
            result = product_term if result is None else result + product_term
    return result


def flipped(weight):
    return jnp.transpose(weight[::-1, ::-1], (0, 1, 3, 2))


def per_device(
    feat_left, feat_right, hidden, disparity, motion_weight, gate_weight, cand_weight, grad_hidden
):
    row_count, col_count, chan_count = feat_left.shape
    hidden_units = hidden.shape[2]
    band_size = DISP
    radius = motion_weight.shape[0] // 2
    scale = 1.0 / math.sqrt(chan_count)
    block_count = col_count // band_size
    previous = from_behind(feat_right, "cols", 1)
    before = previous[:, col_count - band_size :]
    windows = band_windows(feat_right, before)
    left_blocks = feat_left.reshape(row_count, block_count, band_size, chan_count)
    scores = (
        jnp.einsum("hbic,hbjc->hbij", left_blocks, windows, preferred_element_type=jnp.float32)
        * scale
    )
    columns, usable = tap_index(disparity, band_size, radius)
    positions = jnp.arange(2 * band_size, dtype=jnp.int32)
    flat_scores = scores.reshape(row_count, col_count, 2 * band_size)
    picked = []
    for tap in range(2 * radius + 1):
        picked.append(
            jnp.sum(jnp.where(columns[:, :, tap : tap + 1] == positions, flat_scores, 0.0), axis=2)
        )
    taps = jnp.stack(picked, axis=2)
    taps = jnp.where(usable, taps, 0.0).astype(jnp.bfloat16)
    motion_pre = jnp.einsum("hwk,km->hwm", taps, motion_weight, preferred_element_type=jnp.float32)
    motion = jax.nn.silu(motion_pre).astype(jnp.bfloat16)
    inputs = jnp.concatenate([hidden, motion], axis=2)
    padded_inputs = padded_2(inputs, (("rows", 0), ("cols", 1)), 1)
    gates = conv_local(padded_inputs, gate_weight, row_count, col_count)
    update = jax.nn.sigmoid(gates[..., :hidden_units])
    reset = jax.nn.sigmoid(gates[..., hidden_units:])
    hidden_f = hidden.astype(jnp.float32)
    reset_state = (reset * hidden_f).astype(jnp.bfloat16)
    padded_reset = padded_2(reset_state, (("rows", 0), ("cols", 1)), 1)
    cand_in = jnp.concatenate([padded_reset, padded_inputs[:, :, hidden_units:]], axis=2)
    cand = jnp.tanh(conv_local(cand_in, cand_weight, row_count, col_count))
    new_hidden = ((1.0 - update) * hidden_f + update * cand).astype(jnp.bfloat16)
    cotangent = grad_hidden.astype(jnp.float32)
    cand_grad = (cotangent * update * (1.0 - cand * cand)).astype(jnp.bfloat16)
    update_grad = cotangent * (cand - hidden_f) * update * (1.0 - update)
    padded_cand = padded_2(cand_grad, (("rows", 0), ("cols", 1)), 1)
    cand_back = conv_local(padded_cand, flipped(cand_weight), row_count, col_count)
    reset_grad = cand_back[..., :hidden_units] * hidden_f * reset * (1.0 - reset)
    gate_grads = jnp.concatenate([update_grad, reset_grad], axis=2).astype(jnp.bfloat16)
    padded_gates = padded_2(gate_grads, (("rows", 0), ("cols", 1)), 1)
    gate_back = conv_local(padded_gates, flipped(gate_weight), row_count, col_count)
    motion_grad = cand_back[..., hidden_units:] + gate_back[..., hidden_units:]
    sigmas = jax.nn.sigmoid(motion_pre)
    pre_grad = (motion_grad * sigmas * (1.0 + motion_pre * (1.0 - sigmas))).astype(jnp.bfloat16)
    tap_grad = jnp.einsum(
        "hwm,km->hwk", pre_grad, motion_weight, preferred_element_type=jnp.float32
    )
    tap_grad = jnp.where(usable, tap_grad, 0.0)
    score_grad = jnp.zeros((row_count, col_count, 2 * band_size), jnp.float32)
    for tap in range(2 * radius + 1):
        score_grad = score_grad + jnp.where(
            columns[:, :, tap : tap + 1] == positions, tap_grad[:, :, tap : tap + 1], 0.0
        )
    score_grad = score_grad.astype(jnp.bfloat16).reshape(
        row_count, block_count, band_size, 2 * band_size
    )
    grad_left = (
        (
            jnp.einsum("hbij,hbjc->hbic", score_grad, windows, preferred_element_type=jnp.float32)
            * scale
        )
        .reshape(row_count, col_count, chan_count)
        .astype(jnp.bfloat16)
    )
    window_grad = (
        jnp.einsum("hbij,hbic->hbjc", score_grad, left_blocks, preferred_element_type=jnp.float32)
        * scale
    )
    far_part = window_grad[:, :, :band_size].astype(jnp.bfloat16)
    incoming = from_behind(far_part[:, 0], "cols", -1)
    following = jnp.concatenate([far_part[:, 1:], incoming[:, None]], axis=1).astype(jnp.float32)
    grad_right = (
        (window_grad[:, :, band_size:] + following)
        .reshape(row_count, col_count, chan_count)
        .astype(jnp.bfloat16)
    )
    return (new_hidden, grad_left, grad_right)


def solution(mesh):
    return jax.shard_map(
        per_device,
        mesh=mesh,
        in_specs=(
            P("rows", "cols", None),
            P("rows", "cols", None),
            P("rows", "cols", None),
            P("rows", "cols"),
            P(),
            P(),
            P(),
            P("rows", "cols", None),
        ),
        out_specs=(P("rows", "cols", None), P("rows", "cols", None), P("rows", "cols", None)),
        check_vma=False,
    )
```

profile of v0, /device:TPU:35, one launch (start us, length us, event | category | flops | bytes accessed | tf_op | source)
XLA Modules:
  0.0 343.8 jit_solution(5592080115382127659)
XLA Ops:
  0.7 3.9 %collective-permute-start = (bf16[16,256,256]{2,1,0:T(8,128)(2,1)}, bf16[16,256,256]{2,1,0:T(8,128)(2,1)}, u32[]{:S(2)}, u32[]{:S(2)}) collective-permute-start(bf16[16,256,256]{2,1,0:T(8,128)(2,1)} %param.9), channel_id=1, source_target_pairs={{0,1},{1,2},{2,3},{3,4},{4,5},{5,6},{6,7},{8,9},{9,10},{10,11},{11... | collective-permute-start | bytes 6291464 | tf_op jit(solution)/shard_map/ppermute | solution.py:14
  6.0 2.4 copy.182
  8.8 43.1 %collective-permute-done = bf16[16,256,256]{2,1,0:T(8,128)(2,1)} collective-permute-done((bf16[16,256,256]{2,1,0:T(8,128)(2,1)}, bf16[16,256,256]{2,1,0:T(8,128)(2,1)}, u32[]{:S(2)}, u32[]{:S(2)}) %collective-permute-start) | collective-permute-done | bytes 2097184 | tf_op jit(solution)/shard_map/ppermute | solution.py:14
  54.2 6.6 %fusion.14 = (f32[16,2,128]{2,1,0:T(2,128)S(1)}, f32[16,2,128]{2,1,0:T(2,128)S(1)}, f32[16,2,128]{2,1,0:T(2,128)S(1)}, f32[16,2,128]{2,1,0:T(2,128)S(1)}, f32[16...) fusion(s32[16,2,128]{2,1,0:T(2,128)S(1)} %bitcast.270, ...), kind=kOutput, calls=%fused_computation.26 | convolution fusion | flops 574582784 | bytes 6586368 | tf_op jit(solution)/shard_map/hbic,hbjc->hbij/dot_general | solution.py:80
  61.1 2.0 multiply_convert_fusion.1
  63.1 4.6 %collective-permute-start.1 = (bf16[1,256,256]{1,2,0:T(8,128)(2,1)S(1)}, bf16[1,256,256]{1,2,0:T(8,128)(2,1)S(1)}, u32[]{:S(2)}, u32[]{:S(2)}) collective-permute-start(bf16[1,256,256]{1,2,0:T(8,128)(2,1)S(1)} %get-tuple-element.38), channel_id=1, source_target_pairs={{0,8},{8,16},{16,24},{24,32},{32,40},{40,48},{48,56},{56,64},{64,7... | collective-permute-start | bytes 393224 | tf_op jit(solution)/shard_map/ppermute | solution.py:22
  67.7 1.9 collective-permute-start.2
  69.6 3.7 %fusion.111 = f32[16,256,256]{1,2,0:T(8,128)} fusion(bf16[16,256,128]{1,2,0:T(8,128)(2,1)S(1)} %get-tuple-element.68, bf16[16,256,128]{1,2,0:T(8,128)(2,1)S(1)} %copy.118, bf16[3,3,256,256]{3,2,1,0:T(8,128)(2,1)} %param.13), kind=kOutput, calls=%fused_computation.157 | convolution fusion | flops 541065216 | bytes 6422528 | tf_op jit(solution)/shard_map/hwi,io->hwo/dot_general | solution.py:52
  75.1 2.0 fusion.203
  78.9 3.1 collective-permute-start.3
  83.8 4.8 %collective-permute-start.4 = (bf16[18,1,256]{2,0,1:T(8,128)(2,1)S(1)}, bf16[18,1,256]{2,0,1:T(8,128)(2,1)S(1)}, u32[]{:S(2)}, u32[]{:S(2)}) collective-permute-start(bf16[18,1,256]{2,0,1:T(8,128)(2,1)S(1)} %copy.125), channel_id=1, source_target_pairs={{1,0},{2,1},{3,2},{4,3},{5,4},{6,5},{7,6},{9,8},{10,9},{11,10},{12... | collective-permute-start | bytes 27656 | tf_op jit(solution)/shard_map/ppermute | solution.py:25
  88.7 4.0 %fusion.23 = f32[16,256,256]{1,2,0:T(8,128)} fusion(bf16[16,256,128]{1,2,0:T(8,128)(2,1)} %copy-done.10, bf16[16,256,128]{1,2,0:T(8,128)(2,1)S(1)} %copy.118, bf16[1,256,256]{1,2,0:T(8,128)(2,1)S(1)} %collective-permute-done.1, bf16[3,3,256,256]{3,2,1,0:T(8,128)(2,1)} %param.13), kind=kOutput, calls=%fused_computation.63 | convolution fusion | flops 543555584 | bytes 6553600 | tf_op jit(solution)/shard_map/hwi,io->hwo/dot_general | solution.py:52
  92.7 3.7 %fusion.29 = f32[16,256,256]{1,2,0:T(8,128)} fusion(bf16[1,256,256]{1,2,0:T(8,128)(2,1)S(1)} %collective-permute-done.2, bf16[16,256,128]{1,2,0:T(8,128)(2,1)S(1)} %copy-done.11, bf16[16,256,128]{1,2,0:T(8,128)(2,1)S(1)} %copy.118, bf16[3,3,256,256]{3,2,1,0:T(8,128)(2,1)} %param.13), kind=kOutput, calls=%fused_computation.69 | convolution fusion | flops 543555584 | bytes 6553600 | tf_op jit(solution)/shard_map/hwi,io->hwo/dot_general | solution.py:52
  99.3 6.1 %pad_maximum_fusion.1 = (bf16[18,257,256]{1,2,0:T(8,128)(2,1)S(1)}, bf16[18,257,256]{1,2,0:T(8,128)(2,1)S(1)}) fusion(bf16[18,1,256]{1,2,0:T(8,128)(2,1)} %copy.126, bf16[1,256,256]{1,2,0:T(8,128)(2,1)S(1)} %collective-permute-done.2, bf16[16,256,128]{1,2,0:T(8,128)(2,1)} %copy-done.10, bf16[16,256,128]{1,2,0:T(8,128)(2,1)S(1)} %copy.118, ...), kind=kLoop, calls=%fused_computation.53 | loop fusion | flops 23685120 | bytes 7114752 | tf_op jit(solution)/shard_map/concatenate | solution.py:26
  105.5 2.7 fusion.101
  108.2 2.8 fusion.105
  111.0 3.0 fusion.103
  113.9 3.0 fusion.107
  117.0 2.7 fusion.109
  119.7 12.1 %add_add_fusion.2 = f32[16,256,256]{1,2,0:T(8,128)S(1)} fusion(f32[16,256,256]{1,2,0:T(8,128)} %fusion.29, f32[16,256,256]{1,2,0:T(8,128)} %fusion.101, f32[16,256,256]{1,2,0:T(8,128)} %fusion.103, f32[16,256,256]{1,2,0:T(8,128)} %fusion.111, f32[16,256,256]{1,2,0:T(8,128)} %fusion.105, f32[16,256,256]{1,2,0:T(8,128)} %fusion.107, ...), kind=kOutput, calls=%fused_computation.32 | convolution fusion | flops 545259520 | bytes 39976960 | tf_op jit(solution)/shard_map/hwi,io->hwo/dot_general | solution.py:52
  132.4 3.7 %collective-permute-start.5 = (bf16[1,256,128]{1,2,0:T(8,128)(2,1)S(1)}, bf16[1,256,128]{1,2,0:T(8,128)(2,1)S(1)}, u32[]{:S(2)}, u32[]{:S(2)}) collective-permute-start(bf16[1,256,128]{1,2,0:T(8,128)(2,1)S(1)} %get-tuple-element.48), channel_id=1, source_target_pairs={{0,8},{8,16},{16,24},{24,32},{32,40},{40,48},{48,56},{56,64},{64,7... | collective-permute-start | bytes 196616 | tf_op jit(solution)/shard_map/ppermute | solution.py:22
  136.1 1.9 collective-permute-start.6
  139.2 3.4 collective-permute-done.6
  144.1 2.0 copy.142
  146.0 2.2 collective-permute-start.7
  148.2 2.0 copy.143
  150.2 5.7 %collective-permute-start.8 = (bf16[18,1,128]{2,0,1:T(8,128)(2,1)}, bf16[18,1,128]{2,0,1:T(8,128)(2,1)}, u32[]{:S(2)}, u32[]{:S(2)}) collective-permute-start(bf16[18,1,128]{2,0,1:T(8,128)(2,1)} %copy.143), channel_id=1, source_target_pairs={{1,0},{2,1},{3,2},{4,3},{5,4},{6,5},{7,6},{9,8},{10,9},{11,10},{12... | collective-permute-start | bytes 13832 | tf_op jit(solution)/shard_map/ppermute | solution.py:25
  155.9 1.9 reverse_bitcast_fusion.1
  157.8 2.3 copy.166
  163.6 5.8 %fusion.17 = bf16[18,258,256]{1,2,0:T(8,128)(2,1)S(1)} fusion(bf16[18,1,256]{1,2,0:T(8,128)(2,1)} %copy.126, bf16[18,1,256]{1,2,0:T(8,128)(2,1)} %copy.120, bf16[1,256,256]{1,2,0:T(8,128)(2,1)S(1)} %collective-permute-done.2, bf16[1,256,256]{1,2,0:T(8,128)(2,1)S(1)} %collective-permute-done.1, bf16[16,256,128]{1,2,0:T(8,128)(2,1)} %copy-done.10, ...), kind=kLoop, calls=%fused_computation.48 | loop fusion | flops 33288192 | bytes 5944320 | tf_op jit(solution)/shard_map/concatenate | solution.py:103
  174.2 2.3 fusion.87
  178.3 5.5 %fusion.51 = (bf16[16,256,128]{1,2,0:T(8,128)(2,1)}, bf16[16,256,128]{1,2,0:T(8,128)(2,1)}, bf16[16,256,128]{1,2,0:T(8,128)(2,1)S(1)}) fusion(bf16[16,256,128]{1,2,0:T(8,128)(2,1)S(1)} %copy-done.19, bf16[16,256,128]{1,2,0:T(8,128)(2,1)S(1)} %copy.118, f32[16,256,256]{1,2,0:T(8,128)S(1)} %copy-done.4, bf16[3,3,256,128]{3,2,1,0:T(8,128)(2,1)} %param.14, ...), kind=kOutput, calls=%fused_computation.91 | convolution fusion | flops 283115520 | bytes 26279936 | tf_op jit(solution)/shard_map/hwi,io->hwo/dot_general | solution.py:52
  183.9 2.4 collective-permute-start.9
  186.3 1.9 collective-permute-start.10
  188.2 3.5 %fusion.161 = f32[16,256,256]{1,2,0:T(8,128)} fusion(bf16[16,256,128]{1,2,0:T(8,128)(2,1)S(1)} %get-tuple-element.23, bf16[3,3,128,256]{2,3,1,0:T(8,128)(2,1)} %reverse_bitcast_fusion.1), kind=kOutput, calls=%fused_computation.239 | convolution fusion | flops 268435456 | bytes 5308416 | tf_op jit(solution)/shard_map/hwi,io->hwo/dot_general | solution.py:52
  191.8 2.3 copy.208
  198.1 2.4 collective-permute-start.11
  201.8 5.9 %collective-permute-start.12 = (bf16[18,1,128]{2,0,1:T(8,128)(2,1)S(1)}, bf16[18,1,128]{2,0,1:T(8,128)(2,1)S(1)}, u32[]{:S(2)}, u32[]{:S(2)}) collective-permute-start(bf16[18,1,128]{2,0,1:T(8,128)(2,1)S(1)} %copy.171), channel_id=1, source_target_pairs={{1,0},{2,1},{3,2},{4,3},{5,4},{6,5},{7,6},{9,8},{10,9},{11,10},{12... | collective-permute-start | bytes 13832 | tf_op jit(solution)/shard_map/ppermute | solution.py:25
  207.7 3.9 %fusion.133 = f32[16,256,256]{1,2,0:T(8,128)} fusion(bf16[16,256,128]{1,2,0:T(8,128)(2,1)} %copy-done.1, bf16[1,256,128]{1,2,0:T(8,128)(2,1)S(1)} %collective-permute-done.9, bf16[3,3,128,256]{2,3,1,0:T(8,128)(2,1)} %reverse_bitcast_fusion.1), kind=kOutput, calls=%fused_computation.190 | convolution fusion | flops 270532608 | bytes 5373952 | tf_op jit(solution)/shard_map/hwi,io->hwo/dot_general | solution.py:52
  211.6 3.6 %fusion.123 = f32[16,256,256]{1,2,0:T(8,128)} fusion(bf16[1,256,128]{1,2,0:T(8,128)(2,1)S(1)} %collective-permute-done.10, bf16[16,256,128]{1,2,0:T(8,128)(2,1)S(1)} %copy-done.2, bf16[3,3,128,256]{2,3,1,0:T(8,128)(2,1)} %reverse_bitcast_fusion.1), kind=kOutput, calls=%fused_computation.179 | convolution fusion | flops 270532608 | bytes 5373952 | tf_op jit(solution)/shard_map/hwi,io->hwo/dot_general | solution.py:52
  217.4 2.9 pad_maximum_fusion.10
  220.3 2.8 fusion.127
  223.1 2.8 fusion.131
  225.9 2.8 fusion.129
  228.6 2.8 fusion.135
  231.4 2.7 fusion.125
  235.0 13.2 %add_add_fusion.1 = f32[16,256,256]{1,2,0:T(8,128)} fusion(f32[16,256,256]{1,2,0:T(8,128)} %fusion.123, f32[16,256,256]{1,2,0:T(8,128)} %fusion.125, f32[16,256,256]{1,2,0:T(8,128)} %fusion.127, f32[16,256,256]{1,2,0:T(8,128)S(1)} %copy-done.12, f32[16,256,256]{1,2,0:T(8,128)} %fusion.129, f32[16,256,256]{1,2,0:T(8,128)} %fusion.131, ...), kind=kOutput, calls=%fused_computation.31 | convolution fusion | flops 276824064 | bytes 38862848 | tf_op jit(solution)/shard_map/hwi,io->hwo/dot_general | solution.py:52
  248.2 2.4 fusion.57
  250.6 5.1 %collective-permute-start.13 = (bf16[1,256,256]{1,2,0:T(8,128)(2,1)S(1)}, bf16[1,256,256]{1,2,0:T(8,128)(2,1)S(1)}, u32[]{:S(2)}, u32[]{:S(2)}) collective-permute-start(bf16[1,256,256]{1,2,0:T(8,128)(2,1)S(1)} %get-tuple-element.36), channel_id=1, source_target_pairs={{0,8},{8,16},{16,24},{24,32},{32,40},{40,48},{48,56},{56,64},{64,7... | collective-permute-start | bytes 393224 | tf_op jit(solution)/shard_map/ppermute | solution.py:22
  255.7 1.9 collective-permute-start.14
  257.7 3.7 %fusion.115 = f32[16,256,256]{1,2,0:T(8,128)} fusion(bf16[16,256,128]{1,2,0:T(8,128)(2,1)S(1)} %fusion.57, bf16[16,256,128]{1,2,0:T(8,128)(2,1)S(1)} %copy-done.6, bf16[3,3,256,256]{3,2,1,0:T(8,128)(2,1)} %reverse_bitcast_fusion), kind=kOutput, calls=%fused_computation.161 | convolution fusion | flops 541065216 | bytes 6422528 | tf_op jit(solution)/shard_map/hwi,io->hwo/dot_general | solution.py:52
  263.1 2.0 fusion.202
  267.0 1.9 collective-permute-start.15
  270.7 6.1 %collective-permute-start.16 = (bf16[18,1,256]{2,0,1:T(8,128)(2,1)S(1)}, bf16[18,1,256]{2,0,1:T(8,128)(2,1)S(1)}, u32[]{:S(2)}, u32[]{:S(2)}) collective-permute-start(bf16[18,1,256]{2,0,1:T(8,128)(2,1)S(1)} %copy.187), channel_id=1, source_target_pairs={{1,0},{2,1},{3,2},{4,3},{5,4},{6,5},{7,6},{9,8},{10,9},{11,10},{12... | collective-permute-start | bytes 27656 | tf_op jit(solution)/shard_map/ppermute | solution.py:25
  276.8 3.9 %fusion.35 = f32[16,256,256]{1,2,0:T(8,128)} fusion(bf16[16,256,128]{1,2,0:T(8,128)(2,1)} %copy-done.8, bf16[16,256,128]{1,2,0:T(8,128)(2,1)S(1)} %copy-done.7, bf16[1,256,256]{1,2,0:T(8,128)(2,1)S(1)} %collective-permute-done.13, bf16[3,3,256,256]{3,2,1,0:T(8,128)(2,1)} %reverse_bitcast_fusion), kind=kOutput, calls=%fused_computation.75 | convolution fusion | flops 543555584 | bytes 6553600 | tf_op jit(solution)/shard_map/hwi,io->hwo/dot_general | solution.py:52
  280.7 3.7 %fusion.41 = f32[16,256,256]{1,2,0:T(8,128)} fusion(bf16[1,256,256]{1,2,0:T(8,128)(2,1)S(1)} %collective-permute-done.14, bf16[16,256,128]{1,2,0:T(8,128)(2,1)S(1)} %copy-done.9, bf16[16,256,128]{1,2,0:T(8,128)(2,1)S(1)} %copy-done.7, bf16[3,3,256,256]{3,2,1,0:T(8,128)(2,1)} %reverse_bitcast_fusion), kind=kOutput, calls=%fused_computation.81 | convolution fusion | flops 543555584 | bytes 6553600 | tf_op jit(solution)/shard_map/hwi,io->hwo/dot_general | solution.py:52
  287.4 6.1 %maximum_maximum_fusion.1 = (bf16[18,257,256]{1,2,0:T(8,128)(2,1)S(1)}, bf16[18,257,256]{1,2,0:T(8,128)(2,1)S(1)}) fusion(bf16[1,256,256]{1,2,0:T(8,128)(2,1)S(1)} %collective-permute-done.14, bf16[16,256,128]{1,2,0:T(8,128)(2,1)} %copy-done.8, bf16[16,256,128]{1,2,0:T(8,128)(2,1)S(1)} %copy-done.7, bf16[1,256,256]{1,2,0:T(8,128)(2,1)S(1)} %collective-permute-done.13, ...), kind=kLoop, calls=%fused_computation.54 | loop fusion | flops 23685120 | bytes 7114752 | tf_op jit(solution)/shard_map/concatenate | solution.py:26
  297.1 2.8 fusion.68
  299.9 3.8 %add_add_fusion = f32[16,256,256]{1,2,0:T(8,128)S(1)} fusion(f32[16,256,256]{1,2,0:T(8,128)S(1)} %fusion.71, f32[16,256,256]{1,2,0:T(8,128)} %fusion.35, bf16[18,257,256]{1,2,0:T(8,128)(2,1)S(1)} %get-tuple-element.29, bf16[3,3,256,256]{3,2,1,0:T(8,128)(2,1)S(1)} %copy-done.21), kind=kOutput, calls=%fused_computation.30 | convolution fusion | flops 538968064 | bytes 14811136 | tf_op jit(solution)/shard_map/hwi,io->hwo/dot_general | solution.py:52
  304.7 3.8 %convolution_select_fusion = f32[16,256,9]{1,2,0:T(8,128)S(1)} fusion(f32[16,256,256]{1,2,0:T(8,128)S(1)} %fusion.62, f32[16,256,256]{1,2,0:T(8,128)} %fusion.41, f32[16,256,256]{1,2,0:T(8,128)S(1)} %fusion.64, f32[16,256,256]{1,2,0:T(8,128)S(1)} %fusion.66, f32[16,256,256]{1,2,0:T(8,128)S(1)} %copy-done.17, f32[16,256,256]{1,2,0:T(8,128)} %fusion.68, ...), kind=kOutput, calls=%fused_computation.173 | convolution fusion | flops 18010112 | bytes 19042816 | tf_op jit(solution)/shard_map/hwm,km->hwk/dot_general | solution.py:118
  308.6 5.4 %fusion.210 = (bf16[16,2,256,256]{3,2,1,0:T(8,128)(2,1)S(1)}, f32[16,2,256,256]{3,2,1,0:T(8,128)S(1)}) fusion(bf16[16,2,128,256]{3,2,1,0:T(8,128)(2,1)S(1)} %bitcast.263, f32[16,2,128]{2,1,0:T(2,128)S(1)} %bitcast.296, f32[16,2,128]{2,1,0:T(2,128)S(1)} %bitcast.298, f32[16,2,128]{2,1,0:T(2,128)S(1)} %bitcast.300, f32[16,2,128]{2,1,0:T(2,128)S(1)} %bitcast.302, ...), kind=kOutput, calls=%fused_computation.290 | convolution fusion | flops 569376768 | bytes 14974976 | tf_op jit(solution)/shard_map/hbij,hbic->hbjc/dot_general | solution.py:139
  314.3 2.2 collective-permute-start.17
  316.5 6.3 %multiply_convert_fusion = bf16[16,2,128,256]{3,2,1,0:T(8,128)(2,1)} fusion(bf16[16,2,128,256]{3,2,1,0:T(8,128)(2,1)S(1)} %copy-done.28, bf16[16,2,128,256]{3,2,1,0:T(8,128)(2,1)S(1)} %copy-done.26, f32[16,2,128]{2,1,0:T(2,128)S(1)} %bitcast.297, f32[16,2,128]{2,1,0:T(2,128)S(1)} %bitcast.299, f32[16,2,128]{2,1,0:T(2,128)S(1)} %bitcast.301, ...), kind=kOutput, calls=%fused_computation.28 | convolution fusion | flops 575668224 | bytes 6586368 | tf_op jit(solution)/shard_map/hbij,hbjc->hbic/dot_general | solution.py:132
  322.8 18.6 %collective-permute-done.17 = bf16[16,128,256]{2,1,0:T(8,128)(2,1)S(1)} collective-permute-done((bf16[16,128,256]{2,1,0:T(8,128)(2,1)S(1)}, bf16[16,128,256]{2,1,0:T(8,128)(2,1)S(1)}, u32[]{:S(2)}, u32[]{:S(2)}) %collective-permute-start.17) | collective-permute-done | bytes 1048608 | tf_op jit(solution)/shard_map/ppermute | solution.py:14
  (169 shorter events, 49.9 us)
Async XLA Ops:
  0.6 53.5 %copy-start = (bf16[16,256,256]{2,1,0:T(8,128)(2,1)S(1)}, bf16[16,256,256]{2,1,0:T(8,128)(2,1)}, u32[]{:S(2)}) copy-start(bf16[16,256,256]{2,1,0:T(8,128)(2,1)} %param.8) | copy-start | bytes 6291460
  0.6 7.9 %copy-start.29 = (s32[16,256]{1,0:T(8,128)S(1)}, s32[16,256]{1,0:T(8,128)}, u32[]{:S(2)}) copy-start(s32[16,256]{1,0:T(8,128)} %param.11) | copy-start | bytes 49156
  0.7 51.2 %collective-permute-start = (bf16[16,256,256]{2,1,0:T(8,128)(2,1)}, bf16[16,256,256]{2,1,0:T(8,128)(2,1)}, u32[]{:S(2)}, u32[]{:S(2)}) collective-permute-start(bf16[16,256,256]{2,1,0:T(8,128)(2,1)} %param.9), channel_id=1, source_target_pairs={{0,1},{1,2},{2,3},{3,4},{4,5},{5,6},{6,7},{8,9},{9,10},{10,11},{11... | collective-permute-start | bytes 6291464 | tf_op jit(solution)/shard_map/ppermute | solution.py:14
  8.5 44.7 %copy-start.24 = (bf16[16,256,256]{2,1,0:T(8,128)(2,1)S(1)}, bf16[16,256,256]{2,1,0:T(8,128)(2,1)}, u32[]{:S(2)}) copy-start(bf16[16,256,256]{2,1,0:T(8,128)(2,1)} %param.9) | copy-start | bytes 6291460
  8.5 52.5 %copy-start.50 = (s32[9]{0:T(128)}, s32[9]{0:T(128)S(1)}, u32[]{:S(2)}) copy-start(s32[9]{0:T(128)S(1)} %iota_add_fusion) | copy-start | bytes 112
  8.7 45.3 %copy-start.30 = (s32[16,256,1]{1,2,0:T(1,128)}, s32[16,256,1]{1,2,0:T(1,128)S(1)}, u32[]{:S(2)}) copy-start(s32[16,256,1]{1,2,0:T(1,128)S(1)} %get-tuple-element.59) | copy-start | bytes 49156
  8.8 45.3 %copy-start.32 = (s32[16,256,1]{1,2,0:T(1,128)}, s32[16,256,1]{1,2,0:T(1,128)S(1)}, u32[]{:S(2)}) copy-start(s32[16,256,1]{1,2,0:T(1,128)S(1)} %get-tuple-element.60) | copy-start | bytes 49156
  8.8 45.3 %copy-start.34 = (s32[16,256,1]{1,2,0:T(1,128)}, s32[16,256,1]{1,2,0:T(1,128)S(1)}, u32[]{:S(2)}) copy-start(s32[16,256,1]{1,2,0:T(1,128)S(1)} %get-tuple-element.61) | copy-start | bytes 49156
  8.8 45.3 %copy-start.36 = (s32[16,256,1]{1,2,0:T(1,128)}, s32[16,256,1]{1,2,0:T(1,128)S(1)}, u32[]{:S(2)}) copy-start(s32[16,256,1]{1,2,0:T(1,128)S(1)} %get-tuple-element.62) | copy-start | bytes 49156
  8.8 45.3 %copy-start.38 = (s32[16,256,1]{1,2,0:T(1,128)}, s32[16,256,1]{1,2,0:T(1,128)S(1)}, u32[]{:S(2)}) copy-start(s32[16,256,1]{1,2,0:T(1,128)S(1)} %get-tuple-element.63) | copy-start | bytes 49156
  8.8 45.3 %copy-start.40 = (s32[16,256,1]{1,2,0:T(1,128)}, s32[16,256,1]{1,2,0:T(1,128)S(1)}, u32[]{:S(2)}) copy-start(s32[16,256,1]{1,2,0:T(1,128)S(1)} %get-tuple-element.64) | copy-start | bytes 49156
  8.8 45.3 %copy-start.42 = (s32[16,256,1]{1,2,0:T(1,128)}, s32[16,256,1]{1,2,0:T(1,128)S(1)}, u32[]{:S(2)}) copy-start(s32[16,256,1]{1,2,0:T(1,128)S(1)} %get-tuple-element.65) | copy-start | bytes 49156
  8.8 45.3 %copy-start.44 = (s32[16,256,1]{1,2,0:T(1,128)}, s32[16,256,1]{1,2,0:T(1,128)S(1)}, u32[]{:S(2)}) copy-start(s32[16,256,1]{1,2,0:T(1,128)S(1)} %get-tuple-element.66) | copy-start | bytes 49156
  8.8 45.3 %copy-start.46 = (s32[16,256,1]{1,2,0:T(1,128)}, s32[16,256,1]{1,2,0:T(1,128)S(1)}, u32[]{:S(2)}) copy-start(s32[16,256,1]{1,2,0:T(1,128)S(1)} %get-tuple-element.67) | copy-start | bytes 49156
  54.1 6.7 %copy-start.25 = (bf16[16,2,128,256]{3,2,1,0:T(8,128)(2,1)}, bf16[16,2,128,256]{3,2,1,0:T(8,128)(2,1)S(1)}, u32[]{:S(2)}) copy-start(bf16[16,2,128,256]{3,2,1,0:T(8,128)(2,1)S(1)} %get-tuple-element.26) | copy-start | bytes 6291460
  54.1 6.7 %copy-start.27 = (bf16[16,2,128,256]{3,2,1,0:T(8,128)(2,1)}, bf16[16,2,128,256]{3,2,1,0:T(8,128)(2,1)S(1)}, u32[]{:S(2)}) copy-start(bf16[16,2,128,256]{3,2,1,0:T(8,128)(2,1)S(1)} %get-tuple-element.27) | copy-start | bytes 6291460
  54.2 6.9 %copy-start.48 = (bf16[9,128]{1,0:T(8,128)(2,1)S(1)}, bf16[9,128]{1,0:T(8,128)(2,1)}, u32[]{:S(2)}) copy-start(bf16[9,128]{1,0:T(8,128)(2,1)} %param.12) | copy-start | bytes 6916
  63.1 11.8 %copy-start.10 = (bf16[16,256,128]{1,2,0:T(8,128)(2,1)}, bf16[16,256,128]{1,2,0:T(8,128)(2,1)S(1)}, u32[]{:S(2)}) copy-start(bf16[16,256,128]{1,2,0:T(8,128)(2,1)S(1)} %get-tuple-element.68) | copy-start | bytes 3145732
  63.1 10.2 %collective-permute-start.1 = (bf16[1,256,256]{1,2,0:T(8,128)(2,1)S(1)}, bf16[1,256,256]{1,2,0:T(8,128)(2,1)S(1)}, u32[]{:S(2)}, u32[]{:S(2)}) collective-permute-start(bf16[1,256,256]{1,2,0:T(8,128)(2,1)S(1)} %get-tuple-element.38), channel_id=1, source_target_pairs={{0,8},{8,16},{16,24},{24,32},{32,40},{40,48},{48,56},{56,64},{64,7... | collective-permute-start | bytes 393224 | tf_op jit(solution)/shard_map/ppermute | solution.py:22
  67.7 7.2 %collective-permute-start.2 = (bf16[1,256,256]{1,2,0:T(8,128)(2,1)S(1)}, bf16[1,256,256]{1,2,0:T(8,128)(2,1)S(1)}, u32[]{:S(2)}, u32[]{:S(2)}) collective-permute-start(bf16[1,256,256]{1,2,0:T(8,128)(2,1)S(1)} %get-tuple-element.39), channel_id=1, source_target_pairs={{8,0},{16,8},{24,16},{32,24},{40,32},{48,40},{56,48},{64,56},{72,6... | collective-permute-start | bytes 393224 | tf_op jit(solution)/shard_map/ppermute | solution.py:25
  78.9 17.5 %collective-permute-start.3 = (bf16[18,1,256]{2,0,1:T(8,128)(2,1)S(1)}, bf16[18,1,256]{2,0,1:T(8,128)(2,1)S(1)}, u32[]{:S(2)}, u32[]{:S(2)}) collective-permute-start(bf16[18,1,256]{2,0,1:T(8,128)(2,1)S(1)} %copy.119), channel_id=1, source_target_pairs={{0,1},{1,2},{2,3},{3,4},{4,5},{5,6},{6,7},{8,9},{9,10},{10,11},{11... | collective-permute-start | bytes 27656 | tf_op jit(solution)/shard_map/ppermute | solution.py:22
  83.8 8.9 %copy-start.11 = (bf16[16,256,128]{1,2,0:T(8,128)(2,1)S(1)}, bf16[16,256,128]{1,2,0:T(8,128)(2,1)}, u32[]{:S(2)}) copy-start(bf16[16,256,128]{1,2,0:T(8,128)(2,1)} %copy-done.10) | copy-start | bytes 3145732
  83.8 14.0 %collective-permute-start.4 = (bf16[18,1,256]{2,0,1:T(8,128)(2,1)S(1)}, bf16[18,1,256]{2,0,1:T(8,128)(2,1)S(1)}, u32[]{:S(2)}, u32[]{:S(2)}) collective-permute-start(bf16[18,1,256]{2,0,1:T(8,128)(2,1)S(1)} %copy.125), channel_id=1, source_target_pairs={{1,0},{2,1},{3,2},{4,3},{5,4},{6,5},{7,6},{9,8},{10,9},{11,10},{12... | collective-permute-start | bytes 27656 | tf_op jit(solution)/shard_map/ppermute | solution.py:25
  99.3 6.2 %copy-start.20 = (bf16[3,3,256,256]{3,2,1,0:T(8,128)(2,1)S(1)}, bf16[3,3,256,256]{3,2,1,0:T(8,128)(2,1)}, u32[]{:S(2)}) copy-start(bf16[3,3,256,256]{3,2,1,0:T(8,128)(2,1)} %param.13) | copy-start | bytes 3538948
  131.8 10.9 %copy-start.3 = (f32[16,256,256]{1,2,0:T(8,128)}, f32[16,256,256]{1,2,0:T(8,128)S(1)}, u32[]{:S(2)}) copy-start(f32[16,256,256]{1,2,0:T(8,128)S(1)} %add_add_fusion.2) | copy-start | bytes 12582916
  131.8 6.2 %copy-start.18 = (bf16[3,3,256,256]{2,3,1,0:T(8,128)(2,1)S(1)}, bf16[3,3,256,256]{2,3,1,0:T(8,128)(2,1)}, u32[]{:S(2)}) copy-start(bf16[3,3,256,256]{2,3,1,0:T(8,128)(2,1)} %copy.182) | copy-start | bytes 3538948
  132.4 11.6 %copy-start.16 = (bf16[16,256,128]{1,2,0:T(8,128)(2,1)}, bf16[16,256,128]{1,2,0:T(8,128)(2,1)S(1)}, u32[]{:S(2)}) copy-start(bf16[16,256,128]{1,2,0:T(8,128)(2,1)S(1)} %fusion.54) | copy-start | bytes 3145732
  132.4 6.8 %collective-permute-start.5 = (bf16[1,256,128]{1,2,0:T(8,128)(2,1)S(1)}, bf16[1,256,128]{1,2,0:T(8,128)(2,1)S(1)}, u32[]{:S(2)}, u32[]{:S(2)}) collective-permute-start(bf16[1,256,128]{1,2,0:T(8,128)(2,1)S(1)} %get-tuple-element.48), channel_id=1, source_target_pairs={{0,8},{8,16},{16,24},{24,32},{32,40},{40,48},{48,56},{56,64},{64,7... | collective-permute-start | bytes 196616 | tf_op jit(solution)/shard_map/ppermute | solution.py:22
  136.1 6.5 %collective-permute-start.6 = (bf16[1,256,128]{1,2,0:T(8,128)(2,1)S(1)}, bf16[1,256,128]{1,2,0:T(8,128)(2,1)S(1)}, u32[]{:S(2)}, u32[]{:S(2)}) collective-permute-start(bf16[1,256,128]{1,2,0:T(8,128)(2,1)S(1)} %get-tuple-element.49), channel_id=1, source_target_pairs={{8,0},{16,8},{24,16},{32,24},{40,32},{48,40},{56,48},{64,56},{72,6... | collective-permute-start | bytes 196616 | tf_op jit(solution)/shard_map/ppermute | solution.py:25
  146.0 14.0 %collective-permute-start.7 = (bf16[18,1,128]{2,0,1:T(8,128)(2,1)}, bf16[18,1,128]{2,0,1:T(8,128)(2,1)}, u32[]{:S(2)}, u32[]{:S(2)}) collective-permute-start(bf16[18,1,128]{2,0,1:T(8,128)(2,1)} %copy.142), channel_id=1, source_target_pairs={{0,1},{1,2},{2,3},{3,4},{4,5},{5,6},{6,7},{8,9},{9,10},{10,11},{11... | collective-permute-start | bytes 13832 | tf_op jit(solution)/shard_map/ppermute | solution.py:22
  150.2 11.6 %collective-permute-start.8 = (bf16[18,1,128]{2,0,1:T(8,128)(2,1)}, bf16[18,1,128]{2,0,1:T(8,128)(2,1)}, u32[]{:S(2)}, u32[]{:S(2)}) collective-permute-start(bf16[18,1,128]{2,0,1:T(8,128)(2,1)} %copy.143), channel_id=1, source_target_pairs={{1,0},{2,1},{3,2},{4,3},{5,4},{6,5},{7,6},{9,8},{10,9},{11,10},{12... | collective-permute-start | bytes 13832 | tf_op jit(solution)/shard_map/ppermute | solution.py:25
  163.6 5.8 %copy-start.22 = (bf16[3,3,256,128]{3,2,1,0:T(8,128)(2,1)S(1)}, bf16[3,3,256,128]{3,2,1,0:T(8,128)(2,1)}, u32[]{:S(2)}) copy-start(bf16[3,3,256,128]{3,2,1,0:T(8,128)(2,1)} %param.14) | copy-start | bytes 1769476
  174.2 4.1 %copy-start.4 = (f32[16,256,256]{1,2,0:T(8,128)S(1)}, f32[16,256,256]{1,2,0:T(8,128)}, u32[]{:S(2)}) copy-start(f32[16,256,256]{1,2,0:T(8,128)} %copy-done.3) | copy-start | bytes 12582916
  174.2 4.1 %copy-start.19 = (bf16[16,256,128]{1,2,0:T(8,128)(2,1)S(1)}, bf16[16,256,128]{1,2,0:T(8,128)(2,1)}, u32[]{:S(2)}) copy-start(bf16[16,256,128]{1,2,0:T(8,128)(2,1)} %copy.166) | copy-start | bytes 3145732
  183.9 4.4 %copy-start.1 = (bf16[16,256,128]{1,2,0:T(8,128)(2,1)}, bf16[16,256,128]{1,2,0:T(8,128)(2,1)S(1)}, u32[]{:S(2)}) copy-start(bf16[16,256,128]{1,2,0:T(8,128)(2,1)S(1)} %get-tuple-element.23) | copy-start | bytes 3145732
  183.9 10.2 %collective-permute-start.9 = (bf16[1,256,128]{1,2,0:T(8,128)(2,1)S(1)}, bf16[1,256,128]{1,2,0:T(8,128)(2,1)S(1)}, u32[]{:S(2)}, u32[]{:S(2)}) collective-permute-start(bf16[1,256,128]{1,2,0:T(8,128)(2,1)S(1)} %get-tuple-element.46), channel_id=1, source_target_pairs={{0,8},{8,16},{16,24},{24,32},{32,40},{40,48},{48,56},{56,64},{64,7... | collective-permute-start | bytes 196616 | tf_op jit(solution)/shard_map/ppermute | solution.py:22
  186.3 7.8 %collective-permute-start.10 = (bf16[1,256,128]{1,2,0:T(8,128)(2,1)S(1)}, bf16[1,256,128]{1,2,0:T(8,128)(2,1)S(1)}, u32[]{:S(2)}, u32[]{:S(2)}) collective-permute-start(bf16[1,256,128]{1,2,0:T(8,128)(2,1)S(1)} %get-tuple-element.47), channel_id=1, source_target_pairs={{8,0},{16,8},{24,16},{32,24},{40,32},{48,40},{56,48},{64,56},{72,6... | collective-permute-start | bytes 196616 | tf_op jit(solution)/shard_map/ppermute | solution.py:25
  198.1 17.1 %collective-permute-start.11 = (bf16[18,1,128]{2,0,1:T(8,128)(2,1)S(1)}, bf16[18,1,128]{2,0,1:T(8,128)(2,1)S(1)}, u32[]{:S(2)}, u32[]{:S(2)}) collective-permute-start(bf16[18,1,128]{2,0,1:T(8,128)(2,1)S(1)} %copy.167), channel_id=1, source_target_pairs={{0,1},{1,2},{2,3},{3,4},{4,5},{5,6},{6,7},{8,9},{9,10},{10,11},{11... | collective-permute-start | bytes 13832 | tf_op jit(solution)/shard_map/ppermute | solution.py:22
  201.8 9.8 %copy-start.2 = (bf16[16,256,128]{1,2,0:T(8,128)(2,1)S(1)}, bf16[16,256,128]{1,2,0:T(8,128)(2,1)}, u32[]{:S(2)}) copy-start(bf16[16,256,128]{1,2,0:T(8,128)(2,1)} %copy-done.1) | copy-start | bytes 3145732
  201.8 14.5 %collective-permute-start.12 = (bf16[18,1,128]{2,0,1:T(8,128)(2,1)S(1)}, bf16[18,1,128]{2,0,1:T(8,128)(2,1)S(1)}, u32[]{:S(2)}, u32[]{:S(2)}) collective-permute-start(bf16[18,1,128]{2,0,1:T(8,128)(2,1)S(1)} %copy.171), channel_id=1, source_target_pairs={{1,0},{2,1},{3,2},{4,3},{5,4},{6,5},{7,6},{9,8},{10,9},{11,10},{12... | collective-permute-start | bytes 13832 | tf_op jit(solution)/shard_map/ppermute | solution.py:25
  220.3 5.6 %copy-start.15 = (bf16[18,257,128]{1,2,0:T(8,128)(2,1)}, bf16[18,257,128]{1,2,0:T(8,128)(2,1)S(1)}, u32[]{:S(2)}) copy-start(bf16[18,257,128]{1,2,0:T(8,128)(2,1)S(1)} %get-tuple-element.40) | copy-start | bytes 3552772
  228.6 5.5 %copy-start.13 = (f32[16,256,256]{1,2,0:T(8,128)S(1)}, f32[16,256,256]{1,2,0:T(8,128)}, u32[]{:S(2)}) copy-start(f32[16,256,256]{1,2,0:T(8,128)} %fusion.133) | copy-start | bytes 12582916
  235.0 13.2 %copy-start.5 = (f32[16,256,256]{1,2,0:T(8,128)S(1)}, f32[16,256,256]{1,2,0:T(8,128)}, u32[]{:S(2)}) copy-start(f32[16,256,256]{1,2,0:T(8,128)} %copy-done.3) | copy-start | bytes 12582916
  250.6 12.3 %copy-start.8 = (bf16[16,256,128]{1,2,0:T(8,128)(2,1)}, bf16[16,256,128]{1,2,0:T(8,128)(2,1)S(1)}, u32[]{:S(2)}) copy-start(bf16[16,256,128]{1,2,0:T(8,128)(2,1)S(1)} %fusion.57) | copy-start | bytes 3145732
  250.6 10.7 %collective-permute-start.13 = (bf16[1,256,256]{1,2,0:T(8,128)(2,1)S(1)}, bf16[1,256,256]{1,2,0:T(8,128)(2,1)S(1)}, u32[]{:S(2)}, u32[]{:S(2)}) collective-permute-start(bf16[1,256,256]{1,2,0:T(8,128)(2,1)S(1)} %get-tuple-element.36), channel_id=1, source_target_pairs={{0,8},{8,16},{16,24},{24,32},{32,40},{40,48},{48,56},{56,64},{64,7... | collective-permute-start | bytes 393224 | tf_op jit(solution)/shard_map/ppermute | solution.py:22
  255.7 7.2 %collective-permute-start.14 = (bf16[1,256,256]{1,2,0:T(8,128)(2,1)S(1)}, bf16[1,256,256]{1,2,0:T(8,128)(2,1)S(1)}, u32[]{:S(2)}, u32[]{:S(2)}) collective-permute-start(bf16[1,256,256]{1,2,0:T(8,128)(2,1)S(1)} %get-tuple-element.37), channel_id=1, source_target_pairs={{8,0},{16,8},{24,16},{32,24},{40,32},{48,40},{56,48},{64,56},{72,6... | collective-permute-start | bytes 393224 | tf_op jit(solution)/shard_map/ppermute | solution.py:25
  263.1 13.6 %copy-start.7 = (bf16[16,256,128]{1,2,0:T(8,128)(2,1)S(1)}, bf16[16,256,128]{1,2,0:T(8,128)(2,1)}, u32[]{:S(2)}) copy-start(bf16[16,256,128]{1,2,0:T(8,128)(2,1)} %get-tuple-element.21) | copy-start | bytes 3145732
  267.0 17.4 %collective-permute-start.15 = (bf16[18,1,256]{2,0,1:T(8,128)(2,1)S(1)}, bf16[18,1,256]{2,0,1:T(8,128)(2,1)S(1)}, u32[]{:S(2)}, u32[]{:S(2)}) collective-permute-start(bf16[18,1,256]{2,0,1:T(8,128)(2,1)S(1)} %copy.180), channel_id=1, source_target_pairs={{0,1},{1,2},{2,3},{3,4},{4,5},{5,6},{6,7},{8,9},{9,10},{10,11},{11... | collective-permute-start | bytes 27656 | tf_op jit(solution)/shard_map/ppermute | solution.py:22
  270.7 10.0 %copy-start.9 = (bf16[16,256,128]{1,2,0:T(8,128)(2,1)S(1)}, bf16[16,256,128]{1,2,0:T(8,128)(2,1)}, u32[]{:S(2)}) copy-start(bf16[16,256,128]{1,2,0:T(8,128)(2,1)} %copy-done.8) | copy-start | bytes 3145732
  270.7 15.1 %collective-permute-start.16 = (bf16[18,1,256]{2,0,1:T(8,128)(2,1)S(1)}, bf16[18,1,256]{2,0,1:T(8,128)(2,1)S(1)}, u32[]{:S(2)}, u32[]{:S(2)}) collective-permute-start(bf16[18,1,256]{2,0,1:T(8,128)(2,1)S(1)} %copy.187), channel_id=1, source_target_pairs={{1,0},{2,1},{3,2},{4,3},{5,4},{6,5},{7,6},{9,8},{10,9},{11,10},{12... | collective-permute-start | bytes 27656 | tf_op jit(solution)/shard_map/ppermute | solution.py:25
  287.4 6.1 %copy-start.21 = (bf16[3,3,256,256]{3,2,1,0:T(8,128)(2,1)S(1)}, bf16[3,3,256,256]{3,2,1,0:T(8,128)(2,1)}, u32[]{:S(2)}) copy-start(bf16[3,3,256,256]{3,2,1,0:T(8,128)(2,1)} %reverse_bitcast_fusion) | copy-start | bytes 3538948
  299.8 4.7 %copy-start.17 = (f32[16,256,256]{1,2,0:T(8,128)S(1)}, f32[16,256,256]{1,2,0:T(8,128)}, u32[]{:S(2)}) copy-start(f32[16,256,256]{1,2,0:T(8,128)} %fusion.115) | copy-start | bytes 12582916
  299.8 4.7 %copy-start.49 = (bf16[9,128]{1,0:T(8,128)(2,1)S(1)}, bf16[9,128]{1,0:T(8,128)(2,1)}, u32[]{:S(2)}) copy-start(bf16[9,128]{1,0:T(8,128)(2,1)} %param.12) | copy-start | bytes 6916
  299.8 4.7 %copy-start.51 = (s32[9]{0:T(128)S(1)}, s32[9]{0:T(128)}, u32[]{:S(2)}) copy-start(s32[9]{0:T(128)} %copy-done.50) | copy-start | bytes 112
  304.6 4.0 %copy-start.31 = (s32[16,256,1]{1,2,0:T(1,128)S(1)}, s32[16,256,1]{1,2,0:T(1,128)}, u32[]{:S(2)}) copy-start(s32[16,256,1]{1,2,0:T(1,128)} %copy-done.30) | copy-start | bytes 49156
  304.6 4.0 %copy-start.33 = (s32[16,256,1]{1,2,0:T(1,128)S(1)}, s32[16,256,1]{1,2,0:T(1,128)}, u32[]{:S(2)}) copy-start(s32[16,256,1]{1,2,0:T(1,128)} %copy-done.32) | copy-start | bytes 49156
  304.6 4.0 %copy-start.35 = (s32[16,256,1]{1,2,0:T(1,128)S(1)}, s32[16,256,1]{1,2,0:T(1,128)}, u32[]{:S(2)}) copy-start(s32[16,256,1]{1,2,0:T(1,128)} %copy-done.34) | copy-start | bytes 49156
  304.6 4.0 %copy-start.37 = (s32[16,256,1]{1,2,0:T(1,128)S(1)}, s32[16,256,1]{1,2,0:T(1,128)}, u32[]{:S(2)}) copy-start(s32[16,256,1]{1,2,0:T(1,128)} %copy-done.36) | copy-start | bytes 49156
  304.6 4.0 %copy-start.39 = (s32[16,256,1]{1,2,0:T(1,128)S(1)}, s32[16,256,1]{1,2,0:T(1,128)}, u32[]{:S(2)}) copy-start(s32[16,256,1]{1,2,0:T(1,128)} %copy-done.38) | copy-start | bytes 49156
  304.6 4.0 %copy-start.41 = (s32[16,256,1]{1,2,0:T(1,128)S(1)}, s32[16,256,1]{1,2,0:T(1,128)}, u32[]{:S(2)}) copy-start(s32[16,256,1]{1,2,0:T(1,128)} %copy-done.40) | copy-start | bytes 49156
  304.6 4.0 %copy-start.43 = (s32[16,256,1]{1,2,0:T(1,128)S(1)}, s32[16,256,1]{1,2,0:T(1,128)}, u32[]{:S(2)}) copy-start(s32[16,256,1]{1,2,0:T(1,128)} %copy-done.42) | copy-start | bytes 49156
  304.6 4.0 %copy-start.45 = (s32[16,256,1]{1,2,0:T(1,128)S(1)}, s32[16,256,1]{1,2,0:T(1,128)}, u32[]{:S(2)}) copy-start(s32[16,256,1]{1,2,0:T(1,128)} %copy-done.44) | copy-start | bytes 49156
  304.6 4.0 %copy-start.47 = (s32[16,256,1]{1,2,0:T(1,128)S(1)}, s32[16,256,1]{1,2,0:T(1,128)}, u32[]{:S(2)}) copy-start(s32[16,256,1]{1,2,0:T(1,128)} %copy-done.46) | copy-start | bytes 49156
  314.3 27.1 %collective-permute-start.17 = (bf16[16,128,256]{2,1,0:T(8,128)(2,1)S(1)}, bf16[16,128,256]{2,1,0:T(8,128)(2,1)S(1)}, u32[]{:S(2)}, u32[]{:S(2)}) collective-permute-start(bf16[16,128,256]{2,1,0:T(8,128)(2,1)S(1)} %get-tuple-element.25), channel_id=1, source_target_pairs={{1,0},{2,1},{3,2},{4,3},{5,4},{6,5},{7,6},{9,8},{10,9},{11,10},{12... | collective-permute-start | bytes 3145736 | tf_op jit(solution)/shard_map/ppermute | solution.py:14
  (6 other events, 17.5 us)
where the time goes:
time: 350 us; the launch traced here: 344 us
  matrix products  136 us (39%)
  waiting for transfers between devices  68.2 us (19%)
  starting transfers between devices  61.6 us (18%)
  local copies, waits for them, and re-layouts  49.6 us (14%)
  other arithmetic  26.9 us (8%)
    dot_general x36, matrix products, conv_local(): jnp.einsum('hwi,io->hwo', padded[row_off:row_off + row_count, col_off:col...  112 us
    ppermute x2, waiting for transfers between devices, from_behind(): return lax.ppermute(array, axis, pairs)  61.7 us
    ppermute x8, starting transfers between devices, padded_2(): lax.ppermute(lax.slice_in_dim(block, 0, width, axis=dim), axis, backward)  30.1 us
    ppermute x8, starting transfers between devices, padded_2(): lax.ppermute(lax.slice_in_dim(block, block.shape[dim] - width, None, axis...  25.4 us
    concatenate x7, other arithmetic, padded_2(): block = jnp.concatenate([low, block, high], axis=dim)  17 us
    slice x9, local copies, waits for them, and re-layouts, padded_2(): lax.slice_in_dim(block, block.shape[dim] - width, None, axis=dim)  12.2 us
    unnamed x109, local copies, waits for them, and re-layouts  10.6 us
    slice x5, local copies, waits for them, and re-layouts, padded_2(): lax.slice_in_dim(block, 0, width, axis=dim)  8.2 us
  transfers between devices with their start and end apart: 18, of which 5 were waited for; matrix products, arithmetic and copies ran while one was open for 19% of the time, Pallas kernels for 0%

commit v1 on v0

v1 whole, which is shorter than its diff:
```python
import math

import jax
import jax.numpy as jnp
from jax import lax
from jax.experimental import pallas as pl
from jax.experimental.pallas import tpu as pltpu
from jax.sharding import PartitionSpec as P

B = 128
HALO = 4
EDGE = 16
WC = B + EDGE
F32 = jnp.float32
BF16 = jnp.bfloat16
VMEM_LIMIT = 56 * 1024 * 1024


def shift(array, axis, by):
    size = lax.axis_size(axis)
    pairs = [(i, i + by) for i in range(size) if 0 <= i + by < size]
    return lax.ppermute(array, axis, pairs)


def dot_nt(a, b):
    return lax.dot_general(a, b, (((1,), (1,)), ((), ())), preferred_element_type=F32)


def dot(a, b):
    return jnp.dot(a, b, preferred_element_type=F32)


def iota(shape, dim):
    return lax.broadcasted_iota(jnp.int32, shape, dim)


def lane_gather(values, index):
    return jnp.take_along_axis(values, index, axis=1, mode="promise_in_bounds")


def sublane_gather(values, index):
    return jnp.take_along_axis(values, index, axis=0, mode="promise_in_bounds")


def down_lanes(row):
    return jnp.transpose(jnp.broadcast_to(row, (B, B)), (1, 0))


def pick_taps(far, near, disp, taps, radius, scale):
    count = far.shape[0]
    pixel = iota((count, B), 0)
    lane = iota((count, B), 1)
    merged = jnp.where(lane > pixel, far, near)
    level = disp + lane - radius
    usable = (level >= 0) & (level < B) & (lane < taps)
    picked = lane_gather(merged, (pixel - level) & (B - 1))
    return (jnp.where(usable, picked, 0.0) * scale).astype(BF16)


def silu(v):
    return v * jax.nn.sigmoid(v)


def right_corr_kernel(
    taps, radius, scale, left_ref, own_ref, disp_ref, edge_ref, weight_ref, mot_ref, pre_ref, pad_ref
):
    rows = left_ref.shape[0]
    pad_ref[...] = jnp.zeros_like(pad_ref)
    weight = weight_ref[...]
    for r in range(rows):
        left = left_ref[r]
        far = dot_nt(left, own_ref[r, :B])
        near = dot_nt(left, own_ref[r, B:])
        disp = down_lanes(disp_ref[r])
        picked = pick_taps(far, near, disp, taps, radius, scale)
        pre = dot(picked, weight)
        pre_ref[r, :B] = pre
        mot_ref[r, :B] = silu(pre).astype(BF16)
        edge = edge_ref[r]
        chan = own_ref.shape[2]
        pad_ref[:EDGE] = edge[:, chan : 2 * chan]
        left = edge[:, :chan]
        far = dot_nt(left, own_ref[r, B:])
        near = dot_nt(left, pad_ref[...])
        disp = edge[:, 2 * chan + 2 * B : 2 * chan + 3 * B].astype(F32).astype(jnp.int32)
        picked = pick_taps(far, near, disp, taps, radius, scale)
        pre = dot(picked, weight)
        pre_ref[r, B:] = pre
        mot_ref[r, B:] = silu(pre).astype(BF16)


def left_corr_kernel(
    taps,
    radius,
    scale,
    left_ref,
    own_ref,
    before_ref,
    disp_ref,
    edge_mot_ref,
    edge_pre_ref,
    weight_ref,
    mot_ref,
    pre_ref,
):
    rows = left_ref.shape[0]
    weight = weight_ref[...]
    for r in range(rows):
        left = left_ref[r]
        far = dot_nt(left, before_ref[r])
        near = dot_nt(left, own_ref[r])
        disp = down_lanes(disp_ref[r])
        picked = pick_taps(far, near, disp, taps, radius, scale)
        pre = dot(picked, weight)
        pre_ref[r, :B] = pre
        mot_ref[r, :B] = silu(pre).astype(BF16)
        pre_ref[r, B:] = edge_pre_ref[r]
        mot_ref[r, B:] = edge_mot_ref[r]


def store3(buf, row, at, step, value):
    buf[row, :, at : at + B] = pltpu.roll(value, 1, 0).astype(BF16)
    buf[row, :, at + step : at + step + B] = value.astype(BF16)
    buf[row, :, at + 2 * step : at + 2 * step + B] = pltpu.roll(value, WC - 1, 0).astype(BF16)


def chunks(start, stop, size):
    return [list(range(i, min(i + size, stop))) for i in range(start, stop, size)]


def gather_rows(buf, rows):
    return jnp.concatenate([buf[r] for r in rows], axis=0)


def gru_kernel(
    hg_ref,
    hgt_ref,
    hgb_ref,
    mot_ref,
    mott_ref,
    motb_ref,
    pre_ref,
    wg_ref,
    wc_ref,
    wcb_ref,
    wgb_ref,
    nh_ref,
    pg_ref,
    hm_ref,
    rm_ref,
    cg_ref,
    gg_ref,
    g_ref,
    up_ref,
    rs_ref,
    cb_ref,
):
    rows = hg_ref.shape[0]
    total = rows + 2 * HALO

    def piece(top, mid, low, row):
        if row < HALO:
            return top[row]
        if row < HALO + rows:
            return mid[row - HALO]
        return low[row - HALO - rows]

    for row in range(total):
        hg = piece(hgt_ref, hg_ref, hgb_ref, row)
        g_ref[row] = hg[:, B:]
        store3(hm_ref, row, 0, 2 * B, hg[:, :B].astype(F32))
        mot = piece(mott_ref, mot_ref, motb_ref, row).astype(F32)
        left = pltpu.roll(mot, 1, 0).astype(BF16)
        mid = mot.astype(BF16)
        right = pltpu.roll(mot, WC - 1, 0).astype(BF16)
        for buf in (hm_ref, rm_ref):
            buf[row, :, B : 2 * B] = left
            buf[row, :, 3 * B : 4 * B] = mid
            buf[row, :, 5 * B : 6 * B] = right

    def hidden_at(row):
        return hm_ref[row, :, 2 * B : 3 * B].astype(F32)

    for group in chunks(1, total - 1, 4):
        acc = None
        for a in range(3):
            part = dot(gather_rows(hm_ref, [r + a - 1 for r in group]), wg_ref[a])
            acc = part if acc is None else acc + part
        acc = jax.nn.sigmoid(acc)
        for n, row in enumerate(group):
            gate = acc[n * WC : (n + 1) * WC]
            up_ref[row] = gate[:, :B]
            reset = gate[:, B:]
            rs_ref[row] = reset
            store3(rm_ref, row, 0, 2 * B, reset * hidden_at(row))

    pairs = list(range(2, total - 2, 2))
    for i in range(0, len(pairs), 4):
        group = pairs[i : i + 4]
        acc = None
        for t in range(4):
            part = dot(gather_rows(rm_ref, [r + t - 1 for r in group]), wc_ref[t])
            acc = part if acc is None else acc + part
        acc = jnp.tanh(acc)
        for n, first in enumerate(group):
            for s in range(2):
                row = first + s
                cand = acc[n * WC : (n + 1) * WC, s * B : (s + 1) * B]
                hidden = hidden_at(row)
                update = up_ref[row]
                g = g_ref[row].astype(F32)
                if HALO <= row < HALO + rows:
                    nh_ref[row - HALO] = ((1.0 - update) * hidden + update * cand).astype(BF16)
                gu = g * update
                store3(cg_ref, row, 0, B, gu * (1.0 - cand * cand))
                if 3 <= row < total - 3:
                    store3(gg_ref, row, 0, 2 * B, gu * (cand - hidden) * (1.0 - update))

    for group in chunks(3, total - 3, 4):
        lhs = jnp.concatenate(
            [gather_rows(cg_ref, [r + a - 1 for r in group]) for a in range(3)], axis=1
        )
        acc = dot(lhs, wcb_ref[...])
        for n, row in enumerate(group):
            back = acc[n * WC : (n + 1) * WC]
            reset = rs_ref[row]
            value = back[:, :B] * hidden_at(row) * reset * (1.0 - reset)
            store3(gg_ref, row, B, 2 * B, value)
            if HALO <= row < HALO + rows:
                cb_ref[row - HALO] = back[:, B:]

    pairs = list(range(HALO, HALO + rows, 2))
    for i in range(0, len(pairs), 4):
        group = pairs[i : i + 4]
        acc = None
        for t in range(4):
            part = dot(gather_rows(gg_ref, [r + t - 1 for r in group]), wgb_ref[t])
            acc = part if acc is None else acc + part
        for n, first in enumerate(group):
            for s in range(2):
                row = first + s - HALO
                grad = cb_ref[row] + acc[n * WC : (n + 1) * WC, s * B : (s + 1) * B]
                pre = pre_ref[row]
                sig = jax.nn.sigmoid(pre)
                pg_ref[row] = (grad * sig * (1.0 + pre * (1.0 - sig))).astype(BF16)


def tap_grad_kernel(pg_ref, weight_ref, out_ref):
    weight = weight_ref[...]
    for r in range(pg_ref.shape[0]):
        out_ref[r] = dot_nt(weight, pg_ref[r, :B]).astype(BF16)


def spread(grad, disp, taps, radius):
    pixel = iota((B, B), 0)
    lane = iota((B, B), 1)
    tap = ((pixel - lane) & (B - 1)) - disp + radius
    ok = (tap >= 0) & (tap < taps)
    value = jnp.where(ok, lane_gather(grad, tap & (B - 1)), 0.0)
    far = jnp.where(lane > pixel, value, 0.0).astype(BF16)
    near = jnp.where(lane > pixel, 0.0, value).astype(BF16)
    return far, near


def spread_t(grad, disp, taps, radius):
    column = iota((B, B), 0)
    pixel = iota((B, B), 1)
    tap = ((pixel - column) & (B - 1)) - disp + radius
    value = jnp.zeros((B, B), F32)
    for k in range(taps):
        value = jnp.where(tap == k, grad[k : k + 1], value)
    far = jnp.where(column > pixel, value, 0.0).astype(BF16)
    near = jnp.where(column > pixel, 0.0, value).astype(BF16)
    return far, near


def grads_kernel(
    taps,
    radius,
    scale,
    pgl_ref,
    pgr_ref,
    nhl_ref,
    nhr_ref,
    left_ref,
    own_ref,
    before_ref,
    disp_ref,
    weight_ref,
    weight_t_ref,
    nh_ref,
    gl_ref,
    gr_ref,
    near_ref,
):
    rows = left_ref.shape[0]
    weight = weight_ref[...]
    weight_t = weight_t_ref[...]
    first = iota((B, B), 0) < HALO
    for r in range(rows):
        fars = []
        nears = []
        fars_t = []
        nears_t = []
        for block in range(2):
            if block == 0:
                pre_grad = pgl_ref[r, :B].astype(F32)
                new = nhl_ref[r, :B].astype(F32)
            else:
                tail = pgl_ref[r, B:].astype(F32)
                head = pgr_ref[r, :B].astype(F32)
                pre_grad = jnp.where(first, jnp.concatenate([tail, head[EDGE:]], axis=0), head)
                tail = nhl_ref[r, B:].astype(F32)
                head = nhr_ref[r, :B].astype(F32)
                new = jnp.where(first, jnp.concatenate([tail, head[EDGE:]], axis=0), head)
            nh_ref[r, block * B : (block + 1) * B] = new.astype(BF16)
            pre_grad = pre_grad.astype(BF16)
            row = disp_ref[r, :, block * B : (block + 1) * B]
            grad = dot(pre_grad, weight).astype(BF16).astype(F32)
            far, near = spread(grad, down_lanes(row), taps, radius)
            fars.append(far)
            nears.append(near)
            grad = dot_nt(weight_t, pre_grad).astype(BF16).astype(F32)
            far, near = spread_t(grad, row, taps, radius)
            fars_t.append(far)
            nears_t.append(near)
        window = jnp.concatenate([before_ref[r], own_ref[r, :B]], axis=0)
        sg = jnp.concatenate([fars[0], nears[0]], axis=1)
        gl_ref[r, :B] = (dot(sg, window) * scale).astype(BF16)
        sg = jnp.concatenate([fars[1], nears[1]], axis=1)
        gl_ref[r, B:] = (dot(sg, own_ref[r]) * scale).astype(BF16)
        sg = jnp.concatenate([nears_t[0], fars_t[1]], axis=1)
        gr_ref[r] = (dot(sg, left_ref[r]) * scale).astype(BF16)
        near_ref[r] = nears_t[1]


def last_kernel(
    taps, radius, scale, near_ref, grad_ref, disp_ref, left_ref, next_ref, first_ref, gr_ref
):
    rows = left_ref.shape[0]
    for r in range(rows):
        far, _ = spread_t(grad_ref[r].astype(F32), disp_ref[r], taps, radius)
        sg = jnp.concatenate([near_ref[r], far], axis=1)
        window = jnp.concatenate([left_ref[r], next_ref[r]], axis=0)
        gr_ref[r, :B] = first_ref[r]
        gr_ref[r, B:] = (dot(sg, window) * scale).astype(BF16)


def whole(array):
    nd = array.ndim
    return pl.BlockSpec(array.shape, lambda i: (0,) * nd)


def by_rows(array, size, block=None, at=None):
    block = tuple(array.shape[1:]) if block is None else block
    at = (0,) * len(block) if at is None else at
    return pl.BlockSpec((size,) + block, lambda i: (i,) + at)


def per_device(
    feat_left, feat_right, hidden, disparity, motion_weight, gate_weight, cand_weight, grad_hidden
):
    rows, cols, chan = feat_left.shape
    taps = motion_weight.shape[0]
    radius = taps // 2
    scale = 1.0 / math.sqrt(chan)
    args = (taps, radius, scale)
    size = 4
    grid = (rows // size,)
    params = pltpu.CompilerParams(vmem_limit_bytes=VMEM_LIMIT)

    pack = jnp.concatenate(
        [
            feat_left[:, :HALO],
            feat_right[:, :HALO],
            hidden[:, :HALO],
            grad_hidden[:, :HALO],
            jnp.broadcast_to(disparity[:, :HALO, None].astype(BF16), (rows, HALO, B)),
        ],
        axis=2,
    )
    from_right = shift(pack, "cols", -1)
    hg = jnp.concatenate([hidden, grad_hidden], axis=2)
    from_left = shift(hg[:, cols - HALO :], "cols", 1)
    before = shift(feat_right[:, cols - B :], "cols", 1)
    edge = jnp.pad(from_right, ((0, 0), (0, EDGE - HALO), (0, 0)))
    hg_right = jnp.concatenate([hg[:, B:], edge[:, :, 2 * chan : 2 * chan + 2 * B]], axis=1)
    hg_left = jnp.concatenate(
        [hg[:, : B + 8], jnp.zeros((rows, 8 - HALO, 2 * B), BF16), from_left], axis=1
    )

    def row_halo(array):
        return shift(array[rows - HALO :], "rows", 1), shift(array[:HALO], "rows", -1)

    hg_right_t, hg_right_b = row_halo(hg_right)

    wg = gate_weight.reshape(3, 3 * 2 * B, 2 * B)

    def paired(weight):
        return jnp.concatenate(
            [
                jnp.pad(weight, ((0, 1), (0, 0), (0, 0))),
                jnp.pad(weight, ((1, 0), (0, 0), (0, 0))),
            ],
            axis=2,
        )

    def flipped(weight):
        return jnp.transpose(weight[::-1, ::-1], (0, 1, 3, 2))

    wc = paired(cand_weight.reshape(3, 3 * 2 * B, B))
    wcb = flipped(cand_weight).reshape(9 * B, 2 * B)
    wgb = paired(flipped(gate_weight[:, :, B:]).reshape(3, 3 * 2 * B, B))
    mw = jnp.pad(motion_weight, ((0, B - taps), (0, 0)))
    mw_t = jnp.pad(motion_weight.T, ((0, 0), (0, B - taps)))
    mw16 = jnp.pad(motion_weight, ((0, 16 - taps), (0, 0)))
    disp3 = disparity[:, None, :]

    mot_shapes = (
        jax.ShapeDtypeStruct((rows, WC, B), BF16),
        jax.ShapeDtypeStruct((rows, WC, B), F32),
    )

    def cost(flops, bytes_accessed):
        return pl.CostEstimate(flops=flops, bytes_accessed=bytes_accessed, transcendentals=0)

    mot_right, pre_right = pl.pallas_call(
        lambda *refs: right_corr_kernel(*args, *refs),
        grid=grid,
        in_specs=[
            by_rows(feat_left, size, (B, chan), (1, 0)),
            by_rows(feat_right, size),
            by_rows(disp3, size, (1, B), (0, 1)),
            by_rows(edge, size),
            whole(mw),
        ],
        out_specs=[by_rows(s, size) for s in mot_shapes],
        out_shape=mot_shapes,
        scratch_shapes=[pltpu.VMEM((B, chan), BF16)],
        compiler_params=params,
        cost_estimate=cost(2 * rows * B * 2 * B * chan, 6 << 20),
        name="corr_right",
    )(feat_left, feat_right, disp3, edge, mw)
    mot_right_t, mot_right_b = row_halo(mot_right)
    mot_from_left = shift(mot_right[:, B - HALO : B], "cols", 1)

    gru_rows = rows + 2 * HALO

    def gru(hg_parts, mot_parts, pre, name):
        operands = (*hg_parts, *mot_parts, pre, wg, wc, wcb, wgb)
        out = jax.ShapeDtypeStruct((rows, WC, B), BF16)
        return pl.pallas_call(
            gru_kernel,
            out_shape=(out, out),
            in_specs=[pl.BlockSpec(memory_space=pltpu.VMEM)] * len(operands),
            out_specs=[pl.BlockSpec(memory_space=pltpu.VMEM)] * 2,
            scratch_shapes=[
                pltpu.VMEM((gru_rows, WC, 6 * B), BF16),
                pltpu.VMEM((gru_rows, WC, 6 * B), BF16),
                pltpu.VMEM((gru_rows, WC, 3 * B), BF16),
                pltpu.VMEM((gru_rows, WC, 6 * B), BF16),
                pltpu.VMEM((gru_rows, WC, B), BF16),
                pltpu.VMEM((gru_rows, WC, B), F32),
                pltpu.VMEM((gru_rows, WC, B), F32),
                pltpu.VMEM((rows, WC, B), F32),
            ],
            compiler_params=params,
            cost_estimate=cost(2 * 22 * WC * 256 * 256 * 24, 12 << 20),
            name=name,
        )(*operands)

    nh_right, pg_right = gru(
        (hg_right, hg_right_t, hg_right_b), (mot_right, mot_right_t, mot_right_b), pre_right, "gru_right"
    )

    hg_left_t, hg_left_b = row_halo(hg_left)
    edge_mot = jnp.concatenate(
        [mot_right[:, :8], jnp.zeros((rows, 8 - HALO, B), BF16), mot_from_left], axis=1
    )
    edge_pre = pre_right[:, :EDGE]
    mot_left, pre_left = pl.pallas_call(
        lambda *refs: left_corr_kernel(*args, *refs),
        grid=grid,
        in_specs=[
            by_rows(feat_left, size, (B, chan), (0, 0)),
            by_rows(feat_right, size, (B, chan), (0, 0)),
            by_rows(before, size),
            by_rows(disp3, size, (1, B), (0, 0)),
            by_rows(edge_mot, size),
            by_rows(edge_pre, size),
            whole(mw),
        ],
        out_specs=[by_rows(s, size) for s in mot_shapes],
        out_shape=mot_shapes,
        compiler_params=params,
        cost_estimate=cost(2 * rows * B * 2 * B * chan, 6 << 20),
        name="corr_left",
    )(feat_left, feat_right, before, disp3, edge_mot, edge_pre, mw)
    mot_left_t, mot_left_b = row_halo(mot_left)
    first_left, _ = lax.optimization_barrier((feat_left[:, :B], before))
    next_left = shift(first_left, "cols", -1)
    next_disp = shift(disp3[:, :, :B], "cols", -1)
    nh_left, pg_left = gru(
        (hg_left, hg_left_t, hg_left_b), (mot_left, mot_left_t, mot_left_b), pre_left, "gru_left"
    )
    tap_grad = pl.pallas_call(
        tap_grad_kernel,
        out_shape=jax.ShapeDtypeStruct((rows, 16, B), BF16),
        name="tap_grad",
        cost_estimate=cost(1 << 20, 1 << 20),
    )(pg_left, mw16)
    next_grad = shift(tap_grad, "cols", -1)

    out = jax.ShapeDtypeStruct
    grad_shapes = (
        out((rows, cols, B), BF16),
        out((rows, cols, chan), BF16),
        out((rows, B, chan), BF16),
        out((rows, B, B), BF16),
    )
    new_hidden, grad_left, grad_first, near = pl.pallas_call(
        lambda *refs: grads_kernel(*args, *refs),
        grid=grid,
        in_specs=[
            by_rows(pg_left, size),
            by_rows(pg_right, size),
            by_rows(nh_left, size),
            by_rows(nh_right, size),
            by_rows(feat_left, size),
            by_rows(feat_right, size),
            by_rows(before, size),
            by_rows(disp3, size),
            whole(mw_t),
            whole(mw16),
        ],
        out_specs=[by_rows(s, size) for s in grad_shapes],
        out_shape=grad_shapes,
        compiler_params=params,
        cost_estimate=cost(2 * rows * B * 2 * B * chan * 4, 12 << 20),
        name="grads",
    )(pg_left, pg_right, nh_left, nh_right, feat_left, feat_right, before, disp3, mw_t, mw16)
    grad_right = pl.pallas_call(
        lambda *refs: last_kernel(*args, *refs),
        grid=grid,
        in_specs=[
            by_rows(near, size),
            by_rows(next_grad, size),
            by_rows(next_disp, size),
            by_rows(feat_left, size, (B, chan), (1, 0)),
            by_rows(next_left, size),
            by_rows(grad_first, size),
        ],
        out_specs=by_rows(out((rows, cols, chan), BF16), size),
        out_shape=out((rows, cols, chan), BF16),
        compiler_params=params,
        cost_estimate=cost(2 * rows * B * 2 * B * chan, 6 << 20),
        name="grad_right",
    )(near, next_grad, next_disp, feat_left, next_left, grad_first)
    return (new_hidden, grad_left, grad_right)


def solution(mesh):
    grid3 = P("rows", "cols", None)
    return jax.shard_map(
        per_device,
        mesh=mesh,
        in_specs=(grid3, grid3, grid3, P("rows", "cols"), P(), P(), P(), grid3),
        out_specs=(grid3, grid3, grid3),
        check_vma=False,
    )
```

time: 350 us -> 156 us (0.45)
  the two profiles are of different devices: /device:TPU:35 before, /device:TPU:120 now
where the time goes in v1:
time: 156 us; the launch traced here: 155 us
  Pallas kernels  62.6 us (40%)
  starting transfers between devices  48.3 us (31%)
  local copies, waits for them, and re-layouts  25.3 us (16%)
  waiting for transfers between devices  11.5 us (7%)
  other arithmetic  6.31 us (4%)
    ppermute x15, starting transfers between devices, shift(): return lax.ppermute(array, axis, pairs)  48.3 us
    pallas_call x2, Pallas kernels, gru(): pl.pallas_call(gru_kernel, out_shape=(out, out), in_specs=[pl.BlockSpec(m...  30.5 us
    ppermute x15, waiting for transfers between devices, shift(): return lax.ppermute(array, axis, pairs)  11.5 us
    pallas_call x1, Pallas kernels, per_device(): pl.pallas_call(lambda *refs: right_corr_kernel(*args, *refs), grid=grid,...  10 us
    pallas_call x1, Pallas kernels, per_device(): pl.pallas_call(lambda *refs: grads_kernel(*args, *refs), grid=grid, in_sp...  8.51 us
    unnamed x52, local copies, waits for them, and re-layouts  7.93 us
    pallas_call x1, Pallas kernels, per_device(): pl.pallas_call(lambda *refs: left_corr_kernel(*args, *refs), grid=grid, i...  6.82 us
    pallas_call x1, Pallas kernels, per_device(): pl.pallas_call(lambda *refs: last_kernel(*args, *refs), grid=grid, in_spe...  4.68 us
  transfers between devices with their start and end apart: 15, of which 1 were waited for; matrix products, arithmetic and copies ran while one was open for 15% of the time, Pallas kernels for 37%

profile of v1, /device:TPU:120, one launch (start us, length us, event | category | flops | bytes accessed | tf_op | source)
XLA Modules:
  0.0 155.2 jit_solution(5738531182160184495)
XLA Ops:
  0.6 0.0 copy-start.5
  0.6 1.5 slice_dynamic-update-slice_fusion.1
  2.2 0.7 slice_convert_fusion
  2.9 1.5 slice_dynamic-update-slice_fusion
  4.4 1.4 constant_dynamic-update-slice_fusion.4
  5.7 1.4 constant_dynamic-update-slice_fusion.3
  7.1 0.7 constant_dynamic-update-slice_fusion.2
  7.8 4.9 %collective-permute-start.4 = (bf16[16,4,896]{2,1,0:T(4,128)(2,1)}, bf16[16,4,896]{2,1,0:T(4,128)(2,1)S(1)}, u32[]{:S(2)}, u32[]{:S(2)}) collective-permute-start(bf16[16,4,896]{2,1,0:T(4,128)(2,1)} %constant_dynamic-update-slice_fusion.2), channel_id=1, source_target_pairs={{1,0},{2,1},{3,2},{4,3},{5,4},{6,5},{7,6},{9,8},{10,9},{11,10},{12... | collective-permute-start | bytes 344072 | tf_op jit(solution)/shard_map/ppermute | solution.py:22
  12.7 2.3 %slice.77 = bf16[16,128,256]{2,1,0:T(8,128)(2,1)} slice(bf16[16,256,256]{2,1,0:T(8,128)(2,1)} %refs_5_.1), slice={[0:16], [128:256], [0:256]} | slice | bytes 2097152 | tf_op jit(solution)/shard_map/slice | solution.py:385
  15.0 2.6 %collective-permute-start.3 = (bf16[16,128,256]{2,1,0:T(8,128)(2,1)}, bf16[16,128,256]{2,1,0:T(8,128)(2,1)}, u32[]{:S(2)}, u32[]{:S(2)}) collective-permute-start(bf16[16,128,256]{2,1,0:T(8,128)(2,1)} %slice.77), channel_id=1, source_target_pairs={{0,1},{1,2},{2,3},{3,4},{4,5},{5,6},{6,7},{8,9},{9,10},{10,11},{11... | collective-permute-start | bytes 3145736 | tf_op jit(solution)/shard_map/ppermute | solution.py:22
  17.5 0.2 constant_dynamic-update-slice_fusion.1
  17.8 0.0 slice-start
  17.8 0.2 constant_dynamic-update-slice_fusion
  18.0 0.0 copy-start.1
  18.1 0.0 copy-start.4
  18.1 2.1 %collective-permute-start = (bf16[16,4,256]{2,1,0:T(4,128)(2,1)S(1)}, bf16[16,4,256]{2,1,0:T(4,128)(2,1)S(1)}, u32[]{:S(2)}, u32[]{:S(2)}) collective-permute-start(bf16[16,4,256]{2,1,0:T(4,128)(2,1)S(1)} %slice.98), channel_id=1, source_target_pairs={{0,1},{1,2},{2,3},{3,4},{4,5},{5,6},{6,7},{8,9},{9,10},{10,11},{11... | collective-permute-start | bytes 98312 | tf_op jit(solution)/shard_map/ppermute | solution.py:22
  20.2 1.1 copy.12
  21.3 3.2 %fusion.4 = (bf16[4,768,256]{2,1,0:T(8,128)(2,1)}, bf16[4,768,256]{2,1,0:T(8,128)(2,1)}) fusion(bf16[3,768,128]{2,1,0:T(8,128)(2,1)S(1)} %bitcast.11, bf16[3,768,128]{2,1,0:T(8,128)(2,1)} %bitcast.12), kind=kLoop, calls=%fused_computation.9 | loop fusion | flops 11010048 | bytes 4325376 | tf_op jit(solution)/shard_map/concatenate | solution.py:400
  24.5 0.9 reverse_bitcast_fusion.1
  25.4 1.1 slice.97
  26.5 0.1 pad.45.clone
  26.6 0.1 pad.48.clone
  26.7 1.4 slice.102
  28.1 0.6 pad.31.refs_4_.refs_6_
  28.7 0.6 pad.37.refs_9_.weight_ref
  29.3 0.1 copy.13
  29.4 1.0 slice.96
  30.5 2.2 %copy.11 = bf16[3,3,128,256]{3,2,1,0:T(8,128)(2,1)} copy(bf16[3,3,128,256]{2,3,1,0:T(8,128)(2,1)} %reverse_bitcast_fusion.1) | data formatting | bytes 1179648 | tf_op jit(solution)/shard_map/transpose | solution.py:409
  32.7 0.6 pad.36.refs_8_
  33.3 11.5 %collective-permute-done = bf16[16,4,256]{2,1,0:T(4,128)(2,1)S(1)} collective-permute-done((bf16[16,4,256]{2,1,0:T(4,128)(2,1)S(1)}, bf16[16,4,256]{2,1,0:T(4,128)(2,1)S(1)}, u32[]{:S(2)}, u32[]{:S(2)}) %collective-permute-start) | collective-permute-done | bytes 32800 | tf_op jit(solution)/shard_map/ppermute | solution.py:22
  44.8 0.5 pad_maximum_fusion.1.hg_ref
  45.3 0.0 copy-start.3
  45.3 1.9 %collective-permute-start.1 = (bf16[4,144,256]{2,1,0:T(8,128)(2,1)S(1)}, bf16[4,144,256]{2,1,0:T(8,128)(2,1)S(1)}, u32[]{:S(2)}, u32[]{:S(2)}) collective-permute-start(bf16[4,144,256]{2,1,0:T(8,128)(2,1)S(1)} %get-tuple-element.32), channel_id=1, source_target_pairs={{0,8},{8,16},{16,24},{24,32},{32,40},{40,48},{48,56},{56,64},{64,7... | collective-permute-start | bytes 884744 | tf_op jit(solution)/shard_map/ppermute | solution.py:22
  47.2 0.0 collective-permute-done.4
  47.3 0.9 pad.30.refs_3_
  48.1 10.0 %corr_right.1 = (bf16[16,144,128]{2,1,0:T(8,128)(2,1)}, f32[16,144,128]{2,1,0:T(8,128)}) custom-call(bf16[16,256,256]{2,1,0:T(8,128)(2,1)} %refs_3_.1, bf16[16,256,256]{2,1,0:T(8,128)(2,1)} %refs_5_.1, s32[16,1,256]{2,1,0:T(1,128)} %copy-done.9, bf16[16,16,896]{2,1,0:T(8,128)(2,1)} %pad.30.refs_3_, bf16[128,128]{1,0:T(8,128)(2,1)} %pad.31.refs_4_.refs_6_), custom_call_target="tpu_custom_call" | custom-call | flops 268435456 | bytes 6291456 | tf_op jit(solution)/shard_map/corr_right/pallas_call | solution.py:427
  58.1 0.8 slice.84
  59.0 1.9 %collective-permute-start.5 = (bf16[16,4,128]{2,1,0:T(4,128)(2,1)S(1)}, bf16[16,4,128]{2,1,0:T(4,128)(2,1)S(1)}, u32[]{:S(2)}, u32[]{:S(2)}) collective-permute-start(bf16[16,4,128]{2,1,0:T(4,128)(2,1)S(1)} %slice.84), channel_id=1, source_target_pairs={{0,1},{1,2},{2,3},{3,4},{4,5},{5,6},{6,7},{8,9},{9,10},{10,11},{11... | collective-permute-start | bytes 49160 | tf_op jit(solution)/shard_map/ppermute | solution.py:22
  60.9 1.2 pad_maximum_fusion.hg_ref
  62.2 1.6 %slice.85.refs_5_ = f32[16,16,128]{2,1,0:T(8,128)} slice(f32[16,144,128]{2,1,0:T(8,128)} %get-tuple-element.17.pre_ref), slice={[0:16], [0:16], [0:128]} | slice | bytes 262144 | tf_op jit(solution)/shard_map/slice | solution.py:480
  63.8 3.6 %collective-permute-start.10 = (bf16[4,144,128]{2,1,0:T(8,128)(2,1)S(1)}, bf16[4,144,128]{2,1,0:T(8,128)(2,1)S(1)}, u32[]{:S(2)}, u32[]{:S(2)}) collective-permute-start(bf16[4,144,128]{2,1,0:T(8,128)(2,1)S(1)} %get-tuple-element.34), channel_id=1, source_target_pairs={{0,8},{8,16},{16,24},{24,32},{32,40},{40,48},{48,56},{56,64},{64,7... | collective-permute-start | bytes 442376 | tf_op jit(solution)/shard_map/ppermute | solution.py:22
  67.4 1.9 %collective-permute-start.8 = (bf16[4,144,256]{2,1,0:T(8,128)(2,1)S(1)}, bf16[4,144,256]{2,1,0:T(8,128)(2,1)S(1)}, u32[]{:S(2)}, u32[]{:S(2)}) collective-permute-start(bf16[4,144,256]{2,1,0:T(8,128)(2,1)S(1)} %get-tuple-element.30), channel_id=1, source_target_pairs={{0,8},{8,16},{16,24},{24,32},{32,40},{40,48},{48,56},{56,64},{64,7... | collective-permute-start | bytes 884744 | tf_op jit(solution)/shard_map/ppermute | solution.py:22
  69.3 4.5 %collective-permute-start.9 = (bf16[4,144,256]{2,1,0:T(8,128)(2,1)S(1)}, bf16[4,144,256]{2,1,0:T(8,128)(2,1)S(1)}, u32[]{:S(2)}, u32[]{:S(2)}) collective-permute-start(bf16[4,144,256]{2,1,0:T(8,128)(2,1)S(1)} %get-tuple-element.29), channel_id=1, source_target_pairs={{8,0},{16,8},{24,16},{32,24},{40,32},{48,40},{56,48},{64,56},{72,6... | collective-permute-start | bytes 884744 | tf_op jit(solution)/shard_map/ppermute | solution.py:22
  73.9 0.7 pad_maximum_fusion.2.refs_4_
  74.6 2.0 %collective-permute-start.11 = (bf16[4,144,128]{2,1,0:T(8,128)(2,1)S(1)}, bf16[4,144,128]{2,1,0:T(8,128)(2,1)S(1)}, u32[]{:S(2)}, u32[]{:S(2)}) collective-permute-start(bf16[4,144,128]{2,1,0:T(8,128)(2,1)S(1)} %get-tuple-element.33), channel_id=1, source_target_pairs={{8,0},{16,8},{24,16},{32,24},{40,32},{48,40},{56,48},{64,56},{72,6... | collective-permute-start | bytes 442376 | tf_op jit(solution)/shard_map/ppermute | solution.py:22
  76.6 6.8 %corr_left.1 = (bf16[16,144,128]{2,1,0:T(8,128)(2,1)}, f32[16,144,128]{2,1,0:T(8,128)}) custom-call(bf16[16,256,256]{2,1,0:T(8,128)(2,1)} %refs_3_.1, bf16[16,256,256]{2,1,0:T(8,128)(2,1)} %refs_5_.1, bf16[16,128,256]{2,1,0:T(8,128)(2,1)} %collective-permute-done.3.refs_2_.refs_6_, s32[16,1,256]{2,1,0:T(1,128)} %copy-done.9, ...), custom_call_target="tpu_custom_call" | custom-call | flops 268435456 | bytes 6291456 | tf_op jit(solution)/shard_map/corr_left/pallas_call | solution.py:481
  83.4 1.0 fusion.10
  84.5 2.5 %collective-permute-start.2 = (bf16[4,144,256]{2,1,0:T(8,128)(2,1)S(1)}, bf16[4,144,256]{2,1,0:T(8,128)(2,1)S(1)}, u32[]{:S(2)}, u32[]{:S(2)}) collective-permute-start(bf16[4,144,256]{2,1,0:T(8,128)(2,1)S(1)} %get-tuple-element.31), channel_id=1, source_target_pairs={{8,0},{16,8},{24,16},{32,24},{40,32},{48,40},{56,48},{64,56},{72,6... | collective-permute-start | bytes 884744 | tf_op jit(solution)/shard_map/ppermute | solution.py:22
  86.9 1.9 %collective-permute-start.6 = (bf16[4,144,128]{2,1,0:T(8,128)(2,1)S(1)}, bf16[4,144,128]{2,1,0:T(8,128)(2,1)S(1)}, u32[]{:S(2)}, u32[]{:S(2)}) collective-permute-start(bf16[4,144,128]{2,1,0:T(8,128)(2,1)S(1)} %get-tuple-element.36), channel_id=1, source_target_pairs={{0,8},{8,16},{16,24},{24,32},{32,40},{40,48},{48,56},{56,64},{64,7... | collective-permute-start | bytes 442376 | tf_op jit(solution)/shard_map/ppermute | solution.py:22
  88.9 4.5 %collective-permute-start.7 = (bf16[4,144,128]{2,1,0:T(8,128)(2,1)S(1)}, bf16[4,144,128]{2,1,0:T(8,128)(2,1)S(1)}, u32[]{:S(2)}, u32[]{:S(2)}) collective-permute-start(bf16[4,144,128]{2,1,0:T(8,128)(2,1)S(1)} %get-tuple-element.35), channel_id=1, source_target_pairs={{8,0},{16,8},{24,16},{32,24},{40,32},{48,40},{56,48},{64,56},{72,6... | collective-permute-start | bytes 442376 | tf_op jit(solution)/shard_map/ppermute | solution.py:22
  93.5 6.8 %collective-permute-start.14 = (bf16[16,128,256]{2,1,0:T(8,128)(2,1)S(1)}, bf16[16,128,256]{2,1,0:T(8,128)(2,1)S(1)}, u32[]{:S(2)}, u32[]{:S(2)}) collective-permute-start(bf16[16,128,256]{2,1,0:T(8,128)(2,1)S(1)} %copy-done.7), channel_id=1, source_target_pairs={{1,0},{2,1},{3,2},{4,3},{5,4},{6,5},{7,6},{9,8},{10,9},{11,10},{12... | collective-permute-start | bytes 3145736 | tf_op jit(solution)/shard_map/ppermute | solution.py:22
  100.4 15.2 %gru_right.1 = (bf16[16,144,128]{2,1,0:T(8,128)(2,1)}, bf16[16,144,128]{2,1,0:T(8,128)(2,1)}) custom-call(bf16[16,144,256]{2,1,0:T(8,128)(2,1)} %pad_maximum_fusion.hg_ref, bf16[4,144,256]{2,1,0:T(8,128)(2,1)} %copy-done.16, bf16[4,144,256]{2,1,0:T(8,128)(2,1)} %copy-done.18, bf16[16,144,128]{2,1,0:T(8,128)(2,1)} %get-tuple-element.16.mot_ref, ...), custom_call_target="tpu_custom_call" | custom-call | flops 9965666304 | bytes 12582912 | tf_op jit(solution)/shard_map/gru_right/pallas_call | solution.py:452
  115.6 2.1 %collective-permute-start.13 = (s32[16,1,128]{2,1,0:T(1,128)S(1)}, s32[16,1,128]{2,1,0:T(1,128)S(1)}, u32[]{:S(2)}, u32[]{:S(2)}) collective-permute-start(s32[16,1,128]{2,1,0:T(1,128)S(1)} %slice.107), channel_id=1, source_target_pairs={{1,0},{2,1},{3,2},{4,3},{5,4},{6,5},{7,6},{9,8},{10,9},{11,10},{12... | collective-permute-start | bytes 24584 | tf_op jit(solution)/shard_map/ppermute | solution.py:22
  117.8 0.7 copy-done.17
  118.5 0.1 copy-done.20
  118.6 0.1 copy-done.22
  118.6 15.2 %gru_left.1 = (bf16[16,144,128]{2,1,0:T(8,128)(2,1)}, bf16[16,144,128]{2,1,0:T(8,128)(2,1)}) custom-call(bf16[16,144,256]{2,1,0:T(8,128)(2,1)} %copy-done.3, bf16[4,144,256]{2,1,0:T(8,128)(2,1)} %copy-done.15, bf16[4,144,256]{2,1,0:T(8,128)(2,1)} %copy-done.17, bf16[16,144,128]{2,1,0:T(8,128)(2,1)} %get-tuple-element.18.mot_ref, ...), custom_call_target="tpu_custom_call" | custom-call | flops 9965666304 | bytes 12582912 | tf_op jit(solution)/shard_map/gru_left/pallas_call | solution.py:452
  133.9 2.1 %tap_grad.1 = bf16[16,16,128]{2,1,0:T(8,128)(2,1)} custom-call(bf16[16,144,128]{2,1,0:T(8,128)(2,1)} %get-tuple-element.20.refs_0_.pg_ref, bf16[16,128]{1,0:T(8,128)(2,1)} %pad.37.refs_9_.weight_ref), custom_call_target="tpu_custom_call" | custom-call | flops 1048576 | bytes 1048576 | tf_op jit(solution)/shard_map/tap_grad/pallas_call | solution.py:506
  135.9 5.0 %collective-permute-start.12 = (bf16[16,16,128]{2,1,0:T(8,128)(2,1)}, bf16[16,16,128]{2,1,0:T(8,128)(2,1)S(1)}, u32[]{:S(2)}, u32[]{:S(2)}) collective-permute-start(bf16[16,16,128]{2,1,0:T(8,128)(2,1)} %tap_grad.1), channel_id=1, source_target_pairs={{1,0},{2,1},{3,2},{4,3},{5,4},{6,5},{7,6},{9,8},{10,9},{11,10},{12... | collective-permute-start | bytes 196616 | tf_op jit(solution)/shard_map/ppermute | solution.py:22
  140.9 8.5 %grads.1 = (bf16[16,256,128]{2,1,0:T(8,128)(2,1)}, bf16[16,256,256]{2,1,0:T(8,128)(2,1)}, bf16[16,128,256]{2,1,0:T(8,128)(2,1)}, bf16[16,128,128]{2,1,0:T(8,128)(2,1)}) custom-call(bf16[16,144,128]{2,1,0:T(8,128)(2,1)} %get-tuple-element.20.refs_0_.pg_ref, bf16[16,144,128]{2,1,0:T(8,128)(2,1)} %get-tuple-element.21.refs_1_, ...), custom_call_target="tpu_custom_call" | custom-call | flops 1073741824 | bytes 12582912 | tf_op jit(solution)/shard_map/grads/pallas_call | solution.py:521
  149.5 0.5 copy-done.14
  150.0 0.0 copy-done.11
  150.1 0.4 copy-done.8
  150.5 4.7 %grad_right.1 = bf16[16,256,256]{2,1,0:T(8,128)(2,1)} custom-call(bf16[16,128,128]{2,1,0:T(8,128)(2,1)} %get-tuple-element.26.refs_0_, bf16[16,16,128]{2,1,0:T(8,128)(2,1)} %copy-done.11, s32[16,1,128]{2,1,0:T(1,128)} %copy-done.14, bf16[16,256,256]{2,1,0:T(8,128)(2,1)} %refs_3_.1, bf16[16,128,256]{2,1,0:T(8,128)(2,1)} %copy-done.8, ...), custom_call_target="tpu_custom_call" | custom-call | flops 268435456 | bytes 6291456 | tf_op jit(solution)/shard_map/grad_right/pallas_call | solution.py:542
  (60 shorter events, 0.3 us)
Async XLA Ops:
  0.6 16.9 %copy-start.5 = (bf16[16,256,128]{2,1,0:T(8,128)(2,1)S(1)}, bf16[16,256,128]{2,1,0:T(8,128)(2,1)}, u32[]{:S(2)}) copy-start(bf16[16,256,128]{2,1,0:T(8,128)(2,1)} %param.10) | copy-start | bytes 3145732
  7.8 10.0 %copy-start.6 = (bf16[16,256,128]{2,1,0:T(8,128)(2,1)S(1)}, bf16[16,256,128]{2,1,0:T(8,128)(2,1)}, u32[]{:S(2)}) copy-start(bf16[16,256,128]{2,1,0:T(8,128)(2,1)} %param.15) | copy-start | bytes 3145732
  7.8 39.5 %collective-permute-start.4 = (bf16[16,4,896]{2,1,0:T(4,128)(2,1)}, bf16[16,4,896]{2,1,0:T(4,128)(2,1)S(1)}, u32[]{:S(2)}, u32[]{:S(2)}) collective-permute-start(bf16[16,4,896]{2,1,0:T(4,128)(2,1)} %constant_dynamic-update-slice_fusion.2), channel_id=1, source_target_pairs={{1,0},{2,1},{3,2},{4,3},{5,4},{6,5},{7,6},{9,8},{10,9},{11,10},{12... | collective-permute-start | bytes 344072 | tf_op jit(solution)/shard_map/ppermute | solution.py:22
  15.0 59.6 %collective-permute-start.3 = (bf16[16,128,256]{2,1,0:T(8,128)(2,1)}, bf16[16,128,256]{2,1,0:T(8,128)(2,1)}, u32[]{:S(2)}, u32[]{:S(2)}) collective-permute-start(bf16[16,128,256]{2,1,0:T(8,128)(2,1)} %slice.77), channel_id=1, source_target_pairs={{0,1},{1,2},{2,3},{3,4},{4,5},{5,6},{6,7},{8,9},{9,10},{10,11},{11... | collective-permute-start | bytes 3145736 | tf_op jit(solution)/shard_map/ppermute | solution.py:22
  17.8 2.4 %slice-start = ((bf16[3,3,256,256]{3,2,1,0:T(8,128)(2,1)}), bf16[3,3,128,256]{3,2,1,0:T(8,128)(2,1)S(1)}, s32[]{:S(2)}) async-start(bf16[3,3,256,256]{3,2,1,0:T(8,128)(2,1)} %param.13), calls=%async_computation | async-start | bytes 1179648 | tf_op jit(solution)/shard_map/slice | solution.py:413
  18.0 7.3 %copy-start.1 = (bf16[16,256,256]{2,1,0:T(8,128)(2,1)}, bf16[16,256,256]{2,1,0:T(8,128)(2,1)S(1)}, u32[]{:S(2)}) copy-start(bf16[16,256,256]{2,1,0:T(8,128)(2,1)S(1)} %constant_dynamic-update-slice_fusion) | copy-start | bytes 6291460
  18.1 3.2 %copy-start.4 = (bf16[3,3,256,128]{3,2,1,0:T(8,128)(2,1)S(1)}, bf16[3,3,256,128]{3,2,1,0:T(8,128)(2,1)}, u32[]{:S(2)}) copy-start(bf16[3,3,256,128]{3,2,1,0:T(8,128)(2,1)} %param.14) | copy-start | bytes 1769476
  18.1 26.7 %collective-permute-start = (bf16[16,4,256]{2,1,0:T(4,128)(2,1)S(1)}, bf16[16,4,256]{2,1,0:T(4,128)(2,1)S(1)}, u32[]{:S(2)}, u32[]{:S(2)}) collective-permute-start(bf16[16,4,256]{2,1,0:T(4,128)(2,1)S(1)} %slice.98), channel_id=1, source_target_pairs={{0,1},{1,2},{2,3},{3,4},{4,5},{5,6},{6,7},{8,9},{9,10},{10,11},{11... | collective-permute-start | bytes 98312 | tf_op jit(solution)/shard_map/ppermute | solution.py:22
  21.3 4.1 %copy-start.13 = (s32[16,256]{1,0:T(8,128)S(1)}, s32[16,256]{1,0:T(8,128)}, u32[]{:S(2)}) copy-start(s32[16,256]{1,0:T(8,128)} %param.11) | copy-start | bytes 49156
  25.4 7.9 %copy-start.9 = (s32[16,1,256]{2,1,0:T(1,128)}, s32[16,1,256]{2,1,0:T(1,128)S(1)}, u32[]{:S(2)}) copy-start(s32[16,1,256]{2,1,0:T(1,128)S(1)} %broadcast_in_dim.16.refs_2_.refs_3_.refs_7_) | copy-start | bytes 49156
  26.5 1.6 %copy-start.12 = (bf16[9,128]{1,0:T(8,128)(2,1)S(1)}, bf16[9,128]{1,0:T(8,128)(2,1)}, u32[]{:S(2)}) copy-start(bf16[9,128]{1,0:T(8,128)(2,1)} %param.12) | copy-start | bytes 6916
  26.5 2.9 %copy-start = (bf16[16,256,256]{2,1,0:T(8,128)(2,1)S(1)}, bf16[16,256,256]{2,1,0:T(8,128)(2,1)}, u32[]{:S(2)}) copy-start(bf16[16,256,256]{2,1,0:T(8,128)(2,1)} %refs_3_.1) | copy-start | bytes 6291460
  30.5 14.3 %copy-start.2 = (bf16[16,136,256]{2,1,0:T(8,128)(2,1)S(1)}, bf16[16,136,256]{2,1,0:T(8,128)(2,1)}, u32[]{:S(2)}) copy-start(bf16[16,136,256]{2,1,0:T(8,128)(2,1)} %slice.97) | copy-start | bytes 3342340
  45.3 12.9 %copy-start.3 = (bf16[16,144,256]{2,1,0:T(8,128)(2,1)}, bf16[16,144,256]{2,1,0:T(8,128)(2,1)S(1)}, u32[]{:S(2)}) copy-start(bf16[16,144,256]{2,1,0:T(8,128)(2,1)S(1)} %pad_maximum_fusion.1.hg_ref) | copy-start | bytes 3538948
  45.3 70.3 %collective-permute-start.1 = (bf16[4,144,256]{2,1,0:T(8,128)(2,1)S(1)}, bf16[4,144,256]{2,1,0:T(8,128)(2,1)S(1)}, u32[]{:S(2)}, u32[]{:S(2)}) collective-permute-start(bf16[4,144,256]{2,1,0:T(8,128)(2,1)S(1)} %get-tuple-element.32), channel_id=1, source_target_pairs={{0,8},{8,16},{16,24},{24,32},{32,40},{40,48},{48,56},{56,64},{64,7... | collective-permute-start | bytes 884744 | tf_op jit(solution)/shard_map/ppermute | solution.py:22
  58.1 4.0 %copy-start.10 = (bf16[16,144,128]{2,1,0:T(8,128)(2,1)S(1)}, bf16[16,144,128]{2,1,0:T(8,128)(2,1)}, u32[]{:S(2)}) copy-start(bf16[16,144,128]{2,1,0:T(8,128)(2,1)} %get-tuple-element.16.mot_ref) | copy-start | bytes 1769476
  59.0 10.3 %collective-permute-start.5 = (bf16[16,4,128]{2,1,0:T(4,128)(2,1)S(1)}, bf16[16,4,128]{2,1,0:T(4,128)(2,1)S(1)}, u32[]{:S(2)}, u32[]{:S(2)}) collective-permute-start(bf16[16,4,128]{2,1,0:T(4,128)(2,1)S(1)} %slice.84), channel_id=1, source_target_pairs={{0,1},{1,2},{2,3},{3,4},{4,5},{5,6},{6,7},{8,9},{9,10},{10,11},{11... | collective-permute-start | bytes 49160 | tf_op jit(solution)/shard_map/ppermute | solution.py:22
  63.8 20.7 %collective-permute-start.10 = (bf16[4,144,128]{2,1,0:T(8,128)(2,1)S(1)}, bf16[4,144,128]{2,1,0:T(8,128)(2,1)S(1)}, u32[]{:S(2)}, u32[]{:S(2)}) collective-permute-start(bf16[4,144,128]{2,1,0:T(8,128)(2,1)S(1)} %get-tuple-element.34), channel_id=1, source_target_pairs={{0,8},{8,16},{16,24},{24,32},{32,40},{40,48},{48,56},{56,64},{64,7... | collective-permute-start | bytes 442376 | tf_op jit(solution)/shard_map/ppermute | solution.py:22
  67.4 21.5 %collective-permute-start.8 = (bf16[4,144,256]{2,1,0:T(8,128)(2,1)S(1)}, bf16[4,144,256]{2,1,0:T(8,128)(2,1)S(1)}, u32[]{:S(2)}, u32[]{:S(2)}) collective-permute-start(bf16[4,144,256]{2,1,0:T(8,128)(2,1)S(1)} %get-tuple-element.30), channel_id=1, source_target_pairs={{0,8},{8,16},{16,24},{24,32},{32,40},{40,48},{48,56},{56,64},{64,7... | collective-permute-start | bytes 884744 | tf_op jit(solution)/shard_map/ppermute | solution.py:22
  69.3 24.1 %collective-permute-start.9 = (bf16[4,144,256]{2,1,0:T(8,128)(2,1)S(1)}, bf16[4,144,256]{2,1,0:T(8,128)(2,1)S(1)}, u32[]{:S(2)}, u32[]{:S(2)}) collective-permute-start(bf16[4,144,256]{2,1,0:T(8,128)(2,1)S(1)} %get-tuple-element.29), channel_id=1, source_target_pairs={{8,0},{16,8},{24,16},{32,24},{40,32},{48,40},{56,48},{64,56},{72,6... | collective-permute-start | bytes 884744 | tf_op jit(solution)/shard_map/ppermute | solution.py:22
  74.6 18.9 %copy-start.7 = (bf16[16,128,256]{2,1,0:T(8,128)(2,1)S(1)}, bf16[16,128,256]{2,1,0:T(8,128)(2,1)}, u32[]{:S(2)}) copy-start(bf16[16,128,256]{2,1,0:T(8,128)(2,1)} %slice.96) | copy-start | bytes 3145732
  74.6 12.4 %collective-permute-start.11 = (bf16[4,144,128]{2,1,0:T(8,128)(2,1)S(1)}, bf16[4,144,128]{2,1,0:T(8,128)(2,1)S(1)}, u32[]{:S(2)}, u32[]{:S(2)}) collective-permute-start(bf16[4,144,128]{2,1,0:T(8,128)(2,1)S(1)} %get-tuple-element.33), channel_id=1, source_target_pairs={{8,0},{16,8},{24,16},{32,24},{40,32},{48,40},{56,48},{64,56},{72,6... | collective-permute-start | bytes 442376 | tf_op jit(solution)/shard_map/ppermute | solution.py:22
  84.4 15.9 %copy-start.19 = (bf16[4,144,128]{2,1,0:T(8,128)(2,1)}, bf16[4,144,128]{2,1,0:T(8,128)(2,1)S(1)}, u32[]{:S(2)}) copy-start(bf16[4,144,128]{2,1,0:T(8,128)(2,1)S(1)} %collective-permute-done.10.mott_ref) | copy-start | bytes 442372
  84.5 33.3 %collective-permute-start.2 = (bf16[4,144,256]{2,1,0:T(8,128)(2,1)S(1)}, bf16[4,144,256]{2,1,0:T(8,128)(2,1)S(1)}, u32[]{:S(2)}, u32[]{:S(2)}) collective-permute-start(bf16[4,144,256]{2,1,0:T(8,128)(2,1)S(1)} %get-tuple-element.31), channel_id=1, source_target_pairs={{8,0},{16,8},{24,16},{32,24},{40,32},{48,40},{56,48},{64,56},{72,6... | collective-permute-start | bytes 884744 | tf_op jit(solution)/shard_map/ppermute | solution.py:22
  86.9 13.4 %copy-start.21 = (bf16[4,144,128]{2,1,0:T(8,128)(2,1)}, bf16[4,144,128]{2,1,0:T(8,128)(2,1)S(1)}, u32[]{:S(2)}) copy-start(bf16[4,144,128]{2,1,0:T(8,128)(2,1)S(1)} %collective-permute-done.11.motb_ref) | copy-start | bytes 442372
  86.9 30.8 %collective-permute-start.6 = (bf16[4,144,128]{2,1,0:T(8,128)(2,1)S(1)}, bf16[4,144,128]{2,1,0:T(8,128)(2,1)S(1)}, u32[]{:S(2)}, u32[]{:S(2)}) collective-permute-start(bf16[4,144,128]{2,1,0:T(8,128)(2,1)S(1)} %get-tuple-element.36), channel_id=1, source_target_pairs={{0,8},{8,16},{16,24},{24,32},{32,40},{40,48},{48,56},{56,64},{64,7... | collective-permute-start | bytes 442376 | tf_op jit(solution)/shard_map/ppermute | solution.py:22
  88.9 11.5 %copy-start.16 = (bf16[4,144,256]{2,1,0:T(8,128)(2,1)}, bf16[4,144,256]{2,1,0:T(8,128)(2,1)S(1)}, u32[]{:S(2)}) copy-start(bf16[4,144,256]{2,1,0:T(8,128)(2,1)S(1)} %collective-permute-done.8.hgt_ref) | copy-start | bytes 884740
  88.9 28.9 %collective-permute-start.7 = (bf16[4,144,128]{2,1,0:T(8,128)(2,1)S(1)}, bf16[4,144,128]{2,1,0:T(8,128)(2,1)S(1)}, u32[]{:S(2)}, u32[]{:S(2)}) collective-permute-start(bf16[4,144,128]{2,1,0:T(8,128)(2,1)S(1)} %get-tuple-element.35), channel_id=1, source_target_pairs={{8,0},{16,8},{24,16},{32,24},{40,32},{48,40},{56,48},{64,56},{72,6... | collective-permute-start | bytes 442376 | tf_op jit(solution)/shard_map/ppermute | solution.py:22
  93.5 6.9 %copy-start.18 = (bf16[4,144,256]{2,1,0:T(8,128)(2,1)}, bf16[4,144,256]{2,1,0:T(8,128)(2,1)S(1)}, u32[]{:S(2)}) copy-start(bf16[4,144,256]{2,1,0:T(8,128)(2,1)S(1)} %collective-permute-done.9.hgb_ref) | copy-start | bytes 884740
  93.5 56.0 %collective-permute-start.14 = (bf16[16,128,256]{2,1,0:T(8,128)(2,1)S(1)}, bf16[16,128,256]{2,1,0:T(8,128)(2,1)S(1)}, u32[]{:S(2)}, u32[]{:S(2)}) collective-permute-start(bf16[16,128,256]{2,1,0:T(8,128)(2,1)S(1)} %copy-done.7), channel_id=1, source_target_pairs={{1,0},{2,1},{3,2},{4,3},{5,4},{6,5},{7,6},{9,8},{10,9},{11,10},{12... | collective-permute-start | bytes 3145736 | tf_op jit(solution)/shard_map/ppermute | solution.py:22
  115.6 2.2 %copy-start.15 = (bf16[4,144,256]{2,1,0:T(8,128)(2,1)}, bf16[4,144,256]{2,1,0:T(8,128)(2,1)S(1)}, u32[]{:S(2)}) copy-start(bf16[4,144,256]{2,1,0:T(8,128)(2,1)S(1)} %collective-permute-done.1.hgt_ref) | copy-start | bytes 884740
  115.6 33.8 %collective-permute-start.13 = (s32[16,1,128]{2,1,0:T(1,128)S(1)}, s32[16,1,128]{2,1,0:T(1,128)S(1)}, u32[]{:S(2)}, u32[]{:S(2)}) collective-permute-start(s32[16,1,128]{2,1,0:T(1,128)S(1)} %slice.107), channel_id=1, source_target_pairs={{1,0},{2,1},{3,2},{4,3},{5,4},{6,5},{7,6},{9,8},{10,9},{11,10},{12... | collective-permute-start | bytes 24584 | tf_op jit(solution)/shard_map/ppermute | solution.py:22
  117.8 0.7 copy-start.17
  117.8 0.8 copy-start.20
  117.8 0.8 copy-start.22
  135.9 13.5 %collective-permute-start.12 = (bf16[16,16,128]{2,1,0:T(8,128)(2,1)}, bf16[16,16,128]{2,1,0:T(8,128)(2,1)S(1)}, u32[]{:S(2)}, u32[]{:S(2)}) collective-permute-start(bf16[16,16,128]{2,1,0:T(8,128)(2,1)} %tap_grad.1), channel_id=1, source_target_pairs={{1,0},{2,1},{3,2},{4,3},{5,4},{6,5},{7,6},{9,8},{10,9},{11,10},{12... | collective-permute-start | bytes 196616 | tf_op jit(solution)/shard_map/ppermute | solution.py:22
  149.4 0.6 copy-start.14
  149.5 0.6 copy-start.11
  149.5 1.0 copy-start.8

commit v2 on v1

v2 whole, which is shorter than its diff:
```python
import math

import jax
import jax.numpy as jnp
from jax import lax
from jax.experimental import pallas as pl
from jax.experimental.pallas import tpu as pltpu
from jax.sharding import PartitionSpec as P

B = 128
HALO = 4
EDGE = 16
F32 = jnp.float32
BF16 = jnp.bfloat16
VMEM_LIMIT = 56 * 1024 * 1024


def shift(array, axis, by):
    size = lax.axis_size(axis)
    pairs = [(i, i + by) for i in range(size) if 0 <= i + by < size]
    return lax.ppermute(array, axis, pairs)


def dot_nt(a, b):
    return lax.dot_general(a, b, (((1,), (1,)), ((), ())), preferred_element_type=F32)


def dot(a, b):
    return jnp.dot(a, b, preferred_element_type=F32)


def iota(shape, dim):
    return lax.broadcasted_iota(jnp.int32, shape, dim)


def lane_gather(values, index):
    return jnp.take_along_axis(values, index, axis=1, mode="promise_in_bounds")


def sublane_gather(values, index):
    return jnp.take_along_axis(values, index, axis=0, mode="promise_in_bounds")


def down_lanes(row):
    return jnp.transpose(jnp.broadcast_to(row, (B, B)), (1, 0))


def pick_taps(far, near, disp, taps, radius, scale, first=0):
    count = far.shape[0]
    pixel = iota((count, B), 0) + first
    lane = iota((count, B), 1)
    merged = jnp.where(lane > pixel, far, near)
    level = disp + lane - radius
    usable = (level >= 0) & (level < B) & (lane < taps)
    picked = lane_gather(merged, (pixel - level) & (B - 1))
    return (jnp.where(usable, picked, 0.0) * scale).astype(BF16)


def silu(v):
    return v * jax.nn.sigmoid(v)


def edge_disp(values):
    return values[:, :B].astype(jnp.int32)


def right_corr_kernel(
    taps, radius, scale, left_ref, own_ref, disp_ref, edge_ref, weight_ref, mot_ref, pre_ref, pad_ref
):
    rows, _, chan = own_ref.shape
    pad_ref[...] = jnp.zeros_like(pad_ref)
    weight = weight_ref[...]
    for r in range(rows):
        edge = edge_ref[r]
        pad_ref[:EDGE] = edge[:, chan : 2 * chan]
        side = edge[:, :chan]
        scores = dot_nt(jnp.concatenate([left_ref[r], side], axis=0), own_ref[r])
        disp = down_lanes(disp_ref[r])
        main = pick_taps(scores[:B, :B], scores[:B, B:], disp, taps, radius, scale)
        disp = edge[:, 2 * chan + 2 * B :].astype(F32).astype(jnp.int32)
        beside = pick_taps(
            scores[B:, B:], dot_nt(side, pad_ref[...]), disp, taps, radius, scale
        )
        pre = dot(jnp.concatenate([main, beside], axis=0), weight)
        pre_ref[r] = pre[:B]
        mot_ref[r] = silu(pre).astype(BF16)


def left_corr_kernel(
    taps,
    radius,
    scale,
    left_ref,
    own_ref,
    before_ref,
    disp_ref,
    mot_right_ref,
    weight_ref,
    mot_ref,
    top_ref,
    low_ref,
    pre_ref,
    pad_ref,
):
    rows, _, chan = own_ref.shape
    step = pl.program_id(0)
    pad_ref[...] = jnp.zeros_like(pad_ref)
    weight = weight_ref[...]
    last = iota((EDGE, chan), 0) >= EDGE - HALO
    upper = iota((EDGE, B), 0) < EDGE // 2
    for r in range(rows):
        extra = before_ref[r, B:].astype(F32)
        pad_ref[B - EDGE :] = jnp.where(last, pltpu.roll(extra, 12, 0), 0.0).astype(BF16)
        side = jnp.where(last, pltpu.roll(extra, 8, 0), 0.0).astype(BF16)
        window = jnp.concatenate([before_ref[r, :B], own_ref[r]], axis=0)
        scores = dot_nt(jnp.concatenate([left_ref[r], side], axis=0), window)
        disp = down_lanes(disp_ref[r])
        main = pick_taps(scores[:B, :B], scores[:B, B:], disp, taps, radius, scale)
        disp = pltpu.roll(extra, 4, 0)[:, :B].astype(jnp.int32)
        beside = pick_taps(
            dot_nt(side, pad_ref[...]), scores[B:, :B], disp, taps, radius, scale, B - EDGE
        )
        pre = dot(jnp.concatenate([main, beside], axis=0), weight)
        pre_ref[r] = pre[:B]
        mot = silu(pre)
        mot_ref[r, :B] = mot[:B].astype(BF16)
        mot_ref[r, B : 2 * B] = mot_right_ref[r, :B]
        right_edge = mot_right_ref[r, B:].astype(F32)
        mot_ref[r, 2 * B :] = jnp.where(upper, right_edge, mot[B:]).astype(BF16)

    @pl.when(step == 0)
    def _():
        top_ref[...] = mot_ref[...]

    @pl.when(step == pl.num_programs(0) - 1)
    def _():
        low_ref[...] = mot_ref[...]


def shifted(value):
    return (
        pltpu.roll(value, 1, 0).astype(BF16),
        value.astype(BF16),
        pltpu.roll(value, value.shape[0] - 1, 0).astype(BF16),
    )


def store3(buf, row, value):
    for b, part in enumerate(shifted(value)):
        buf[row, :, b * B : (b + 1) * B] = part


def lanes(buf, rows, b):
    return jnp.concatenate([buf[r, :, b * B : (b + 1) * B] for r in rows], axis=0)


def patches(bufs, row_sets):
    return jnp.concatenate(
        [lanes(buf, rows, b) for rows in row_sets for b in range(3) for buf in bufs], axis=1
    )


def chunks(values, size):
    values = list(values)
    return [values[i : i + size] for i in range(0, len(values), size)]


CHUNK = 2


def gru_kernel(
    hid_ref,
    grad_ref,
    side_ref,
    hgt_ref,
    hgb_ref,
    mot_ref,
    mott_ref,
    motb_ref,
    prel_ref,
    prer_ref,
    disp_ref,
    wg_ref,
    wc_ref,
    wcb_ref,
    wgb_ref,
    mw_ref,
    nh_ref,
    pg_ref,
    tg_ref,
    h3_ref,
    m3_ref,
    r3_ref,
    c3_ref,
    h_ref,
    g_ref,
    up_ref,
    rs_ref,
    cb_ref,
):
    rows, own, _ = hid_ref.shape
    wide = own + EDGE
    total = rows + 2 * HALO
    inner = range(HALO, HALO + rows)

    for row in range(total):
        if row in inner:
            h_ref[row, :own] = hid_ref[row - HALO]
            h_ref[row, own:] = side_ref[row - HALO, :, :B]
            g_ref[row, :own] = grad_ref[row - HALO]
            g_ref[row, own:] = side_ref[row - HALO, :, B:]
            mot = mot_ref[row - HALO]
        elif row < HALO:
            h_ref[row] = hgt_ref[row, :, :B]
            g_ref[row] = hgt_ref[row, :, B:]
            mot = mott_ref[row]
        else:
            h_ref[row] = hgb_ref[row - HALO - rows, :, :B]
            g_ref[row] = hgb_ref[row - HALO - rows, :, B:]
            mot = motb_ref[row - HALO - rows]
        store3(h3_ref, row, h_ref[row].astype(F32))
        store3(m3_ref, row, mot.astype(F32))

    for group in chunks(range(1, total - 1), CHUNK * 2):
        lhs = patches((h3_ref, m3_ref), [[r + a - 1 for r in group] for a in range(3)])
        acc = jax.nn.sigmoid(dot(lhs, wg_ref[...]))
        for n, row in enumerate(group):
            gate = acc[n * wide : (n + 1) * wide]
            up_ref[row] = gate[:, :B]
            reset = gate[:, B:]
            rs_ref[row] = reset
            store3(r3_ref, row, reset * h_ref[row].astype(F32))

    for group in chunks(range(2, total - 2, 2), CHUNK * 2):
        lhs = patches((r3_ref, m3_ref), [[r + t - 1 for r in group] for t in range(4)])
        acc = jnp.tanh(dot(lhs, wc_ref[...]))
        for n, first in enumerate(group):
            for row in (first, first + 1):
                s = row - first
                cand = acc[n * wide : (n + 1) * wide, s * B : (s + 1) * B]
                hidden = h_ref[row].astype(F32)
                update = up_ref[row]
                if row in inner:
                    new = (1.0 - update) * hidden + update * cand
                    nh_ref[row - HALO] = new[:own].astype(BF16)
                gu = g_ref[row].astype(F32) * update
                store3(c3_ref, row, gu * (1.0 - cand * cand))
                store3(h3_ref, row, gu * (cand - hidden) * (1.0 - update))

    for group in chunks(range(3, total - 3), CHUNK * 2):
        lhs = patches((c3_ref,), [[r + a - 1 for r in group] for a in range(3)])
        acc = dot(lhs, wcb_ref[...])
        for n, row in enumerate(group):
            back = acc[n * wide : (n + 1) * wide]
            reset = rs_ref[row]
            store3(m3_ref, row, back[:, :B] * h_ref[row].astype(F32) * reset * (1.0 - reset))
            if row in inner:
                cb_ref[row - HALO] = back[:own, B:]

    for group in chunks(range(HALO, HALO + rows, 2), CHUNK * 2):
        lhs = patches((h3_ref, m3_ref), [[r + t - 1 for r in group] for t in range(4)])
        acc = dot(lhs, wgb_ref[...])
        for n, first in enumerate(group):
            for row in (first - HALO, first + 1 - HALO):
                s = row + HALO - first
                back = acc[n * wide : n * wide + own, s * B : (s + 1) * B]
                pre = jnp.concatenate([prel_ref[row], prer_ref[row]], axis=0)
                sig = jax.nn.sigmoid(pre)
                grad = (cb_ref[row] + back) * sig * (1.0 + pre * (1.0 - sig))
                grad = grad.astype(BF16)
                pg_ref[row] = grad
                tap = dot_nt(mw_ref[...], grad[:B])
                level = jnp.broadcast_to(disp_ref[row, :, :B].astype(F32), tap.shape)
                tg_ref[row] = jnp.where(iota(tap.shape, 0) == 15, level, tap).astype(BF16)


def spread(grad, disp, taps, radius):
    pixel = iota((B, B), 0)
    lane = iota((B, B), 1)
    tap = ((pixel - lane) & (B - 1)) - disp + radius
    ok = (tap >= 0) & (tap < taps)
    value = jnp.where(ok, lane_gather(grad, tap & (B - 1)), 0.0)
    far = jnp.where(lane > pixel, value, 0.0).astype(BF16)
    near = jnp.where(lane > pixel, 0.0, value).astype(BF16)
    return far, near


def spread_t(grad, disp, taps, radius):
    column = iota((B, B), 0)
    pixel = iota((B, B), 1)
    tap = ((pixel - column) & (B - 1)) - disp + radius
    value = jnp.zeros((B, B), F32)
    for k in range(taps):
        value = jnp.where(tap == k, grad[k : k + 1], value)
    far = jnp.where(column > pixel, value, 0.0).astype(BF16)
    near = jnp.where(column > pixel, 0.0, value).astype(BF16)
    return far, near


def grads_kernel(
    taps,
    radius,
    scale,
    pg_ref,
    left_ref,
    own_ref,
    before_ref,
    disp_ref,
    weight_ref,
    weight_t_ref,
    gl_ref,
    gr_ref,
    near_ref,
):
    rows = left_ref.shape[0]
    weight = weight_ref[...]
    weight_t = weight_t_ref[...]
    for r in range(rows):
        grads = dot(pg_ref[r], weight).astype(BF16).astype(F32)
        grads_t = dot_nt(weight_t, pg_ref[r]).astype(BF16).astype(F32)
        parts = []
        parts_t = []
        for block in range(2):
            at = slice(block * B, (block + 1) * B)
            row = disp_ref[r, :, at]
            parts.append(spread(grads[at], down_lanes(row), taps, radius))
            parts_t.append(spread_t(grads_t[:, at], row, taps, radius))
        window = jnp.concatenate([before_ref[r, :B], own_ref[r, :B]], axis=0)
        gl_ref[r, :B] = (dot(jnp.concatenate(parts[0], axis=1), window) * scale).astype(BF16)
        gl_ref[r, B:] = (dot(jnp.concatenate(parts[1], axis=1), own_ref[r]) * scale).astype(BF16)
        sg = jnp.concatenate([parts_t[0][1], parts_t[1][0]], axis=1)
        gr_ref[r] = (dot(sg, left_ref[r]) * scale).astype(BF16)
        near_ref[r] = parts_t[1][1]


def last_kernel(taps, radius, scale, near_ref, grad_ref, left_ref, next_ref, first_ref, gr_ref):
    del first_ref
    rows = left_ref.shape[0]
    for r in range(rows):
        grad = grad_ref[r].astype(F32)
        disp = grad[15:16].astype(jnp.int32)
        far, _ = spread_t(grad, disp, taps, radius)
        sg = jnp.concatenate([near_ref[r], far], axis=1)
        window = jnp.concatenate([left_ref[r], next_ref[r]], axis=0)
        gr_ref[r] = (dot(sg, window) * scale).astype(BF16)


def whole(array):
    nd = array.ndim
    return pl.BlockSpec(array.shape, lambda i: (0,) * nd)


def by_rows(array, size, block=None, at=None):
    block = tuple(array.shape[1:]) if block is None else block
    at = (0,) * len(block) if at is None else at
    return pl.BlockSpec((size,) + block, lambda i: (i,) + at)


def cost(flops, bytes_accessed):
    return pl.CostEstimate(flops=flops, bytes_accessed=bytes_accessed, transcendentals=0)


def paired(weight):
    rows = [
        jnp.pad(weight, ((0, 1), (0, 0), (0, 0))),
        jnp.pad(weight, ((1, 0), (0, 0), (0, 0))),
    ]
    return jnp.concatenate(rows, axis=2).reshape(-1, 2 * B)


def flipped(weight):
    return jnp.transpose(weight[::-1, ::-1], (0, 1, 3, 2))


def per_device(
    feat_left, feat_right, hidden, disparity, motion_weight, gate_weight, cand_weight, grad_hidden
):
    rows, cols, chan = feat_left.shape
    taps = motion_weight.shape[0]
    radius = taps // 2
    scale = 1.0 / math.sqrt(chan)
    args = (taps, radius, scale)
    size = 4
    grid = (rows // size,)
    wide = cols + EDGE
    params = pltpu.CompilerParams(vmem_limit_bytes=VMEM_LIMIT)
    shape = jax.ShapeDtypeStruct

    level = disparity.astype(BF16)[:, :, None]
    before = shift(
        jnp.concatenate(
            [
                feat_right[:, cols - B :],
                feat_right[:, cols - B - HALO : cols - B],
                feat_left[:, cols - HALO :],
                jnp.broadcast_to(level[:, cols - HALO :], (rows, HALO, chan)),
                jnp.zeros((rows, HALO, chan), BF16),
            ],
            axis=1,
        ),
        "cols",
        1,
    )
    from_right = shift(
        jnp.concatenate(
            [
                feat_left[:, :HALO],
                feat_right[:, :HALO],
                hidden[:, :HALO],
                grad_hidden[:, :HALO],
                jnp.broadcast_to(level[:, :HALO], (rows, HALO, B)),
            ],
            axis=2,
        ),
        "cols",
        -1,
    )
    from_left = shift(
        jnp.concatenate([hidden[:, cols - HALO :], grad_hidden[:, cols - HALO :]], axis=2), "cols", 1
    )
    edge = jnp.pad(from_right, ((0, 0), (0, EDGE - HALO), (0, 0)))
    side = jnp.concatenate(
        [
            from_right[:, :, 2 * chan : 2 * chan + 2 * B],
            jnp.zeros((rows, EDGE - 2 * HALO, 2 * B), BF16),
            from_left,
        ],
        axis=1,
    )

    def rim(at):
        own = jnp.concatenate([hidden[at : at + HALO], grad_hidden[at : at + HALO]], axis=2)
        return jnp.concatenate([own, side[at : at + HALO]], axis=1)

    hg_top = shift(rim(rows - HALO), "rows", 1)
    hg_low = shift(rim(0), "rows", -1)

    wg = gate_weight.reshape(-1, 2 * B)
    wc = paired(cand_weight.reshape(3, 6 * B, B))
    wcb = flipped(cand_weight).reshape(-1, 2 * B)
    wgb = paired(flipped(gate_weight[:, :, B:]).reshape(3, 6 * B, B))
    mw = jnp.pad(motion_weight, ((0, B - taps), (0, 0)))
    mw_t = jnp.pad(motion_weight.T, ((0, 0), (0, B - taps)))
    mw16 = jnp.pad(motion_weight, ((0, 16 - taps), (0, 0)))
    disp3 = disparity[:, None, :]

    pad = [pltpu.VMEM((B, chan), BF16)]
    lookup_cost = cost(2 * rows * B * 2 * B * chan, 6 << 20)
    right_shapes = (shape((rows, B + EDGE, B), BF16), shape((rows, B, B), F32))
    mot_right, pre_right = pl.pallas_call(
        lambda *refs: right_corr_kernel(*args, *refs),
        grid=grid,
        in_specs=[
            by_rows(feat_left, size, (B, chan), (1, 0)),
            by_rows(feat_right, size),
            by_rows(disp3, size, (1, B), (0, 1)),
            by_rows(edge, size),
            whole(mw),
        ],
        out_specs=[by_rows(s, size) for s in right_shapes],
        out_shape=right_shapes,
        scratch_shapes=pad,
        compiler_params=params,
        cost_estimate=lookup_cost,
        name="corr_right",
    )(feat_left, feat_right, disp3, edge, mw)

    mot_shape = shape((rows, wide, B), BF16)
    rim_shape = shape((HALO, wide, B), BF16)
    motion, mot_first, mot_last, pre_left = pl.pallas_call(
        lambda *refs: left_corr_kernel(*args, *refs),
        grid=grid,
        in_specs=[
            by_rows(feat_left, size, (B, chan), (0, 0)),
            by_rows(feat_right, size, (B, chan), (0, 0)),
            by_rows(before, size),
            by_rows(disp3, size, (1, B), (0, 0)),
            by_rows(mot_right, size),
            whole(mw),
        ],
        out_specs=[
            by_rows(mot_shape, size),
            whole(rim_shape),
            whole(rim_shape),
            by_rows(right_shapes[1], size),
        ],
        out_shape=(mot_shape, rim_shape, rim_shape, right_shapes[1]),
        scratch_shapes=pad,
        compiler_params=params,
        cost_estimate=lookup_cost,
        name="corr_left",
    )(feat_left, feat_right, before, disp3, mot_right, mw)
    mot_top = shift(mot_last, "rows", 1)
    mot_low = shift(mot_first, "rows", -1)
    first_left, _ = lax.optimization_barrier((feat_left[:, :B], motion))
    next_left = shift(first_left, "cols", -1)

    total = rows + 2 * HALO
    own_shape = shape((rows, cols, B), BF16)
    operands = (
        hidden,
        grad_hidden,
        side,
        hg_top,
        hg_low,
        motion,
        mot_top,
        mot_low,
        pre_left,
        pre_right,
        disp3,
        wg,
        wc,
        wcb,
        wgb,
        mw16,
    )
    vmem = pl.BlockSpec(memory_space=pltpu.VMEM)
    new_hidden, pre_grad, tap_grad = pl.pallas_call(
        gru_kernel,
        in_specs=[vmem] * len(operands),
        out_specs=[vmem] * 3,
        out_shape=(own_shape, own_shape, shape((rows, 16, B), BF16)),
        scratch_shapes=[pltpu.VMEM((total, wide, 3 * B), BF16)] * 4
        + [pltpu.VMEM((total, wide, B), BF16)] * 2
        + [pltpu.VMEM((total, wide, B), F32)] * 2
        + [pltpu.VMEM((rows, cols, B), F32)],
        compiler_params=params,
        cost_estimate=cost(2 * 22 * wide * 256 * 256 * 24, 16 << 20),
        name="gru",
    )(*operands)
    next_grad = shift(tap_grad, "cols", -1)

    feat_shape = shape((rows, cols, chan), BF16)
    near_shape = shape((rows, B, B), BF16)
    grad_left, grad_first, near = pl.pallas_call(
        lambda *refs: grads_kernel(*args, *refs),
        grid=grid,
        in_specs=[
            by_rows(pre_grad, size),
            by_rows(feat_left, size),
            by_rows(feat_right, size),
            by_rows(before, size),
            by_rows(disp3, size),
            whole(mw_t),
            whole(mw16),
        ],
        out_specs=[
            by_rows(feat_shape, size),
            by_rows(feat_shape, size, (B, chan), (0, 0)),
            by_rows(near_shape, size),
        ],
        out_shape=(feat_shape, feat_shape, near_shape),
        compiler_params=params,
        cost_estimate=cost(2 * rows * B * 2 * B * chan * 4, 12 << 20),
        name="grads",
    )(pre_grad, feat_left, feat_right, before, disp3, mw_t, mw16)
    grad_right = pl.pallas_call(
        lambda *refs: last_kernel(*args, *refs),
        grid=grid,
        in_specs=[
            by_rows(near, size),
            by_rows(next_grad, size),
            by_rows(feat_left, size, (B, chan), (1, 0)),
            by_rows(next_left, size),
            pl.BlockSpec(memory_space=pl.ANY),
        ],
        out_specs=by_rows(feat_shape, size, (B, chan), (1, 0)),
        out_shape=feat_shape,
        input_output_aliases={4: 0},
        compiler_params=params,
        cost_estimate=cost(2 * rows * B * 2 * B * chan, 4 << 20),
        name="grad_right",
    )(near, next_grad, feat_left, next_left, grad_first)
    return (new_hidden, grad_left, grad_right)


def solution(mesh):
    grid3 = P("rows", "cols", None)
    return jax.shard_map(
        per_device,
        mesh=mesh,
        in_specs=(grid3, grid3, grid3, P("rows", "cols"), P(), P(), P(), grid3),
        out_specs=(grid3, grid3, grid3),
        check_vma=False,
    )
```

time: 156 us -> 144 us (0.923)
  starting transfers between devices: 48.3 us -> 28.9 us
  waiting for transfers between devices: 11.5 us -> 28.2 us
  Pallas kernels: 62.6 us -> 57 us
  local copies, waits for them, and re-layouts: 25.3 us -> 21.8 us
    ppermute x15 -> x9, starting transfers between devices: 48.3 us -> 28.9 us  [shift(): return lax.ppermute(array, axis, pairs)]
    ppermute x15 -> x9, waiting for transfers between devices: 11.5 us -> 28.2 us  [shift(): return lax.ppermute(array, axis, pairs)]
    slice x15 -> x11, local copies, waits for them, and re-layouts: 9.39 us -> 5.32 us  [the longest x1 1.6 us: per_device(): feat_left[:, cols - HALO:]]
    concatenate x3 -> x2, local copies, waits for them, and re-layouts: 0.4 us -> 4.2 us  [the longest x1 4.12 us: per_device(): jnp.concatenate([feat_right[:, cols - B:], feat_right[:, cols - B - HALO:...]
    pallas_call x1, Pallas kernels: 10 us -> 6.68 us  [per_device(): pl.pallas_call(lambda *refs: right_corr_kernel(*args, *refs), grid=grid,...]
    transpose x4 -> x2, local copies, waits for them, and re-layouts: 4.17 us -> 1.12 us  [flipped(): return jnp.transpose(weight[::-1, ::-1], (0, 1, 3, 2))]
    pallas_call x3 -> x1, Pallas kernels: 32.6 us -> 30.5 us  [per_device(): pl.pallas_call(gru_kernel, in_specs=[vmem] * len(operands), out_specs=[vm...]
    concatenate x5 -> x6, other arithmetic: 5.61 us -> 4.41 us  [the longest x2 2.57 us: paired(): return jnp.concatenate(rows, axis=2).reshape(-1, 2 * B)]
  transfers between devices with their start and end apart: 15 -> 9, of which waited for: 1 -> 2; matrix products, arithmetic and copies ran while one was open for 15% -> 11% of each run, Pallas kernels for 37% -> 37%
where the time goes in v2:
time: 144 us; the launch traced here: 142 us
  Pallas kernels  57 us (40%)
  starting transfers between devices  28.9 us (20%)
  waiting for transfers between devices  28.2 us (20%)
  local copies, waits for them, and re-layouts  21.8 us (15%)
  other arithmetic  5.13 us (4%)
    pallas_call x1, Pallas kernels, per_device(): pl.pallas_call(gru_kernel, in_specs=[vmem] * len(operands), out_specs=[vm...  30.5 us
    ppermute x9, starting transfers between devices, shift(): return lax.ppermute(array, axis, pairs)  28.9 us
    ppermute x9, waiting for transfers between devices, shift(): return lax.ppermute(array, axis, pairs)  28.2 us
    pallas_call x1, Pallas kernels, per_device(): pl.pallas_call(lambda *refs: grads_kernel(*args, *refs), grid=grid, in_sp...  8.29 us
    pallas_call x1, Pallas kernels, per_device(): pl.pallas_call(lambda *refs: left_corr_kernel(*args, *refs), grid=grid, i...  7.22 us
    unnamed x30, local copies, waits for them, and re-layouts  6.96 us
    pallas_call x1, Pallas kernels, per_device(): pl.pallas_call(lambda *refs: right_corr_kernel(*args, *refs), grid=grid,...  6.68 us
    pallas_call x1, Pallas kernels, per_device(): pl.pallas_call(lambda *refs: last_kernel(*args, *refs), grid=grid, in_spe...  4.32 us
  transfers between devices with their start and end apart: 9, of which 2 were waited for; matrix products, arithmetic and copies ran while one was open for 11% of the time, Pallas kernels for 37%

profile of v2, /device:TPU:120, one launch (start us, length us, event | category | flops | bytes accessed | tf_op | source)
XLA Modules:
  0.0 142.0 jit_solution(4940055547499701520)
XLA Ops:
  0.6 0.0 slice-start
  0.6 1.6 %fusion.6 = (bf16[16,4,256]{2,1,0:T(4,128)(2,1)S(1)}, bf16[16,4,896]{2,1,0:T(4,128)(2,1)}) fusion(bf16[16,256,256]{2,1,0:T(8,128)(2,1)} %refs_2_.3), kind=kLoop, calls=%fused_computation.21 | loop fusion | bytes 131072 | tf_op jit(solution)/shard_map/slice | solution.py:395
  2.2 0.7 convert_bitcast_fusion
  3.0 0.1 slice_bitcast_fusion
  3.0 1.5 %fusion.7 = (bf16[16,4,256]{2,1,0:T(4,128)(2,1)S(1)}, bf16[16,4,896]{2,1,0:T(4,128)(2,1)}) fusion(bf16[16,256,256]{2,1,0:T(8,128)(2,1)} %refs_2_.2, bf16[16,4,896]{2,1,0:T(4,128)(2,1)} %get-tuple-element.30), kind=kLoop, calls=%fused_computation.22 | loop fusion | bytes 131072 | tf_op jit(solution)/shard_map/slice | solution.py:394
  4.6 1.4 slice_dynamic-update-slice_fusion.3
  6.0 1.4 slice_dynamic-update-slice_fusion.2
  7.3 0.7 constant_dynamic-update-slice_fusion
  8.0 4.8 %collective-permute-start = (bf16[16,4,896]{2,1,0:T(4,128)(2,1)}, bf16[16,4,896]{2,1,0:T(4,128)(2,1)S(1)}, u32[]{:S(2)}, u32[]{:S(2)}) collective-permute-start(bf16[16,4,896]{2,1,0:T(4,128)(2,1)} %constant_dynamic-update-slice_fusion), channel_id=1, source_target_pairs={{1,0},{2,1},{3,2},{4,3},{5,4},{6,5},{7,6},{9,8},{10,9},{11,10},{12... | collective-permute-start | bytes 344072 | tf_op jit(solution)/shard_map/ppermute | solution.py:21
  12.8 0.0 copy-start.5
  12.8 0.1 broadcast_in_dim.31
  12.9 0.0 copy-start.6
  12.9 4.1 %concatenate.37 = bf16[16,144,256]{2,1,0:T(8,128)(2,1)} concatenate(bf16[16,128,256]{2,1,0:T(8,128)(2,1)S(1)} %slice-done, bf16[16,4,256]{2,1,0:T(4,128)(2,1)S(1)} %get-tuple-element.31, bf16[16,4,256]{2,1,0:T(4,128)(2,1)S(1)} %get-tuple-element.29, bf16[16,4,256]{2,1,0:T(4,128)(2,1)S(1)} %broadcast_in_dim.31, bf16[16,4,256]{2,1,0:T(4,128)(2,1)S(1)} %broadcast_in_dim.32), dimensions={1} | concatenate | bytes 2359296 | tf_op jit(solution)/shard_map/concatenate | solution.py:391
  17.1 2.6 %collective-permute-start.4 = (bf16[16,144,256]{2,1,0:T(8,128)(2,1)}, bf16[16,144,256]{2,1,0:T(8,128)(2,1)S(1)}, u32[]{:S(2)}, u32[]{:S(2)}) collective-permute-start(bf16[16,144,256]{2,1,0:T(8,128)(2,1)} %concatenate.37), channel_id=1, source_target_pairs={{0,1},{1,2},{2,3},{3,4},{4,5},{5,6},{6,7},{8,9},{9,10},{10,11},{11... | collective-permute-start | bytes 3538952 | tf_op jit(solution)/shard_map/ppermute | solution.py:21
  19.7 1.9 %collective-permute-start.1 = (bf16[16,4,256]{2,1,0:T(4,128)(2,1)S(1)}, bf16[16,4,256]{2,1,0:T(4,128)(2,1)S(1)}, u32[]{:S(2)}, u32[]{:S(2)}) collective-permute-start(bf16[16,4,256]{2,1,0:T(4,128)(2,1)S(1)} %pad_maximum_fusion.3), channel_id=1, source_target_pairs={{0,1},{1,2},{2,3},{3,4},{4,5},{5,6},{6,7},{8,9},{9,10},{10,11},{11... | collective-permute-start | bytes 98312 | tf_op jit(solution)/shard_map/ppermute | solution.py:21
  21.7 0.0 copy-start.9
  21.7 0.0 copy-start.10
  21.7 0.0 copy-start
  21.7 0.1 pad.49.clone
  21.8 0.0 collective-permute-done
  21.8 27.8 %collective-permute-done.1 = bf16[16,4,256]{2,1,0:T(4,128)(2,1)S(1)} collective-permute-done((bf16[16,4,256]{2,1,0:T(4,128)(2,1)S(1)}, bf16[16,4,256]{2,1,0:T(4,128)(2,1)S(1)}, u32[]{:S(2)}, u32[]{:S(2)}) %collective-permute-start.1) | collective-permute-done | bytes 32800 | tf_op jit(solution)/shard_map/ppermute | solution.py:21
  49.7 0.1 pad_maximum_fusion.2.side_ref
  49.8 0.9 pad_maximum_fusion
  50.7 1.9 %collective-permute-start.2 = (bf16[4,272,256]{2,1,0:T(8,128)(2,1)}, bf16[4,272,256]{2,1,0:T(8,128)(2,1)}, u32[]{:S(2)}, u32[]{:S(2)}) collective-permute-start(bf16[4,272,256]{2,1,0:T(8,128)(2,1)} %pad_maximum_fusion), channel_id=1, source_target_pairs={{0,8},{8,16},{16,24},{24,32},{32,40},{40,48},{48,56},{56,64},{64,7... | collective-permute-start | bytes 1671176 | tf_op jit(solution)/shard_map/ppermute | solution.py:21
  52.6 0.9 pad_maximum_fusion.1
  53.5 4.5 %collective-permute-start.3 = (bf16[4,272,256]{2,1,0:T(8,128)(2,1)}, bf16[4,272,256]{2,1,0:T(8,128)(2,1)}, u32[]{:S(2)}, u32[]{:S(2)}) collective-permute-start(bf16[4,272,256]{2,1,0:T(8,128)(2,1)} %pad_maximum_fusion.1), channel_id=1, source_target_pairs={{8,0},{16,8},{24,16},{32,24},{40,32},{48,40},{56,48},{64,56},{72,6... | collective-permute-start | bytes 1671176 | tf_op jit(solution)/shard_map/ppermute | solution.py:21
  58.0 0.6 broadcast_in_dim.33.refs_2_.refs_3_.disp_ref.refs_4_
  58.6 0.6 pad.31.refs_4_.refs_5_
  59.2 0.6 pad.36.mw_ref.refs_6_
  59.8 0.8 copy.24
  60.6 0.0 copy-done
  60.6 1.0 slice.79
  61.7 1.1 slice-done.1
  62.8 0.3 copy.27
  63.2 1.1 copy.22
  64.3 0.6 pad.37.refs_5_
  64.9 0.8 pad.30.refs_3_
  65.7 6.7 %corr_right.1 = (bf16[16,144,128]{2,1,0:T(8,128)(2,1)}, f32[16,128,128]{2,1,0:T(8,128)}) custom-call(bf16[16,256,256]{2,1,0:T(8,128)(2,1)} %refs_2_.3, bf16[16,256,256]{2,1,0:T(8,128)(2,1)} %refs_2_.2, s32[16,1,256]{2,1,0:T(1,128)} %broadcast_in_dim.33.refs_2_.refs_3_.disp_ref.refs_4_, bf16[16,16,896]{2,1,0:T(8,128)(2,1)} %pad.30.refs_3_, ...), custom_call_target="tpu_custom_call" | custom-call | flops 268435456 | bytes 6291456 | tf_op jit(solution)/shard_map/corr_right/pallas_call | solution.py:450
  72.4 0.0 collective-permute-done.4.refs_2_.refs_3_
  72.4 0.0 copy-start.1
  72.4 1.0 copy-done.1
  73.4 7.2 %corr_left.1 = (bf16[16,272,128]{2,1,0:T(8,128)(2,1)}, bf16[4,272,128]{2,1,0:T(8,128)(2,1)}, bf16[4,272,128]{2,1,0:T(8,128)(2,1)}, f32[16,128,128]{2,1,0:T(8,128)}) custom-call(bf16[16,256,256]{2,1,0:T(8,128)(2,1)} %refs_2_.3, bf16[16,256,256]{2,1,0:T(8,128)(2,1)} %refs_2_.2, bf16[16,144,256]{2,1,0:T(8,128)(2,1)} %copy-done.1, ...), custom_call_target="tpu_custom_call" | custom-call | flops 268435456 | bytes 6291456 | tf_op jit(solution)/shard_map/corr_left/pallas_call | solution.py:470
  80.7 1.9 %collective-permute-start.5 = (bf16[4,272,128]{2,1,0:T(8,128)(2,1)}, bf16[4,272,128]{2,1,0:T(8,128)(2,1)S(1)}, u32[]{:S(2)}, u32[]{:S(2)}) collective-permute-start(bf16[4,272,128]{2,1,0:T(8,128)(2,1)} %get-tuple-element.18), channel_id=1, source_target_pairs={{0,8},{8,16},{16,24},{24,32},{32,40},{40,48},{48,56},{56,64},{64,7... | collective-permute-start | bytes 835592 | tf_op jit(solution)/shard_map/ppermute | solution.py:21
  82.6 4.5 %collective-permute-start.6 = (bf16[4,272,128]{2,1,0:T(8,128)(2,1)}, bf16[4,272,128]{2,1,0:T(8,128)(2,1)S(1)}, u32[]{:S(2)}, u32[]{:S(2)}) collective-permute-start(bf16[4,272,128]{2,1,0:T(8,128)(2,1)} %get-tuple-element.19), channel_id=1, source_target_pairs={{8,0},{16,8},{24,16},{32,24},{40,32},{48,40},{56,48},{64,56},{72,6... | collective-permute-start | bytes 835592 | tf_op jit(solution)/shard_map/ppermute | solution.py:21
  87.1 1.3 fusion.5
  88.4 1.3 fusion.4
  89.7 0.3 copy-done.4
  90.0 2.1 %collective-permute-start.8 = (bf16[16,128,256]{2,1,0:T(8,128)(2,1)S(1)}, bf16[16,128,256]{2,1,0:T(8,128)(2,1)S(1)}, u32[]{:S(2)}, u32[]{:S(2)}) collective-permute-start(bf16[16,128,256]{2,1,0:T(8,128)(2,1)S(1)} %copy-done.4), channel_id=1, source_target_pairs={{1,0},{2,1},{3,2},{4,3},{5,4},{6,5},{7,6},{9,8},{10,9},{11,10},{12... | collective-permute-start | bytes 3145736 | tf_op jit(solution)/shard_map/ppermute | solution.py:21
  92.1 0.0 collective-permute-done.2.hgt_ref
  92.1 0.0 collective-permute-done.3.hgb_ref
  92.1 0.0 collective-permute-done.5.mott_ref
  92.1 0.0 copy-start.11
  92.2 0.3 collective-permute-done.6.motb_ref
  92.5 0.4 copy-done.11
  92.9 0.3 copy-done.12
  93.2 30.5 %gru.1 = (bf16[16,256,128]{2,1,0:T(8,128)(2,1)}, bf16[16,256,128]{2,1,0:T(8,128)(2,1)}, bf16[16,16,128]{2,1,0:T(8,128)(2,1)}) custom-call(bf16[16,256,128]{2,1,0:T(8,128)(2,1)} %hid_ref.1, bf16[16,256,128]{2,1,0:T(8,128)(2,1)} %grad_ref.1, bf16[16,16,256]{2,1,0:T(8,128)(2,1)} %copy-done.7, bf16[4,272,256]{2,1,0:T(8,128)(2,1)} %collective-permute-done.2.hgt_ref, ...), custom_call_target="tpu_custom_call" | custom-call | flops 18824036352 | bytes 16777216 | tf_op jit(solution)/shard_map/gru/pallas_call | solution.py:519
  123.7 4.7 %collective-permute-start.7 = (bf16[16,16,128]{2,1,0:T(8,128)(2,1)}, bf16[16,16,128]{2,1,0:T(8,128)(2,1)S(1)}, u32[]{:S(2)}, u32[]{:S(2)}) collective-permute-start(bf16[16,16,128]{2,1,0:T(8,128)(2,1)} %get-tuple-element.26), channel_id=1, source_target_pairs={{1,0},{2,1},{3,2},{4,3},{5,4},{6,5},{7,6},{9,8},{10,9},{11,10},{12... | collective-permute-start | bytes 196616 | tf_op jit(solution)/shard_map/ppermute | solution.py:21
  128.4 8.3 %grads.1 = (bf16[16,256,256]{2,1,0:T(8,128)(2,1)}, bf16[16,256,256]{2,1,0:T(8,128)(2,1)}, bf16[16,128,128]{2,1,0:T(8,128)(2,1)}) custom-call(bf16[16,256,128]{2,1,0:T(8,128)(2,1)} %get-tuple-element.23.refs_0_, bf16[16,256,256]{2,1,0:T(8,128)(2,1)} %refs_2_.3, bf16[16,256,256]{2,1,0:T(8,128)(2,1)} %refs_2_.2, bf16[16,144,256]{2,1,0:T(8,128)(2,1)} %copy-done.1, ...), custom_call_target="tpu_custom_call" | custom-call | flops 1073741824 | bytes 12582912 | tf_op jit(solution)/shard_map/grads/pallas_call | solution.py:536
  136.7 0.0 collective-permute-done.7.refs_1_
  136.7 0.0 collective-permute-done.8.refs_3_
  136.7 0.0 copy-start.3
  136.7 0.6 copy-done.8
  137.3 0.4 copy-done.3
  137.7 4.3 %grad_right.1 = bf16[16,256,256]{2,1,0:T(8,128)(2,1)} custom-call(bf16[16,128,128]{2,1,0:T(8,128)(2,1)} %get-tuple-element.25.refs_0_, bf16[16,16,128]{2,1,0:T(8,128)(2,1)} %copy-done.8, bf16[16,256,256]{2,1,0:T(8,128)(2,1)} %refs_2_.3, bf16[16,128,256]{2,1,0:T(8,128)(2,1)} %copy-done.3, ...), custom_call_target="tpu_custom_call", output_to_operand_aliasing={{}: (4, {})} | custom-call | flops 268435456 | bytes 4194304 | tf_op jit(solution)/shard_map/grad_right/pallas_call | solution.py:558
  (22 shorter events, 0.2 us)
Async XLA Ops:
  0.6 12.3 %slice-start = ((bf16[16,256,256]{2,1,0:T(8,128)(2,1)}), bf16[16,128,256]{2,1,0:T(8,128)(2,1)S(1)}, s32[]{:S(2)}) async-start(bf16[16,256,256]{2,1,0:T(8,128)(2,1)} %refs_2_.2), calls=%async_computation | async-start | bytes 2097152 | tf_op jit(solution)/shard_map/slice | solution.py:393
  8.0 13.8 %collective-permute-start = (bf16[16,4,896]{2,1,0:T(4,128)(2,1)}, bf16[16,4,896]{2,1,0:T(4,128)(2,1)S(1)}, u32[]{:S(2)}, u32[]{:S(2)}) collective-permute-start(bf16[16,4,896]{2,1,0:T(4,128)(2,1)} %constant_dynamic-update-slice_fusion), channel_id=1, source_target_pairs={{1,0},{2,1},{3,2},{4,3},{5,4},{6,5},{7,6},{9,8},{10,9},{11,10},{12... | collective-permute-start | bytes 344072 | tf_op jit(solution)/shard_map/ppermute | solution.py:21
  12.8 8.8 %copy-start.5 = (bf16[16,256,128]{2,1,0:T(8,128)(2,1)S(1)}, bf16[16,256,128]{2,1,0:T(8,128)(2,1)}, u32[]{:S(2)}) copy-start(bf16[16,256,128]{2,1,0:T(8,128)(2,1)} %hid_ref.1) | copy-start | bytes 3145732
  12.9 8.7 %copy-start.6 = (bf16[16,256,128]{2,1,0:T(8,128)(2,1)S(1)}, bf16[16,256,128]{2,1,0:T(8,128)(2,1)}, u32[]{:S(2)}) copy-start(bf16[16,256,128]{2,1,0:T(8,128)(2,1)} %grad_ref.1) | copy-start | bytes 3145732
  17.1 55.3 %collective-permute-start.4 = (bf16[16,144,256]{2,1,0:T(8,128)(2,1)}, bf16[16,144,256]{2,1,0:T(8,128)(2,1)S(1)}, u32[]{:S(2)}, u32[]{:S(2)}) collective-permute-start(bf16[16,144,256]{2,1,0:T(8,128)(2,1)} %concatenate.37), channel_id=1, source_target_pairs={{0,1},{1,2},{2,3},{3,4},{4,5},{5,6},{6,7},{8,9},{9,10},{10,11},{11... | collective-permute-start | bytes 3538952 | tf_op jit(solution)/shard_map/ppermute | solution.py:21
  19.7 30.0 %collective-permute-start.1 = (bf16[16,4,256]{2,1,0:T(4,128)(2,1)S(1)}, bf16[16,4,256]{2,1,0:T(4,128)(2,1)S(1)}, u32[]{:S(2)}, u32[]{:S(2)}) collective-permute-start(bf16[16,4,256]{2,1,0:T(4,128)(2,1)S(1)} %pad_maximum_fusion.3), channel_id=1, source_target_pairs={{0,1},{1,2},{2,3},{3,4},{4,5},{5,6},{6,7},{8,9},{9,10},{10,11},{11... | collective-permute-start | bytes 98312 | tf_op jit(solution)/shard_map/ppermute | solution.py:21
  21.7 36.3 %copy-start.9 = (s32[16,256]{1,0:T(8,128)S(1)}, s32[16,256]{1,0:T(8,128)}, u32[]{:S(2)}) copy-start(s32[16,256]{1,0:T(8,128)} %param.11) | copy-start | bytes 49156
  21.7 36.9 %copy-start.10 = (bf16[9,128]{1,0:T(8,128)(2,1)S(1)}, bf16[9,128]{1,0:T(8,128)(2,1)}, u32[]{:S(2)}) copy-start(bf16[9,128]{1,0:T(8,128)(2,1)} %param.12) | copy-start | bytes 6916
  21.7 38.9 %copy-start = (bf16[16,256,256]{2,1,0:T(8,128)(2,1)S(1)}, bf16[16,256,256]{2,1,0:T(8,128)(2,1)}, u32[]{:S(2)}) copy-start(bf16[16,256,256]{2,1,0:T(8,128)(2,1)} %refs_2_.3) | copy-start | bytes 6291460
  49.8 11.9 %copy-start.7 = (bf16[16,16,256]{2,1,0:T(8,128)(2,1)}, bf16[16,16,256]{2,1,0:T(8,128)(2,1)S(1)}, u32[]{:S(2)}) copy-start(bf16[16,16,256]{2,1,0:T(8,128)(2,1)S(1)} %pad_maximum_fusion.2.side_ref) | copy-start | bytes 393220
  50.7 41.4 %collective-permute-start.2 = (bf16[4,272,256]{2,1,0:T(8,128)(2,1)}, bf16[4,272,256]{2,1,0:T(8,128)(2,1)}, u32[]{:S(2)}, u32[]{:S(2)}) collective-permute-start(bf16[4,272,256]{2,1,0:T(8,128)(2,1)} %pad_maximum_fusion), channel_id=1, source_target_pairs={{0,8},{8,16},{16,24},{24,32},{32,40},{40,48},{48,56},{56,64},{64,7... | collective-permute-start | bytes 1671176 | tf_op jit(solution)/shard_map/ppermute | solution.py:21
  53.5 38.7 %collective-permute-start.3 = (bf16[4,272,256]{2,1,0:T(8,128)(2,1)}, bf16[4,272,256]{2,1,0:T(8,128)(2,1)}, u32[]{:S(2)}, u32[]{:S(2)}) collective-permute-start(bf16[4,272,256]{2,1,0:T(8,128)(2,1)} %pad_maximum_fusion.1), channel_id=1, source_target_pairs={{8,0},{16,8},{24,16},{32,24},{40,32},{48,40},{56,48},{64,56},{72,6... | collective-permute-start | bytes 1671176 | tf_op jit(solution)/shard_map/ppermute | solution.py:21
  61.7 1.1 slice-start.1
  61.7 1.4 copy-start.2
  72.4 1.0 copy-start.1
  80.7 11.5 %collective-permute-start.5 = (bf16[4,272,128]{2,1,0:T(8,128)(2,1)}, bf16[4,272,128]{2,1,0:T(8,128)(2,1)S(1)}, u32[]{:S(2)}, u32[]{:S(2)}) collective-permute-start(bf16[4,272,128]{2,1,0:T(8,128)(2,1)} %get-tuple-element.18), channel_id=1, source_target_pairs={{0,8},{8,16},{16,24},{24,32},{32,40},{40,48},{48,56},{56,64},{64,7... | collective-permute-start | bytes 835592 | tf_op jit(solution)/shard_map/ppermute | solution.py:21
  82.6 9.9 %collective-permute-start.6 = (bf16[4,272,128]{2,1,0:T(8,128)(2,1)}, bf16[4,272,128]{2,1,0:T(8,128)(2,1)S(1)}, u32[]{:S(2)}, u32[]{:S(2)}) collective-permute-start(bf16[4,272,128]{2,1,0:T(8,128)(2,1)} %get-tuple-element.19), channel_id=1, source_target_pairs={{8,0},{16,8},{24,16},{32,24},{40,32},{48,40},{56,48},{64,56},{72,6... | collective-permute-start | bytes 835592 | tf_op jit(solution)/shard_map/ppermute | solution.py:21
  88.4 1.6 %copy-start.4 = (bf16[16,128,256]{2,1,0:T(8,128)(2,1)S(1)}, bf16[16,128,256]{2,1,0:T(8,128)(2,1)}, u32[]{:S(2)}) copy-start(bf16[16,128,256]{2,1,0:T(8,128)(2,1)} %slice.79) | copy-start | bytes 3145732
  90.0 46.7 %collective-permute-start.8 = (bf16[16,128,256]{2,1,0:T(8,128)(2,1)S(1)}, bf16[16,128,256]{2,1,0:T(8,128)(2,1)S(1)}, u32[]{:S(2)}, u32[]{:S(2)}) collective-permute-start(bf16[16,128,256]{2,1,0:T(8,128)(2,1)S(1)} %copy-done.4), channel_id=1, source_target_pairs={{1,0},{2,1},{3,2},{4,3},{5,4},{6,5},{7,6},{9,8},{10,9},{11,10},{12... | collective-permute-start | bytes 3145736 | tf_op jit(solution)/shard_map/ppermute | solution.py:21
  92.1 0.7 copy-start.11
  92.5 0.7 copy-start.12
  123.7 13.0 %collective-permute-start.7 = (bf16[16,16,128]{2,1,0:T(8,128)(2,1)}, bf16[16,16,128]{2,1,0:T(8,128)(2,1)S(1)}, u32[]{:S(2)}, u32[]{:S(2)}) collective-permute-start(bf16[16,16,128]{2,1,0:T(8,128)(2,1)} %get-tuple-element.26), channel_id=1, source_target_pairs={{1,0},{2,1},{3,2},{4,3},{5,4},{6,5},{7,6},{9,8},{10,9},{11,10},{12... | collective-permute-start | bytes 196616 | tf_op jit(solution)/shard_map/ppermute | solution.py:21
  136.7 0.6 copy-start.8
  136.7 1.0 copy-start.3

commit v3 on v2

v3 whole, which is shorter than its diff:
```python
import math

import jax
import jax.numpy as jnp
from jax import lax
from jax.experimental import pallas as pl
from jax.experimental.pallas import tpu as pltpu
from jax.sharding import PartitionSpec as P

B = 128
HALO = 4
EDGE = 16
F32 = jnp.float32
BF16 = jnp.bfloat16
ROWS = 4
SMALL_VMEM = 16 * 1024 * 1024
GRU_VMEM = 56 * 1024 * 1024


def shift(array, axis, by):
    size = lax.axis_size(axis)
    pairs = [(i, i + by) for i in range(size) if 0 <= i + by < size]
    return lax.ppermute(array, axis, pairs)


def dot_nt(a, b):
    return lax.dot_general(a, b, (((1,), (1,)), ((), ())), preferred_element_type=F32)


def dot(a, b):
    return jnp.dot(a, b, preferred_element_type=F32)


def iota(shape, dim):
    return lax.broadcasted_iota(jnp.int32, shape, dim)


def lane_gather(values, index):
    return jnp.take_along_axis(values, index, axis=1, mode="promise_in_bounds")


def down_lanes(row):
    return jnp.transpose(jnp.broadcast_to(row, (B, B)), (1, 0))


def pick_taps(far, near, disp, taps, radius, scale, first=0):
    count = far.shape[0]
    pixel = iota((count, B), 0) + first
    lane = iota((count, B), 1)
    merged = jnp.where(lane > pixel, far, near)
    level = disp + lane - radius
    usable = (level >= 0) & (level < B) & (lane < taps)
    picked = lane_gather(merged, (pixel - level) & (B - 1))
    return (jnp.where(usable, picked, 0.0) * scale).astype(BF16)


def silu(v):
    return v * jax.nn.sigmoid(v)


def level_columns(disp_ref, at):
    return jnp.transpose(disp_ref[:, at : at + B].astype(F32), (1, 0))


def level_row(disp_ref, row, at):
    levels = disp_ref[:, at : at + B]
    return jnp.sum(jnp.where(iota(levels.shape, 0) == row, levels, 0), axis=0, keepdims=True)


def pack_left_kernel(left_ref, own_ref, hid_ref, grad_ref, disp_ref, out_ref):
    rows, _, chan = left_ref.shape
    levels = level_columns(disp_ref, 0)
    for r in range(rows):
        out_ref[r, :, :chan] = left_ref[r, :HALO]
        out_ref[r, :, chan : 2 * chan] = own_ref[r, :HALO]
        out_ref[r, :, 2 * chan : 2 * chan + B] = hid_ref[r, :HALO]
        out_ref[r, :, 2 * chan + B : 2 * chan + 2 * B] = grad_ref[r, :HALO]
        level = jnp.broadcast_to(levels[:8, r : r + 1], (8, B))
        out_ref[r, :, 2 * chan + 2 * B :] = level.astype(BF16)[:HALO]


def pack_right_kernel(
    start, own_ref, beside_ref, left_ref, hid_ref, grad_ref, disp_ref, out_ref
):
    rows, _, chan = own_ref.shape
    first = start + pl.program_id(0) * rows
    low = iota((8, chan), 0) < HALO
    for r in range(rows):
        out_ref[r, :B] = own_ref[r]
        beside = pltpu.roll(beside_ref[r].astype(F32), HALO, 0)
        upper = jnp.where(low, beside, left_ref[r].astype(F32))
        row = level_row(disp_ref, first + r, disp_ref.shape[1] - B).astype(F32)
        level = jnp.transpose(jnp.broadcast_to(row, (8, B)), (1, 0))[B - 8 :, :1]
        level = pltpu.roll(jnp.broadcast_to(level, (8, chan)), HALO, 0)
        hg = jnp.concatenate([hid_ref[r], grad_ref[r]], axis=1).astype(F32)
        out_ref[r, B:] = jnp.concatenate([upper, jnp.where(low, level, hg)], axis=0).astype(BF16)


def rim_kernel(
    hid_first_ref, grad_first_ref, hid_last_ref, grad_last_ref, side_ref, first_ref, last_ref, edge_ref, pad_ref
):
    rows = side_ref.shape[0]
    own = hid_first_ref.shape[1]
    chan = (side_ref.shape[2] - 3 * B) // 2
    pad_ref[...] = jnp.zeros_like(pad_ref)
    for r in range(rows):
        pad_ref[:HALO] = side_ref[r, :, 2 * chan : 2 * chan + 2 * B].astype(F32)
        edge_ref[r] = pad_ref[...].astype(BF16)
    for r in range(HALO):
        for out, hid, grad, row in (
            (first_ref, hid_first_ref, grad_first_ref, r),
            (last_ref, hid_last_ref, grad_last_ref, rows - HALO + r),
        ):
            out[r, :own, :B] = hid[r]
            out[r, :own, B:] = grad[r]
            out[r, own:] = edge_ref[row]


def taps_matrix(weight_ref, pad_ref):
    pad_ref[...] = jnp.zeros_like(pad_ref)
    pad_ref[: weight_ref.shape[0]] = weight_ref[...]
    return pad_ref[...]


def right_corr_kernel(
    taps,
    radius,
    scale,
    left_ref,
    own_ref,
    disp_ref,
    edge_ref,
    weight_ref,
    mot_ref,
    pre_ref,
    pad_ref,
    mw_ref,
    side_ref,
):
    rows, _, chan = own_ref.shape
    first = pl.program_id(0) * rows
    pad_ref[...] = jnp.zeros_like(pad_ref)
    side_ref[...] = jnp.zeros_like(side_ref)
    weight = taps_matrix(weight_ref, mw_ref)
    for r in range(rows):
        side_ref[r, :HALO] = edge_ref[r].astype(F32)
        edge = side_ref[r]
        pad_ref[r, :EDGE] = edge[:, chan : 2 * chan].astype(BF16)
        side = edge[:, :chan].astype(BF16)
        scores = dot_nt(jnp.concatenate([left_ref[r], side], axis=0), own_ref[r])
        disp = down_lanes(level_row(disp_ref, first + r, B))
        main = pick_taps(scores[:B, :B], scores[:B, B:], disp, taps, radius, scale)
        disp = edge[:, 2 * chan + 2 * B :].astype(jnp.int32)
        beside = pick_taps(
            scores[B:, B:], dot_nt(side, pad_ref[r]), disp, taps, radius, scale
        )
        pre = dot(jnp.concatenate([main, beside], axis=0), weight)
        pre_ref[r] = pre[:B]
        mot_ref[r] = silu(pre).astype(BF16)


def left_corr_kernel(
    taps,
    radius,
    scale,
    start,
    rim_step,
    left_ref,
    own_ref,
    before_ref,
    disp_ref,
    mot_right_ref,
    weight_ref,
    mot_ref,
    pre_ref,
    hg_ref,
    rim_ref,
    pad_ref,
    mw_ref,
):
    rows, _, chan = own_ref.shape
    step = pl.program_id(0)
    first = start + step * rows
    pad_ref[...] = jnp.zeros_like(pad_ref)
    weight = taps_matrix(weight_ref, mw_ref)
    last = iota((EDGE, chan), 0) >= EDGE - HALO
    upper = iota((EDGE, B), 0) < EDGE // 2
    wide = mot_ref.shape[1]
    for r in range(rows):
        extra = before_ref[r, B:].astype(F32)
        pad_ref[r, B - EDGE :] = jnp.where(last, pltpu.roll(extra, 12, 0), 0.0).astype(BF16)
        side = jnp.where(last, pltpu.roll(extra, 8, 0), 0.0).astype(BF16)
        window = jnp.concatenate([before_ref[r, :B], own_ref[r]], axis=0)
        scores = dot_nt(jnp.concatenate([left_ref[r], side], axis=0), window)
        disp = down_lanes(level_row(disp_ref, first + r, 0))
        main = pick_taps(scores[:B, :B], scores[:B, B:], disp, taps, radius, scale)
        disp = pltpu.roll(extra, 4, 0)[:, :B].astype(jnp.int32)
        beside = pick_taps(
            dot_nt(side, pad_ref[r]), scores[B:, :B], disp, taps, radius, scale, B - EDGE
        )
        pre = dot(jnp.concatenate([main, beside], axis=0), weight)
        pre_ref[r] = pre[:B]
        mot = silu(pre)
        mot_ref[r, :B] = mot[:B].astype(BF16)
        mot_ref[r, B : 2 * B] = mot_right_ref[r, :B]
        right_edge = mot_right_ref[r, B:].astype(F32)
        mot_ref[r, 2 * B :] = jnp.where(upper, right_edge, mot[B:]).astype(BF16)
        hg_ref[r] = jnp.where(last, extra, 0.0).astype(BF16)

    @pl.when(step == rim_step)
    def _():
        for r in range(rows):
            rim_ref[r, :wide] = mot_ref[r]
            hg = hg_ref[r].astype(F32)
            rim_ref[r, wide:] = (hg[:, :B] + pltpu.roll(hg[:, B:], EDGE // 2, 0)).astype(BF16)


def shifted(value):
    return (
        pltpu.roll(value, 1, 0).astype(BF16),
        value.astype(BF16),
        pltpu.roll(value, value.shape[0] - 1, 0).astype(BF16),
    )


def store3(buf, row, value):
    for b, part in enumerate(shifted(value)):
        buf[row, :, b * B : (b + 1) * B] = part


def lanes(buf, rows, b):
    return jnp.concatenate([buf[r, :, b * B : (b + 1) * B] for r in rows], axis=0)


def patches(bufs, row_sets):
    return jnp.concatenate(
        [lanes(buf, rows, b) for rows in row_sets for b in range(3) for buf in bufs], axis=1
    )


def chunks(values, size):
    values = list(values)
    return [values[i : i + size] for i in range(0, len(values), size)]


CHUNK = 4


def gru_kernel(
    hid_hbm,
    grad_hbm,
    hgt_hbm,
    hgb_hbm,
    mota_hbm,
    motb_hbm,
    gate_hbm,
    cand_hbm,
    prela_hbm,
    prelb_hbm,
    prer_hbm,
    right_ref,
    lefta_ref,
    leftb_ref,
    mott_ref,
    motl_ref,
    disp_ref,
    mw_ref,
    nh_hbm,
    pg_hbm,
    tg_ref,
    h3_ref,
    m3_ref,
    r3_ref,
    c3_ref,
    h_ref,
    g_ref,
    up_ref,
    rs_ref,
    cb_ref,
    hid_ref,
    grad_ref,
    hgt_ref,
    hgb_ref,
    mota_ref,
    motb_ref,
    wg_ref,
    cw_ref,
    prel_ref,
    prer_ref,
    wc_ref,
    wcb_ref,
    wgb_ref,
    nh_ref,
    pg_ref,
    sems,
):
    rows, own, _ = hid_ref.shape
    half = rows // 2
    wide = own + EDGE
    total = rows + 2 * HALO
    inner = range(HALO, HALO + rows)
    moves = (
        (hid_hbm, hid_ref),
        (hgt_hbm, hgt_ref),
        (hgb_hbm, hgb_ref),
        (mota_hbm, mota_ref),
        (motb_hbm, motb_ref),
        (grad_hbm, grad_ref),
        (gate_hbm, wg_ref),
        (cand_hbm, cw_ref),
        (prela_hbm, prel_ref.at[:half]),
        (prelb_hbm, prel_ref.at[half:]),
        (prer_hbm, prer_ref),
    )
    copies = [pltpu.make_async_copy(s, d, sems.at[n]) for n, (s, d) in enumerate(moves)]
    for copy in copies:
        copy.start()
    wc_ref[9 * B * 2 :, :B] = jnp.zeros((6 * B, B), BF16)
    wc_ref[: 6 * B, B:] = jnp.zeros((6 * B, B), BF16)
    wgb_ref[:B, 18 * B :] = jnp.zeros((B, 6 * B), BF16)
    wgb_ref[B:, : 6 * B] = jnp.zeros((B, 6 * B), BF16)
    for copy in copies[:6]:
        copy.wait()

    upper = iota((EDGE, B), 0) < EDGE // 2
    last = iota((EDGE, B), 0) >= EDGE - HALO

    def join(first, second):
        return jnp.where(upper, first.astype(F32), second.astype(F32)).astype(BF16)

    for row in range(total):
        if row in inner:
            n = row - HALO
            left = lefta_ref[n] if n < half else leftb_ref[n - half]
            h_ref[row, :own] = hid_ref[n]
            h_ref[row, own:] = join(right_ref[n, :, :B], left[:, :B])
            g_ref[row, :own] = grad_ref[n]
            g_ref[row, own:] = join(right_ref[n, :, B:], left[:, B:])
            mot = mota_ref[n] if n < half else motb_ref[n - half]
        else:
            top = row < HALO
            n = row if top else row - HALO - rows
            hg = hgt_ref[n] if top else hgb_ref[n]
            mot = mott_ref[n] if top else motl_ref[n]
            left = mot[wide:].astype(F32)
            mot = mot[:wide]
            h_ref[row, :own] = hg[:own, :B]
            h_ref[row, own:] = join(hg[own:, :B], jnp.where(last, left, 0.0))
            g_ref[row, :own] = hg[:own, B:]
            left = jnp.where(last, pltpu.roll(left, EDGE // 2, 0), 0.0)
            g_ref[row, own:] = join(hg[own:, B:], left)
        store3(h3_ref, row, h_ref[row].astype(F32))
        store3(m3_ref, row, mot.astype(F32))

    copies[6].wait()
    for group in chunks(range(1, total - 1), CHUNK):
        lhs = patches((h3_ref, m3_ref), [[r + a - 1 for r in group] for a in range(3)])
        acc = jax.nn.sigmoid(dot(lhs, wg_ref[...]))
        for n, row in enumerate(group):
            gate = acc[n * wide : (n + 1) * wide]
            up_ref[row] = gate[:, :B]
            reset = gate[:, B:]
            rs_ref[row] = reset
            store3(r3_ref, row, reset * h_ref[row].astype(F32))

    copies[7].wait()
    wc_ref[: 18 * B, :B] = cw_ref[...]
    wc_ref[6 * B :, B:] = cw_ref[...]
    for n in range(9):
        at = (8 - n) * 2 * B
        wcb_ref[:, n * B : (n + 1) * B] = cw_ref[at : at + 2 * B]
        for s in range(2):
            col = (n + 3 * s) * 2 * B
            wgb_ref[s * B : (s + 1) * B, col : col + 2 * B] = wg_ref[at + B : at + 2 * B]

    for group in chunks(range(2, total - 2, 2), CHUNK):
        lhs = patches((r3_ref, m3_ref), [[r + t - 1 for r in group] for t in range(4)])
        acc = jnp.tanh(dot(lhs, wc_ref[...]))
        for n, first in enumerate(group):
            for row in (first, first + 1):
                s = row - first
                cand = acc[n * wide : (n + 1) * wide, s * B : (s + 1) * B]
                hidden = h_ref[row].astype(F32)
                update = up_ref[row]
                if row in inner:
                    new = (1.0 - update) * hidden + update * cand
                    nh_ref[row - HALO] = new[:own].astype(BF16)
                gu = g_ref[row].astype(F32) * update
                store3(c3_ref, row, gu * (1.0 - cand * cand))
                store3(h3_ref, row, gu * (cand - hidden) * (1.0 - update))
    new_copy = pltpu.make_async_copy(nh_ref, nh_hbm, sems.at[len(moves)])
    new_copy.start()

    for group in chunks(range(3, total - 3), CHUNK):
        lhs = patches((c3_ref,), [[r + a - 1 for r in group] for a in range(3)])
        acc = dot_nt(lhs, wcb_ref[...])
        for n, row in enumerate(group):
            back = acc[n * wide : (n + 1) * wide]
            reset = rs_ref[row]
            store3(m3_ref, row, back[:, :B] * h_ref[row].astype(F32) * reset * (1.0 - reset))
            if row in inner:
                cb_ref[row - HALO] = back[:own, B:]

    for copy in copies[8:]:
        copy.wait()
    pieces = []
    for group in chunks(range(HALO, HALO + rows, 2), CHUNK):
        lhs = patches((h3_ref, m3_ref), [[r + t - 1 for r in group] for t in range(4)])
        acc = dot_nt(lhs, wgb_ref[...])
        for n, first in enumerate(group):
            for row in (first - HALO, first + 1 - HALO):
                s = row + HALO - first
                back = acc[n * wide : n * wide + own, s * B : (s + 1) * B]
                pre = jnp.concatenate([prel_ref[row], prer_ref[row]], axis=0)
                sig = jax.nn.sigmoid(pre)
                grad = (cb_ref[row] + back) * sig * (1.0 + pre * (1.0 - sig))
                grad = grad.astype(BF16)
                pg_ref[row] = grad
                tap = dot_nt(mw_ref[...], grad[:B])
                level = jnp.broadcast_to(disp_ref[row : row + 1, :B].astype(F32), tap.shape)
                tg_ref[row] = jnp.where(iota(tap.shape, 0) == 15, level, tap).astype(BF16)
        done = pl.ds(group[0] - HALO, 2 * len(group))
        at = len(moves) + 1 + len(pieces)
        piece = pltpu.make_async_copy(pg_ref.at[done], pg_hbm.at[done], sems.at[at])
        piece.start()
        pieces.append(piece)
    new_copy.wait()
    for piece in pieces:
        piece.wait()


def spread(grad, disp, taps, radius):
    pixel = iota((B, B), 0)
    lane = iota((B, B), 1)
    tap = ((pixel - lane) & (B - 1)) - disp + radius
    ok = (tap >= 0) & (tap < taps)
    value = jnp.where(ok, lane_gather(grad, tap & (B - 1)), 0.0)
    far = jnp.where(lane > pixel, value, 0.0).astype(BF16)
    near = jnp.where(lane > pixel, 0.0, value).astype(BF16)
    return far, near


def spread_t(grad, disp, taps, radius):
    column = iota((B, B), 0)
    pixel = iota((B, B), 1)
    tap = ((pixel - column) & (B - 1)) - disp + radius
    value = jnp.zeros((B, B), F32)
    for k in range(taps):
        value = jnp.where(tap == k, grad[k : k + 1], value)
    far = jnp.where(column > pixel, value, 0.0).astype(BF16)
    near = jnp.where(column > pixel, 0.0, value).astype(BF16)
    return far, near


def grads_kernel(
    taps,
    radius,
    scale,
    pg_ref,
    left_ref,
    own_ref,
    before_a_ref,
    before_b_ref,
    disp_ref,
    weight_ref,
    gl_ref,
    gr_ref,
    near_ref,
    mw_ref,
):
    rows = left_ref.shape[0]
    step = pl.program_id(0)
    head = step < pl.num_programs(0) // 2
    weight_t = weight_ref[...]
    weight = taps_matrix(weight_ref, mw_ref)
    for r in range(rows):
        grads = dot_nt(pg_ref[r], weight).astype(BF16).astype(F32)
        grads_t = dot_nt(weight_t, pg_ref[r]).astype(BF16).astype(F32)
        parts = []
        parts_t = []
        for block in range(2):
            at = slice(block * B, (block + 1) * B)
            row = level_row(disp_ref, step * rows + r, block * B)
            parts.append(spread(grads[at], down_lanes(row), taps, radius))
            parts_t.append(spread_t(grads_t[:, at], row, taps, radius))
        before = jnp.where(head, before_a_ref[r, :B], before_b_ref[r, :B])
        window = jnp.concatenate([before, own_ref[r, :B]], axis=0)
        gl_ref[r, :B] = (dot(jnp.concatenate(parts[0], axis=1), window) * scale).astype(BF16)
        gl_ref[r, B:] = (dot(jnp.concatenate(parts[1], axis=1), own_ref[r]) * scale).astype(BF16)
        sg = jnp.concatenate([parts_t[0][1], parts_t[1][0]], axis=1)
        gr_ref[r] = (dot(sg, left_ref[r]) * scale).astype(BF16)
        near_ref[r] = parts_t[1][1]


def last_kernel(taps, radius, scale, near_ref, grad_ref, left_ref, next_ref, first_ref, gr_ref):
    del first_ref
    rows = left_ref.shape[0]
    for r in range(rows):
        grad = grad_ref[r].astype(F32)
        disp = grad[15:16].astype(jnp.int32)
        far, _ = spread_t(grad, disp, taps, radius)
        sg = jnp.concatenate([near_ref[r], far], axis=1)
        window = jnp.concatenate([left_ref[r], next_ref[r]], axis=0)
        gr_ref[r] = (dot(sg, window) * scale).astype(BF16)


def whole(array):
    nd = array.ndim
    return pl.BlockSpec(array.shape, lambda i: (0,) * nd)


def by_rows(array, size, block=None, at=None):
    block = tuple(array.shape[1:]) if block is None else block
    at = (0,) * len(block) if at is None else at
    return pl.BlockSpec((size,) + block, lambda i: (i,) + at)


def cost(flops, bytes_accessed):
    return pl.CostEstimate(flops=flops, bytes_accessed=bytes_accessed, transcendentals=0)


def block(shape, *at):
    return pl.BlockSpec(shape, lambda i: (i + at[0],) + at[1:])


def per_device(
    feat_left, feat_right, hidden, disparity, motion_weight, gate_weight, cand_weight, grad_hidden
):
    rows, cols, chan = feat_left.shape
    taps = motion_weight.shape[0]
    radius = taps // 2
    scale = 1.0 / math.sqrt(chan)
    args = (taps, radius, scale)
    size = ROWS
    steps = rows // size
    half = rows // 2
    wide = cols + EDGE
    packed = 2 * chan + 3 * B
    params = pltpu.CompilerParams(vmem_limit_bytes=SMALL_VMEM)
    shape = jax.ShapeDtypeStruct
    vmem = pl.BlockSpec(memory_space=pltpu.VMEM)
    last8 = cols // 8 - 1

    from_right = shift(
        pl.pallas_call(
            pack_left_kernel,
            grid=(1,),
            in_specs=[
                block((rows, 8, chan), 0, 0, 0),
                block((rows, 8, chan), 0, 0, 0),
                block((rows, 8, B), 0, 0, 0),
                block((rows, 8, B), 0, 0, 0),
                whole(disparity),
            ],
            out_specs=whole(shape((rows, HALO, packed), BF16)),
            out_shape=shape((rows, HALO, packed), BF16),
            compiler_params=params,
            cost_estimate=cost(1 << 16, 1 << 18),
            name="pack_left",
        )(feat_left, feat_right, hidden, grad_hidden, disparity),
        "cols",
        -1,
    )

    def features_before(start):
        at = start // size
        out = shape((half, B + EDGE, chan), BF16)
        return shift(
            pl.pallas_call(
                lambda *refs: pack_right_kernel(start, *refs),
                grid=(half // size,),
                in_specs=[
                    block((size, B, chan), at, cols // B - 1, 0),
                    block((size, 8, chan), at, (cols - B) // 8 - 1, 0),
                    block((size, 8, chan), at, last8, 0),
                    block((size, 8, B), at, last8, 0),
                    block((size, 8, B), at, last8, 0),
                    whole(disparity),
                ],
                out_specs=by_rows(out, size),
                out_shape=out,
                compiler_params=params,
                cost_estimate=cost(1 << 16, 2 << 20),
                name="pack_right",
            )(feat_right, feat_right, feat_left, hidden, grad_hidden, disparity),
            "cols",
            1,
        )

    before = [features_before(0), features_before(half)]

    rim = shape((HALO, wide, 2 * B), BF16)
    edge_shape = shape((rows, EDGE, 2 * B), BF16)
    first_rim, last_rim, edge = pl.pallas_call(
        rim_kernel,
        grid=(1,),
        in_specs=[
            block((HALO, cols, B), 0, 0, 0),
            block((HALO, cols, B), 0, 0, 0),
            block((HALO, cols, B), rows // HALO - 1, 0, 0),
            block((HALO, cols, B), rows // HALO - 1, 0, 0),
            whole(from_right),
        ],
        out_specs=[whole(rim), whole(rim), whole(edge_shape)],
        out_shape=(rim, rim, edge_shape),
        scratch_shapes=[pltpu.VMEM((EDGE, 2 * B), F32)],
        compiler_params=params,
        cost_estimate=cost(1 << 16, 2 << 20),
        name="rims",
    )(hidden, grad_hidden, hidden, grad_hidden, from_right)
    hg_top = shift(last_rim, "rows", 1)
    hg_low = shift(first_rim, "rows", -1)

    mw16 = jnp.pad(motion_weight, ((0, 16 - taps), (0, 0)))
    pads = [pltpu.VMEM((size, B, chan), BF16), pltpu.VMEM((B, B), BF16)]
    right_shapes = (shape((rows, B + EDGE, B), BF16), shape((rows, B, B), F32))
    mot_right, pre_right = pl.pallas_call(
        lambda *refs: right_corr_kernel(*args, *refs),
        grid=(steps,),
        in_specs=[
            block((size, B, chan), 0, 1, 0),
            by_rows(feat_right, size),
            whole(disparity),
            by_rows(from_right, size),
            whole(mw16),
        ],
        out_specs=[by_rows(s, size) for s in right_shapes],
        out_shape=right_shapes,
        scratch_shapes=pads + [pltpu.VMEM((size, EDGE, packed), F32)],
        compiler_params=params,
        cost_estimate=cost(2 * rows * B * 2 * B * chan, 6 << 20),
        name="corr_right",
    )(feat_left, feat_right, disparity, from_right, mw16)

    def left_lookup(start, before, rim_step):
        at = start // size
        shapes = (
            shape((half, wide, B), BF16),
            shape((half, B, B), F32),
            shape((half, EDGE, 2 * B), BF16),
            shape((HALO, wide + EDGE, B), BF16),
        )
        return pl.pallas_call(
            lambda *refs: left_corr_kernel(*args, start, rim_step, *refs),
            grid=(half // size,),
            in_specs=[
                block((size, B, chan), at, 0, 0),
                block((size, B, chan), at, 0, 0),
                by_rows(before, size),
                whole(disparity),
                block((size, B + EDGE, B), at, 0, 0),
                whole(mw16),
            ],
            out_specs=[by_rows(s, size) for s in shapes[:3]] + [whole(shapes[3])],
            out_shape=shapes,
            scratch_shapes=pads,
            compiler_params=params,
            cost_estimate=cost(rows * B * 2 * B * chan, 3 << 20),
            name="corr_left",
        )(feat_left, feat_right, before, disparity, mot_right, mw16)

    mot_a, pre_a, left_a, rim_a = left_lookup(0, before[0], 0)
    mot_low = shift(rim_a, "rows", -1)
    mot_b, pre_b, left_b, rim_b = left_lookup(half, before[1], half // size - 1)
    mot_top = shift(rim_b, "rows", 1)
    first_left, _ = lax.optimization_barrier((feat_left[:, :B], mot_b))
    next_left = shift(first_left, "cols", -1)

    total = rows + 2 * HALO
    own_shape = shape((rows, cols, B), BF16)
    big = (
        hidden,
        grad_hidden,
        hg_top,
        hg_low,
        mot_a,
        mot_b,
        gate_weight.reshape(-1, 2 * B),
        cand_weight.reshape(-1, B),
        pre_a,
        pre_b,
        pre_right,
    )
    small = (edge, left_a, left_b, mot_top, mot_low, disparity, mw16)
    anywhere = pl.BlockSpec(memory_space=pl.ANY)
    new_hidden, pre_grad, tap_grad = pl.pallas_call(
        gru_kernel,
        in_specs=[anywhere] * len(big) + [vmem] * len(small),
        out_specs=[anywhere, anywhere, vmem],
        out_shape=(own_shape, own_shape, shape((rows, 16, B), BF16)),
        scratch_shapes=[pltpu.VMEM((total, wide, 3 * B), BF16)] * 4
        + [pltpu.VMEM((total, wide, B), BF16)] * 2
        + [pltpu.VMEM((total, wide, B), F32)] * 2
        + [pltpu.VMEM((rows, cols, B), F32)]
        + [pltpu.VMEM(a.shape, BF16) for a in big[:8]]
        + [pltpu.VMEM((rows, B, B), F32)] * 2
        + [
            pltpu.VMEM((24 * B, 2 * B), BF16),
            pltpu.VMEM((2 * B, 9 * B), BF16),
            pltpu.VMEM((2 * B, 24 * B), BF16),
            pltpu.VMEM((rows, cols, B), BF16),
            pltpu.VMEM((rows, cols, B), BF16),
            pltpu.SemaphoreType.DMA((len(big) + 1 + rows,)),
        ],
        compiler_params=pltpu.CompilerParams(vmem_limit_bytes=GRU_VMEM),
        cost_estimate=cost(2 * 22 * wide * 256 * 256 * 24, 16 << 20),
        name="gru",
    )(*big, *small)
    next_grad = shift(tap_grad, "cols", -1)

    feat_shape = shape((rows, cols, chan), BF16)
    near_shape = shape((rows, B, B), BF16)
    mid = steps // 2
    grad_left, grad_first, near = pl.pallas_call(
        lambda *refs: grads_kernel(*args, *refs),
        grid=(steps,),
        in_specs=[
            by_rows(pre_grad, size),
            by_rows(feat_left, size),
            by_rows(feat_right, size),
            pl.BlockSpec((size, B + EDGE, chan), lambda i: (jnp.minimum(i, mid - 1), 0, 0)),
            pl.BlockSpec((size, B + EDGE, chan), lambda i: (jnp.maximum(i - mid, 0), 0, 0)),
            whole(disparity),
            whole(mw16),
        ],
        out_specs=[
            by_rows(feat_shape, size),
            block((size, B, chan), 0, 0, 0),
            by_rows(near_shape, size),
        ],
        out_shape=(feat_shape, feat_shape, near_shape),
        scratch_shapes=[pltpu.VMEM((B, B), BF16)],
        compiler_params=params,
        cost_estimate=cost(2 * rows * B * 2 * B * chan * 4, 12 << 20),
        name="grads",
    )(pre_grad, feat_left, feat_right, before[0], before[1], disparity, mw16)
    grad_right = pl.pallas_call(
        lambda *refs: last_kernel(*args, *refs),
        grid=(steps,),
        in_specs=[
            by_rows(near, size),
            by_rows(next_grad, size),
            block((size, B, chan), 0, 1, 0),
            by_rows(next_left, size),
            anywhere,
        ],
        out_specs=block((size, B, chan), 0, 1, 0),
        out_shape=feat_shape,
        input_output_aliases={4: 0},
        compiler_params=params,
        cost_estimate=cost(2 * rows * B * 2 * B * chan, 4 << 20),
        name="grad_right",
    )(near, next_grad, feat_left, next_left, grad_first)
    return (new_hidden, grad_left, grad_right)


def solution(mesh):
    grid3 = P("rows", "cols", None)
    return jax.shard_map(
        per_device,
        mesh=mesh,
        in_specs=(grid3, grid3, grid3, P("rows", "cols"), P(), P(), P(), grid3),
        out_specs=(grid3, grid3, grid3),
        check_vma=False,
    )
```

time: 144 us -> 124 us (0.86)
  local copies, waits for them, and re-layouts: 21.8 us -> 8.84 us
  starting transfers between devices: 28.9 us -> 39.8 us
  waiting for transfers between devices: 28.2 us -> 18.5 us
  other arithmetic: 5.13 us -> 0 us
  Pallas kernels: 57 us -> 54.1 us
    ppermute x9, starting transfers between devices: 28.9 us -> 39.8 us  [shift(): return lax.ppermute(array, axis, pairs)]
    ppermute x9, waiting for transfers between devices: 28.2 us -> 18.5 us  [shift(): return lax.ppermute(array, axis, pairs)]
    slice x11 -> x1, local copies, waits for them, and re-layouts: 5.32 us -> 0.07 us  [per_device(): first_left, _ = lax.optimization_barrier((feat_left[:, :B], mot_b))]
    concatenate x3 -> x0, local copies, waits for them, and re-layouts: 4.89 us -> none  [the longest x1 4.12 us: per_device(): jnp.concatenate([feat_right[:, cols - B:], feat_right[:, cols - B - HALO:...]
    concatenate x6 -> x0, other arithmetic: 4.41 us -> none  [the longest x2 2.57 us: paired(): return jnp.concatenate(rows, axis=2).reshape(-1, 2 * B)]
    pallas_call x5 -> x10, Pallas kernels: 57 us -> 54.1 us  [the longest x1 34 us: per_device(): pl.pallas_call(gru_kernel, in_specs=[anywhere] * len(big) + [vmem] * len(...]
    pad x3 -> x0, local copies, waits for them, and re-layouts: 2.07 us -> none  [the longest x1 0.84 us: per_device(): edge = jnp.pad(from_right, ((0, 0), (0, EDGE - HALO), (0, 0)))]
    unnamed x30 -> x50, local copies, waits for them, and re-layouts: 6.96 us -> 8.76 us
  transfers between devices with their start and end apart: 9 -> 9, of which waited for: 2 -> 1; matrix products, arithmetic and copies ran while one was open for 11% -> 0% of each run, Pallas kernels for 37% -> 42%
where the time goes in v3:
time: 124 us; the launch traced here: 122 us
  Pallas kernels  54.1 us (44%)
  starting transfers between devices  39.8 us (32%)
  waiting for transfers between devices  18.5 us (15%)
  local copies, waits for them, and re-layouts  8.84 us (7%)
    ppermute x9, starting transfers between devices, shift(): return lax.ppermute(array, axis, pairs)  39.8 us
    pallas_call x1, Pallas kernels, per_device(): pl.pallas_call(gru_kernel, in_specs=[anywhere] * len(big) + [vmem] * len(...  34 us
    ppermute x9, waiting for transfers between devices, shift(): return lax.ppermute(array, axis, pairs)  18.5 us
    unnamed x50, local copies, waits for them, and re-layouts  8.76 us
    pallas_call x1, Pallas kernels, per_device(): pl.pallas_call(lambda *refs: grads_kernel(*args, *refs), grid=(steps,), i...  6.66 us
    pallas_call x2, Pallas kernels, left_lookup(): pl.pallas_call(lambda *refs: left_corr_kernel(*args, start, rim_step, *re...  4.89 us
    pallas_call x1, Pallas kernels, per_device(): pl.pallas_call(lambda *refs: right_corr_kernel(*args, *refs), grid=(steps...  4.76 us
    pallas_call x1, Pallas kernels, per_device(): pl.pallas_call(lambda *refs: last_kernel(*args, *refs), grid=(steps,), in...  2.49 us
  transfers between devices with their start and end apart: 9, of which 1 were waited for; matrix products, arithmetic and copies ran while one was open for 0% of the time, Pallas kernels for 42%

profile of v3, /device:TPU:120, one launch (start us, length us, event | category | flops | bytes accessed | tf_op | source)
XLA Modules:
  0.0 122.3 jit_solution(18285322087525549009)
XLA Ops:
  0.6 0.0 copy-start
  0.6 1.6 %copy-done = bf16[16,256,256]{2,1,0:T(8,128)(2,1)S(1)} copy-done((bf16[16,256,256]{2,1,0:T(8,128)(2,1)S(1)}, bf16[16,256,256]{2,1,0:T(8,128)(2,1)}, u32[]{:S(2)}) %copy-start) | copy-done | bytes 2097176
  2.2 1.6 %copy-done.2 = bf16[16,256,256]{2,1,0:T(8,128)(2,1)S(1)} copy-done((bf16[16,256,256]{2,1,0:T(8,128)(2,1)S(1)}, bf16[16,256,256]{2,1,0:T(8,128)(2,1)}, u32[]{:S(2)}) %copy-start.2) | copy-done | bytes 2097176
  3.8 1.2 copy-done.4
  5.0 1.2 copy-done.5
  6.3 0.7 copy-done.7
  7.0 0.4 pack_right.3
  7.4 4.9 %collective-permute-start.4 = (bf16[8,144,256]{2,1,0:T(8,128)(2,1)S(1)}, bf16[8,144,256]{2,1,0:T(8,128)(2,1)S(1)}, u32[]{:S(2)}, u32[]{:S(2)}) collective-permute-start(bf16[8,144,256]{2,1,0:T(8,128)(2,1)S(1)} %pack_right.3), channel_id=1, source_target_pairs={{0,1},{1,2},{2,3},{3,4},{4,5},{5,6},{6,7},{8,9},{9,10},{10,11},{11... | collective-permute-start | bytes 1769480 | tf_op jit(solution)/shard_map/ppermute | solution.py:23
  12.4 0.5 pack_right.2
  12.8 1.9 %collective-permute-start.3 = (bf16[8,144,256]{2,1,0:T(8,128)(2,1)S(1)}, bf16[8,144,256]{2,1,0:T(8,128)(2,1)S(1)}, u32[]{:S(2)}, u32[]{:S(2)}) collective-permute-start(bf16[8,144,256]{2,1,0:T(8,128)(2,1)S(1)} %pack_right.2), channel_id=1, source_target_pairs={{0,1},{1,2},{2,3},{3,4},{4,5},{5,6},{6,7},{8,9},{9,10},{10,11},{11... | collective-permute-start | bytes 1769480 | tf_op jit(solution)/shard_map/ppermute | solution.py:23
  14.7 0.2 pack_left.1
  14.9 0.0 copy-start.1
  14.9 0.0 copy-start.3
  15.0 6.6 %collective-permute-start = (bf16[16,4,896]{2,1,0:T(4,128)(2,1)S(1)}, bf16[16,4,896]{2,1,0:T(4,128)(2,1)S(1)}, u32[]{:S(2)}, u32[]{:S(2)}) collective-permute-start(bf16[16,4,896]{2,1,0:T(4,128)(2,1)S(1)} %pack_left.1), channel_id=1, source_target_pairs={{1,0},{2,1},{3,2},{4,3},{5,4},{6,5},{7,6},{9,8},{10,9},{11,10},{12... | collective-permute-start | bytes 344072 | tf_op jit(solution)/shard_map/ppermute | solution.py:23
  21.6 18.5 %collective-permute-done.side_ref.refs_3_ = bf16[16,4,896]{2,1,0:T(4,128)(2,1)S(1)} collective-permute-done((bf16[16,4,896]{2,1,0:T(4,128)(2,1)S(1)}, bf16[16,4,896]{2,1,0:T(4,128)(2,1)S(1)}, u32[]{:S(2)}, u32[]{:S(2)}) %collective-permute-start) | collective-permute-done | bytes 114720 | tf_op jit(solution)/shard_map/ppermute | solution.py:23
  40.0 0.2 rims.1
  40.2 0.0 copy-start.17
  40.3 1.9 %collective-permute-start.1 = (bf16[4,272,256]{2,1,0:T(8,128)(2,1)S(1)}, bf16[4,272,256]{2,1,0:T(8,128)(2,1)S(1)}, u32[]{:S(2)}, u32[]{:S(2)}) collective-permute-start(bf16[4,272,256]{2,1,0:T(8,128)(2,1)S(1)} %get-tuple-element.23), channel_id=1, source_target_pairs={{0,8},{8,16},{16,24},{24,32},{32,40},{40,48},{48,56},{56,64},{64,7... | collective-permute-start | bytes 1671176 | tf_op jit(solution)/shard_map/ppermute | solution.py:23
  42.2 4.5 %collective-permute-start.2 = (bf16[4,272,256]{2,1,0:T(8,128)(2,1)S(1)}, bf16[4,272,256]{2,1,0:T(8,128)(2,1)S(1)}, u32[]{:S(2)}, u32[]{:S(2)}) collective-permute-start(bf16[4,272,256]{2,1,0:T(8,128)(2,1)S(1)} %get-tuple-element.24), channel_id=1, source_target_pairs={{8,0},{16,8},{24,16},{32,24},{40,32},{48,40},{56,48},{64,56},{72,6... | collective-permute-start | bytes 1671176 | tf_op jit(solution)/shard_map/ppermute | solution.py:23
  46.7 0.0 copy-done.20
  46.8 0.0 copy-done.1
  46.8 0.0 copy-done.3
  46.8 0.0 copy-start.10
  46.8 0.0 copy-start.8
  46.8 4.8 %corr_right.1 = (bf16[16,144,128]{2,1,0:T(8,128)(2,1)S(1)}, f32[16,128,128]{2,1,0:T(8,128)S(1)}) custom-call(bf16[16,256,256]{2,1,0:T(8,128)(2,1)S(1)} %copy-done.3, bf16[16,256,256]{2,1,0:T(8,128)(2,1)S(1)} %copy-done.1, s32[16,256]{1,0:T(8,128)S(1)} %copy-done.7, bf16[16,4,896]{2,1,0:T(4,128)(2,1)S(1)} %collective-permute-done.side_ref.refs_3_, ...), custom_call_target="tpu_custom_call" | custom-call | flops 268435456 | bytes 6291456 | tf_op jit(solution)/shard_map/corr_right/pallas_call | solution.py:617
  51.6 0.0 copy-done.17
  51.6 0.0 copy-start.12
  51.6 0.0 collective-permute-done.4.refs_2_.refs_4_
  51.6 0.0 copy-done.8
  51.6 2.4 %corr_left.3 = (bf16[8,272,128]{2,1,0:T(8,128)(2,1)S(1)}, f32[8,128,128]{2,1,0:T(8,128)S(1)}, bf16[8,16,256]{2,1,0:T(8,128)(2,1)S(1)}, bf16[4,288,128]{2,1,0:T(8,128)(2,1)S(1)}) custom-call(bf16[16,256,256]{2,1,0:T(8,128)(2,1)S(1)} %copy-done.3, bf16[16,256,256]{2,1,0:T(8,128)(2,1)S(1)} %copy-done.1, ...), custom_call_target="tpu_custom_call" | custom-call | flops 134217728 | bytes 3145728 | tf_op jit(solution)/shard_map/corr_left/pallas_call | solution.py:643
  54.1 0.0 copy-done.12
  54.1 0.0 copy-start.13
  54.1 0.0 copy-start.15
  54.1 0.0 copy-start.18
  54.1 1.9 %collective-permute-start.5 = (bf16[4,288,128]{2,1,0:T(8,128)(2,1)S(1)}, bf16[4,288,128]{2,1,0:T(8,128)(2,1)S(1)}, u32[]{:S(2)}, u32[]{:S(2)}) collective-permute-start(bf16[4,288,128]{2,1,0:T(8,128)(2,1)S(1)} %get-tuple-element.34), channel_id=1, source_target_pairs={{0,8},{8,16},{16,24},{24,32},{32,40},{40,48},{48,56},{56,64},{64,7... | collective-permute-start | bytes 884744 | tf_op jit(solution)/shard_map/ppermute | solution.py:23
  56.0 0.0 collective-permute-done.3.refs_2_.refs_3_
  56.0 0.0 copy-done.10
  56.1 2.4 %corr_left.2 = (bf16[8,272,128]{2,1,0:T(8,128)(2,1)S(1)}, f32[8,128,128]{2,1,0:T(8,128)S(1)}, bf16[8,16,256]{2,1,0:T(8,128)(2,1)S(1)}, bf16[4,288,128]{2,1,0:T(8,128)(2,1)S(1)}) custom-call(bf16[16,256,256]{2,1,0:T(8,128)(2,1)S(1)} %copy-done.3, bf16[16,256,256]{2,1,0:T(8,128)(2,1)S(1)} %copy-done.1, ...), custom_call_target="tpu_custom_call" | custom-call | flops 134217728 | bytes 3145728 | tf_op jit(solution)/shard_map/corr_left/pallas_call | solution.py:643
  58.5 0.0 copy-done.13
  58.5 0.0 copy-done.15
  58.5 0.0 copy-done.18
  58.6 4.5 %collective-permute-start.6 = (bf16[4,288,128]{2,1,0:T(8,128)(2,1)S(1)}, bf16[4,288,128]{2,1,0:T(8,128)(2,1)S(1)}, u32[]{:S(2)}, u32[]{:S(2)}) collective-permute-start(bf16[4,288,128]{2,1,0:T(8,128)(2,1)S(1)} %get-tuple-element.35), channel_id=1, source_target_pairs={{8,0},{16,8},{24,16},{32,24},{40,32},{48,40},{56,48},{64,56},{72,6... | collective-permute-start | bytes 884744 | tf_op jit(solution)/shard_map/ppermute | solution.py:23
  63.1 0.1 slice.3
  63.2 0.0 copy-done.16
  63.2 0.0 copy-done.19
  63.2 7.0 %collective-permute-start.8 = (bf16[16,128,256]{2,1,0:T(8,128)(2,1)S(1)}, bf16[16,128,256]{2,1,0:T(8,128)(2,1)S(1)}, u32[]{:S(2)}, u32[]{:S(2)}) collective-permute-start(bf16[16,128,256]{2,1,0:T(8,128)(2,1)S(1)} %slice.3), channel_id=1, source_target_pairs={{1,0},{2,1},{3,2},{4,3},{5,4},{6,5},{7,6},{9,8},{10,9},{11,10},{12... | collective-permute-start | bytes 3145736 | tf_op jit(solution)/shard_map/ppermute | solution.py:23
  70.2 0.0 collective-permute-done.1.hgt_hbm
  70.2 0.0 collective-permute-done.2.hgb_hbm
  70.2 0.0 collective-permute-done.5.mott_ref
  70.3 0.0 collective-permute-done.6.motl_ref
  70.3 0.8 copy-done.22
  71.1 0.1 copy-done.23
  71.2 0.1 copy-done.24
  71.3 0.1 copy-done.21
  71.4 34.0 %gru.1 = (bf16[16,256,128]{2,1,0:T(8,128)(2,1)}, bf16[16,256,128]{2,1,0:T(8,128)(2,1)}, bf16[16,16,128]{2,1,0:T(8,128)(2,1)}) custom-call(bf16[16,256,128]{2,1,0:T(8,128)(2,1)} %hid_hbm.1, bf16[16,256,128]{2,1,0:T(8,128)(2,1)} %grad_hbm.1, bf16[4,272,256]{2,1,0:T(8,128)(2,1)} %copy-done.21, bf16[4,272,256]{2,1,0:T(8,128)(2,1)} %copy-done.22, ...), custom_call_target="tpu_custom_call" | custom-call | flops 18824036352 | bytes 16777216 | tf_op jit(solution)/shard_map/gru/pallas_call | solution.py:686
  105.4 6.5 %collective-permute-start.7 = (bf16[16,16,128]{2,1,0:T(8,128)(2,1)}, bf16[16,16,128]{2,1,0:T(8,128)(2,1)S(1)}, u32[]{:S(2)}, u32[]{:S(2)}) collective-permute-start(bf16[16,16,128]{2,1,0:T(8,128)(2,1)} %get-tuple-element.40), channel_id=1, source_target_pairs={{1,0},{2,1},{3,2},{4,3},{5,4},{6,5},{7,6},{9,8},{10,9},{11,10},{12... | collective-permute-start | bytes 196616 | tf_op jit(solution)/shard_map/ppermute | solution.py:23
  111.9 0.0 copy-done.9
  111.9 0.0 copy-done.11
  111.9 0.0 copy-start.6
  111.9 1.2 copy-done.6
  113.2 6.7 %grads.1 = (bf16[16,256,256]{2,1,0:T(8,128)(2,1)}, bf16[16,256,256]{2,1,0:T(8,128)(2,1)}, bf16[16,128,128]{2,1,0:T(8,128)(2,1)S(1)}) custom-call(bf16[16,256,128]{2,1,0:T(8,128)(2,1)S(1)} %copy-done.6, bf16[16,256,256]{2,1,0:T(8,128)(2,1)S(1)} %copy-done.3, bf16[16,256,256]{2,1,0:T(8,128)(2,1)S(1)} %copy-done.1, ...), custom_call_target="tpu_custom_call" | custom-call | flops 1073741824 | bytes 12582912 | tf_op jit(solution)/shard_map/grads/pallas_call | solution.py:714
  119.8 0.0 collective-permute-done.7.refs_1_
  119.8 0.0 collective-permute-done.8.refs_3_
  119.8 2.5 %grad_right.1 = bf16[16,256,256]{2,1,0:T(8,128)(2,1)} custom-call(bf16[16,128,128]{2,1,0:T(8,128)(2,1)S(1)} %get-tuple-element.39.refs_0_, bf16[16,16,128]{2,1,0:T(8,128)(2,1)S(1)} %collective-permute-done.7.refs_1_, bf16[16,256,256]{2,1,0:T(8,128)(2,1)S(1)} %copy-done.3, ...), custom_call_target="tpu_custom_call", output_to_operand_aliasing={{}: (4, {})} | custom-call | flops 268435456 | bytes 4194304 | tf_op jit(solution)/shard_map/grad_right/pallas_call | solution.py:737
  (16 shorter events, 0.0 us)
Async XLA Ops:
  0.6 1.6 %copy-start = (bf16[16,256,256]{2,1,0:T(8,128)(2,1)S(1)}, bf16[16,256,256]{2,1,0:T(8,128)(2,1)}, u32[]{:S(2)}) copy-start(bf16[16,256,256]{2,1,0:T(8,128)(2,1)} %refs_2_.8) | copy-start | bytes 6291460
  2.2 1.6 %copy-start.2 = (bf16[16,256,256]{2,1,0:T(8,128)(2,1)S(1)}, bf16[16,256,256]{2,1,0:T(8,128)(2,1)}, u32[]{:S(2)}) copy-start(bf16[16,256,256]{2,1,0:T(8,128)(2,1)} %refs_2_.9) | copy-start | bytes 6291460
  3.8 1.2 %copy-start.4 = (bf16[16,256,128]{2,1,0:T(8,128)(2,1)S(1)}, bf16[16,256,128]{2,1,0:T(8,128)(2,1)}, u32[]{:S(2)}) copy-start(bf16[16,256,128]{2,1,0:T(8,128)(2,1)} %hid_hbm.1) | copy-start | bytes 3145732
  5.0 1.2 %copy-start.5 = (bf16[16,256,128]{2,1,0:T(8,128)(2,1)S(1)}, bf16[16,256,128]{2,1,0:T(8,128)(2,1)}, u32[]{:S(2)}) copy-start(bf16[16,256,128]{2,1,0:T(8,128)(2,1)} %grad_hbm.1) | copy-start | bytes 3145732
  6.3 0.7 copy-start.7
  7.4 44.2 %collective-permute-start.4 = (bf16[8,144,256]{2,1,0:T(8,128)(2,1)S(1)}, bf16[8,144,256]{2,1,0:T(8,128)(2,1)S(1)}, u32[]{:S(2)}, u32[]{:S(2)}) collective-permute-start(bf16[8,144,256]{2,1,0:T(8,128)(2,1)S(1)} %pack_right.3), channel_id=1, source_target_pairs={{0,1},{1,2},{2,3},{3,4},{4,5},{5,6},{6,7},{8,9},{9,10},{10,11},{11... | collective-permute-start | bytes 1769480 | tf_op jit(solution)/shard_map/ppermute | solution.py:23
  12.8 43.2 %collective-permute-start.3 = (bf16[8,144,256]{2,1,0:T(8,128)(2,1)S(1)}, bf16[8,144,256]{2,1,0:T(8,128)(2,1)S(1)}, u32[]{:S(2)}, u32[]{:S(2)}) collective-permute-start(bf16[8,144,256]{2,1,0:T(8,128)(2,1)S(1)} %pack_right.2), channel_id=1, source_target_pairs={{0,1},{1,2},{2,3},{3,4},{4,5},{5,6},{6,7},{8,9},{9,10},{10,11},{11... | collective-permute-start | bytes 1769480 | tf_op jit(solution)/shard_map/ppermute | solution.py:23
  14.9 31.8 %copy-start.20 = (bf16[9,128]{1,0:T(8,128)(2,1)S(1)}, bf16[9,128]{1,0:T(8,128)(2,1)}, u32[]{:S(2)}) copy-start(bf16[9,128]{1,0:T(8,128)(2,1)} %param.12) | copy-start | bytes 6916
  14.9 31.8 %copy-start.1 = (bf16[16,256,256]{2,1,0:T(8,128)(2,1)S(1)}, bf16[16,256,256]{2,1,0:T(8,128)(2,1)}, u32[]{:S(2)}) copy-start(bf16[16,256,256]{2,1,0:T(8,128)(2,1)} %refs_2_.8) | copy-start | bytes 6291460
  14.9 31.8 %copy-start.3 = (bf16[16,256,256]{2,1,0:T(8,128)(2,1)S(1)}, bf16[16,256,256]{2,1,0:T(8,128)(2,1)}, u32[]{:S(2)}) copy-start(bf16[16,256,256]{2,1,0:T(8,128)(2,1)} %refs_2_.9) | copy-start | bytes 6291460
  15.0 25.1 %collective-permute-start = (bf16[16,4,896]{2,1,0:T(4,128)(2,1)S(1)}, bf16[16,4,896]{2,1,0:T(4,128)(2,1)S(1)}, u32[]{:S(2)}, u32[]{:S(2)}) collective-permute-start(bf16[16,4,896]{2,1,0:T(4,128)(2,1)S(1)} %pack_left.1), channel_id=1, source_target_pairs={{1,0},{2,1},{3,2},{4,3},{5,4},{6,5},{7,6},{9,8},{10,9},{11,10},{12... | collective-permute-start | bytes 344072 | tf_op jit(solution)/shard_map/ppermute | solution.py:23
  40.2 11.3 %copy-start.17 = (bf16[16,16,256]{2,1,0:T(8,128)(2,1)}, bf16[16,16,256]{2,1,0:T(8,128)(2,1)S(1)}, u32[]{:S(2)}) copy-start(bf16[16,16,256]{2,1,0:T(8,128)(2,1)S(1)} %get-tuple-element.31.right_ref) | copy-start | bytes 393220
  40.3 29.9 %collective-permute-start.1 = (bf16[4,272,256]{2,1,0:T(8,128)(2,1)S(1)}, bf16[4,272,256]{2,1,0:T(8,128)(2,1)S(1)}, u32[]{:S(2)}, u32[]{:S(2)}) collective-permute-start(bf16[4,272,256]{2,1,0:T(8,128)(2,1)S(1)} %get-tuple-element.23), channel_id=1, source_target_pairs={{0,8},{8,16},{16,24},{24,32},{32,40},{40,48},{48,56},{56,64},{64,7... | collective-permute-start | bytes 1671176 | tf_op jit(solution)/shard_map/ppermute | solution.py:23
  42.2 28.0 %collective-permute-start.2 = (bf16[4,272,256]{2,1,0:T(8,128)(2,1)S(1)}, bf16[4,272,256]{2,1,0:T(8,128)(2,1)S(1)}, u32[]{:S(2)}, u32[]{:S(2)}) collective-permute-start(bf16[4,272,256]{2,1,0:T(8,128)(2,1)S(1)} %get-tuple-element.24), channel_id=1, source_target_pairs={{8,0},{16,8},{24,16},{32,24},{40,32},{48,40},{56,48},{64,56},{72,6... | collective-permute-start | bytes 1671176 | tf_op jit(solution)/shard_map/ppermute | solution.py:23
  46.8 9.3 %copy-start.10 = (bf16[16,128]{1,0:T(8,128)(2,1)}, bf16[16,128]{1,0:T(8,128)(2,1)S(1)}, u32[]{:S(2)}) copy-start(bf16[16,128]{1,0:T(8,128)(2,1)S(1)} %pad.4.refs_4_.refs_5_.mw_ref.refs_6_) | copy-start | bytes 12292
  46.8 4.8 %copy-start.8 = (s32[16,256]{1,0:T(8,128)S(1)}, s32[16,256]{1,0:T(8,128)}, u32[]{:S(2)}) copy-start(s32[16,256]{1,0:T(8,128)} %refs_5_.5) | copy-start | bytes 49156
  51.6 2.5 %copy-start.12 = (f32[16,128,128]{2,1,0:T(8,128)}, f32[16,128,128]{2,1,0:T(8,128)S(1)}, u32[]{:S(2)}) copy-start(f32[16,128,128]{2,1,0:T(8,128)S(1)} %get-tuple-element.30.prer_hbm) | copy-start | bytes 3145732
  54.1 4.4 %copy-start.13 = (bf16[8,272,128]{2,1,0:T(8,128)(2,1)}, bf16[8,272,128]{2,1,0:T(8,128)(2,1)S(1)}, u32[]{:S(2)}) copy-start(bf16[8,272,128]{2,1,0:T(8,128)(2,1)S(1)} %get-tuple-element.27.motb_hbm) | copy-start | bytes 1671172
  54.1 4.4 %copy-start.15 = (f32[8,128,128]{2,1,0:T(8,128)}, f32[8,128,128]{2,1,0:T(8,128)S(1)}, u32[]{:S(2)}) copy-start(f32[8,128,128]{2,1,0:T(8,128)S(1)} %get-tuple-element.29.prelb_hbm) | copy-start | bytes 1572868
  54.1 4.4 %copy-start.18 = (bf16[8,16,256]{2,1,0:T(8,128)(2,1)}, bf16[8,16,256]{2,1,0:T(8,128)(2,1)S(1)}, u32[]{:S(2)}) copy-start(bf16[8,16,256]{2,1,0:T(8,128)(2,1)S(1)} %get-tuple-element.33.leftb_ref) | copy-start | bytes 196612
  54.1 16.1 %collective-permute-start.5 = (bf16[4,288,128]{2,1,0:T(8,128)(2,1)S(1)}, bf16[4,288,128]{2,1,0:T(8,128)(2,1)S(1)}, u32[]{:S(2)}, u32[]{:S(2)}) collective-permute-start(bf16[4,288,128]{2,1,0:T(8,128)(2,1)S(1)} %get-tuple-element.34), channel_id=1, source_target_pairs={{0,8},{8,16},{16,24},{24,32},{32,40},{40,48},{48,56},{56,64},{64,7... | collective-permute-start | bytes 884744 | tf_op jit(solution)/shard_map/ppermute | solution.py:23
  58.5 4.7 %copy-start.16 = (f32[8,128,128]{2,1,0:T(8,128)}, f32[8,128,128]{2,1,0:T(8,128)S(1)}, u32[]{:S(2)}) copy-start(f32[8,128,128]{2,1,0:T(8,128)S(1)} %get-tuple-element.28.prela_hbm) | copy-start | bytes 1572868
  58.5 4.7 %copy-start.19 = (bf16[8,16,256]{2,1,0:T(8,128)(2,1)}, bf16[8,16,256]{2,1,0:T(8,128)(2,1)S(1)}, u32[]{:S(2)}) copy-start(bf16[8,16,256]{2,1,0:T(8,128)(2,1)S(1)} %get-tuple-element.32.lefta_ref) | copy-start | bytes 196612
  58.6 11.7 %copy-start.14 = (bf16[8,272,128]{2,1,0:T(8,128)(2,1)}, bf16[8,272,128]{2,1,0:T(8,128)(2,1)S(1)}, u32[]{:S(2)}) copy-start(bf16[8,272,128]{2,1,0:T(8,128)(2,1)S(1)} %get-tuple-element.26.mota_hbm) | copy-start | bytes 1671172
  58.6 11.7 %collective-permute-start.6 = (bf16[4,288,128]{2,1,0:T(8,128)(2,1)S(1)}, bf16[4,288,128]{2,1,0:T(8,128)(2,1)S(1)}, u32[]{:S(2)}, u32[]{:S(2)}) collective-permute-start(bf16[4,288,128]{2,1,0:T(8,128)(2,1)S(1)} %get-tuple-element.35), channel_id=1, source_target_pairs={{8,0},{16,8},{24,16},{32,24},{40,32},{48,40},{56,48},{64,56},{72,6... | collective-permute-start | bytes 884744 | tf_op jit(solution)/shard_map/ppermute | solution.py:23
  63.2 56.6 %collective-permute-start.8 = (bf16[16,128,256]{2,1,0:T(8,128)(2,1)S(1)}, bf16[16,128,256]{2,1,0:T(8,128)(2,1)S(1)}, u32[]{:S(2)}, u32[]{:S(2)}) collective-permute-start(bf16[16,128,256]{2,1,0:T(8,128)(2,1)S(1)} %slice.3), channel_id=1, source_target_pairs={{1,0},{2,1},{3,2},{4,3},{5,4},{6,5},{7,6},{9,8},{10,9},{11,10},{12... | collective-permute-start | bytes 3145736 | tf_op jit(solution)/shard_map/ppermute | solution.py:23
  70.2 1.2 copy-start.21
  70.2 0.9 copy-start.22
  70.2 1.0 copy-start.23
  70.3 1.0 copy-start.24
  71.4 40.5 %copy-start.9 = (s32[16,256]{1,0:T(8,128)S(1)}, s32[16,256]{1,0:T(8,128)}, u32[]{:S(2)}) copy-start(s32[16,256]{1,0:T(8,128)} %refs_5_.5) | copy-start | bytes 49156
  71.4 40.5 %copy-start.11 = (bf16[16,128]{1,0:T(8,128)(2,1)S(1)}, bf16[16,128]{1,0:T(8,128)(2,1)}, u32[]{:S(2)}) copy-start(bf16[16,128]{1,0:T(8,128)(2,1)} %copy-done.10) | copy-start | bytes 12292
  105.4 14.4 %collective-permute-start.7 = (bf16[16,16,128]{2,1,0:T(8,128)(2,1)}, bf16[16,16,128]{2,1,0:T(8,128)(2,1)S(1)}, u32[]{:S(2)}, u32[]{:S(2)}) collective-permute-start(bf16[16,16,128]{2,1,0:T(8,128)(2,1)} %get-tuple-element.40), channel_id=1, source_target_pairs={{1,0},{2,1},{3,2},{4,3},{5,4},{6,5},{7,6},{9,8},{10,9},{11,10},{12... | collective-permute-start | bytes 196616 | tf_op jit(solution)/shard_map/ppermute | solution.py:23
  111.9 1.2 %copy-start.6 = (bf16[16,256,128]{2,1,0:T(8,128)(2,1)S(1)}, bf16[16,256,128]{2,1,0:T(8,128)(2,1)}, u32[]{:S(2)}) copy-start(bf16[16,256,128]{2,1,0:T(8,128)(2,1)} %get-tuple-element.37.refs_0_) | copy-start | bytes 3145732

commit v4 on v3

--- a/solution.py
+++ b/solution.py
@@ -14,7 +14,9 @@
 BF16 = jnp.bfloat16
 ROWS = 4
 SMALL_VMEM = 16 * 1024 * 1024
-GRU_VMEM = 56 * 1024 * 1024
+GRU_VMEM = 32 * 1024 * 1024
+GATES_VMEM = 12 * 1024 * 1024
+PACK_VMEM = 60 * 1024 * 1024
 
 
 def shift(array, axis, by):
@@ -67,9 +69,11 @@
     return jnp.sum(jnp.where(iota(levels.shape, 0) == row, levels, 0), axis=0, keepdims=True)
 
 
-def pack_left_kernel(left_ref, own_ref, hid_ref, grad_ref, disp_ref, out_ref):
+def pack_small_kernel(
+    left_ref, own_ref, hid_ref, grad_ref, hid_last_ref, grad_last_ref, disp_ref, out_ref, last_ref
+):
     rows, _, chan = left_ref.shape
-    levels = level_columns(disp_ref, 0)
+    levels = jnp.transpose(disp_ref[:, :B].astype(F32), (1, 0))
     for r in range(rows):
         out_ref[r, :, :chan] = left_ref[r, :HALO]
         out_ref[r, :, chan : 2 * chan] = own_ref[r, :HALO]
@@ -77,11 +81,11 @@
         out_ref[r, :, 2 * chan + B : 2 * chan + 2 * B] = grad_ref[r, :HALO]
         level = jnp.broadcast_to(levels[:8, r : r + 1], (8, B))
         out_ref[r, :, 2 * chan + 2 * B :] = level.astype(BF16)[:HALO]
-
-
-def pack_right_kernel(
-    start, own_ref, beside_ref, left_ref, hid_ref, grad_ref, disp_ref, out_ref
-):
+        hg = jnp.concatenate([hid_last_ref[r], grad_last_ref[r]], axis=1).astype(F32)
+        last_ref[r] = pltpu.roll(hg, HALO, 0)[:HALO].astype(BF16)
+
+
+def pack_right_kernel(start, own_ref, beside_ref, left_ref, disp_ref, out_ref):
     rows, _, chan = own_ref.shape
     first = start + pl.program_id(0) * rows
     low = iota((8, chan), 0) < HALO
@@ -92,20 +96,31 @@
         row = level_row(disp_ref, first + r, disp_ref.shape[1] - B).astype(F32)
         level = jnp.transpose(jnp.broadcast_to(row, (8, B)), (1, 0))[B - 8 :, :1]
         level = pltpu.roll(jnp.broadcast_to(level, (8, chan)), HALO, 0)
-        hg = jnp.concatenate([hid_ref[r], grad_ref[r]], axis=1).astype(F32)
-        out_ref[r, B:] = jnp.concatenate([upper, jnp.where(low, level, hg)], axis=0).astype(BF16)
+        out_ref[r, B:] = jnp.concatenate([upper, jnp.where(low, level, 0.0)], axis=0).astype(BF16)
 
 
 def rim_kernel(
-    hid_first_ref, grad_first_ref, hid_last_ref, grad_last_ref, side_ref, first_ref, last_ref, edge_ref, pad_ref
+    hid_first_ref,
+    grad_first_ref,
+    hid_last_ref,
+    grad_last_ref,
+    right_ref,
+    left_ref,
+    first_ref,
+    last_ref,
+    edge_ref,
+    pad_ref,
 ):
-    rows = side_ref.shape[0]
+    rows = right_ref.shape[0]
     own = hid_first_ref.shape[1]
-    chan = (side_ref.shape[2] - 3 * B) // 2
+    chan = (right_ref.shape[2] - 3 * B) // 2
     pad_ref[...] = jnp.zeros_like(pad_ref)
     for r in range(rows):
-        pad_ref[:HALO] = side_ref[r, :, 2 * chan : 2 * chan + 2 * B].astype(F32)
-        edge_ref[r] = pad_ref[...].astype(BF16)
+        pad_ref[:HALO] = right_ref[r, :, 2 * chan : 2 * chan + 2 * B].astype(F32)
+        pad_ref[8 : 8 + HALO] = left_ref[r].astype(F32)
+        value = pad_ref[...]
+        low = pltpu.roll(value[8:], HALO, 0)
+        edge_ref[r] = jnp.concatenate([value[:8], low], axis=0).astype(BF16)
     for r in range(HALO):
         for out, hid, grad, row in (
             (first_ref, hid_first_ref, grad_first_ref, r),
@@ -173,7 +188,6 @@
     weight_ref,
     mot_ref,
     pre_ref,
-    hg_ref,
     rim_ref,
     pad_ref,
     mw_ref,
@@ -185,7 +199,6 @@
     weight = taps_matrix(weight_ref, mw_ref)
     last = iota((EDGE, chan), 0) >= EDGE - HALO
     upper = iota((EDGE, B), 0) < EDGE // 2
-    wide = mot_ref.shape[1]
     for r in range(rows):
         extra = before_ref[r, B:].astype(F32)
         pad_ref[r, B - EDGE :] = jnp.where(last, pltpu.roll(extra, 12, 0), 0.0).astype(BF16)
@@ -205,14 +218,10 @@
         mot_ref[r, B : 2 * B] = mot_right_ref[r, :B]
         right_edge = mot_right_ref[r, B:].astype(F32)
         mot_ref[r, 2 * B :] = jnp.where(upper, right_edge, mot[B:]).astype(BF16)
-        hg_ref[r] = jnp.where(last, extra, 0.0).astype(BF16)
 
     @pl.when(step == rim_step)
     def _():
-        for r in range(rows):
-            rim_ref[r, :wide] = mot_ref[r]
-            hg = hg_ref[r].astype(F32)
-            rim_ref[r, wide:] = (hg[:, :B] + pltpu.roll(hg[:, B:], EDGE // 2, 0)).astype(BF16)
+        rim_ref[...] = mot_ref[...]
 
 
 def shifted(value):
@@ -246,172 +255,147 @@
 CHUNK = 4
 
 
+def gates_hidden_kernel(
+    hid_ref,
+    grad_ref,
+    hgt_ref,
+    hgb_ref,
+    edge_ref,
+    gate_ref,
+    cand_ref,
+    h_ref,
+    g_ref,
+    gh_ref,
+    wgm_ref,
+    wc_ref,
+    wcb_ref,
+    wgb_ref,
+    h3_ref,
+    wgh_ref,
+):
+    rows, own, _ = hid_ref.shape
+    wide = own + EDGE
+    total = rows + 2 * HALO
+    for row in range(total):
+        n = row - HALO
+        if 0 <= n < rows:
+            h_ref[row, :own] = hid_ref[n]
+            h_ref[row, own:] = edge_ref[n, :, :B]
+            g_ref[row, :own] = grad_ref[n]
+            g_ref[row, own:] = edge_ref[n, :, B:]
+        else:
+            hg = hgt_ref[row] if n < 0 else hgb_ref[n - rows]
+            h_ref[row] = hg[:, :B]
+            g_ref[row] = hg[:, B:]
+        store3(h3_ref, row, h_ref[row].astype(F32))
+    zeros = jnp.zeros((6 * B, B), BF16)
+    wc_ref[18 * B :, :B] = zeros
+    wc_ref[: 6 * B, B:] = zeros
+    wc_ref[: 18 * B, :B] = cand_ref[...]
+    wc_ref[6 * B :, B:] = cand_ref[...]
+    wgb_ref[:B, 18 * B :] = jnp.zeros((B, 6 * B), BF16)
+    wgb_ref[B:, : 6 * B] = jnp.zeros((B, 6 * B), BF16)
+    for n in range(9):
+        wgh_ref[n * B : (n + 1) * B] = gate_ref[2 * n * B : (2 * n + 1) * B]
+        wgm_ref[n * B : (n + 1) * B] = gate_ref[(2 * n + 1) * B : (2 * n + 2) * B]
+        at = (8 - n) * 2 * B
+        wcb_ref[:, n * B : (n + 1) * B] = cand_ref[at : at + 2 * B]
+        for s in range(2):
+            col = (n + 3 * s) * 2 * B
+            wgb_ref[s * B : (s + 1) * B, col : col + 2 * B] = gate_ref[at + B : at + 2 * B]
+    for group in chunks(range(1, total - 1), CHUNK):
+        lhs = patches((h3_ref,), [[r + a - 1 for r in group] for a in range(3)])
+        acc = dot(lhs, wgh_ref[...])
+        for n, row in enumerate(group):
+            gh_ref[row - 1] = acc[n * wide : (n + 1) * wide]
+
+
 def gru_kernel(
-    hid_hbm,
-    grad_hbm,
-    hgt_hbm,
-    hgb_hbm,
-    mota_hbm,
-    motb_hbm,
-    gate_hbm,
-    cand_hbm,
-    prela_hbm,
-    prelb_hbm,
-    prer_hbm,
-    right_ref,
-    lefta_ref,
-    leftb_ref,
+    mota_ref,
+    motb_ref,
+    wgm_ref,
+    h_ref,
+    gates_ref,
+    g_ref,
+    wc_ref,
+    wcb_ref,
+    wgb_ref,
+    prela_ref,
+    prelb_ref,
+    prer_ref,
     mott_ref,
     motl_ref,
     disp_ref,
     mw_ref,
-    nh_hbm,
-    pg_hbm,
+    nh_ref,
+    pg_ref,
     tg_ref,
-    h3_ref,
+    gh_ref,
+    u3_ref,
     m3_ref,
     r3_ref,
     c3_ref,
-    h_ref,
-    g_ref,
-    up_ref,
-    rs_ref,
     cb_ref,
-    hid_ref,
-    grad_ref,
-    hgt_ref,
-    hgb_ref,
-    mota_ref,
-    motb_ref,
-    wg_ref,
-    cw_ref,
-    prel_ref,
-    prer_ref,
-    wc_ref,
-    wcb_ref,
-    wgb_ref,
-    nh_ref,
-    pg_ref,
-    sems,
 ):
-    rows, own, _ = hid_ref.shape
+    rows, own, _ = nh_ref.shape
     half = rows // 2
     wide = own + EDGE
     total = rows + 2 * HALO
     inner = range(HALO, HALO + rows)
-    moves = (
-        (hid_hbm, hid_ref),
-        (hgt_hbm, hgt_ref),
-        (hgb_hbm, hgb_ref),
-        (mota_hbm, mota_ref),
-        (motb_hbm, motb_ref),
-        (grad_hbm, grad_ref),
-        (gate_hbm, wg_ref),
-        (cand_hbm, cw_ref),
-        (prela_hbm, prel_ref.at[:half]),
-        (prelb_hbm, prel_ref.at[half:]),
-        (prer_hbm, prer_ref),
-    )
-    copies = [pltpu.make_async_copy(s, d, sems.at[n]) for n, (s, d) in enumerate(moves)]
-    for copy in copies:
-        copy.start()
-    wc_ref[9 * B * 2 :, :B] = jnp.zeros((6 * B, B), BF16)
-    wc_ref[: 6 * B, B:] = jnp.zeros((6 * B, B), BF16)
-    wgb_ref[:B, 18 * B :] = jnp.zeros((B, 6 * B), BF16)
-    wgb_ref[B:, : 6 * B] = jnp.zeros((B, 6 * B), BF16)
-    for copy in copies[:6]:
-        copy.wait()
-
-    upper = iota((EDGE, B), 0) < EDGE // 2
-    last = iota((EDGE, B), 0) >= EDGE - HALO
-
-    def join(first, second):
-        return jnp.where(upper, first.astype(F32), second.astype(F32)).astype(BF16)
-
+    gate_groups = chunks(range(1, total - 1), CHUNK)
     for row in range(total):
-        if row in inner:
-            n = row - HALO
-            left = lefta_ref[n] if n < half else leftb_ref[n - half]
-            h_ref[row, :own] = hid_ref[n]
-            h_ref[row, own:] = join(right_ref[n, :, :B], left[:, :B])
-            g_ref[row, :own] = grad_ref[n]
-            g_ref[row, own:] = join(right_ref[n, :, B:], left[:, B:])
+        n = row - HALO
+        if n < 0:
+            mot = mott_ref[row]
+        elif n >= rows:
+            mot = motl_ref[n - rows]
+        else:
             mot = mota_ref[n] if n < half else motb_ref[n - half]
-        else:
-            top = row < HALO
-            n = row if top else row - HALO - rows
-            hg = hgt_ref[n] if top else hgb_ref[n]
-            mot = mott_ref[n] if top else motl_ref[n]
-            left = mot[wide:].astype(F32)
-            mot = mot[:wide]
-            h_ref[row, :own] = hg[:own, :B]
-            h_ref[row, own:] = join(hg[own:, :B], jnp.where(last, left, 0.0))
-            g_ref[row, :own] = hg[:own, B:]
-            left = jnp.where(last, pltpu.roll(left, EDGE // 2, 0), 0.0)
-            g_ref[row, own:] = join(hg[own:, B:], left)
-        store3(h3_ref, row, h_ref[row].astype(F32))
         store3(m3_ref, row, mot.astype(F32))
 
-    copies[6].wait()
-    for group in chunks(range(1, total - 1), CHUNK):
-        lhs = patches((h3_ref, m3_ref), [[r + a - 1 for r in group] for a in range(3)])
-        acc = jax.nn.sigmoid(dot(lhs, wg_ref[...]))
+    for group in gate_groups:
+        lhs = patches((m3_ref,), [[r + a - 1 for r in group] for a in range(3)])
+        acc = dot(lhs, wgm_ref[...])
         for n, row in enumerate(group):
-            gate = acc[n * wide : (n + 1) * wide]
-            up_ref[row] = gate[:, :B]
-            reset = gate[:, B:]
-            rs_ref[row] = reset
-            store3(r3_ref, row, reset * h_ref[row].astype(F32))
-
-    copies[7].wait()
-    wc_ref[: 18 * B, :B] = cw_ref[...]
-    wc_ref[6 * B :, B:] = cw_ref[...]
-    for n in range(9):
-        at = (8 - n) * 2 * B
-        wcb_ref[:, n * B : (n + 1) * B] = cw_ref[at : at + 2 * B]
-        for s in range(2):
-            col = (n + 3 * s) * 2 * B
-            wgb_ref[s * B : (s + 1) * B, col : col + 2 * B] = wg_ref[at + B : at + 2 * B]
+            gate = jax.nn.sigmoid(acc[n * wide : (n + 1) * wide] + gates_ref[row - 1])
+            gh_ref[row - 1] = gate
+            store3(r3_ref, row, gate[:, B:] * h_ref[row].astype(F32))
 
     for group in chunks(range(2, total - 2, 2), CHUNK):
         lhs = patches((r3_ref, m3_ref), [[r + t - 1 for r in group] for t in range(4)])
         acc = jnp.tanh(dot(lhs, wc_ref[...]))
-        for n, first in enumerate(group):
-            for row in (first, first + 1):
-                s = row - first
+        for n, top in enumerate(group):
+            for row in (top, top + 1):
+                s = row - top
                 cand = acc[n * wide : (n + 1) * wide, s * B : (s + 1) * B]
                 hidden = h_ref[row].astype(F32)
-                update = up_ref[row]
+                update = gh_ref[row - 1, :, :B]
                 if row in inner:
                     new = (1.0 - update) * hidden + update * cand
                     nh_ref[row - HALO] = new[:own].astype(BF16)
                 gu = g_ref[row].astype(F32) * update
                 store3(c3_ref, row, gu * (1.0 - cand * cand))
-                store3(h3_ref, row, gu * (cand - hidden) * (1.0 - update))
-    new_copy = pltpu.make_async_copy(nh_ref, nh_hbm, sems.at[len(moves)])
-    new_copy.start()
+                store3(u3_ref, row, gu * (cand - hidden) * (1.0 - update))
 
     for group in chunks(range(3, total - 3), CHUNK):
         lhs = patches((c3_ref,), [[r + a - 1 for r in group] for a in range(3)])
         acc = dot_nt(lhs, wcb_ref[...])
         for n, row in enumerate(group):
             back = acc[n * wide : (n + 1) * wide]
-            reset = rs_ref[row]
+            reset = gh_ref[row - 1, :, B:]
             store3(m3_ref, row, back[:, :B] * h_ref[row].astype(F32) * reset * (1.0 - reset))
             if row in inner:
                 cb_ref[row - HALO] = back[:own, B:]
 
-    for copy in copies[8:]:
-        copy.wait()
-    pieces = []
     for group in chunks(range(HALO, HALO + rows, 2), CHUNK):
-        lhs = patches((h3_ref, m3_ref), [[r + t - 1 for r in group] for t in range(4)])
+        lhs = patches((u3_ref, m3_ref), [[r + t - 1 for r in group] for t in range(4)])
         acc = dot_nt(lhs, wgb_ref[...])
-        for n, first in enumerate(group):
-            for row in (first - HALO, first + 1 - HALO):
-                s = row + HALO - first
+        for n, top in enumerate(group):
+            for row in (top - HALO, top + 1 - HALO):
+                s = row + HALO - top
                 back = acc[n * wide : n * wide + own, s * B : (s + 1) * B]
-                pre = jnp.concatenate([prel_ref[row], prer_ref[row]], axis=0)
+                prel = prela_ref[row] if row < half else prelb_ref[row - half]
+                pre = jnp.concatenate([prel, prer_ref[row]], axis=0)
                 sig = jax.nn.sigmoid(pre)
                 grad = (cb_ref[row] + back) * sig * (1.0 + pre * (1.0 - sig))
                 grad = grad.astype(BF16)
@@ -419,14 +403,6 @@
                 tap = dot_nt(mw_ref[...], grad[:B])
                 level = jnp.broadcast_to(disp_ref[row : row + 1, :B].astype(F32), tap.shape)
                 tg_ref[row] = jnp.where(iota(tap.shape, 0) == 15, level, tap).astype(BF16)
-        done = pl.ds(group[0] - HALO, 2 * len(group))
-        at = len(moves) + 1 + len(pieces)
-        piece = pltpu.make_async_copy(pg_ref.at[done], pg_hbm.at[done], sems.at[at])
-        piece.start()
-        pieces.append(piece)
-    new_copy.wait()
-    for piece in pieces:
-        piece.wait()
 
 
 def spread(grad, disp, taps, radius):
@@ -540,54 +516,53 @@
     shape = jax.ShapeDtypeStruct
     vmem = pl.BlockSpec(memory_space=pltpu.VMEM)
     last8 = cols // 8 - 1
-
-    from_right = shift(
-        pl.pallas_call(
-            pack_left_kernel,
-            grid=(1,),
+    pack_params = pltpu.CompilerParams(vmem_limit_bytes=PACK_VMEM)
+
+    small_shapes = (shape((rows, HALO, packed), BF16), shape((rows, HALO, 2 * B), BF16))
+    to_left, to_right = pl.pallas_call(
+        pack_small_kernel,
+        grid=(1,),
+        in_specs=[
+            block((rows, 8, chan), 0, 0, 0),
+            block((rows, 8, chan), 0, 0, 0),
+            block((rows, 8, B), 0, 0, 0),
+            block((rows, 8, B), 0, 0, 0),
+            block((rows, 8, B), 0, last8, 0),
+            block((rows, 8, B), 0, last8, 0),
+            whole(disparity),
+        ],
+        out_specs=[whole(s) for s in small_shapes],
+        out_shape=small_shapes,
+        compiler_params=pack_params,
+        cost_estimate=cost(1 << 16, 1 << 18),
+        name="pack_small",
+    )(feat_left, feat_right, hidden, grad_hidden, hidden, grad_hidden, disparity)
+    from_right = shift(to_left, "cols", -1)
+    from_left = shift(to_right, "cols", 1)
+
+    def features_for_right(start):
+        at = start // size
+        out = shape((half, B + EDGE, chan), BF16)
+        return pl.pallas_call(
+            lambda *refs: pack_right_kernel(start, *refs),
+            grid=(half // size,),
             in_specs=[
-                block((rows, 8, chan), 0, 0, 0),
-                block((rows, 8, chan), 0, 0, 0),
-                block((rows, 8, B), 0, 0, 0),
-                block((rows, 8, B), 0, 0, 0),
+                block((size, B, chan), at, cols // B - 1, 0),
+                block((size, 8, chan), at, (cols - B) // 8 - 1, 0),
+                block((size, 8, chan), at, last8, 0),
                 whole(disparity),
             ],
-            out_specs=whole(shape((rows, HALO, packed), BF16)),
-            out_shape=shape((rows, HALO, packed), BF16),
-            compiler_params=params,
-            cost_estimate=cost(1 << 16, 1 << 18),
-            name="pack_left",
-        )(feat_left, feat_right, hidden, grad_hidden, disparity),
-        "cols",
-        -1,
+            out_specs=by_rows(out, size),
+            out_shape=out,
+            compiler_params=pack_params,
+            cost_estimate=cost(1 << 16, 2 << 20),
+            name="pack_right",
+        )(feat_right, feat_right, feat_left, disparity)
+
+    packs, from_right, from_left = lax.optimization_barrier(
+        ([features_for_right(0), features_for_right(half)], from_right, from_left)
     )
-
-    def features_before(start):
-        at = start // size
-        out = shape((half, B + EDGE, chan), BF16)
-        return shift(
-            pl.pallas_call(
-                lambda *refs: pack_right_kernel(start, *refs),
-                grid=(half // size,),
-                in_specs=[
-                    block((size, B, chan), at, cols // B - 1, 0),
-                    block((size, 8, chan), at, (cols - B) // 8 - 1, 0),
-                    block((size, 8, chan), at, last8, 0),
-                    block((size, 8, B), at, last8, 0),
-                    block((size, 8, B), at, last8, 0),
-                    whole(disparity),
-                ],
-                out_specs=by_rows(out, size),
-                out_shape=out,
-                compiler_params=params,
-                cost_estimate=cost(1 << 16, 2 << 20),
-                name="pack_right",
-            )(feat_right, feat_right, feat_left, hidden, grad_hidden, disparity),
-            "cols",
-            1,
-        )
-
-    before = [features_before(0), features_before(half)]
+    before = [shift(pack, "cols", 1) for pack in packs]
 
     rim = shape((HALO, wide, 2 * B), BF16)
     edge_shape = shape((rows, EDGE, 2 * B), BF16)
@@ -600,6 +575,7 @@
             block((HALO, cols, B), rows // HALO - 1, 0, 0),
             block((HALO, cols, B), rows // HALO - 1, 0, 0),
             whole(from_right),
+            whole(from_left),
         ],
         out_specs=[whole(rim), whole(rim), whole(edge_shape)],
         out_shape=(rim, rim, edge_shape),
@@ -607,7 +583,7 @@
         compiler_params=params,
         cost_estimate=cost(1 << 16, 2 << 20),
         name="rims",
-    )(hidden, grad_hidden, hidden, grad_hidden, from_right)
+    )(hidden, grad_hidden, hidden, grad_hidden, from_right, from_left)
     hg_top = shift(last_rim, "rows", 1)
     hg_low = shift(first_rim, "rows", -1)
 
@@ -637,8 +613,7 @@
         shapes = (
             shape((half, wide, B), BF16),
             shape((half, B, B), F32),
-            shape((half, EDGE, 2 * B), BF16),
-            shape((HALO, wide + EDGE, B), BF16),
+            shape((HALO, wide, B), BF16),
         )
         return pl.pallas_call(
             lambda *refs: left_corr_kernel(*args, start, rim_step, *refs),
@@ -651,7 +626,7 @@
                 block((size, B + EDGE, B), at, 0, 0),
                 whole(mw16),
             ],
-            out_specs=[by_rows(s, size) for s in shapes[:3]] + [whole(shapes[3])],
+            out_specs=[by_rows(s, size) for s in shapes[:2]] + [whole(shapes[2])],
             out_shape=shapes,
             scratch_shapes=pads,
             compiler_params=params,
@@ -659,51 +634,59 @@
             name="corr_left",
         )(feat_left, feat_right, before, disparity, mot_right, mw16)
 
-    mot_a, pre_a, left_a, rim_a = left_lookup(0, before[0], 0)
+    mot_a, pre_a, rim_a = left_lookup(0, before[0], 0)
     mot_low = shift(rim_a, "rows", -1)
-    mot_b, pre_b, left_b, rim_b = left_lookup(half, before[1], half // size - 1)
+    mot_b, pre_b, rim_b = left_lookup(half, before[1], half // size - 1)
     mot_top = shift(rim_b, "rows", 1)
     first_left, _ = lax.optimization_barrier((feat_left[:, :B], mot_b))
     next_left = shift(first_left, "cols", -1)
 
     total = rows + 2 * HALO
     own_shape = shape((rows, cols, B), BF16)
-    big = (
+    halo_shape = shape((total, wide, B), BF16)
+    gate_shape = shape((total - 2, wide, 2 * B), F32)
+    weight_shapes = [
+        shape((9 * B, 2 * B), BF16),
+        shape((24 * B, 2 * B), BF16),
+        shape((2 * B, 9 * B), BF16),
+        shape((2 * B, 24 * B), BF16),
+    ]
+    hid_operands = (
         hidden,
         grad_hidden,
         hg_top,
         hg_low,
-        mot_a,
-        mot_b,
+        edge,
         gate_weight.reshape(-1, 2 * B),
         cand_weight.reshape(-1, B),
-        pre_a,
-        pre_b,
-        pre_right,
     )
-    small = (edge, left_a, left_b, mot_top, mot_low, disparity, mw16)
+    hid_shapes = (halo_shape, halo_shape, gate_shape, *weight_shapes)
+    hid, grad, gates, wgm, wc, wcb, wgb = pl.pallas_call(
+        gates_hidden_kernel,
+        in_specs=[vmem] * len(hid_operands),
+        out_specs=[vmem] * len(hid_shapes),
+        out_shape=hid_shapes,
+        scratch_shapes=[
+            pltpu.VMEM((total, wide, 3 * B), BF16),
+            pltpu.VMEM((9 * B, 2 * B), BF16),
+        ],
+        compiler_params=pltpu.CompilerParams(vmem_limit_bytes=GATES_VMEM),
+        cost_estimate=cost(2 * 22 * wide * 9 * B * 2 * B, 16 << 20),
+        name="gates_hidden",
+    )(*hid_operands)
+    big = (mot_a, mot_b, wgm, hid, gates, grad, wc, wcb, wgb, pre_a, pre_b, pre_right)
+    small = (mot_top, mot_low, disparity, mw16)
     anywhere = pl.BlockSpec(memory_space=pl.ANY)
-    new_hidden, pre_grad, tap_grad = pl.pallas_call(
+    new_hidden, pre_grad, tap_grad, _ = pl.pallas_call(
         gru_kernel,
-        in_specs=[anywhere] * len(big) + [vmem] * len(small),
-        out_specs=[anywhere, anywhere, vmem],
-        out_shape=(own_shape, own_shape, shape((rows, 16, B), BF16)),
+        in_specs=[vmem] * (len(big) + len(small)),
+        out_specs=[vmem] * 4,
+        out_shape=(own_shape, own_shape, shape((rows, 16, B), BF16), gate_shape),
+        input_output_aliases={4: 3},
         scratch_shapes=[pltpu.VMEM((total, wide, 3 * B), BF16)] * 4
-        + [pltpu.VMEM((total, wide, B), BF16)] * 2
-        + [pltpu.VMEM((total, wide, B), F32)] * 2
-        + [pltpu.VMEM((rows, cols, B), F32)]
-        + [pltpu.VMEM(a.shape, BF16) for a in big[:8]]
-        + [pltpu.VMEM((rows, B, B), F32)] * 2
-        + [
-            pltpu.VMEM((24 * B, 2 * B), BF16),
-            pltpu.VMEM((2 * B, 9 * B), BF16),
-            pltpu.VMEM((2 * B, 24 * B), BF16),
-            pltpu.VMEM((rows, cols, B), BF16),
-            pltpu.VMEM((rows, cols, B), BF16),
-            pltpu.SemaphoreType.DMA((len(big) + 1 + rows,)),
-        ],
+        + [pltpu.VMEM((rows, cols, B), F32)],
         compiler_params=pltpu.CompilerParams(vmem_limit_bytes=GRU_VMEM),
-        cost_estimate=cost(2 * 22 * wide * 256 * 256 * 24, 16 << 20),
+        cost_estimate=cost(2 * 22 * wide * 256 * 256 * 20, 16 << 20),
         name="gru",
     )(*big, *small)
     next_grad = shift(tap_grad, "cols", -1)

time: 124 us -> 106 us (0.85)
  local copies, waits for them, and re-layouts: 8.84 us -> 0.14 us
  starting transfers between devices: 39.8 us -> 31.6 us
    unnamed x50 -> x18, local copies, waits for them, and re-layouts: 8.76 us -> 0.05 us
    ppermute x9 -> x10, starting transfers between devices: 39.8 us -> 31.6 us  [shift(): return lax.ppermute(array, axis, pairs)]
    ppermute x9 -> x10, waiting for transfers between devices: 18.5 us -> 17.5 us  [shift(): return lax.ppermute(array, axis, pairs)]
    pallas_call x4 -> x5, Pallas kernels: 35.1 us -> 34.6 us  [the longest x1 23.4 us: per_device(): pl.pallas_call(gru_kernel, in_specs=[vmem] * (len(big) + len(small)), out...]
  transfers between devices with their start and end apart: 9 -> 10, of which waited for: 1 -> 4; matrix products, arithmetic and copies ran while one was open for 0% -> 0% of each run, Pallas kernels for 42% -> 48%
where the time goes in v4:
time: 106 us; the launch traced here: 104 us
  Pallas kernels  53.7 us (51%)
  starting transfers between devices  31.6 us (30%)
  waiting for transfers between devices  17.5 us (17%)
    ppermute x10, starting transfers between devices, shift(): return lax.ppermute(array, axis, pairs)  31.6 us
    pallas_call x1, Pallas kernels, per_device(): pl.pallas_call(gru_kernel, in_specs=[vmem] * (len(big) + len(small)), out...  23.4 us
    ppermute x10, waiting for transfers between devices, shift(): return lax.ppermute(array, axis, pairs)  17.5 us
    pallas_call x1, Pallas kernels, per_device(): pl.pallas_call(lambda *refs: grads_kernel(*args, *refs), grid=(steps,), i...  6.7 us
    pallas_call x1, Pallas kernels, per_device(): pl.pallas_call(gates_hidden_kernel, in_specs=[vmem] * len(hid_operands),...  5.17 us
    pallas_call x2, Pallas kernels, left_lookup(): pl.pallas_call(lambda *refs: left_corr_kernel(*args, start, rim_step, *re...  4.85 us
    pallas_call x1, Pallas kernels, per_device(): pl.pallas_call(lambda *refs: right_corr_kernel(*args, *refs), grid=(steps...  4.76 us
    pallas_call x2, Pallas kernels, features_for_right(): pl.pallas_call(lambda *refs: pack_right_kernel(start, *refs), grid=(half...  4.29 us
  transfers between devices with their start and end apart: 10, of which 4 were waited for; matrix products, arithmetic and copies ran while one was open for 0% of the time, Pallas kernels for 48%

profile of v4, /device:TPU:120, one launch (start us, length us, event | category | flops | bytes accessed | tf_op | source)
XLA Modules:
  0.0 103.8 jit_solution(13154907858449998321)
XLA Ops:
  0.6 1.7 %pack_small.1 = (bf16[16,4,896]{2,1,0:T(4,128)(2,1)}, bf16[16,4,256]{2,1,0:T(4,128)(2,1)}) custom-call(bf16[16,256,256]{2,1,0:T(8,128)(2,1)} %refs_2_.9, bf16[16,256,256]{2,1,0:T(8,128)(2,1)} %refs_2_.8, bf16[16,256,128]{2,1,0:T(8,128)(2,1)} %hid_ref.3, bf16[16,256,128]{2,1,0:T(8,128)(2,1)} %grad_ref.3, bf16[16,256,128]{2,1,0:T(8,128)(2,1)} %hid_ref.3, ...), custom_call_target="tpu_custom_call" | custom-call | flops 65536 | bytes 262144 | tf_op jit(solution)/shard_map/pack_small/pallas_call | solution.py:522
  2.4 4.8 %collective-permute-start = (bf16[16,4,896]{2,1,0:T(4,128)(2,1)}, bf16[16,4,896]{2,1,0:T(4,128)(2,1)S(1)}, u32[]{:S(2)}, u32[]{:S(2)}) collective-permute-start(bf16[16,4,896]{2,1,0:T(4,128)(2,1)} %get-tuple-element.34), channel_id=1, source_target_pairs={{1,0},{2,1},{3,2},{4,3},{5,4},{6,5},{7,6},{9,8},{10,9},{11,10},{12... | collective-permute-start | bytes 344072 | tf_op jit(solution)/shard_map/ppermute | solution.py:25
  7.1 2.6 %collective-permute-start.1 = (bf16[16,4,256]{2,1,0:T(4,128)(2,1)}, bf16[16,4,256]{2,1,0:T(4,128)(2,1)S(1)}, u32[]{:S(2)}, u32[]{:S(2)}) collective-permute-start(bf16[16,4,256]{2,1,0:T(4,128)(2,1)} %get-tuple-element.35), channel_id=1, source_target_pairs={{0,1},{1,2},{2,3},{3,4},{4,5},{5,6},{6,7},{8,9},{9,10},{10,11},{11... | collective-permute-start | bytes 98312 | tf_op jit(solution)/shard_map/ppermute | solution.py:25
  9.7 2.1 %pack_right.2 = bf16[8,144,256]{2,1,0:T(8,128)(2,1)} custom-call(bf16[16,256,256]{2,1,0:T(8,128)(2,1)} %refs_2_.8, bf16[16,256,256]{2,1,0:T(8,128)(2,1)} %refs_2_.8, bf16[16,256,256]{2,1,0:T(8,128)(2,1)} %refs_2_.9, s32[16,256]{1,0:T(8,128)} %refs_5_.1), custom_call_target="tpu_custom_call" | custom-call | flops 65536 | bytes 2097152 | tf_op jit(solution)/shard_map/pack_right/pallas_call | solution.py:546
  11.8 0.0 copy-start.7
  11.8 0.0 copy-start.2
  11.8 0.0 copy-start.3
  11.8 2.2 %pack_right.3 = bf16[8,144,256]{2,1,0:T(8,128)(2,1)} custom-call(bf16[16,256,256]{2,1,0:T(8,128)(2,1)} %refs_2_.8, bf16[16,256,256]{2,1,0:T(8,128)(2,1)} %refs_2_.8, bf16[16,256,256]{2,1,0:T(8,128)(2,1)} %refs_2_.9, s32[16,256]{1,0:T(8,128)} %refs_5_.1), custom_call_target="tpu_custom_call" | custom-call | flops 65536 | bytes 2097152 | tf_op jit(solution)/shard_map/pack_right/pallas_call | solution.py:546
  14.0 0.0 copy-start.1
  14.0 1.5 %collective-permute-done.1.left_ref = bf16[16,4,256]{2,1,0:T(4,128)(2,1)S(1)} collective-permute-done((bf16[16,4,256]{2,1,0:T(4,128)(2,1)}, bf16[16,4,256]{2,1,0:T(4,128)(2,1)S(1)}, u32[]{:S(2)}, u32[]{:S(2)}) %collective-permute-start.1) | collective-permute-done | bytes 32800 | tf_op jit(solution)/shard_map/ppermute | solution.py:25
  15.6 0.0 collective-permute-done.refs_3_.right_ref
  15.6 1.9 %collective-permute-start.3 = (bf16[8,144,256]{2,1,0:T(8,128)(2,1)}, bf16[8,144,256]{2,1,0:T(8,128)(2,1)S(1)}, u32[]{:S(2)}, u32[]{:S(2)}) collective-permute-start(bf16[8,144,256]{2,1,0:T(8,128)(2,1)} %pack_right.3), channel_id=1, source_target_pairs={{0,1},{1,2},{2,3},{3,4},{4,5},{5,6},{6,7},{8,9},{9,10},{10,11},{11... | collective-permute-start | bytes 1769480 | tf_op jit(solution)/shard_map/ppermute | solution.py:25
  17.5 0.0 copy-done.7
  17.5 1.9 %collective-permute-start.2 = (bf16[8,144,256]{2,1,0:T(8,128)(2,1)S(1)}, bf16[8,144,256]{2,1,0:T(8,128)(2,1)S(1)}, u32[]{:S(2)}, u32[]{:S(2)}) collective-permute-start(bf16[8,144,256]{2,1,0:T(8,128)(2,1)S(1)} %copy-done.7), channel_id=1, source_target_pairs={{0,1},{1,2},{2,3},{3,4},{4,5},{5,6},{6,7},{8,9},{9,10},{10,11},{11... | collective-permute-start | bytes 1769480 | tf_op jit(solution)/shard_map/ppermute | solution.py:25
  19.4 0.0 copy-done.2
  19.4 0.0 copy-done.3
  19.4 0.0 copy-start.8
  19.5 0.0 copy-start.4
  19.5 0.2 rims.1
  19.7 0.0 copy-start
  19.7 2.1 %collective-permute-start.4 = (bf16[4,272,256]{2,1,0:T(8,128)(2,1)S(1)}, bf16[4,272,256]{2,1,0:T(8,128)(2,1)S(1)}, u32[]{:S(2)}, u32[]{:S(2)}) collective-permute-start(bf16[4,272,256]{2,1,0:T(8,128)(2,1)S(1)} %get-tuple-element.43), channel_id=1, source_target_pairs={{0,8},{8,16},{16,24},{24,32},{32,40},{40,48},{48,56},{56,64},{64,7... | collective-permute-start | bytes 1671176 | tf_op jit(solution)/shard_map/ppermute | solution.py:25
  21.8 4.5 %collective-permute-start.5 = (bf16[4,272,256]{2,1,0:T(8,128)(2,1)S(1)}, bf16[4,272,256]{2,1,0:T(8,128)(2,1)S(1)}, u32[]{:S(2)}, u32[]{:S(2)}) collective-permute-start(bf16[4,272,256]{2,1,0:T(8,128)(2,1)S(1)} %get-tuple-element.44), channel_id=1, source_target_pairs={{8,0},{16,8},{24,16},{32,24},{40,32},{48,40},{56,48},{64,56},{72,6... | collective-permute-start | bytes 1671176 | tf_op jit(solution)/shard_map/ppermute | solution.py:25
  26.3 0.0 copy-done.1
  26.3 0.1 slice.3
  26.4 0.0 copy-done.8
  26.4 0.0 copy-done.4
  26.5 0.0 copy-done
  26.5 4.8 %corr_right.1 = (bf16[16,144,128]{2,1,0:T(8,128)(2,1)S(1)}, f32[16,128,128]{2,1,0:T(8,128)S(1)}) custom-call(bf16[16,256,256]{2,1,0:T(8,128)(2,1)S(1)} %copy-done.1, bf16[16,256,256]{2,1,0:T(8,128)(2,1)S(1)} %copy-done, s32[16,256]{1,0:T(8,128)S(1)} %copy-done.4, bf16[16,4,896]{2,1,0:T(4,128)(2,1)S(1)} %collective-permute-done.refs_3_.right_ref, ...), custom_call_target="tpu_custom_call" | custom-call | flops 268435456 | bytes 6291456 | tf_op jit(solution)/shard_map/corr_right/pallas_call | solution.py:593
  31.2 5.1 %collective-permute-done.3.refs_2_.refs_4_ = bf16[8,144,256]{2,1,0:T(8,128)(2,1)S(1)} collective-permute-done((bf16[8,144,256]{2,1,0:T(8,128)(2,1)}, bf16[8,144,256]{2,1,0:T(8,128)(2,1)S(1)}, u32[]{:S(2)}, u32[]{:S(2)}) %collective-permute-start.3) | collective-permute-done | bytes 589856 | tf_op jit(solution)/shard_map/ppermute | solution.py:25
  36.3 2.4 %corr_left.3 = (bf16[8,272,128]{2,1,0:T(8,128)(2,1)S(1)}, f32[8,128,128]{2,1,0:T(8,128)S(1)}, bf16[4,272,128]{2,1,0:T(8,128)(2,1)S(1)}) custom-call(bf16[16,256,256]{2,1,0:T(8,128)(2,1)S(1)} %copy-done.1, bf16[16,256,256]{2,1,0:T(8,128)(2,1)S(1)} %copy-done, bf16[8,144,256]{2,1,0:T(8,128)(2,1)S(1)} %collective-permute-done.3.refs_2_.refs_4_, ...), custom_call_target="tpu_custom_call" | custom-call | flops 134217728 | bytes 3145728 | tf_op jit(solution)/shard_map/corr_left/pallas_call | solution.py:618
  38.8 0.0 copy-start.5
  38.8 0.0 copy-start.6
  38.8 2.1 %collective-permute-start.6 = (bf16[4,272,128]{2,1,0:T(8,128)(2,1)S(1)}, bf16[4,272,128]{2,1,0:T(8,128)(2,1)S(1)}, u32[]{:S(2)}, u32[]{:S(2)}) collective-permute-start(bf16[4,272,128]{2,1,0:T(8,128)(2,1)S(1)} %get-tuple-element.56), channel_id=1, source_target_pairs={{0,8},{8,16},{16,24},{24,32},{32,40},{40,48},{48,56},{56,64},{64,7... | collective-permute-start | bytes 835592 | tf_op jit(solution)/shard_map/ppermute | solution.py:25
  40.8 8.1 %collective-permute-done.2.refs_2_.refs_3_ = bf16[8,144,256]{2,1,0:T(8,128)(2,1)S(1)} collective-permute-done((bf16[8,144,256]{2,1,0:T(8,128)(2,1)S(1)}, bf16[8,144,256]{2,1,0:T(8,128)(2,1)S(1)}, u32[]{:S(2)}, u32[]{:S(2)}) %collective-permute-start.2) | collective-permute-done | bytes 589856 | tf_op jit(solution)/shard_map/ppermute | solution.py:25
  49.0 2.4 %corr_left.2 = (bf16[8,272,128]{2,1,0:T(8,128)(2,1)S(1)}, f32[8,128,128]{2,1,0:T(8,128)S(1)}, bf16[4,272,128]{2,1,0:T(8,128)(2,1)S(1)}) custom-call(bf16[16,256,256]{2,1,0:T(8,128)(2,1)S(1)} %copy-done.1, bf16[16,256,256]{2,1,0:T(8,128)(2,1)S(1)} %copy-done, bf16[8,144,256]{2,1,0:T(8,128)(2,1)S(1)} %collective-permute-done.2.refs_2_.refs_3_, ...), custom_call_target="tpu_custom_call" | custom-call | flops 134217728 | bytes 3145728 | tf_op jit(solution)/shard_map/corr_left/pallas_call | solution.py:618
  51.4 1.9 %collective-permute-start.7 = (bf16[4,272,128]{2,1,0:T(8,128)(2,1)S(1)}, bf16[4,272,128]{2,1,0:T(8,128)(2,1)S(1)}, u32[]{:S(2)}, u32[]{:S(2)}) collective-permute-start(bf16[4,272,128]{2,1,0:T(8,128)(2,1)S(1)} %get-tuple-element.57), channel_id=1, source_target_pairs={{8,0},{16,8},{24,16},{32,24},{40,32},{48,40},{56,48},{64,56},{72,6... | collective-permute-start | bytes 835592 | tf_op jit(solution)/shard_map/ppermute | solution.py:25
  53.3 0.0 collective-permute-done.4.hgt_ref
  53.3 2.7 %collective-permute-done.5.hgb_ref = bf16[4,272,256]{2,1,0:T(8,128)(2,1)S(1)} collective-permute-done((bf16[4,272,256]{2,1,0:T(8,128)(2,1)S(1)}, bf16[4,272,256]{2,1,0:T(8,128)(2,1)S(1)}, u32[]{:S(2)}, u32[]{:S(2)}) %collective-permute-start.5) | collective-permute-done | bytes 557088 | tf_op jit(solution)/shard_map/ppermute | solution.py:25
  56.0 0.0 copy-done.5
  56.0 0.0 copy-done.6
  56.0 5.2 %gates_hidden.1 = (bf16[24,272,128]{2,1,0:T(8,128)(2,1)S(1)}, bf16[24,272,128]{2,1,0:T(8,128)(2,1)S(1)}, f32[22,272,256]{2,1,0:T(8,128)S(1)}, bf16[1152,256]{1,0...) custom-call(bf16[16,256,128]{2,1,0:T(8,128)(2,1)S(1)} %copy-done.2, ...), custom_call_target="tpu_custom_call" | custom-call | flops 3529506816 | bytes 16777216 | tf_op jit(solution)/shard_map/gates_hidden/pallas_call | solution.py:664
  61.2 6.5 %collective-permute-start.9 = (bf16[16,128,256]{2,1,0:T(8,128)(2,1)S(1)}, bf16[16,128,256]{2,1,0:T(8,128)(2,1)S(1)}, u32[]{:S(2)}, u32[]{:S(2)}) collective-permute-start(bf16[16,128,256]{2,1,0:T(8,128)(2,1)S(1)} %slice.3), channel_id=1, source_target_pairs={{1,0},{2,1},{3,2},{4,3},{5,4},{6,5},{7,6},{9,8},{10,9},{11,10},{12... | collective-permute-start | bytes 3145736 | tf_op jit(solution)/shard_map/ppermute | solution.py:25
  67.7 0.0 collective-permute-done.6.mott_ref
  67.7 0.0 collective-permute-done.7.motl_ref
  67.8 23.4 %gru.1 = (bf16[16,256,128]{2,1,0:T(8,128)(2,1)}, bf16[16,256,128]{2,1,0:T(8,128)(2,1)S(1)}, bf16[16,16,128]{2,1,0:T(8,128)(2,1)S(1)}, f32[22,272,256]{2,1,0:T(8,128)S(1)}) custom-call(bf16[8,272,128]{2,1,0:T(8,128)(2,1)S(1)} %get-tuple-element.39.mota_ref, bf16[8,272,128]{2,1,0:T(8,128)(2,1)S(1)} %get-tuple-element.41.motb_ref, ...), custom_call_target="tpu_custom_call", output_to_operand_aliasing={{3}: (4, {})} | custom-call | flops 15686696960 | bytes 16777216 | tf_op jit(solution)/shard_map/gru/pallas_call | solution.py:680
  91.2 3.4 %collective-permute-start.8 = (bf16[16,16,128]{2,1,0:T(8,128)(2,1)S(1)}, bf16[16,16,128]{2,1,0:T(8,128)(2,1)S(1)}, u32[]{:S(2)}, u32[]{:S(2)}) collective-permute-start(bf16[16,16,128]{2,1,0:T(8,128)(2,1)S(1)} %get-tuple-element.62), channel_id=1, source_target_pairs={{1,0},{2,1},{3,2},{4,3},{5,4},{6,5},{7,6},{9,8},{10,9},{11,10},{12... | collective-permute-start | bytes 196616 | tf_op jit(solution)/shard_map/ppermute | solution.py:25
  94.6 6.7 %grads.1 = (bf16[16,256,256]{2,1,0:T(8,128)(2,1)}, bf16[16,256,256]{2,1,0:T(8,128)(2,1)}, bf16[16,128,128]{2,1,0:T(8,128)(2,1)S(1)}) custom-call(bf16[16,256,128]{2,1,0:T(8,128)(2,1)S(1)} %get-tuple-element.59.refs_0_, bf16[16,256,256]{2,1,0:T(8,128)(2,1)S(1)} %copy-done.1, bf16[16,256,256]{2,1,0:T(8,128)(2,1)S(1)} %copy-done, ...), custom_call_target="tpu_custom_call" | custom-call | flops 1073741824 | bytes 12582912 | tf_op jit(solution)/shard_map/grads/pallas_call | solution.py:697
  101.3 0.0 collective-permute-done.8.refs_1_
  101.3 0.0 collective-permute-done.9.refs_3_
  101.3 2.5 %grad_right.1 = bf16[16,256,256]{2,1,0:T(8,128)(2,1)} custom-call(bf16[16,128,128]{2,1,0:T(8,128)(2,1)S(1)} %get-tuple-element.61.refs_0_, bf16[16,16,128]{2,1,0:T(8,128)(2,1)S(1)} %collective-permute-done.8.refs_1_, bf16[16,256,256]{2,1,0:T(8,128)(2,1)S(1)} %copy-done.1, ...), custom_call_target="tpu_custom_call", output_to_operand_aliasing={{}: (4, {})} | custom-call | flops 268435456 | bytes 4194304 | tf_op jit(solution)/shard_map/grad_right/pallas_call | solution.py:720
  (1 shorter events, 0.0 us)
Async XLA Ops:
  2.4 13.2 %collective-permute-start = (bf16[16,4,896]{2,1,0:T(4,128)(2,1)}, bf16[16,4,896]{2,1,0:T(4,128)(2,1)S(1)}, u32[]{:S(2)}, u32[]{:S(2)}) collective-permute-start(bf16[16,4,896]{2,1,0:T(4,128)(2,1)} %get-tuple-element.34), channel_id=1, source_target_pairs={{1,0},{2,1},{3,2},{4,3},{5,4},{6,5},{7,6},{9,8},{10,9},{11,10},{12... | collective-permute-start | bytes 344072 | tf_op jit(solution)/shard_map/ppermute | solution.py:25
  7.1 8.4 %collective-permute-start.1 = (bf16[16,4,256]{2,1,0:T(4,128)(2,1)}, bf16[16,4,256]{2,1,0:T(4,128)(2,1)S(1)}, u32[]{:S(2)}, u32[]{:S(2)}) collective-permute-start(bf16[16,4,256]{2,1,0:T(4,128)(2,1)} %get-tuple-element.35), channel_id=1, source_target_pairs={{0,1},{1,2},{2,3},{3,4},{4,5},{5,6},{6,7},{8,9},{9,10},{10,11},{11... | collective-permute-start | bytes 98312 | tf_op jit(solution)/shard_map/ppermute | solution.py:25
  11.8 5.7 %copy-start.7 = (bf16[8,144,256]{2,1,0:T(8,128)(2,1)S(1)}, bf16[8,144,256]{2,1,0:T(8,128)(2,1)}, u32[]{:S(2)}) copy-start(bf16[8,144,256]{2,1,0:T(8,128)(2,1)} %pack_right.2) | copy-start | bytes 1769476
  11.8 7.6 %copy-start.2 = (bf16[16,256,128]{2,1,0:T(8,128)(2,1)S(1)}, bf16[16,256,128]{2,1,0:T(8,128)(2,1)}, u32[]{:S(2)}) copy-start(bf16[16,256,128]{2,1,0:T(8,128)(2,1)} %hid_ref.3) | copy-start | bytes 3145732
  11.8 7.6 %copy-start.3 = (bf16[16,256,128]{2,1,0:T(8,128)(2,1)S(1)}, bf16[16,256,128]{2,1,0:T(8,128)(2,1)}, u32[]{:S(2)}) copy-start(bf16[16,256,128]{2,1,0:T(8,128)(2,1)} %grad_ref.3) | copy-start | bytes 3145732
  14.0 12.3 %copy-start.1 = (bf16[16,256,256]{2,1,0:T(8,128)(2,1)S(1)}, bf16[16,256,256]{2,1,0:T(8,128)(2,1)}, u32[]{:S(2)}) copy-start(bf16[16,256,256]{2,1,0:T(8,128)(2,1)} %refs_2_.9) | copy-start | bytes 6291460
  15.6 20.8 %collective-permute-start.3 = (bf16[8,144,256]{2,1,0:T(8,128)(2,1)}, bf16[8,144,256]{2,1,0:T(8,128)(2,1)S(1)}, u32[]{:S(2)}, u32[]{:S(2)}) collective-permute-start(bf16[8,144,256]{2,1,0:T(8,128)(2,1)} %pack_right.3), channel_id=1, source_target_pairs={{0,1},{1,2},{2,3},{3,4},{4,5},{5,6},{6,7},{8,9},{9,10},{10,11},{11... | collective-permute-start | bytes 1769480 | tf_op jit(solution)/shard_map/ppermute | solution.py:25
  17.5 31.5 %collective-permute-start.2 = (bf16[8,144,256]{2,1,0:T(8,128)(2,1)S(1)}, bf16[8,144,256]{2,1,0:T(8,128)(2,1)S(1)}, u32[]{:S(2)}, u32[]{:S(2)}) collective-permute-start(bf16[8,144,256]{2,1,0:T(8,128)(2,1)S(1)} %copy-done.7), channel_id=1, source_target_pairs={{0,1},{1,2},{2,3},{3,4},{4,5},{5,6},{6,7},{8,9},{9,10},{10,11},{11... | collective-permute-start | bytes 1769480 | tf_op jit(solution)/shard_map/ppermute | solution.py:25
  19.4 7.0 %copy-start.8 = (bf16[9,128]{1,0:T(8,128)(2,1)S(1)}, bf16[9,128]{1,0:T(8,128)(2,1)}, u32[]{:S(2)}) copy-start(bf16[9,128]{1,0:T(8,128)(2,1)} %param.12) | copy-start | bytes 6916
  19.5 7.0 %copy-start.4 = (s32[16,256]{1,0:T(8,128)S(1)}, s32[16,256]{1,0:T(8,128)}, u32[]{:S(2)}) copy-start(s32[16,256]{1,0:T(8,128)} %refs_5_.1) | copy-start | bytes 49156
  19.7 6.8 %copy-start = (bf16[16,256,256]{2,1,0:T(8,128)(2,1)S(1)}, bf16[16,256,256]{2,1,0:T(8,128)(2,1)}, u32[]{:S(2)}) copy-start(bf16[16,256,256]{2,1,0:T(8,128)(2,1)} %refs_2_.8) | copy-start | bytes 6291460
  19.7 33.6 %collective-permute-start.4 = (bf16[4,272,256]{2,1,0:T(8,128)(2,1)S(1)}, bf16[4,272,256]{2,1,0:T(8,128)(2,1)S(1)}, u32[]{:S(2)}, u32[]{:S(2)}) collective-permute-start(bf16[4,272,256]{2,1,0:T(8,128)(2,1)S(1)} %get-tuple-element.43), channel_id=1, source_target_pairs={{0,8},{8,16},{16,24},{24,32},{32,40},{40,48},{48,56},{56,64},{64,7... | collective-permute-start | bytes 1671176 | tf_op jit(solution)/shard_map/ppermute | solution.py:25
  21.8 34.3 %collective-permute-start.5 = (bf16[4,272,256]{2,1,0:T(8,128)(2,1)S(1)}, bf16[4,272,256]{2,1,0:T(8,128)(2,1)S(1)}, u32[]{:S(2)}, u32[]{:S(2)}) collective-permute-start(bf16[4,272,256]{2,1,0:T(8,128)(2,1)S(1)} %get-tuple-element.44), channel_id=1, source_target_pairs={{8,0},{16,8},{24,16},{32,24},{40,32},{48,40},{56,48},{64,56},{72,6... | collective-permute-start | bytes 1671176 | tf_op jit(solution)/shard_map/ppermute | solution.py:25
  38.8 17.3 %copy-start.5 = (bf16[3,3,256,256]{3,2,1,0:T(8,128)(2,1)S(1)}, bf16[3,3,256,256]{3,2,1,0:T(8,128)(2,1)}, u32[]{:S(2)}) copy-start(bf16[3,3,256,256]{3,2,1,0:T(8,128)(2,1)} %param.13) | copy-start | bytes 3538948
  38.8 17.3 %copy-start.6 = (bf16[3,3,256,128]{3,2,1,0:T(8,128)(2,1)S(1)}, bf16[3,3,256,128]{3,2,1,0:T(8,128)(2,1)}, u32[]{:S(2)}) copy-start(bf16[3,3,256,128]{3,2,1,0:T(8,128)(2,1)} %param.14) | copy-start | bytes 1769476
  38.8 29.0 %collective-permute-start.6 = (bf16[4,272,128]{2,1,0:T(8,128)(2,1)S(1)}, bf16[4,272,128]{2,1,0:T(8,128)(2,1)S(1)}, u32[]{:S(2)}, u32[]{:S(2)}) collective-permute-start(bf16[4,272,128]{2,1,0:T(8,128)(2,1)S(1)} %get-tuple-element.56), channel_id=1, source_target_pairs={{0,8},{8,16},{16,24},{24,32},{32,40},{40,48},{48,56},{56,64},{64,7... | collective-permute-start | bytes 835592 | tf_op jit(solution)/shard_map/ppermute | solution.py:25
  51.4 16.3 %collective-permute-start.7 = (bf16[4,272,128]{2,1,0:T(8,128)(2,1)S(1)}, bf16[4,272,128]{2,1,0:T(8,128)(2,1)S(1)}, u32[]{:S(2)}, u32[]{:S(2)}) collective-permute-start(bf16[4,272,128]{2,1,0:T(8,128)(2,1)S(1)} %get-tuple-element.57), channel_id=1, source_target_pairs={{8,0},{16,8},{24,16},{32,24},{40,32},{48,40},{56,48},{64,56},{72,6... | collective-permute-start | bytes 835592 | tf_op jit(solution)/shard_map/ppermute | solution.py:25
  61.2 40.1 %collective-permute-start.9 = (bf16[16,128,256]{2,1,0:T(8,128)(2,1)S(1)}, bf16[16,128,256]{2,1,0:T(8,128)(2,1)S(1)}, u32[]{:S(2)}, u32[]{:S(2)}) collective-permute-start(bf16[16,128,256]{2,1,0:T(8,128)(2,1)S(1)} %slice.3), channel_id=1, source_target_pairs={{1,0},{2,1},{3,2},{4,3},{5,4},{6,5},{7,6},{9,8},{10,9},{11,10},{12... | collective-permute-start | bytes 3145736 | tf_op jit(solution)/shard_map/ppermute | solution.py:25
  91.2 10.1 %collective-permute-start.8 = (bf16[16,16,128]{2,1,0:T(8,128)(2,1)S(1)}, bf16[16,16,128]{2,1,0:T(8,128)(2,1)S(1)}, u32[]{:S(2)}, u32[]{:S(2)}) collective-permute-start(bf16[16,16,128]{2,1,0:T(8,128)(2,1)S(1)} %get-tuple-element.62), channel_id=1, source_target_pairs={{1,0},{2,1},{3,2},{4,3},{5,4},{6,5},{7,6},{9,8},{10,9},{11,10},{12... | collective-permute-start | bytes 196616 | tf_op jit(solution)/shard_map/ppermute | solution.py:25

commit v5 on v4

--- a/solution.py
+++ b/solution.py
@@ -14,7 +14,7 @@
 BF16 = jnp.bfloat16
 ROWS = 4
 SMALL_VMEM = 16 * 1024 * 1024
-GRU_VMEM = 32 * 1024 * 1024
+GRU_VMEM = 36 * 1024 * 1024
 GATES_VMEM = 12 * 1024 * 1024
 PACK_VMEM = 60 * 1024 * 1024
 
@@ -70,10 +70,22 @@
 
 
 def pack_small_kernel(
-    left_ref, own_ref, hid_ref, grad_ref, hid_last_ref, grad_last_ref, disp_ref, out_ref, last_ref
+    left_ref,
+    own_ref,
+    hid_ref,
+    grad_ref,
+    beside_ref,
+    left_last_ref,
+    hid_last_ref,
+    grad_last_ref,
+    disp_ref,
+    out_ref,
+    last_ref,
 ):
     rows, _, chan = left_ref.shape
     levels = jnp.transpose(disp_ref[:, :B].astype(F32), (1, 0))
+    last_levels = jnp.transpose(disp_ref[:, disp_ref.shape[1] - B :].astype(F32), (1, 0))
+    low = iota((8, chan), 0) < HALO
     for r in range(rows):
         out_ref[r, :, :chan] = left_ref[r, :HALO]
         out_ref[r, :, chan : 2 * chan] = own_ref[r, :HALO]
@@ -81,22 +93,12 @@
         out_ref[r, :, 2 * chan + B : 2 * chan + 2 * B] = grad_ref[r, :HALO]
         level = jnp.broadcast_to(levels[:8, r : r + 1], (8, B))
         out_ref[r, :, 2 * chan + 2 * B :] = level.astype(BF16)[:HALO]
+        beside = pltpu.roll(beside_ref[r].astype(F32), HALO, 0)
+        upper = jnp.where(low, beside, left_last_ref[r].astype(F32))
+        level = jnp.broadcast_to(last_levels[B - 8 :, r : r + 1], (8, chan))
         hg = jnp.concatenate([hid_last_ref[r], grad_last_ref[r]], axis=1).astype(F32)
-        last_ref[r] = pltpu.roll(hg, HALO, 0)[:HALO].astype(BF16)
-
-
-def pack_right_kernel(start, own_ref, beside_ref, left_ref, disp_ref, out_ref):
-    rows, _, chan = own_ref.shape
-    first = start + pl.program_id(0) * rows
-    low = iota((8, chan), 0) < HALO
-    for r in range(rows):
-        out_ref[r, :B] = own_ref[r]
-        beside = pltpu.roll(beside_ref[r].astype(F32), HALO, 0)
-        upper = jnp.where(low, beside, left_ref[r].astype(F32))
-        row = level_row(disp_ref, first + r, disp_ref.shape[1] - B).astype(F32)
-        level = jnp.transpose(jnp.broadcast_to(row, (8, B)), (1, 0))[B - 8 :, :1]
-        level = pltpu.roll(jnp.broadcast_to(level, (8, chan)), HALO, 0)
-        out_ref[r, B:] = jnp.concatenate([upper, jnp.where(low, level, 0.0)], axis=0).astype(BF16)
+        lower = jnp.where(low, pltpu.roll(level, HALO, 0), hg)
+        last_ref[r] = jnp.concatenate([upper, lower], axis=0).astype(BF16)
 
 
 def rim_kernel(
@@ -115,12 +117,10 @@
     own = hid_first_ref.shape[1]
     chan = (right_ref.shape[2] - 3 * B) // 2
     pad_ref[...] = jnp.zeros_like(pad_ref)
+    last = iota(pad_ref.shape, 0) >= EDGE - HALO
     for r in range(rows):
         pad_ref[:HALO] = right_ref[r, :, 2 * chan : 2 * chan + 2 * B].astype(F32)
-        pad_ref[8 : 8 + HALO] = left_ref[r].astype(F32)
-        value = pad_ref[...]
-        low = pltpu.roll(value[8:], HALO, 0)
-        edge_ref[r] = jnp.concatenate([value[:8], low], axis=0).astype(BF16)
+        edge_ref[r] = jnp.where(last, left_ref[r].astype(F32), pad_ref[...]).astype(BF16)
     for r in range(HALO):
         for out, hid, grad, row in (
             (first_ref, hid_first_ref, grad_first_ref, r),
@@ -183,6 +183,7 @@
     left_ref,
     own_ref,
     before_ref,
+    extra_ref,
     disp_ref,
     mot_right_ref,
     weight_ref,
@@ -200,10 +201,10 @@
     last = iota((EDGE, chan), 0) >= EDGE - HALO
     upper = iota((EDGE, B), 0) < EDGE // 2
     for r in range(rows):
-        extra = before_ref[r, B:].astype(F32)
+        extra = extra_ref[r].astype(F32)
         pad_ref[r, B - EDGE :] = jnp.where(last, pltpu.roll(extra, 12, 0), 0.0).astype(BF16)
         side = jnp.where(last, pltpu.roll(extra, 8, 0), 0.0).astype(BF16)
-        window = jnp.concatenate([before_ref[r, :B], own_ref[r]], axis=0)
+        window = jnp.concatenate([before_ref[r], own_ref[r]], axis=0)
         scores = dot_nt(jnp.concatenate([left_ref[r], side], axis=0), window)
         disp = down_lanes(level_row(disp_ref, first + r, 0))
         main = pick_taps(scores[:B, :B], scores[:B, B:], disp, taps, radius, scale)
@@ -255,39 +256,31 @@
 CHUNK = 4
 
 
+def join_columns(buf, row, own_row, edge_row):
+    own = own_row.shape[0]
+    buf[row, :own] = own_row
+    buf[row, own:] = edge_row
+
+
 def gates_hidden_kernel(
     hid_ref,
-    grad_ref,
-    hgt_ref,
-    hgb_ref,
     edge_ref,
     gate_ref,
     cand_ref,
-    h_ref,
-    g_ref,
     gh_ref,
     wgm_ref,
     wc_ref,
     wcb_ref,
     wgb_ref,
+    h_ref,
     h3_ref,
     wgh_ref,
 ):
     rows, own, _ = hid_ref.shape
     wide = own + EDGE
-    total = rows + 2 * HALO
-    for row in range(total):
-        n = row - HALO
-        if 0 <= n < rows:
-            h_ref[row, :own] = hid_ref[n]
-            h_ref[row, own:] = edge_ref[n, :, :B]
-            g_ref[row, :own] = grad_ref[n]
-            g_ref[row, own:] = edge_ref[n, :, B:]
-        else:
-            hg = hgt_ref[row] if n < 0 else hgb_ref[n - rows]
-            h_ref[row] = hg[:, :B]
-            g_ref[row] = hg[:, B:]
-        store3(h3_ref, row, h_ref[row].astype(F32))
+    for row in range(rows):
+        join_columns(h_ref, 0, hid_ref[row], edge_ref[row, :, :B])
+        store3(h3_ref, row, h_ref[0].astype(F32))
     zeros = jnp.zeros((6 * B, B), BF16)
     wc_ref[18 * B :, :B] = zeros
     wc_ref[: 6 * B, B:] = zeros
@@ -303,7 +296,7 @@
         for s in range(2):
             col = (n + 3 * s) * 2 * B
             wgb_ref[s * B : (s + 1) * B, col : col + 2 * B] = gate_ref[at + B : at + 2 * B]
-    for group in chunks(range(1, total - 1), CHUNK):
+    for group in chunks(range(1, rows - 1), CHUNK):
         lhs = patches((h3_ref,), [[r + a - 1 for r in group] for a in range(3)])
         acc = dot(lhs, wgh_ref[...])
         for n, row in enumerate(group):
@@ -311,55 +304,74 @@
 
 
 def gru_kernel(
+    hid_ref,
+    grad_ref,
+    hgt_ref,
+    hgb_ref,
+    edge_ref,
     mota_ref,
     motb_ref,
+    mott_ref,
+    motl_ref,
+    wg_ref,
     wgm_ref,
-    h_ref,
     gates_ref,
-    g_ref,
     wc_ref,
     wcb_ref,
     wgb_ref,
     prela_ref,
     prelb_ref,
     prer_ref,
-    mott_ref,
-    motl_ref,
     disp_ref,
     mw_ref,
     nh_ref,
     pg_ref,
     tg_ref,
-    gh_ref,
     u3_ref,
     m3_ref,
     r3_ref,
     c3_ref,
     cb_ref,
+    h_ref,
+    g_ref,
+    gh_ref,
 ):
     rows, own, _ = nh_ref.shape
     half = rows // 2
     wide = own + EDGE
     total = rows + 2 * HALO
     inner = range(HALO, HALO + rows)
-    gate_groups = chunks(range(1, total - 1), CHUNK)
+    known = range(HALO + 1, HALO + rows - 1)
     for row in range(total):
         n = row - HALO
-        if n < 0:
-            mot = mott_ref[row]
-        elif n >= rows:
-            mot = motl_ref[n - rows]
+        if n < 0 or n >= rows:
+            hg = hgt_ref[row] if n < 0 else hgb_ref[n - rows]
+            mot = mott_ref[row] if n < 0 else motl_ref[n - rows]
+            h_ref[row] = hg[:, :B]
+            g_ref[row] = hg[:, B:]
         else:
             mot = mota_ref[n] if n < half else motb_ref[n - half]
+            join_columns(h_ref, row, hid_ref[n], edge_ref[n, :, :B])
+            join_columns(g_ref, row, grad_ref[n], edge_ref[n, :, B:])
         store3(m3_ref, row, mot.astype(F32))
-
-    for group in gate_groups:
+        if row <= known[0] or row >= known[-1]:
+            store3(u3_ref, row, h_ref[row].astype(F32))
+
+    def gate(row, value):
+        value = jax.nn.sigmoid(value)
+        gh_ref[row - 1] = value
+        store3(r3_ref, row, value[:, B:] * h_ref[row].astype(F32))
+
+    for group in (list(range(1, known[0])), list(range(known[-1] + 1, total - 1))):
+        lhs = patches((u3_ref, m3_ref), [[r + a - 1 for r in group] for a in range(3)])
+        acc = dot(lhs, wg_ref[...])
+        for n, row in enumerate(group):
+            gate(row, acc[n * wide : (n + 1) * wide])
+    for group in chunks(known, CHUNK):
         lhs = patches((m3_ref,), [[r + a - 1 for r in group] for a in range(3)])
         acc = dot(lhs, wgm_ref[...])
         for n, row in enumerate(group):
-            gate = jax.nn.sigmoid(acc[n * wide : (n + 1) * wide] + gates_ref[row - 1])
-            gh_ref[row - 1] = gate
-            store3(r3_ref, row, gate[:, B:] * h_ref[row].astype(F32))
+            gate(row, acc[n * wide : (n + 1) * wide] + gates_ref[row - known[0]])
 
     for group in chunks(range(2, total - 2, 2), CHUNK):
         lhs = patches((r3_ref, m3_ref), [[r + t - 1 for r in group] for t in range(4)])
@@ -459,7 +471,7 @@
             row = level_row(disp_ref, step * rows + r, block * B)
             parts.append(spread(grads[at], down_lanes(row), taps, radius))
             parts_t.append(spread_t(grads_t[:, at], row, taps, radius))
-        before = jnp.where(head, before_a_ref[r, :B], before_b_ref[r, :B])
+        before = jnp.where(head, before_a_ref[r], before_b_ref[r])
         window = jnp.concatenate([before, own_ref[r, :B]], axis=0)
         gl_ref[r, :B] = (dot(jnp.concatenate(parts[0], axis=1), window) * scale).astype(BF16)
         gl_ref[r, B:] = (dot(jnp.concatenate(parts[1], axis=1), own_ref[r]) * scale).astype(BF16)
@@ -518,7 +530,7 @@
     last8 = cols // 8 - 1
     pack_params = pltpu.CompilerParams(vmem_limit_bytes=PACK_VMEM)
 
-    small_shapes = (shape((rows, HALO, packed), BF16), shape((rows, HALO, 2 * B), BF16))
+    small_shapes = (shape((rows, HALO, packed), BF16), shape((rows, EDGE, chan), BF16))
     to_left, to_right = pl.pallas_call(
         pack_small_kernel,
         grid=(1,),
@@ -527,6 +539,8 @@
             block((rows, 8, chan), 0, 0, 0),
             block((rows, 8, B), 0, 0, 0),
             block((rows, 8, B), 0, 0, 0),
+            block((rows, 8, chan), 0, (cols - B) // 8 - 1, 0),
+            block((rows, 8, chan), 0, last8, 0),
             block((rows, 8, B), 0, last8, 0),
             block((rows, 8, B), 0, last8, 0),
             whole(disparity),
@@ -536,33 +550,24 @@
         compiler_params=pack_params,
         cost_estimate=cost(1 << 16, 1 << 18),
         name="pack_small",
-    )(feat_left, feat_right, hidden, grad_hidden, hidden, grad_hidden, disparity)
+    )(
+        feat_left,
+        feat_right,
+        hidden,
+        grad_hidden,
+        feat_right,
+        feat_left,
+        hidden,
+        grad_hidden,
+        disparity,
+    )
     from_right = shift(to_left, "cols", -1)
     from_left = shift(to_right, "cols", 1)
-
-    def features_for_right(start):
-        at = start // size
-        out = shape((half, B + EDGE, chan), BF16)
-        return pl.pallas_call(
-            lambda *refs: pack_right_kernel(start, *refs),
-            grid=(half // size,),
-            in_specs=[
-                block((size, B, chan), at, cols // B - 1, 0),
-                block((size, 8, chan), at, (cols - B) // 8 - 1, 0),
-                block((size, 8, chan), at, last8, 0),
-                whole(disparity),
-            ],
-            out_specs=by_rows(out, size),
-            out_shape=out,
-            compiler_params=pack_params,
-            cost_estimate=cost(1 << 16, 2 << 20),
-            name="pack_right",
-        )(feat_right, feat_right, feat_left, disparity)
-
-    packs, from_right, from_left = lax.optimization_barrier(
-        ([features_for_right(0), features_for_right(half)], from_right, from_left)
+    features = feat_right[:, cols - B :]
+    second, from_right, from_left = lax.optimization_barrier(
+        (features[half:], from_right, from_left)
     )
-    before = [shift(pack, "cols", 1) for pack in packs]
+    before = [shift(features[:half], "cols", 1), shift(second, "cols", 1)]
 
     rim = shape((HALO, wide, 2 * B), BF16)
     edge_shape = shape((rows, EDGE, 2 * B), BF16)
@@ -622,6 +627,7 @@
                 block((size, B, chan), at, 0, 0),
                 block((size, B, chan), at, 0, 0),
                 by_rows(before, size),
+                block((size, EDGE, chan), at, 0, 0),
                 whole(disparity),
                 block((size, B + EDGE, B), at, 0, 0),
                 whole(mw16),
@@ -632,7 +638,7 @@
             compiler_params=params,
             cost_estimate=cost(rows * B * 2 * B * chan, 3 << 20),
             name="corr_left",
-        )(feat_left, feat_right, before, disparity, mot_right, mw16)
+        )(feat_left, feat_right, before, from_left, disparity, mot_right, mw16)
 
     mot_a, pre_a, rim_a = left_lookup(0, before[0], 0)
     mot_low = shift(rim_a, "rows", -1)
@@ -643,52 +649,66 @@
 
     total = rows + 2 * HALO
     own_shape = shape((rows, cols, B), BF16)
-    halo_shape = shape((total, wide, B), BF16)
-    gate_shape = shape((total - 2, wide, 2 * B), F32)
+    gate_shape = shape((rows - 2, wide, 2 * B), F32)
     weight_shapes = [
         shape((9 * B, 2 * B), BF16),
         shape((24 * B, 2 * B), BF16),
         shape((2 * B, 9 * B), BF16),
         shape((2 * B, 24 * B), BF16),
     ]
-    hid_operands = (
-        hidden,
-        grad_hidden,
-        hg_top,
-        hg_low,
-        edge,
-        gate_weight.reshape(-1, 2 * B),
-        cand_weight.reshape(-1, B),
-    )
-    hid_shapes = (halo_shape, halo_shape, gate_shape, *weight_shapes)
-    hid, grad, gates, wgm, wc, wcb, wgb = pl.pallas_call(
+    wg = gate_weight.reshape(-1, 2 * B)
+    hid_operands = (hidden, edge, wg, cand_weight.reshape(-1, B))
+    hid_shapes = (gate_shape, *weight_shapes)
+    gates, wgm, wc, wcb, wgb = pl.pallas_call(
         gates_hidden_kernel,
         in_specs=[vmem] * len(hid_operands),
         out_specs=[vmem] * len(hid_shapes),
         out_shape=hid_shapes,
         scratch_shapes=[
-            pltpu.VMEM((total, wide, 3 * B), BF16),
+            pltpu.VMEM((1, wide, B), BF16),
+            pltpu.VMEM((rows, wide, 3 * B), BF16),
             pltpu.VMEM((9 * B, 2 * B), BF16),
         ],
         compiler_params=pltpu.CompilerParams(vmem_limit_bytes=GATES_VMEM),
         cost_estimate=cost(2 * 22 * wide * 9 * B * 2 * B, 16 << 20),
         name="gates_hidden",
     )(*hid_operands)
-    big = (mot_a, mot_b, wgm, hid, gates, grad, wc, wcb, wgb, pre_a, pre_b, pre_right)
-    small = (mot_top, mot_low, disparity, mw16)
+    operands = (
+        hidden,
+        grad_hidden,
+        hg_top,
+        hg_low,
+        edge,
+        mot_a,
+        mot_b,
+        mot_top,
+        mot_low,
+        wg,
+        wgm,
+        gates,
+        wc,
+        wcb,
+        wgb,
+        pre_a,
+        pre_b,
+        pre_right,
+        disparity,
+        mw16,
+    )
     anywhere = pl.BlockSpec(memory_space=pl.ANY)
-    new_hidden, pre_grad, tap_grad, _ = pl.pallas_call(
+    halo_buffer = pltpu.VMEM((total, wide, B), BF16)
+    new_hidden, pre_grad, tap_grad = pl.pallas_call(
         gru_kernel,
-        in_specs=[vmem] * (len(big) + len(small)),
-        out_specs=[vmem] * 4,
-        out_shape=(own_shape, own_shape, shape((rows, 16, B), BF16), gate_shape),
-        input_output_aliases={4: 3},
+        in_specs=[vmem] * len(operands),
+        out_specs=[vmem] * 3,
+        out_shape=(own_shape, own_shape, shape((rows, 16, B), BF16)),
         scratch_shapes=[pltpu.VMEM((total, wide, 3 * B), BF16)] * 4
-        + [pltpu.VMEM((rows, cols, B), F32)],
+        + [pltpu.VMEM((rows, cols, B), F32), halo_buffer, halo_buffer]
+        + [pltpu.VMEM((total - 2, wide, 2 * B), F32)],
         compiler_params=pltpu.CompilerParams(vmem_limit_bytes=GRU_VMEM),
         cost_estimate=cost(2 * 22 * wide * 256 * 256 * 20, 16 << 20),
         name="gru",
-    )(*big, *small)
+    )(*operands)
     next_grad = shift(tap_grad, "cols", -1)
 
     feat_shape = shape((rows, cols, chan), BF16)
@@ -701,8 +721,8 @@
             by_rows(pre_grad, size),
             by_rows(feat_left, size),
             by_rows(feat_right, size),
-            pl.BlockSpec((size, B + EDGE, chan), lambda i: (jnp.minimum(i, mid - 1), 0, 0)),
-            pl.BlockSpec((size, B + EDGE, chan), lambda i: (jnp.maximum(i - mid, 0), 0, 0)),
+            pl.BlockSpec((size, B, chan), lambda i: (jnp.minimum(i, mid - 1), 0, 0)),
+            pl.BlockSpec((size, B, chan), lambda i: (jnp.maximum(i - mid, 0), 0, 0)),
             whole(disparity),
             whole(mw16),
         ],

time: 106 us -> 97.1 us (0.916)
  the two profiles are of different devices: /device:TPU:120 before, /device:TPU:49 now
where the time goes in v5:
time: 97.1 us; the launch traced here: 96.7 us
  Pallas kernels  48.4 us (50%)
  starting transfers between devices  43.3 us (45%)
  waiting for transfers between devices  3.84 us (4%)
    ppermute x10, starting transfers between devices, shift(): return lax.ppermute(array, axis, pairs)  43.3 us
    pallas_call x1, Pallas kernels, per_device(): pl.pallas_call(gru_kernel, in_specs=[vmem] * len(operands), out_specs=[vm...  24 us
    pallas_call x1, Pallas kernels, per_device(): pl.pallas_call(lambda *refs: grads_kernel(*args, *refs), grid=(steps,), i...  6.71 us
    pallas_call x2, Pallas kernels, left_lookup(): pl.pallas_call(lambda *refs: left_corr_kernel(*args, start, rim_step, *re...  4.86 us
    pallas_call x1, Pallas kernels, per_device(): pl.pallas_call(lambda *refs: right_corr_kernel(*args, *refs), grid=(steps...  4.76 us
    ppermute x10, waiting for transfers between devices, shift(): return lax.ppermute(array, axis, pairs)  3.84 us
    pallas_call x1, Pallas kernels, per_device(): pl.pallas_call(gates_hidden_kernel, in_specs=[vmem] * len(hid_operands),...  3.37 us
    pallas_call x1, Pallas kernels, per_device(): pl.pallas_call(lambda *refs: last_kernel(*args, *refs), grid=(steps,), in...  2.5 us
  transfers between devices with their start and end apart: 10, of which 3 were waited for; matrix products, arithmetic and copies ran while one was open for 0% of the time, Pallas kernels for 45%

profile of v5, /device:TPU:49, one launch (start us, length us, event | category | flops | bytes accessed | tf_op | source)
XLA Modules:
  0.0 96.7 jit_solution(2545288560700668045)
XLA Ops:
  0.6 0.0 copy-start.1
  0.6 2.0 %pack_small.1 = (bf16[16,4,896]{2,1,0:T(4,128)(2,1)}, bf16[16,16,256]{2,1,0:T(8,128)(2,1)}) custom-call(bf16[16,256,256]{2,1,0:T(8,128)(2,1)} %refs_2_.5, bf16[16,256,256]{2,1,0:T(8,128)(2,1)} %refs_2_.4, bf16[16,256,128]{2,1,0:T(8,128)(2,1)} %hid_ref.5, bf16[16,256,128]{2,1,0:T(8,128)(2,1)} %grad_ref.3, bf16[16,256,256]{2,1,0:T(8,128)(2,1)} %refs_2_.4, ...), custom_call_target="tpu_custom_call" | custom-call | flops 65536 | bytes 262144 | tf_op jit(solution)/shard_map/pack_small/pallas_call | solution.py:534
  2.7 0.0 copy-start.2
  2.7 0.0 copy-start.3
  2.7 4.8 %collective-permute-start.1 = (bf16[16,16,256]{2,1,0:T(8,128)(2,1)}, bf16[16,16,256]{2,1,0:T(8,128)(2,1)S(1)}, u32[]{:S(2)}, u32[]{:S(2)}) collective-permute-start(bf16[16,16,256]{2,1,0:T(8,128)(2,1)} %get-tuple-element.32), channel_id=1, source_target_pairs={{0,1},{1,2},{2,3},{3,4},{4,5},{5,6},{6,7},{8,9},{9,10},{10,11},{11... | collective-permute-start | bytes 393224 | tf_op jit(solution)/shard_map/ppermute | solution.py:25
  7.5 3.0 %collective-permute-start = (bf16[16,4,896]{2,1,0:T(4,128)(2,1)}, bf16[16,4,896]{2,1,0:T(4,128)(2,1)S(1)}, u32[]{:S(2)}, u32[]{:S(2)}) collective-permute-start(bf16[16,4,896]{2,1,0:T(4,128)(2,1)} %get-tuple-element.31), channel_id=1, source_target_pairs={{1,0},{2,1},{3,2},{4,3},{5,4},{6,5},{7,6},{9,8},{10,9},{11,10},{12... | collective-permute-start | bytes 344072 | tf_op jit(solution)/shard_map/ppermute | solution.py:25
  10.5 0.0 copy-done.1
  10.5 0.1 fusion
  10.6 3.8 %collective-permute-start.4 = (bf16[8,128,256]{2,1,0:T(8,128)(2,1)S(1)}, bf16[8,128,256]{2,1,0:T(8,128)(2,1)S(1)}, u32[]{:S(2)}, u32[]{:S(2)}) collective-permute-start(bf16[8,128,256]{2,1,0:T(8,128)(2,1)S(1)} %get-tuple-element.59), channel_id=1, source_target_pairs={{0,1},{1,2},{2,3},{3,4},{4,5},{5,6},{6,7},{8,9},{9,10},{10,11},{11... | collective-permute-start | bytes 1572872 | tf_op jit(solution)/shard_map/ppermute | solution.py:25
  14.3 0.4 collective-permute-done.right_ref.refs_3_
  14.7 0.0 collective-permute-done.1.left_ref.refs_3_
  14.7 0.0 copy-start
  14.7 4.5 %collective-permute-start.5 = (bf16[8,128,256]{2,1,0:T(8,128)(2,1)S(1)}, bf16[8,128,256]{2,1,0:T(8,128)(2,1)S(1)}, u32[]{:S(2)}, u32[]{:S(2)}) collective-permute-start(bf16[8,128,256]{2,1,0:T(8,128)(2,1)S(1)} %get-tuple-element.40), channel_id=1, source_target_pairs={{0,1},{1,2},{2,3},{3,4},{4,5},{5,6},{6,7},{8,9},{9,10},{10,11},{11... | collective-permute-start | bytes 1572872 | tf_op jit(solution)/shard_map/ppermute | solution.py:25
  19.2 0.0 copy-done.2
  19.2 0.0 copy-done.3
  19.3 0.2 rims.1
  19.5 0.0 copy-start.7
  19.5 0.0 copy-start.4
  19.5 5.4 %collective-permute-start.2 = (bf16[4,272,256]{2,1,0:T(8,128)(2,1)S(1)}, bf16[4,272,256]{2,1,0:T(8,128)(2,1)S(1)}, u32[]{:S(2)}, u32[]{:S(2)}) collective-permute-start(bf16[4,272,256]{2,1,0:T(8,128)(2,1)S(1)} %get-tuple-element.35), channel_id=1, source_target_pairs={{0,8},{8,16},{16,24},{24,32},{32,40},{40,48},{48,56},{56,64},{64,7... | collective-permute-start | bytes 1671176 | tf_op jit(solution)/shard_map/ppermute | solution.py:25
  24.9 1.9 %collective-permute-start.3 = (bf16[4,272,256]{2,1,0:T(8,128)(2,1)S(1)}, bf16[4,272,256]{2,1,0:T(8,128)(2,1)S(1)}, u32[]{:S(2)}, u32[]{:S(2)}) collective-permute-start(bf16[4,272,256]{2,1,0:T(8,128)(2,1)S(1)} %get-tuple-element.36), channel_id=1, source_target_pairs={{8,0},{16,8},{24,16},{32,24},{40,32},{48,40},{56,48},{64,56},{72,6... | collective-permute-start | bytes 1671176 | tf_op jit(solution)/shard_map/ppermute | solution.py:25
  26.8 0.0 copy-done
  26.8 0.1 slice.14
  26.9 0.0 copy-done.7
  26.9 0.0 copy-done.4
  26.9 4.8 %corr_right.1 = (bf16[16,144,128]{2,1,0:T(8,128)(2,1)S(1)}, f32[16,128,128]{2,1,0:T(8,128)S(1)}) custom-call(bf16[16,256,256]{2,1,0:T(8,128)(2,1)S(1)} %copy-done, bf16[16,256,256]{2,1,0:T(8,128)(2,1)S(1)} %copy-done.1, s32[16,256]{1,0:T(8,128)S(1)} %copy-done.4, bf16[16,4,896]{2,1,0:T(4,128)(2,1)S(1)} %collective-permute-done.right_ref.refs_3_, ...), custom_call_target="tpu_custom_call" | custom-call | flops 268435456 | bytes 6291456 | tf_op jit(solution)/shard_map/corr_right/pallas_call | solution.py:598
  31.7 0.0 collective-permute-done.4.refs_2_.refs_3_
  31.7 2.4 %corr_left.2 = (bf16[8,272,128]{2,1,0:T(8,128)(2,1)S(1)}, f32[8,128,128]{2,1,0:T(8,128)S(1)}, bf16[4,272,128]{2,1,0:T(8,128)(2,1)S(1)}) custom-call(bf16[16,256,256]{2,1,0:T(8,128)(2,1)S(1)} %copy-done, bf16[16,256,256]{2,1,0:T(8,128)(2,1)S(1)} %copy-done.1, bf16[8,128,256]{2,1,0:T(8,128)(2,1)S(1)} %collective-permute-done.4.refs_2_.refs_3_, ...), custom_call_target="tpu_custom_call" | custom-call | flops 134217728 | bytes 3145728 | tf_op jit(solution)/shard_map/corr_left/pallas_call | solution.py:623
  34.2 0.0 copy-start.5
  34.2 0.0 copy-start.6
  34.2 3.6 %collective-permute-start.7 = (bf16[4,272,128]{2,1,0:T(8,128)(2,1)S(1)}, bf16[4,272,128]{2,1,0:T(8,128)(2,1)S(1)}, u32[]{:S(2)}, u32[]{:S(2)}) collective-permute-start(bf16[4,272,128]{2,1,0:T(8,128)(2,1)S(1)} %get-tuple-element.43), channel_id=1, source_target_pairs={{8,0},{16,8},{24,16},{32,24},{40,32},{48,40},{56,48},{64,56},{72,6... | collective-permute-start | bytes 835592 | tf_op jit(solution)/shard_map/ppermute | solution.py:25
  37.8 0.5 collective-permute-done.5.refs_2_.refs_4_
  38.3 2.4 %corr_left.3 = (bf16[8,272,128]{2,1,0:T(8,128)(2,1)S(1)}, f32[8,128,128]{2,1,0:T(8,128)S(1)}, bf16[4,272,128]{2,1,0:T(8,128)(2,1)S(1)}) custom-call(bf16[16,256,256]{2,1,0:T(8,128)(2,1)S(1)} %copy-done, bf16[16,256,256]{2,1,0:T(8,128)(2,1)S(1)} %copy-done.1, bf16[8,128,256]{2,1,0:T(8,128)(2,1)S(1)} %collective-permute-done.5.refs_2_.refs_4_, ...), custom_call_target="tpu_custom_call" | custom-call | flops 134217728 | bytes 3145728 | tf_op jit(solution)/shard_map/corr_left/pallas_call | solution.py:623
  40.7 6.9 %collective-permute-start.6 = (bf16[4,272,128]{2,1,0:T(8,128)(2,1)S(1)}, bf16[4,272,128]{2,1,0:T(8,128)(2,1)S(1)}, u32[]{:S(2)}, u32[]{:S(2)}) collective-permute-start(bf16[4,272,128]{2,1,0:T(8,128)(2,1)S(1)} %get-tuple-element.42), channel_id=1, source_target_pairs={{0,8},{8,16},{16,24},{24,32},{32,40},{40,48},{48,56},{56,64},{64,7... | collective-permute-start | bytes 835592 | tf_op jit(solution)/shard_map/ppermute | solution.py:25
  47.7 0.0 copy-done.5
  47.7 0.0 copy-done.6
  47.7 3.4 %gates_hidden.1 = (f32[14,272,256]{2,1,0:T(8,128)S(1)}, bf16[1152,256]{1,0:T(8,128)(2,1)S(1)}, bf16[3072,256]{1,0:T(8,128)(2,1)S(1)}, bf16[256,1152]{1,0:T(8,128)(2,1)S(1)}, bf16[256,3072]{1,0:T(8,128)(2,1)S(1)}) custom-call(bf16[16,256,128]{2,1,0:T(8,128)(2,1)S(1)} %copy-done.2, bf16[16,16,256]{2,1,0:T(8,128)(2,1)S(1)} %get-tuple-element.37.edge_ref, ...), custom_call_target="tpu_custom_call" | custom-call | flops 3529506816 | bytes 16777216 | tf_op jit(solution)/shard_map/gates_hidden/pallas_call | solution.py:662
  51.1 2.3 %collective-permute-start.9 = (bf16[16,128,256]{2,1,0:T(8,128)(2,1)S(1)}, bf16[16,128,256]{2,1,0:T(8,128)(2,1)S(1)}, u32[]{:S(2)}, u32[]{:S(2)}) collective-permute-start(bf16[16,128,256]{2,1,0:T(8,128)(2,1)S(1)} %slice.14), channel_id=1, source_target_pairs={{1,0},{2,1},{3,2},{4,3},{5,4},{6,5},{7,6},{9,8},{10,9},{11,10},{12... | collective-permute-start | bytes 3145736 | tf_op jit(solution)/shard_map/ppermute | solution.py:25
  53.4 0.0 collective-permute-done.2.hgt_ref
  53.4 0.0 collective-permute-done.3.hgb_ref
  53.4 2.9 %collective-permute-done.7.motl_ref = bf16[4,272,128]{2,1,0:T(8,128)(2,1)S(1)} collective-permute-done((bf16[4,272,128]{2,1,0:T(8,128)(2,1)S(1)}, bf16[4,272,128]{2,1,0:T(8,128)(2,1)S(1)}, u32[]{:S(2)}, u32[]{:S(2)}) %collective-permute-start.7) | collective-permute-done | bytes 278560 | tf_op jit(solution)/shard_map/ppermute | solution.py:25
  56.3 0.0 collective-permute-done.6.mott_ref
  56.3 24.0 %gru.1 = (bf16[16,256,128]{2,1,0:T(8,128)(2,1)}, bf16[16,256,128]{2,1,0:T(8,128)(2,1)S(1)}, bf16[16,16,128]{2,1,0:T(8,128)(2,1)S(1)}) custom-call(bf16[16,256,128]{2,1,0:T(8,128)(2,1)S(1)} %copy-done.2, bf16[16,256,128]{2,1,0:T(8,128)(2,1)S(1)} %copy-done.3, bf16[4,272,256]{2,1,0:T(8,128)(2,1)S(1)} %collective-permute-done.2.hgt_ref, ...), custom_call_target="tpu_custom_call" | custom-call | flops 15686696960 | bytes 16777216 | tf_op jit(solution)/shard_map/gru/pallas_call | solution.py:700
  80.3 7.1 %collective-permute-start.8 = (bf16[16,16,128]{2,1,0:T(8,128)(2,1)S(1)}, bf16[16,16,128]{2,1,0:T(8,128)(2,1)S(1)}, u32[]{:S(2)}, u32[]{:S(2)}) collective-permute-start(bf16[16,16,128]{2,1,0:T(8,128)(2,1)S(1)} %get-tuple-element.56), channel_id=1, source_target_pairs={{1,0},{2,1},{3,2},{4,3},{5,4},{6,5},{7,6},{9,8},{10,9},{11,10},{12... | collective-permute-start | bytes 196616 | tf_op jit(solution)/shard_map/ppermute | solution.py:25
  87.5 6.7 %grads.1 = (bf16[16,256,256]{2,1,0:T(8,128)(2,1)}, bf16[16,256,256]{2,1,0:T(8,128)(2,1)}, bf16[16,128,128]{2,1,0:T(8,128)(2,1)S(1)}) custom-call(bf16[16,256,128]{2,1,0:T(8,128)(2,1)S(1)} %get-tuple-element.53.refs_0_, bf16[16,256,256]{2,1,0:T(8,128)(2,1)S(1)} %copy-done, bf16[16,256,256]{2,1,0:T(8,128)(2,1)S(1)} %copy-done.1, ...), custom_call_target="tpu_custom_call" | custom-call | flops 1073741824 | bytes 12582912 | tf_op jit(solution)/shard_map/grads/pallas_call | solution.py:717
  94.2 0.0 collective-permute-done.8.refs_1_
  94.2 0.0 collective-permute-done.9.refs_3_
  94.2 2.5 %grad_right.1 = bf16[16,256,256]{2,1,0:T(8,128)(2,1)} custom-call(bf16[16,128,128]{2,1,0:T(8,128)(2,1)S(1)} %get-tuple-element.55.refs_0_, bf16[16,16,128]{2,1,0:T(8,128)(2,1)S(1)} %collective-permute-done.8.refs_1_, bf16[16,256,256]{2,1,0:T(8,128)(2,1)S(1)} %copy-done, ...), custom_call_target="tpu_custom_call", output_to_operand_aliasing={{}: (4, {})} | custom-call | flops 268435456 | bytes 4194304 | tf_op jit(solution)/shard_map/grad_right/pallas_call | solution.py:740
  (1 shorter events, 0.0 us)
Async XLA Ops:
  0.6 9.9 %copy-start.1 = (bf16[16,256,256]{2,1,0:T(8,128)(2,1)S(1)}, bf16[16,256,256]{2,1,0:T(8,128)(2,1)}, u32[]{:S(2)}) copy-start(bf16[16,256,256]{2,1,0:T(8,128)(2,1)} %refs_2_.4) | copy-start | bytes 6291460
  2.7 16.6 %copy-start.2 = (bf16[16,256,128]{2,1,0:T(8,128)(2,1)S(1)}, bf16[16,256,128]{2,1,0:T(8,128)(2,1)}, u32[]{:S(2)}) copy-start(bf16[16,256,128]{2,1,0:T(8,128)(2,1)} %hid_ref.5) | copy-start | bytes 3145732
  2.7 16.6 %copy-start.3 = (bf16[16,256,128]{2,1,0:T(8,128)(2,1)S(1)}, bf16[16,256,128]{2,1,0:T(8,128)(2,1)}, u32[]{:S(2)}) copy-start(bf16[16,256,128]{2,1,0:T(8,128)(2,1)} %grad_ref.3) | copy-start | bytes 3145732
  2.7 12.0 %collective-permute-start.1 = (bf16[16,16,256]{2,1,0:T(8,128)(2,1)}, bf16[16,16,256]{2,1,0:T(8,128)(2,1)S(1)}, u32[]{:S(2)}, u32[]{:S(2)}) collective-permute-start(bf16[16,16,256]{2,1,0:T(8,128)(2,1)} %get-tuple-element.32), channel_id=1, source_target_pairs={{0,1},{1,2},{2,3},{3,4},{4,5},{5,6},{6,7},{8,9},{9,10},{10,11},{11... | collective-permute-start | bytes 393224 | tf_op jit(solution)/shard_map/ppermute | solution.py:25
  7.5 7.3 %collective-permute-start = (bf16[16,4,896]{2,1,0:T(4,128)(2,1)}, bf16[16,4,896]{2,1,0:T(4,128)(2,1)S(1)}, u32[]{:S(2)}, u32[]{:S(2)}) collective-permute-start(bf16[16,4,896]{2,1,0:T(4,128)(2,1)} %get-tuple-element.31), channel_id=1, source_target_pairs={{1,0},{2,1},{3,2},{4,3},{5,4},{6,5},{7,6},{9,8},{10,9},{11,10},{12... | collective-permute-start | bytes 344072 | tf_op jit(solution)/shard_map/ppermute | solution.py:25
  10.6 21.1 %collective-permute-start.4 = (bf16[8,128,256]{2,1,0:T(8,128)(2,1)S(1)}, bf16[8,128,256]{2,1,0:T(8,128)(2,1)S(1)}, u32[]{:S(2)}, u32[]{:S(2)}) collective-permute-start(bf16[8,128,256]{2,1,0:T(8,128)(2,1)S(1)} %get-tuple-element.59), channel_id=1, source_target_pairs={{0,1},{1,2},{2,3},{3,4},{4,5},{5,6},{6,7},{8,9},{9,10},{10,11},{11... | collective-permute-start | bytes 1572872 | tf_op jit(solution)/shard_map/ppermute | solution.py:25
  14.7 12.1 %copy-start = (bf16[16,256,256]{2,1,0:T(8,128)(2,1)S(1)}, bf16[16,256,256]{2,1,0:T(8,128)(2,1)}, u32[]{:S(2)}) copy-start(bf16[16,256,256]{2,1,0:T(8,128)(2,1)} %refs_2_.5) | copy-start | bytes 6291460
  14.7 23.6 %collective-permute-start.5 = (bf16[8,128,256]{2,1,0:T(8,128)(2,1)S(1)}, bf16[8,128,256]{2,1,0:T(8,128)(2,1)S(1)}, u32[]{:S(2)}, u32[]{:S(2)}) collective-permute-start(bf16[8,128,256]{2,1,0:T(8,128)(2,1)S(1)} %get-tuple-element.40), channel_id=1, source_target_pairs={{0,1},{1,2},{2,3},{3,4},{4,5},{5,6},{6,7},{8,9},{9,10},{10,11},{11... | collective-permute-start | bytes 1572872 | tf_op jit(solution)/shard_map/ppermute | solution.py:25
  19.5 7.4 %copy-start.7 = (bf16[9,128]{1,0:T(8,128)(2,1)S(1)}, bf16[9,128]{1,0:T(8,128)(2,1)}, u32[]{:S(2)}) copy-start(bf16[9,128]{1,0:T(8,128)(2,1)} %param.12) | copy-start | bytes 6916
  19.5 7.5 %copy-start.4 = (s32[16,256]{1,0:T(8,128)S(1)}, s32[16,256]{1,0:T(8,128)}, u32[]{:S(2)}) copy-start(s32[16,256]{1,0:T(8,128)} %refs_5_.1) | copy-start | bytes 49156
  19.5 33.9 %collective-permute-start.2 = (bf16[4,272,256]{2,1,0:T(8,128)(2,1)S(1)}, bf16[4,272,256]{2,1,0:T(8,128)(2,1)S(1)}, u32[]{:S(2)}, u32[]{:S(2)}) collective-permute-start(bf16[4,272,256]{2,1,0:T(8,128)(2,1)S(1)} %get-tuple-element.35), channel_id=1, source_target_pairs={{0,8},{8,16},{16,24},{24,32},{32,40},{40,48},{48,56},{56,64},{64,7... | collective-permute-start | bytes 1671176 | tf_op jit(solution)/shard_map/ppermute | solution.py:25
  24.9 28.5 %collective-permute-start.3 = (bf16[4,272,256]{2,1,0:T(8,128)(2,1)S(1)}, bf16[4,272,256]{2,1,0:T(8,128)(2,1)S(1)}, u32[]{:S(2)}, u32[]{:S(2)}) collective-permute-start(bf16[4,272,256]{2,1,0:T(8,128)(2,1)S(1)} %get-tuple-element.36), channel_id=1, source_target_pairs={{8,0},{16,8},{24,16},{32,24},{40,32},{48,40},{56,48},{64,56},{72,6... | collective-permute-start | bytes 1671176 | tf_op jit(solution)/shard_map/ppermute | solution.py:25
  34.2 13.5 %copy-start.5 = (bf16[3,3,256,256]{3,2,1,0:T(8,128)(2,1)S(1)}, bf16[3,3,256,256]{3,2,1,0:T(8,128)(2,1)}, u32[]{:S(2)}) copy-start(bf16[3,3,256,256]{3,2,1,0:T(8,128)(2,1)} %param.13) | copy-start | bytes 3538948
  34.2 13.5 %copy-start.6 = (bf16[3,3,256,128]{3,2,1,0:T(8,128)(2,1)S(1)}, bf16[3,3,256,128]{3,2,1,0:T(8,128)(2,1)}, u32[]{:S(2)}) copy-start(bf16[3,3,256,128]{3,2,1,0:T(8,128)(2,1)} %param.14) | copy-start | bytes 1769476
  34.2 22.1 %collective-permute-start.7 = (bf16[4,272,128]{2,1,0:T(8,128)(2,1)S(1)}, bf16[4,272,128]{2,1,0:T(8,128)(2,1)S(1)}, u32[]{:S(2)}, u32[]{:S(2)}) collective-permute-start(bf16[4,272,128]{2,1,0:T(8,128)(2,1)S(1)} %get-tuple-element.43), channel_id=1, source_target_pairs={{8,0},{16,8},{24,16},{32,24},{40,32},{48,40},{56,48},{64,56},{72,6... | collective-permute-start | bytes 835592 | tf_op jit(solution)/shard_map/ppermute | solution.py:25
  40.7 15.6 %collective-permute-start.6 = (bf16[4,272,128]{2,1,0:T(8,128)(2,1)S(1)}, bf16[4,272,128]{2,1,0:T(8,128)(2,1)S(1)}, u32[]{:S(2)}, u32[]{:S(2)}) collective-permute-start(bf16[4,272,128]{2,1,0:T(8,128)(2,1)S(1)} %get-tuple-element.42), channel_id=1, source_target_pairs={{0,8},{8,16},{16,24},{24,32},{32,40},{40,48},{48,56},{56,64},{64,7... | collective-permute-start | bytes 835592 | tf_op jit(solution)/shard_map/ppermute | solution.py:25
  51.1 43.1 %collective-permute-start.9 = (bf16[16,128,256]{2,1,0:T(8,128)(2,1)S(1)}, bf16[16,128,256]{2,1,0:T(8,128)(2,1)S(1)}, u32[]{:S(2)}, u32[]{:S(2)}) collective-permute-start(bf16[16,128,256]{2,1,0:T(8,128)(2,1)S(1)} %slice.14), channel_id=1, source_target_pairs={{1,0},{2,1},{3,2},{4,3},{5,4},{6,5},{7,6},{9,8},{10,9},{11,10},{12... | collective-permute-start | bytes 3145736 | tf_op jit(solution)/shard_map/ppermute | solution.py:25
  80.3 13.8 %collective-permute-start.8 = (bf16[16,16,128]{2,1,0:T(8,128)(2,1)S(1)}, bf16[16,16,128]{2,1,0:T(8,128)(2,1)S(1)}, u32[]{:S(2)}, u32[]{:S(2)}) collective-permute-start(bf16[16,16,128]{2,1,0:T(8,128)(2,1)S(1)} %get-tuple-element.56), channel_id=1, source_target_pairs={{1,0},{2,1},{3,2},{4,3},{5,4},{6,5},{7,6},{9,8},{10,9},{11,10},{12... | collective-permute-start | bytes 196616 | tf_op jit(solution)/shard_map/ppermute | solution.py:25

commit v6 on v5

--- a/solution.py
+++ b/solution.py
@@ -78,11 +78,15 @@
     left_last_ref,
     hid_last_ref,
     grad_last_ref,
+    features_ref,
     disp_ref,
     out_ref,
     last_ref,
 ):
     rows, _, chan = left_ref.shape
+    half = features_ref.shape[0]
+    for r in range(half):
+        last_ref[r * B : (r + 1) * B] = features_ref[r]
     levels = jnp.transpose(disp_ref[:, :B].astype(F32), (1, 0))
     last_levels = jnp.transpose(disp_ref[:, disp_ref.shape[1] - B :].astype(F32), (1, 0))
     low = iota((8, chan), 0) < HALO
@@ -98,7 +102,14 @@
         level = jnp.broadcast_to(last_levels[B - 8 :, r : r + 1], (8, chan))
         hg = jnp.concatenate([hid_last_ref[r], grad_last_ref[r]], axis=1).astype(F32)
         lower = jnp.where(low, pltpu.roll(level, HALO, 0), hg)
-        last_ref[r] = jnp.concatenate([upper, lower], axis=0).astype(BF16)
+        at = half * B + r * EDGE
+        last_ref[at : at + EDGE] = jnp.concatenate([upper, lower], axis=0).astype(BF16)
+
+
+def join_columns(buf, row, own_row, edge_row):
+    own = own_row.shape[0]
+    buf[row, :own] = own_row
+    buf[row, own:] = edge_row
 
 
 def rim_kernel(
@@ -115,20 +126,20 @@
 ):
     rows = right_ref.shape[0]
     own = hid_first_ref.shape[1]
-    chan = (right_ref.shape[2] - 3 * B) // 2
+    chan = left_ref.shape[1]
     pad_ref[...] = jnp.zeros_like(pad_ref)
     last = iota(pad_ref.shape, 0) >= EDGE - HALO
     for r in range(rows):
         pad_ref[:HALO] = right_ref[r, :, 2 * chan : 2 * chan + 2 * B].astype(F32)
-        edge_ref[r] = jnp.where(last, left_ref[r].astype(F32), pad_ref[...]).astype(BF16)
+        left = left_ref[r * EDGE : (r + 1) * EDGE].astype(F32)
+        edge_ref[r] = jnp.where(last, left, pad_ref[...]).astype(BF16)
     for r in range(HALO):
-        for out, hid, grad, row in (
-            (first_ref, hid_first_ref, grad_first_ref, r),
-            (last_ref, hid_last_ref, grad_last_ref, rows - HALO + r),
-        ):
-            out[r, :own, :B] = hid[r]
-            out[r, :own, B:] = grad[r]
-            out[r, own:] = edge_ref[row]
+        join_columns(first_ref, r, hid_first_ref[r], edge_ref[r, :, :B])
+        join_columns(last_ref, r, hid_last_ref[r], edge_ref[rows - HALO + r, :, :B])
+    for r in range(HALO // 2):
+        join_columns(first_ref, HALO + r, grad_first_ref[r], edge_ref[r, :, B:])
+        row = HALO - HALO // 2 + r
+        join_columns(last_ref, HALO + r, grad_last_ref[row], edge_ref[rows - HALO + row, :, B:])
 
 
 def taps_matrix(weight_ref, pad_ref):
@@ -201,10 +212,10 @@
     last = iota((EDGE, chan), 0) >= EDGE - HALO
     upper = iota((EDGE, B), 0) < EDGE // 2
     for r in range(rows):
-        extra = extra_ref[r].astype(F32)
+        extra = extra_ref[r * EDGE : (r + 1) * EDGE].astype(F32)
         pad_ref[r, B - EDGE :] = jnp.where(last, pltpu.roll(extra, 12, 0), 0.0).astype(BF16)
         side = jnp.where(last, pltpu.roll(extra, 8, 0), 0.0).astype(BF16)
-        window = jnp.concatenate([before_ref[r], own_ref[r]], axis=0)
+        window = jnp.concatenate([before_ref[r * B : (r + 1) * B], own_ref[r]], axis=0)
         scores = dot_nt(jnp.concatenate([left_ref[r], side], axis=0), window)
         disp = down_lanes(level_row(disp_ref, first + r, 0))
         main = pick_taps(scores[:B, :B], scores[:B, B:], disp, taps, radius, scale)
@@ -254,12 +265,6 @@
 
 
 CHUNK = 4
-
-
-def join_columns(buf, row, own_row, edge_row):
-    own = own_row.shape[0]
-    buf[row, :own] = own_row
-    buf[row, own:] = edge_row
 
 
 def gates_hidden_kernel(
@@ -347,8 +352,7 @@
         if n < 0 or n >= rows:
             hg = hgt_ref[row] if n < 0 else hgb_ref[n - rows]
             mot = mott_ref[row] if n < 0 else motl_ref[n - rows]
-            h_ref[row] = hg[:, :B]
-            g_ref[row] = hg[:, B:]
+            h_ref[row] = hg
         else:
             mot = mota_ref[n] if n < half else motb_ref[n - half]
             join_columns(h_ref, row, hid_ref[n], edge_ref[n, :, :B])
@@ -356,6 +360,10 @@
         store3(m3_ref, row, mot.astype(F32))
         if row <= known[0] or row >= known[-1]:
             store3(u3_ref, row, h_ref[row].astype(F32))
+
+    for n in range(HALO // 2):
+        g_ref[HALO - HALO // 2 + n] = hgt_ref[HALO + n]
+        g_ref[HALO + rows + n] = hgb_ref[HALO + n]
 
     def gate(row, value):
         value = jax.nn.sigmoid(value)
@@ -471,7 +479,8 @@
             row = level_row(disp_ref, step * rows + r, block * B)
             parts.append(spread(grads[at], down_lanes(row), taps, radius))
             parts_t.append(spread_t(grads_t[:, at], row, taps, radius))
-        before = jnp.where(head, before_a_ref[r], before_b_ref[r])
+        at = slice(r * B, (r + 1) * B)
+        before = jnp.where(head, before_a_ref[at], before_b_ref[at])
         window = jnp.concatenate([before, own_ref[r, :B]], axis=0)
         gl_ref[r, :B] = (dot(jnp.concatenate(parts[0], axis=1), window) * scale).astype(BF16)
         gl_ref[r, B:] = (dot(jnp.concatenate(parts[1], axis=1), own_ref[r]) * scale).astype(BF16)
@@ -530,7 +539,7 @@
     last8 = cols // 8 - 1
     pack_params = pltpu.CompilerParams(vmem_limit_bytes=PACK_VMEM)
 
-    small_shapes = (shape((rows, HALO, packed), BF16), shape((rows, EDGE, chan), BF16))
+    small_shapes = (shape((rows, HALO, packed), BF16), shape((half * B + rows * EDGE, chan), BF16))
     to_left, to_right = pl.pallas_call(
         pack_small_kernel,
         grid=(1,),
@@ -543,6 +552,7 @@
             block((rows, 8, chan), 0, last8, 0),
             block((rows, 8, B), 0, last8, 0),
             block((rows, 8, B), 0, last8, 0),
+            block((half, B, chan), 0, cols // B - 1, 0),
             whole(disparity),
         ],
         out_specs=[whole(s) for s in small_shapes],
@@ -559,39 +569,12 @@
         feat_left,
         hidden,
         grad_hidden,
+        feat_right,
         disparity,
     )
     from_right = shift(to_left, "cols", -1)
     from_left = shift(to_right, "cols", 1)
-    features = feat_right[:, cols - B :]
-    second, from_right, from_left = lax.optimization_barrier(
-        (features[half:], from_right, from_left)
-    )
-    before = [shift(features[:half], "cols", 1), shift(second, "cols", 1)]
-
-    rim = shape((HALO, wide, 2 * B), BF16)
-    edge_shape = shape((rows, EDGE, 2 * B), BF16)
-    first_rim, last_rim, edge = pl.pallas_call(
-        rim_kernel,
-        grid=(1,),
-        in_specs=[
-            block((HALO, cols, B), 0, 0, 0),
-            block((HALO, cols, B), 0, 0, 0),
-            block((HALO, cols, B), rows // HALO - 1, 0, 0),
-            block((HALO, cols, B), rows // HALO - 1, 0, 0),
-            whole(from_right),
-            whole(from_left),
-        ],
-        out_specs=[whole(rim), whole(rim), whole(edge_shape)],
-        out_shape=(rim, rim, edge_shape),
-        scratch_shapes=[pltpu.VMEM((EDGE, 2 * B), F32)],
-        compiler_params=params,
-        cost_estimate=cost(1 << 16, 2 << 20),
-        name="rims",
-    )(hidden, grad_hidden, hidden, grad_hidden, from_right, from_left)
-    hg_top = shift(last_rim, "rows", 1)
-    hg_low = shift(first_rim, "rows", -1)
-
+    second, from_right = lax.optimization_barrier((feat_right[half:, cols - B :], from_right))
     mw16 = jnp.pad(motion_weight, ((0, 16 - taps), (0, 0)))
     pads = [pltpu.VMEM((size, B, chan), BF16), pltpu.VMEM((B, B), BF16)]
     right_shapes = (shape((rows, B + EDGE, B), BF16), shape((rows, B, B), F32))
@@ -612,6 +595,31 @@
         cost_estimate=cost(2 * rows * B * 2 * B * chan, 6 << 20),
         name="corr_right",
     )(feat_left, feat_right, disparity, from_right, mw16)
+    from_left, mot_right = lax.optimization_barrier((from_left, mot_right))
+    before = [from_left, shift(second, "cols", 1).reshape(half * B, chan)]
+
+    rim = shape((HALO + HALO // 2, wide, B), BF16)
+    edge_shape = shape((rows, EDGE, 2 * B), BF16)
+    first_rim, last_rim, edge = pl.pallas_call(
+        rim_kernel,
+        grid=(1,),
+        in_specs=[
+            block((HALO, cols, B), 0, 0, 0),
+            block((HALO, cols, B), 0, 0, 0),
+            block((HALO, cols, B), rows // HALO - 1, 0, 0),
+            block((HALO, cols, B), rows // HALO - 1, 0, 0),
+            whole(from_right),
+            block((rows * EDGE, chan), half * B // (rows * EDGE), 0),
+        ],
+        out_specs=[whole(rim), whole(rim), whole(edge_shape)],
+        out_shape=(rim, rim, edge_shape),
+        scratch_shapes=[pltpu.VMEM((EDGE, 2 * B), F32)],
+        compiler_params=params,
+        cost_estimate=cost(1 << 16, 2 << 20),
+        name="rims",
+    )(hidden, grad_hidden, hidden, grad_hidden, from_right, from_left)
+    hg_top = shift(last_rim, "rows", 1)
+    hg_low = shift(first_rim, "rows", -1)
 
     def left_lookup(start, before, rim_step):
         at = start // size
@@ -626,8 +634,8 @@
             in_specs=[
                 block((size, B, chan), at, 0, 0),
                 block((size, B, chan), at, 0, 0),
-                by_rows(before, size),
-                block((size, EDGE, chan), at, 0, 0),
+                block((size * B, chan), 0, 0),
+                block((size * EDGE, chan), half * B // (size * EDGE) + at, 0),
                 whole(disparity),
                 block((size, B + EDGE, B), at, 0, 0),
                 whole(mw16),
@@ -642,6 +650,7 @@
 
     mot_a, pre_a, rim_a = left_lookup(0, before[0], 0)
     mot_low = shift(rim_a, "rows", -1)
+    before[1], mot_a = lax.optimization_barrier((before[1], mot_a))
     mot_b, pre_b, rim_b = left_lookup(half, before[1], half // size - 1)
     mot_top = shift(rim_b, "rows", 1)
     first_left, _ = lax.optimization_barrier((feat_left[:, :B], mot_b))
@@ -721,8 +730,8 @@
             by_rows(pre_grad, size),
             by_rows(feat_left, size),
             by_rows(feat_right, size),
-            pl.BlockSpec((size, B, chan), lambda i: (jnp.minimum(i, mid - 1), 0, 0)),
-            pl.BlockSpec((size, B, chan), lambda i: (jnp.maximum(i - mid, 0), 0, 0)),
+            pl.BlockSpec((size * B, chan), lambda i: (jnp.minimum(i, mid - 1), 0)),
+            pl.BlockSpec((size * B, chan), lambda i: (jnp.maximum(i - mid, 0), 0)),
             whole(disparity),
             whole(mw16),
         ],

time: 97.1 us -> 101 us (1.040)
  the two profiles are of different devices: /device:TPU:49 before, /device:TPU:120 now
where the time goes in v6:
time: 101 us; the launch traced here: 99.9 us
  Pallas kernels  48.3 us (48%)
  starting transfers between devices  35.2 us (35%)
  waiting for transfers between devices  12.6 us (12%)
  local copies, waits for them, and re-layouts  2.8 us (3%)
    ppermute x9, starting transfers between devices, shift(): return lax.ppermute(array, axis, pairs)  35.2 us
    pallas_call x1, Pallas kernels, per_device(): pl.pallas_call(gru_kernel, in_specs=[vmem] * len(operands), out_specs=[vm...  23.6 us
    ppermute x9, waiting for transfers between devices, shift(): return lax.ppermute(array, axis, pairs)  12.6 us
    pallas_call x1, Pallas kernels, per_device(): pl.pallas_call(lambda *refs: grads_kernel(*args, *refs), grid=(steps,), i...  6.69 us
    pallas_call x2, Pallas kernels, left_lookup(): pl.pallas_call(lambda *refs: left_corr_kernel(*args, start, rim_step, *re...  4.86 us
    pallas_call x1, Pallas kernels, per_device(): pl.pallas_call(lambda *refs: right_corr_kernel(*args, *refs), grid=(steps...  4.75 us
    pallas_call x1, Pallas kernels, per_device(): pl.pallas_call(gates_hidden_kernel, in_specs=[vmem] * len(hid_operands),...  3.37 us
    pallas_call x1, Pallas kernels, per_device(): pl.pallas_call(lambda *refs: last_kernel(*args, *refs), grid=(steps,), in...  2.5 us
  transfers between devices with their start and end apart: 9, of which 2 were waited for; matrix products, arithmetic and copies ran while one was open for 1% of the time, Pallas kernels for 43%

profile of v6, /device:TPU:120, one launch (start us, length us, event | category | flops | bytes accessed | tf_op | source)
XLA Modules:
  0.0 99.9 jit_solution(13670864111617402734)
XLA Ops:
  0.6 0.0 copy-start.5
  0.6 0.0 copy-start.8
  0.7 0.0 copy-start
  0.7 2.5 %pack_small.1 = (bf16[16,4,896]{2,1,0:T(4,128)(2,1)}, bf16[1280,256]{1,0:T(8,128)(2,1)}) custom-call(bf16[16,256,256]{2,1,0:T(8,128)(2,1)} %refs_2_.5, bf16[16,256,256]{2,1,0:T(8,128)(2,1)} %refs_2_.4, bf16[16,256,128]{2,1,0:T(8,128)(2,1)} %hid_ref.5, bf16[16,256,128]{2,1,0:T(8,128)(2,1)} %grad_ref.3, bf16[16,256,256]{2,1,0:T(8,128)(2,1)} %refs_2_.4, ...), custom_call_target="tpu_custom_call" | custom-call | flops 65536 | bytes 262144 | tf_op jit(solution)/shard_map/pack_small/pallas_call | solution.py:543
  3.1 4.9 %collective-permute-start.1 = (bf16[1280,256]{1,0:T(8,128)(2,1)}, bf16[1280,256]{1,0:T(8,128)(2,1)S(1)}, u32[]{:S(2)}, u32[]{:S(2)}) collective-permute-start(bf16[1280,256]{1,0:T(8,128)(2,1)} %get-tuple-element.36), channel_id=1, source_target_pairs={{0,1},{1,2},{2,3},{3,4},{4,5},{5,6},{6,7},{8,9},{9,10},{10,11},{11... | collective-permute-start | bytes 1966088 | tf_op jit(solution)/shard_map/ppermute | solution.py:25
  8.1 3.3 %collective-permute-start = (bf16[16,4,896]{2,1,0:T(4,128)(2,1)}, bf16[16,4,896]{2,1,0:T(4,128)(2,1)S(1)}, u32[]{:S(2)}, u32[]{:S(2)}) collective-permute-start(bf16[16,4,896]{2,1,0:T(4,128)(2,1)} %get-tuple-element.34), channel_id=1, source_target_pairs={{1,0},{2,1},{3,2},{4,3},{5,4},{6,5},{7,6},{9,8},{10,9},{11,10},{12... | collective-permute-start | bytes 344072 | tf_op jit(solution)/shard_map/ppermute | solution.py:25
  11.4 1.1 %slice.6 = bf16[8,128,256]{2,1,0:T(8,128)(2,1)S(1)} slice(bf16[16,256,256]{2,1,0:T(8,128)(2,1)} %refs_2_.4), slice={[8:16], [128:256], [0:256]} | slice | bytes 1048576 | tf_op jit(solution)/shard_map/slice | solution.py:577
  12.5 12.3 %collective-permute-done.refs_3_.right_ref = bf16[16,4,896]{2,1,0:T(4,128)(2,1)S(1)} collective-permute-done((bf16[16,4,896]{2,1,0:T(4,128)(2,1)}, bf16[16,4,896]{2,1,0:T(4,128)(2,1)S(1)}, u32[]{:S(2)}, u32[]{:S(2)}) %collective-permute-start) | collective-permute-done | bytes 114720 | tf_op jit(solution)/shard_map/ppermute | solution.py:25
  24.8 1.9 %collective-permute-start.4 = (bf16[8,128,256]{2,1,0:T(8,128)(2,1)S(1)}, bf16[8,128,256]{2,1,0:T(8,128)(2,1)S(1)}, u32[]{:S(2)}, u32[]{:S(2)}) collective-permute-start(bf16[8,128,256]{2,1,0:T(8,128)(2,1)S(1)} %slice.6), channel_id=1, source_target_pairs={{0,1},{1,2},{2,3},{3,4},{4,5},{5,6},{6,7},{8,9},{9,10},{10,11},{11... | collective-permute-start | bytes 1572872 | tf_op jit(solution)/shard_map/ppermute | solution.py:25
  26.7 0.0 copy-done.8
  26.7 0.0 copy-done.5
  26.8 0.0 copy-done
  26.8 0.0 copy-start.1
  26.8 1.6 %copy-done.1 = bf16[16,256,256]{2,1,0:T(8,128)(2,1)S(1)} copy-done((bf16[16,256,256]{2,1,0:T(8,128)(2,1)S(1)}, bf16[16,256,256]{2,1,0:T(8,128)(2,1)}, u32[]{:S(2)}) %copy-start.1) | copy-done | bytes 2097176
  28.4 0.0 copy-start.3
  28.4 0.0 copy-start.4
  28.4 4.7 %corr_right.1 = (bf16[16,144,128]{2,1,0:T(8,128)(2,1)S(1)}, f32[16,128,128]{2,1,0:T(8,128)S(1)}) custom-call(bf16[16,256,256]{2,1,0:T(8,128)(2,1)S(1)} %copy-done, bf16[16,256,256]{2,1,0:T(8,128)(2,1)S(1)} %copy-done.1, s32[16,256]{1,0:T(8,128)S(1)} %copy-done.5, bf16[16,4,896]{2,1,0:T(4,128)(2,1)S(1)} %collective-permute-done.refs_3_.right_ref, ...), custom_call_target="tpu_custom_call" | custom-call | flops 268435456 | bytes 6291456 | tf_op jit(solution)/shard_map/corr_right/pallas_call | solution.py:581
  33.1 0.0 collective-permute-done.1.left_ref.refs_2_.refs_3_
  33.1 0.0 copy-done.3
  33.1 0.0 copy-done.4
  33.1 0.1 rims.1
  33.3 0.0 copy-start.2
  33.3 2.1 %collective-permute-start.2 = (bf16[6,272,128]{2,1,0:T(8,128)(2,1)S(1)}, bf16[6,272,128]{2,1,0:T(8,128)(2,1)S(1)}, u32[]{:S(2)}, u32[]{:S(2)}) collective-permute-start(bf16[6,272,128]{2,1,0:T(8,128)(2,1)S(1)} %get-tuple-element.39), channel_id=1, source_target_pairs={{0,8},{8,16},{16,24},{24,32},{32,40},{40,48},{48,56},{56,64},{64,7... | collective-permute-start | bytes 1253384 | tf_op jit(solution)/shard_map/ppermute | solution.py:25
  35.3 4.5 %collective-permute-start.3 = (bf16[6,272,128]{2,1,0:T(8,128)(2,1)S(1)}, bf16[6,272,128]{2,1,0:T(8,128)(2,1)S(1)}, u32[]{:S(2)}, u32[]{:S(2)}) collective-permute-start(bf16[6,272,128]{2,1,0:T(8,128)(2,1)S(1)} %get-tuple-element.40), channel_id=1, source_target_pairs={{8,0},{16,8},{24,16},{32,24},{40,32},{48,40},{56,48},{64,56},{72,6... | collective-permute-start | bytes 1253384 | tf_op jit(solution)/shard_map/ppermute | solution.py:25
  39.9 0.1 slice.7
  40.0 0.0 copy-done.2
  40.0 2.4 %corr_left.2 = (bf16[8,272,128]{2,1,0:T(8,128)(2,1)S(1)}, f32[8,128,128]{2,1,0:T(8,128)S(1)}, bf16[4,272,128]{2,1,0:T(8,128)(2,1)S(1)}) custom-call(bf16[16,256,256]{2,1,0:T(8,128)(2,1)S(1)} %copy-done, bf16[16,256,256]{2,1,0:T(8,128)(2,1)S(1)} %copy-done.2, bf16[1280,256]{1,0:T(8,128)(2,1)S(1)} %collective-permute-done.1.left_ref.refs_2_.refs_3_, ...), custom_call_target="tpu_custom_call" | custom-call | flops 134217728 | bytes 3145728 | tf_op jit(solution)/shard_map/corr_left/pallas_call | solution.py:631
  42.4 0.3 collective-permute-done.4
  42.7 0.0 copy-start.6
  42.7 0.0 copy-start.7
  42.7 2.4 %corr_left.3 = (bf16[8,272,128]{2,1,0:T(8,128)(2,1)S(1)}, f32[8,128,128]{2,1,0:T(8,128)S(1)}, bf16[4,272,128]{2,1,0:T(8,128)(2,1)S(1)}) custom-call(bf16[16,256,256]{2,1,0:T(8,128)(2,1)S(1)} %copy-done, bf16[16,256,256]{2,1,0:T(8,128)(2,1)S(1)} %copy-done.2, bf16[1024,256]{1,0:T(8,128)(2,1)S(1)} %bitcast.3, ...), custom_call_target="tpu_custom_call" | custom-call | flops 134217728 | bytes 3145728 | tf_op jit(solution)/shard_map/corr_left/pallas_call | solution.py:631
  45.2 1.9 %collective-permute-start.5 = (bf16[4,272,128]{2,1,0:T(8,128)(2,1)S(1)}, bf16[4,272,128]{2,1,0:T(8,128)(2,1)S(1)}, u32[]{:S(2)}, u32[]{:S(2)}) collective-permute-start(bf16[4,272,128]{2,1,0:T(8,128)(2,1)S(1)} %get-tuple-element.48), channel_id=1, source_target_pairs={{0,8},{8,16},{16,24},{24,32},{32,40},{40,48},{48,56},{56,64},{64,7... | collective-permute-start | bytes 835592 | tf_op jit(solution)/shard_map/ppermute | solution.py:25
  47.1 4.5 %collective-permute-start.6 = (bf16[4,272,128]{2,1,0:T(8,128)(2,1)S(1)}, bf16[4,272,128]{2,1,0:T(8,128)(2,1)S(1)}, u32[]{:S(2)}, u32[]{:S(2)}) collective-permute-start(bf16[4,272,128]{2,1,0:T(8,128)(2,1)S(1)} %get-tuple-element.49), channel_id=1, source_target_pairs={{8,0},{16,8},{24,16},{32,24},{40,32},{48,40},{56,48},{64,56},{72,6... | collective-permute-start | bytes 835592 | tf_op jit(solution)/shard_map/ppermute | solution.py:25
  51.6 6.6 %collective-permute-start.8 = (bf16[16,128,256]{2,1,0:T(8,128)(2,1)S(1)}, bf16[16,128,256]{2,1,0:T(8,128)(2,1)S(1)}, u32[]{:S(2)}, u32[]{:S(2)}) collective-permute-start(bf16[16,128,256]{2,1,0:T(8,128)(2,1)S(1)} %slice.7), channel_id=1, source_target_pairs={{1,0},{2,1},{3,2},{4,3},{5,4},{6,5},{7,6},{9,8},{10,9},{11,10},{12... | collective-permute-start | bytes 3145736 | tf_op jit(solution)/shard_map/ppermute | solution.py:25
  58.3 0.0 copy-done.6
  58.3 0.0 copy-done.7
  58.3 3.4 %gates_hidden.1 = (f32[14,272,256]{2,1,0:T(8,128)S(1)}, bf16[1152,256]{1,0:T(8,128)(2,1)S(1)}, bf16[3072,256]{1,0:T(8,128)(2,1)S(1)}, bf16[256,1152]{1,0:T(8,128)(2,1)S(1)}, bf16[256,3072]{1,0:T(8,128)(2,1)S(1)}) custom-call(bf16[16,256,128]{2,1,0:T(8,128)(2,1)S(1)} %copy-done.3, bf16[16,16,256]{2,1,0:T(8,128)(2,1)S(1)} %get-tuple-element.41.edge_ref, ...), custom_call_target="tpu_custom_call" | custom-call | flops 3529506816 | bytes 16777216 | tf_op jit(solution)/shard_map/gates_hidden/pallas_call | solution.py:671
  61.7 0.0 collective-permute-done.5.mott_ref
  61.7 0.0 collective-permute-done.6.motl_ref
  61.7 0.0 collective-permute-done.2.hgt_ref
  61.7 0.0 collective-permute-done.3.hgb_ref
  61.7 23.6 %gru.1 = (bf16[16,256,128]{2,1,0:T(8,128)(2,1)}, bf16[16,256,128]{2,1,0:T(8,128)(2,1)S(1)}, bf16[16,16,128]{2,1,0:T(8,128)(2,1)S(1)}) custom-call(bf16[16,256,128]{2,1,0:T(8,128)(2,1)S(1)} %copy-done.3, bf16[16,256,128]{2,1,0:T(8,128)(2,1)S(1)} %copy-done.4, bf16[6,272,128]{2,1,0:T(8,128)(2,1)S(1)} %collective-permute-done.2.hgt_ref, ...), custom_call_target="tpu_custom_call" | custom-call | flops 15686696960 | bytes 16777216 | tf_op jit(solution)/shard_map/gru/pallas_call | solution.py:709
  85.3 5.4 %collective-permute-start.7 = (bf16[16,16,128]{2,1,0:T(8,128)(2,1)S(1)}, bf16[16,16,128]{2,1,0:T(8,128)(2,1)S(1)}, u32[]{:S(2)}, u32[]{:S(2)}) collective-permute-start(bf16[16,16,128]{2,1,0:T(8,128)(2,1)S(1)} %get-tuple-element.62), channel_id=1, source_target_pairs={{1,0},{2,1},{3,2},{4,3},{5,4},{6,5},{7,6},{9,8},{10,9},{11,10},{12... | collective-permute-start | bytes 196616 | tf_op jit(solution)/shard_map/ppermute | solution.py:25
  90.7 6.7 %grads.1 = (bf16[16,256,256]{2,1,0:T(8,128)(2,1)}, bf16[16,256,256]{2,1,0:T(8,128)(2,1)}, bf16[16,128,128]{2,1,0:T(8,128)(2,1)S(1)}) custom-call(bf16[16,256,128]{2,1,0:T(8,128)(2,1)S(1)} %get-tuple-element.59.refs_0_, bf16[16,256,256]{2,1,0:T(8,128)(2,1)S(1)} %copy-done, bf16[16,256,256]{2,1,0:T(8,128)(2,1)S(1)} %copy-done.2, ...), custom_call_target="tpu_custom_call" | custom-call | flops 1073741824 | bytes 12582912 | tf_op jit(solution)/shard_map/grads/pallas_call | solution.py:726
  97.4 0.0 collective-permute-done.7.refs_1_
  97.4 0.0 collective-permute-done.8.refs_3_
  97.4 2.5 %grad_right.1 = bf16[16,256,256]{2,1,0:T(8,128)(2,1)} custom-call(bf16[16,128,128]{2,1,0:T(8,128)(2,1)S(1)} %get-tuple-element.61.refs_0_, bf16[16,16,128]{2,1,0:T(8,128)(2,1)S(1)} %collective-permute-done.7.refs_1_, bf16[16,256,256]{2,1,0:T(8,128)(2,1)S(1)} %copy-done, ...), custom_call_target="tpu_custom_call", output_to_operand_aliasing={{}: (4, {})} | custom-call | flops 268435456 | bytes 4194304 | tf_op jit(solution)/shard_map/grad_right/pallas_call | solution.py:749
  (1 shorter events, 0.0 us)
Async XLA Ops:
  0.6 26.1 %copy-start.5 = (s32[16,256]{1,0:T(8,128)S(1)}, s32[16,256]{1,0:T(8,128)}, u32[]{:S(2)}) copy-start(s32[16,256]{1,0:T(8,128)} %refs_5_.1) | copy-start | bytes 49156
  0.6 26.1 %copy-start.8 = (bf16[9,128]{1,0:T(8,128)(2,1)S(1)}, bf16[9,128]{1,0:T(8,128)(2,1)}, u32[]{:S(2)}) copy-start(bf16[9,128]{1,0:T(8,128)(2,1)} %param.12) | copy-start | bytes 6916
  0.7 26.1 %copy-start = (bf16[16,256,256]{2,1,0:T(8,128)(2,1)S(1)}, bf16[16,256,256]{2,1,0:T(8,128)(2,1)}, u32[]{:S(2)}) copy-start(bf16[16,256,256]{2,1,0:T(8,128)(2,1)} %refs_2_.5) | copy-start | bytes 6291460
  3.1 30.0 %collective-permute-start.1 = (bf16[1280,256]{1,0:T(8,128)(2,1)}, bf16[1280,256]{1,0:T(8,128)(2,1)S(1)}, u32[]{:S(2)}, u32[]{:S(2)}) collective-permute-start(bf16[1280,256]{1,0:T(8,128)(2,1)} %get-tuple-element.36), channel_id=1, source_target_pairs={{0,1},{1,2},{2,3},{3,4},{4,5},{5,6},{6,7},{8,9},{9,10},{10,11},{11... | collective-permute-start | bytes 1966088 | tf_op jit(solution)/shard_map/ppermute | solution.py:25
  8.1 16.7 %collective-permute-start = (bf16[16,4,896]{2,1,0:T(4,128)(2,1)}, bf16[16,4,896]{2,1,0:T(4,128)(2,1)S(1)}, u32[]{:S(2)}, u32[]{:S(2)}) collective-permute-start(bf16[16,4,896]{2,1,0:T(4,128)(2,1)} %get-tuple-element.34), channel_id=1, source_target_pairs={{1,0},{2,1},{3,2},{4,3},{5,4},{6,5},{7,6},{9,8},{10,9},{11,10},{12... | collective-permute-start | bytes 344072 | tf_op jit(solution)/shard_map/ppermute | solution.py:25
  24.8 17.9 %collective-permute-start.4 = (bf16[8,128,256]{2,1,0:T(8,128)(2,1)S(1)}, bf16[8,128,256]{2,1,0:T(8,128)(2,1)S(1)}, u32[]{:S(2)}, u32[]{:S(2)}) collective-permute-start(bf16[8,128,256]{2,1,0:T(8,128)(2,1)S(1)} %slice.6), channel_id=1, source_target_pairs={{0,1},{1,2},{2,3},{3,4},{4,5},{5,6},{6,7},{8,9},{9,10},{10,11},{11... | collective-permute-start | bytes 1572872 | tf_op jit(solution)/shard_map/ppermute | solution.py:25
  26.8 1.6 %copy-start.1 = (bf16[16,256,256]{2,1,0:T(8,128)(2,1)S(1)}, bf16[16,256,256]{2,1,0:T(8,128)(2,1)}, u32[]{:S(2)}) copy-start(bf16[16,256,256]{2,1,0:T(8,128)(2,1)} %refs_2_.4) | copy-start | bytes 6291460
  28.4 4.8 %copy-start.3 = (bf16[16,256,128]{2,1,0:T(8,128)(2,1)S(1)}, bf16[16,256,128]{2,1,0:T(8,128)(2,1)}, u32[]{:S(2)}) copy-start(bf16[16,256,128]{2,1,0:T(8,128)(2,1)} %hid_ref.5) | copy-start | bytes 3145732
  28.4 4.8 %copy-start.4 = (bf16[16,256,128]{2,1,0:T(8,128)(2,1)S(1)}, bf16[16,256,128]{2,1,0:T(8,128)(2,1)}, u32[]{:S(2)}) copy-start(bf16[16,256,128]{2,1,0:T(8,128)(2,1)} %grad_ref.3) | copy-start | bytes 3145732
  33.3 6.7 %copy-start.2 = (bf16[16,256,256]{2,1,0:T(8,128)(2,1)S(1)}, bf16[16,256,256]{2,1,0:T(8,128)(2,1)}, u32[]{:S(2)}) copy-start(bf16[16,256,256]{2,1,0:T(8,128)(2,1)} %refs_2_.4) | copy-start | bytes 6291460
  33.3 28.4 %collective-permute-start.2 = (bf16[6,272,128]{2,1,0:T(8,128)(2,1)S(1)}, bf16[6,272,128]{2,1,0:T(8,128)(2,1)S(1)}, u32[]{:S(2)}, u32[]{:S(2)}) collective-permute-start(bf16[6,272,128]{2,1,0:T(8,128)(2,1)S(1)} %get-tuple-element.39), channel_id=1, source_target_pairs={{0,8},{8,16},{16,24},{24,32},{32,40},{40,48},{48,56},{56,64},{64,7... | collective-permute-start | bytes 1253384 | tf_op jit(solution)/shard_map/ppermute | solution.py:25
  35.3 26.4 %collective-permute-start.3 = (bf16[6,272,128]{2,1,0:T(8,128)(2,1)S(1)}, bf16[6,272,128]{2,1,0:T(8,128)(2,1)S(1)}, u32[]{:S(2)}, u32[]{:S(2)}) collective-permute-start(bf16[6,272,128]{2,1,0:T(8,128)(2,1)S(1)} %get-tuple-element.40), channel_id=1, source_target_pairs={{8,0},{16,8},{24,16},{32,24},{40,32},{48,40},{56,48},{64,56},{72,6... | collective-permute-start | bytes 1253384 | tf_op jit(solution)/shard_map/ppermute | solution.py:25
  42.7 15.6 %copy-start.6 = (bf16[3,3,256,256]{3,2,1,0:T(8,128)(2,1)S(1)}, bf16[3,3,256,256]{3,2,1,0:T(8,128)(2,1)}, u32[]{:S(2)}) copy-start(bf16[3,3,256,256]{3,2,1,0:T(8,128)(2,1)} %param.13) | copy-start | bytes 3538948
  42.7 15.6 %copy-start.7 = (bf16[3,3,256,128]{3,2,1,0:T(8,128)(2,1)S(1)}, bf16[3,3,256,128]{3,2,1,0:T(8,128)(2,1)}, u32[]{:S(2)}) copy-start(bf16[3,3,256,128]{3,2,1,0:T(8,128)(2,1)} %param.14) | copy-start | bytes 1769476
  45.2 16.5 %collective-permute-start.5 = (bf16[4,272,128]{2,1,0:T(8,128)(2,1)S(1)}, bf16[4,272,128]{2,1,0:T(8,128)(2,1)S(1)}, u32[]{:S(2)}, u32[]{:S(2)}) collective-permute-start(bf16[4,272,128]{2,1,0:T(8,128)(2,1)S(1)} %get-tuple-element.48), channel_id=1, source_target_pairs={{0,8},{8,16},{16,24},{24,32},{32,40},{40,48},{48,56},{56,64},{64,7... | collective-permute-start | bytes 835592 | tf_op jit(solution)/shard_map/ppermute | solution.py:25
  47.1 14.6 %collective-permute-start.6 = (bf16[4,272,128]{2,1,0:T(8,128)(2,1)S(1)}, bf16[4,272,128]{2,1,0:T(8,128)(2,1)S(1)}, u32[]{:S(2)}, u32[]{:S(2)}) collective-permute-start(bf16[4,272,128]{2,1,0:T(8,128)(2,1)S(1)} %get-tuple-element.49), channel_id=1, source_target_pairs={{8,0},{16,8},{24,16},{32,24},{40,32},{48,40},{56,48},{64,56},{72,6... | collective-permute-start | bytes 835592 | tf_op jit(solution)/shard_map/ppermute | solution.py:25
  51.6 45.8 %collective-permute-start.8 = (bf16[16,128,256]{2,1,0:T(8,128)(2,1)S(1)}, bf16[16,128,256]{2,1,0:T(8,128)(2,1)S(1)}, u32[]{:S(2)}, u32[]{:S(2)}) collective-permute-start(bf16[16,128,256]{2,1,0:T(8,128)(2,1)S(1)} %slice.7), channel_id=1, source_target_pairs={{1,0},{2,1},{3,2},{4,3},{5,4},{6,5},{7,6},{9,8},{10,9},{11,10},{12... | collective-permute-start | bytes 3145736 | tf_op jit(solution)/shard_map/ppermute | solution.py:25
  85.3 12.1 %collective-permute-start.7 = (bf16[16,16,128]{2,1,0:T(8,128)(2,1)S(1)}, bf16[16,16,128]{2,1,0:T(8,128)(2,1)S(1)}, u32[]{:S(2)}, u32[]{:S(2)}) collective-permute-start(bf16[16,16,128]{2,1,0:T(8,128)(2,1)S(1)} %get-tuple-element.62), channel_id=1, source_target_pairs={{1,0},{2,1},{3,2},{4,3},{5,4},{6,5},{7,6},{9,8},{10,9},{11,10},{12... | collective-permute-start | bytes 196616 | tf_op jit(solution)/shard_map/ppermute | solution.py:25

commit v7 on v6

--- a/solution.py
+++ b/solution.py
@@ -69,27 +69,9 @@
     return jnp.sum(jnp.where(iota(levels.shape, 0) == row, levels, 0), axis=0, keepdims=True)
 
 
-def pack_small_kernel(
-    left_ref,
-    own_ref,
-    hid_ref,
-    grad_ref,
-    beside_ref,
-    left_last_ref,
-    hid_last_ref,
-    grad_last_ref,
-    features_ref,
-    disp_ref,
-    out_ref,
-    last_ref,
-):
+def pack_left_kernel(left_ref, own_ref, hid_ref, grad_ref, disp_ref, out_ref):
     rows, _, chan = left_ref.shape
-    half = features_ref.shape[0]
-    for r in range(half):
-        last_ref[r * B : (r + 1) * B] = features_ref[r]
     levels = jnp.transpose(disp_ref[:, :B].astype(F32), (1, 0))
-    last_levels = jnp.transpose(disp_ref[:, disp_ref.shape[1] - B :].astype(F32), (1, 0))
-    low = iota((8, chan), 0) < HALO
     for r in range(rows):
         out_ref[r, :, :chan] = left_ref[r, :HALO]
         out_ref[r, :, chan : 2 * chan] = own_ref[r, :HALO]
@@ -97,6 +79,18 @@
         out_ref[r, :, 2 * chan + B : 2 * chan + 2 * B] = grad_ref[r, :HALO]
         level = jnp.broadcast_to(levels[:8, r : r + 1], (8, B))
         out_ref[r, :, 2 * chan + 2 * B :] = level.astype(BF16)[:HALO]
+
+
+def pack_right_kernel(
+    beside_ref, left_last_ref, hid_last_ref, grad_last_ref, features_ref, disp_ref, last_ref
+):
+    rows, _, chan = beside_ref.shape
+    half = features_ref.shape[0]
+    last_levels = jnp.transpose(disp_ref[:, disp_ref.shape[1] - B :].astype(F32), (1, 0))
+    low = iota((8, chan), 0) < HALO
+    for r in range(half):
+        last_ref[r * B : (r + 1) * B] = features_ref[r]
+    for r in range(rows):
         beside = pltpu.roll(beside_ref[r].astype(F32), HALO, 0)
         upper = jnp.where(low, beside, left_last_ref[r].astype(F32))
         level = jnp.broadcast_to(last_levels[B - 8 :, r : r + 1], (8, chan))
@@ -539,15 +533,29 @@
     last8 = cols // 8 - 1
     pack_params = pltpu.CompilerParams(vmem_limit_bytes=PACK_VMEM)
 
-    small_shapes = (shape((rows, HALO, packed), BF16), shape((half * B + rows * EDGE, chan), BF16))
-    to_left, to_right = pl.pallas_call(
-        pack_small_kernel,
+    left_shape = shape((rows, HALO, packed), BF16)
+    to_left = pl.pallas_call(
+        pack_left_kernel,
         grid=(1,),
         in_specs=[
             block((rows, 8, chan), 0, 0, 0),
             block((rows, 8, chan), 0, 0, 0),
             block((rows, 8, B), 0, 0, 0),
             block((rows, 8, B), 0, 0, 0),
+            whole(disparity),
+        ],
+        out_specs=whole(left_shape),
+        out_shape=left_shape,
+        compiler_params=pack_params,
+        cost_estimate=cost(1 << 16, 1 << 18),
+        name="pack_left",
+    )(feat_left, feat_right, hidden, grad_hidden, disparity)
+    from_right = shift(to_left, "cols", -1)
+    right_shape = shape((half * B + rows * EDGE, chan), BF16)
+    to_right = pl.pallas_call(
+        pack_right_kernel,
+        grid=(1,),
+        in_specs=[
             block((rows, 8, chan), 0, (cols - B) // 8 - 1, 0),
             block((rows, 8, chan), 0, last8, 0),
             block((rows, 8, B), 0, last8, 0),
@@ -555,26 +563,17 @@
             block((half, B, chan), 0, cols // B - 1, 0),
             whole(disparity),
         ],
-        out_specs=[whole(s) for s in small_shapes],
-        out_shape=small_shapes,
+        out_specs=whole(right_shape),
+        out_shape=right_shape,
         compiler_params=pack_params,
-        cost_estimate=cost(1 << 16, 1 << 18),
-        name="pack_small",
-    )(
-        feat_left,
-        feat_right,
-        hidden,
-        grad_hidden,
-        feat_right,
-        feat_left,
-        hidden,
-        grad_hidden,
-        feat_right,
-        disparity,
+        cost_estimate=cost(1 << 16, 1 << 20),
+        name="pack_right",
+    )(feat_right, feat_left, hidden, grad_hidden, feat_right, disparity)
+    first, second, from_right = lax.optimization_barrier(
+        (to_right, feat_right[half:, cols - B :], from_right)
     )
-    from_right = shift(to_left, "cols", -1)
-    from_left = shift(to_right, "cols", 1)
-    second, from_right = lax.optimization_barrier((feat_right[half:, cols - B :], from_right))
+    from_left = shift(first, "cols", 1)
+    second = shift(second, "cols", 1).reshape(half * B, chan)
     mw16 = jnp.pad(motion_weight, ((0, 16 - taps), (0, 0)))
     pads = [pltpu.VMEM((size, B, chan), BF16), pltpu.VMEM((B, B), BF16)]
     right_shapes = (shape((rows, B + EDGE, B), BF16), shape((rows, B, B), F32))
@@ -596,7 +595,7 @@
         name="corr_right",
     )(feat_left, feat_right, disparity, from_right, mw16)
     from_left, mot_right = lax.optimization_barrier((from_left, mot_right))
-    before = [from_left, shift(second, "cols", 1).reshape(half * B, chan)]
+    before = [from_left, second]
 
     rim = shape((HALO + HALO // 2, wide, B), BF16)
     edge_shape = shape((rows, EDGE, 2 * B), BF16)

time: 101 us -> 99.9 us (0.989)
  starting transfers between devices: 35.2 us -> 30.5 us
  Pallas kernels: 48.3 us -> 50.3 us
  waiting for transfers between devices: 12.6 us -> 13.8 us
    ppermute x9, starting transfers between devices: 35.2 us -> 30.5 us  [shift(): return lax.ppermute(array, axis, pairs)]
    pallas_call x1 -> x2, Pallas kernels: 2.47 us -> 4.06 us  [the longest x1 2.34 us: per_device(): pl.pallas_call(pack_right_kernel, grid=(1,), in_specs=[block((rows, 8, ch...]
    ppermute x9, waiting for transfers between devices: 12.6 us -> 13.8 us  [shift(): return lax.ppermute(array, axis, pairs)]
  transfers between devices with their start and end apart: 9 -> 9, of which waited for: 2 -> 3; matrix products, arithmetic and copies ran while one was open for 1% -> 1% of each run, Pallas kernels for 43% -> 47%
where the time goes in v7:
time: 99.9 us; the launch traced here: 98.2 us
  Pallas kernels  50.3 us (50%)
  starting transfers between devices  30.5 us (31%)
  waiting for transfers between devices  13.8 us (14%)
  local copies, waits for them, and re-layouts  2.77 us (3%)
    ppermute x9, starting transfers between devices, shift(): return lax.ppermute(array, axis, pairs)  30.5 us
    pallas_call x1, Pallas kernels, per_device(): pl.pallas_call(gru_kernel, in_specs=[vmem] * len(operands), out_specs=[vm...  24 us
    ppermute x9, waiting for transfers between devices, shift(): return lax.ppermute(array, axis, pairs)  13.8 us
    pallas_call x1, Pallas kernels, per_device(): pl.pallas_call(lambda *refs: grads_kernel(*args, *refs), grid=(steps,), i...  6.69 us
    pallas_call x2, Pallas kernels, left_lookup(): pl.pallas_call(lambda *refs: left_corr_kernel(*args, start, rim_step, *re...  4.86 us
    pallas_call x1, Pallas kernels, per_device(): pl.pallas_call(lambda *refs: right_corr_kernel(*args, *refs), grid=(steps...  4.75 us
    pallas_call x1, Pallas kernels, per_device(): pl.pallas_call(gates_hidden_kernel, in_specs=[vmem] * len(hid_operands),...  3.38 us
    pallas_call x1, Pallas kernels, per_device(): pl.pallas_call(lambda *refs: last_kernel(*args, *refs), grid=(steps,), in...  2.5 us
  transfers between devices with their start and end apart: 9, of which 3 were waited for; matrix products, arithmetic and copies ran while one was open for 1% of the time, Pallas kernels for 47%

profile of v7, /device:TPU:120, one launch (start us, length us, event | category | flops | bytes accessed | tf_op | source)
XLA Modules:
  0.0 98.2 jit_solution(9184174133443042719)
XLA Ops:
  0.6 1.7 %pack_left.1 = bf16[16,4,896]{2,1,0:T(4,128)(2,1)} custom-call(bf16[16,256,256]{2,1,0:T(8,128)(2,1)} %refs_2_.5, bf16[16,256,256]{2,1,0:T(8,128)(2,1)} %refs_2_.4, bf16[16,256,128]{2,1,0:T(8,128)(2,1)} %hid_ref.5, bf16[16,256,128]{2,1,0:T(8,128)(2,1)} %grad_ref.3, s32[16,256]{1,0:T(8,128)} %refs_5_.1), custom_call_target="tpu_custom_call" | custom-call | flops 65536 | bytes 262144 | tf_op jit(solution)/shard_map/pack_left/pallas_call | solution.py:537
  2.3 0.0 copy-start.8
  2.3 0.0 copy-start.5
  2.4 4.9 %collective-permute-start = (bf16[16,4,896]{2,1,0:T(4,128)(2,1)}, bf16[16,4,896]{2,1,0:T(4,128)(2,1)S(1)}, u32[]{:S(2)}, u32[]{:S(2)}) collective-permute-start(bf16[16,4,896]{2,1,0:T(4,128)(2,1)} %pack_left.1), channel_id=1, source_target_pairs={{1,0},{2,1},{3,2},{4,3},{5,4},{6,5},{7,6},{9,8},{10,9},{11,10},{12... | collective-permute-start | bytes 344072 | tf_op jit(solution)/shard_map/ppermute | solution.py:25
  7.2 0.0 copy-start
  7.3 2.3 %pack_right.1 = bf16[1280,256]{1,0:T(8,128)(2,1)} custom-call(bf16[16,256,256]{2,1,0:T(8,128)(2,1)} %refs_2_.4, bf16[16,256,256]{2,1,0:T(8,128)(2,1)} %refs_2_.5, bf16[16,256,128]{2,1,0:T(8,128)(2,1)} %hid_ref.5, bf16[16,256,128]{2,1,0:T(8,128)(2,1)} %grad_ref.3, bf16[16,256,256]{2,1,0:T(8,128)(2,1)} %refs_2_.4, s32[16,256]{1,0:T(8,128)} %refs_5_.1), custom_call_target="tpu_custom_call" | custom-call | flops 65536 | bytes 1048576 | tf_op jit(solution)/shard_map/pack_right/pallas_call | solution.py:555
  9.6 1.1 %slice.6 = bf16[8,128,256]{2,1,0:T(8,128)(2,1)S(1)} slice(bf16[16,256,256]{2,1,0:T(8,128)(2,1)} %refs_2_.4), slice={[8:16], [128:256], [0:256]} | slice | bytes 1048576 | tf_op jit(solution)/shard_map/slice | solution.py:573
  10.7 0.3 collective-permute-done.refs_3_.right_ref
  11.0 2.3 %collective-permute-start.1 = (bf16[1280,256]{1,0:T(8,128)(2,1)}, bf16[1280,256]{1,0:T(8,128)(2,1)S(1)}, u32[]{:S(2)}, u32[]{:S(2)}) collective-permute-start(bf16[1280,256]{1,0:T(8,128)(2,1)} %pack_right.1), channel_id=1, source_target_pairs={{0,1},{1,2},{2,3},{3,4},{4,5},{5,6},{6,7},{8,9},{9,10},{10,11},{11... | collective-permute-start | bytes 1966088 | tf_op jit(solution)/shard_map/ppermute | solution.py:25
  13.3 1.9 %collective-permute-start.4 = (bf16[8,128,256]{2,1,0:T(8,128)(2,1)S(1)}, bf16[8,128,256]{2,1,0:T(8,128)(2,1)S(1)}, u32[]{:S(2)}, u32[]{:S(2)}) collective-permute-start(bf16[8,128,256]{2,1,0:T(8,128)(2,1)S(1)} %slice.6), channel_id=1, source_target_pairs={{0,1},{1,2},{2,3},{3,4},{4,5},{5,6},{6,7},{8,9},{9,10},{10,11},{11... | collective-permute-start | bytes 1572872 | tf_op jit(solution)/shard_map/ppermute | solution.py:25
  15.2 0.0 copy-done.8
  15.2 0.0 copy-done.5
  15.2 0.0 copy-done
  15.3 0.0 copy-start.1
  15.3 1.6 %copy-done.1 = bf16[16,256,256]{2,1,0:T(8,128)(2,1)S(1)} copy-done((bf16[16,256,256]{2,1,0:T(8,128)(2,1)S(1)}, bf16[16,256,256]{2,1,0:T(8,128)(2,1)}, u32[]{:S(2)}) %copy-start.1) | copy-done | bytes 2097176
  16.8 0.0 copy-start.3
  16.8 0.0 copy-start.4
  16.8 4.8 %corr_right.1 = (bf16[16,144,128]{2,1,0:T(8,128)(2,1)S(1)}, f32[16,128,128]{2,1,0:T(8,128)S(1)}) custom-call(bf16[16,256,256]{2,1,0:T(8,128)(2,1)S(1)} %copy-done, bf16[16,256,256]{2,1,0:T(8,128)(2,1)S(1)} %copy-done.1, s32[16,256]{1,0:T(8,128)S(1)} %copy-done.5, bf16[16,4,896]{2,1,0:T(4,128)(2,1)S(1)} %collective-permute-done.refs_3_.right_ref, ...), custom_call_target="tpu_custom_call" | custom-call | flops 268435456 | bytes 6291456 | tf_op jit(solution)/shard_map/corr_right/pallas_call | solution.py:580
  21.6 11.5 %collective-permute-done.1.left_ref.refs_2_.refs_3_ = bf16[1280,256]{1,0:T(8,128)(2,1)S(1)} collective-permute-done((bf16[1280,256]{1,0:T(8,128)(2,1)}, bf16[1280,256]{1,0:T(8,128)(2,1)S(1)}, u32[]{:S(2)}, u32[]{:S(2)}) %collective-permute-start.1) | collective-permute-done | bytes 655392 | tf_op jit(solution)/shard_map/ppermute | solution.py:25
  33.1 0.0 copy-done.3
  33.1 0.0 copy-done.4
  33.1 0.1 rims.1
  33.3 0.0 copy-start.2
  33.3 2.1 %collective-permute-start.2 = (bf16[6,272,128]{2,1,0:T(8,128)(2,1)S(1)}, bf16[6,272,128]{2,1,0:T(8,128)(2,1)S(1)}, u32[]{:S(2)}, u32[]{:S(2)}) collective-permute-start(bf16[6,272,128]{2,1,0:T(8,128)(2,1)S(1)} %get-tuple-element.37), channel_id=1, source_target_pairs={{0,8},{8,16},{16,24},{24,32},{32,40},{40,48},{48,56},{56,64},{64,7... | collective-permute-start | bytes 1253384 | tf_op jit(solution)/shard_map/ppermute | solution.py:25
  35.3 4.5 %collective-permute-start.3 = (bf16[6,272,128]{2,1,0:T(8,128)(2,1)S(1)}, bf16[6,272,128]{2,1,0:T(8,128)(2,1)S(1)}, u32[]{:S(2)}, u32[]{:S(2)}) collective-permute-start(bf16[6,272,128]{2,1,0:T(8,128)(2,1)S(1)} %get-tuple-element.38), channel_id=1, source_target_pairs={{8,0},{16,8},{24,16},{32,24},{40,32},{48,40},{56,48},{64,56},{72,6... | collective-permute-start | bytes 1253384 | tf_op jit(solution)/shard_map/ppermute | solution.py:25
  39.9 0.1 slice.7
  40.0 0.0 copy-done.2
  40.0 2.4 %corr_left.2 = (bf16[8,272,128]{2,1,0:T(8,128)(2,1)S(1)}, f32[8,128,128]{2,1,0:T(8,128)S(1)}, bf16[4,272,128]{2,1,0:T(8,128)(2,1)S(1)}) custom-call(bf16[16,256,256]{2,1,0:T(8,128)(2,1)S(1)} %copy-done, bf16[16,256,256]{2,1,0:T(8,128)(2,1)S(1)} %copy-done.2, bf16[1280,256]{1,0:T(8,128)(2,1)S(1)} %collective-permute-done.1.left_ref.refs_2_.refs_3_, ...), custom_call_target="tpu_custom_call" | custom-call | flops 134217728 | bytes 3145728 | tf_op jit(solution)/shard_map/corr_left/pallas_call | solution.py:630
  42.4 1.9 %collective-permute-done.4 = bf16[8,128,256]{2,1,0:T(8,128)(2,1)S(1)} collective-permute-done((bf16[8,128,256]{2,1,0:T(8,128)(2,1)S(1)}, bf16[8,128,256]{2,1,0:T(8,128)(2,1)S(1)}, u32[]{:S(2)}, u32[]{:S(2)}) %collective-permute-start.4) | collective-permute-done | bytes 524320 | tf_op jit(solution)/shard_map/ppermute | solution.py:25
  44.4 0.0 copy-start.6
  44.4 0.0 copy-start.7
  44.4 2.4 %corr_left.3 = (bf16[8,272,128]{2,1,0:T(8,128)(2,1)S(1)}, f32[8,128,128]{2,1,0:T(8,128)S(1)}, bf16[4,272,128]{2,1,0:T(8,128)(2,1)S(1)}) custom-call(bf16[16,256,256]{2,1,0:T(8,128)(2,1)S(1)} %copy-done, bf16[16,256,256]{2,1,0:T(8,128)(2,1)S(1)} %copy-done.2, bf16[1024,256]{1,0:T(8,128)(2,1)S(1)} %bitcast.3, ...), custom_call_target="tpu_custom_call" | custom-call | flops 134217728 | bytes 3145728 | tf_op jit(solution)/shard_map/corr_left/pallas_call | solution.py:630
  46.8 1.9 %collective-permute-start.5 = (bf16[4,272,128]{2,1,0:T(8,128)(2,1)S(1)}, bf16[4,272,128]{2,1,0:T(8,128)(2,1)S(1)}, u32[]{:S(2)}, u32[]{:S(2)}) collective-permute-start(bf16[4,272,128]{2,1,0:T(8,128)(2,1)S(1)} %get-tuple-element.46), channel_id=1, source_target_pairs={{0,8},{8,16},{16,24},{24,32},{32,40},{40,48},{48,56},{56,64},{64,7... | collective-permute-start | bytes 835592 | tf_op jit(solution)/shard_map/ppermute | solution.py:25
  48.7 4.5 %collective-permute-start.6 = (bf16[4,272,128]{2,1,0:T(8,128)(2,1)S(1)}, bf16[4,272,128]{2,1,0:T(8,128)(2,1)S(1)}, u32[]{:S(2)}, u32[]{:S(2)}) collective-permute-start(bf16[4,272,128]{2,1,0:T(8,128)(2,1)S(1)} %get-tuple-element.47), channel_id=1, source_target_pairs={{8,0},{16,8},{24,16},{32,24},{40,32},{48,40},{56,48},{64,56},{72,6... | collective-permute-start | bytes 835592 | tf_op jit(solution)/shard_map/ppermute | solution.py:25
  53.3 4.9 %collective-permute-start.8 = (bf16[16,128,256]{2,1,0:T(8,128)(2,1)S(1)}, bf16[16,128,256]{2,1,0:T(8,128)(2,1)S(1)}, u32[]{:S(2)}, u32[]{:S(2)}) collective-permute-start(bf16[16,128,256]{2,1,0:T(8,128)(2,1)S(1)} %slice.7), channel_id=1, source_target_pairs={{1,0},{2,1},{3,2},{4,3},{5,4},{6,5},{7,6},{9,8},{10,9},{11,10},{12... | collective-permute-start | bytes 3145736 | tf_op jit(solution)/shard_map/ppermute | solution.py:25
  58.2 0.0 copy-done.6
  58.2 0.0 copy-done.7
  58.3 3.4 %gates_hidden.1 = (f32[14,272,256]{2,1,0:T(8,128)S(1)}, bf16[1152,256]{1,0:T(8,128)(2,1)S(1)}, bf16[3072,256]{1,0:T(8,128)(2,1)S(1)}, bf16[256,1152]{1,0:T(8,128)(2,1)S(1)}, bf16[256,3072]{1,0:T(8,128)(2,1)S(1)}) custom-call(bf16[16,256,128]{2,1,0:T(8,128)(2,1)S(1)} %copy-done.3, bf16[16,16,256]{2,1,0:T(8,128)(2,1)S(1)} %get-tuple-element.39.edge_ref, ...), custom_call_target="tpu_custom_call" | custom-call | flops 3529506816 | bytes 16777216 | tf_op jit(solution)/shard_map/gates_hidden/pallas_call | solution.py:670
  61.6 0.0 collective-permute-done.5.mott_ref
  61.7 0.0 collective-permute-done.6.motl_ref
  61.7 0.0 collective-permute-done.2.hgt_ref
  61.7 0.0 collective-permute-done.3.hgb_ref
  61.7 24.0 %gru.1 = (bf16[16,256,128]{2,1,0:T(8,128)(2,1)}, bf16[16,256,128]{2,1,0:T(8,128)(2,1)S(1)}, bf16[16,16,128]{2,1,0:T(8,128)(2,1)S(1)}) custom-call(bf16[16,256,128]{2,1,0:T(8,128)(2,1)S(1)} %copy-done.3, bf16[16,256,128]{2,1,0:T(8,128)(2,1)S(1)} %copy-done.4, bf16[6,272,128]{2,1,0:T(8,128)(2,1)S(1)} %collective-permute-done.2.hgt_ref, ...), custom_call_target="tpu_custom_call" | custom-call | flops 15686696960 | bytes 16777216 | tf_op jit(solution)/shard_map/gru/pallas_call | solution.py:708
  85.6 3.3 %collective-permute-start.7 = (bf16[16,16,128]{2,1,0:T(8,128)(2,1)S(1)}, bf16[16,16,128]{2,1,0:T(8,128)(2,1)S(1)}, u32[]{:S(2)}, u32[]{:S(2)}) collective-permute-start(bf16[16,16,128]{2,1,0:T(8,128)(2,1)S(1)} %get-tuple-element.60), channel_id=1, source_target_pairs={{1,0},{2,1},{3,2},{4,3},{5,4},{6,5},{7,6},{9,8},{10,9},{11,10},{12... | collective-permute-start | bytes 196616 | tf_op jit(solution)/shard_map/ppermute | solution.py:25
  89.0 6.7 %grads.1 = (bf16[16,256,256]{2,1,0:T(8,128)(2,1)}, bf16[16,256,256]{2,1,0:T(8,128)(2,1)}, bf16[16,128,128]{2,1,0:T(8,128)(2,1)S(1)}) custom-call(bf16[16,256,128]{2,1,0:T(8,128)(2,1)S(1)} %get-tuple-element.57.refs_0_, bf16[16,256,256]{2,1,0:T(8,128)(2,1)S(1)} %copy-done, bf16[16,256,256]{2,1,0:T(8,128)(2,1)S(1)} %copy-done.2, ...), custom_call_target="tpu_custom_call" | custom-call | flops 1073741824 | bytes 12582912 | tf_op jit(solution)/shard_map/grads/pallas_call | solution.py:725
  95.7 0.0 collective-permute-done.7.refs_1_
  95.7 0.0 collective-permute-done.8.refs_3_
  95.7 2.5 %grad_right.1 = bf16[16,256,256]{2,1,0:T(8,128)(2,1)} custom-call(bf16[16,128,128]{2,1,0:T(8,128)(2,1)S(1)} %get-tuple-element.59.refs_0_, bf16[16,16,128]{2,1,0:T(8,128)(2,1)S(1)} %collective-permute-done.7.refs_1_, bf16[16,256,256]{2,1,0:T(8,128)(2,1)S(1)} %copy-done, ...), custom_call_target="tpu_custom_call", output_to_operand_aliasing={{}: (4, {})} | custom-call | flops 268435456 | bytes 4194304 | tf_op jit(solution)/shard_map/grad_right/pallas_call | solution.py:748
  (1 shorter events, 0.0 us)
Async XLA Ops:
  2.3 12.9 %copy-start.8 = (bf16[9,128]{1,0:T(8,128)(2,1)S(1)}, bf16[9,128]{1,0:T(8,128)(2,1)}, u32[]{:S(2)}) copy-start(bf16[9,128]{1,0:T(8,128)(2,1)} %param.12) | copy-start | bytes 6916
  2.3 12.9 %copy-start.5 = (s32[16,256]{1,0:T(8,128)S(1)}, s32[16,256]{1,0:T(8,128)}, u32[]{:S(2)}) copy-start(s32[16,256]{1,0:T(8,128)} %refs_5_.1) | copy-start | bytes 49156
  2.4 8.6 %collective-permute-start = (bf16[16,4,896]{2,1,0:T(4,128)(2,1)}, bf16[16,4,896]{2,1,0:T(4,128)(2,1)S(1)}, u32[]{:S(2)}, u32[]{:S(2)}) collective-permute-start(bf16[16,4,896]{2,1,0:T(4,128)(2,1)} %pack_left.1), channel_id=1, source_target_pairs={{1,0},{2,1},{3,2},{4,3},{5,4},{6,5},{7,6},{9,8},{10,9},{11,10},{12... | collective-permute-start | bytes 344072 | tf_op jit(solution)/shard_map/ppermute | solution.py:25
  7.2 8.0 %copy-start = (bf16[16,256,256]{2,1,0:T(8,128)(2,1)S(1)}, bf16[16,256,256]{2,1,0:T(8,128)(2,1)}, u32[]{:S(2)}) copy-start(bf16[16,256,256]{2,1,0:T(8,128)(2,1)} %refs_2_.5) | copy-start | bytes 6291460
  11.0 22.2 %collective-permute-start.1 = (bf16[1280,256]{1,0:T(8,128)(2,1)}, bf16[1280,256]{1,0:T(8,128)(2,1)S(1)}, u32[]{:S(2)}, u32[]{:S(2)}) collective-permute-start(bf16[1280,256]{1,0:T(8,128)(2,1)} %pack_right.1), channel_id=1, source_target_pairs={{0,1},{1,2},{2,3},{3,4},{4,5},{5,6},{6,7},{8,9},{9,10},{10,11},{11... | collective-permute-start | bytes 1966088 | tf_op jit(solution)/shard_map/ppermute | solution.py:25
  13.3 31.1 %collective-permute-start.4 = (bf16[8,128,256]{2,1,0:T(8,128)(2,1)S(1)}, bf16[8,128,256]{2,1,0:T(8,128)(2,1)S(1)}, u32[]{:S(2)}, u32[]{:S(2)}) collective-permute-start(bf16[8,128,256]{2,1,0:T(8,128)(2,1)S(1)} %slice.6), channel_id=1, source_target_pairs={{0,1},{1,2},{2,3},{3,4},{4,5},{5,6},{6,7},{8,9},{9,10},{10,11},{11... | collective-permute-start | bytes 1572872 | tf_op jit(solution)/shard_map/ppermute | solution.py:25
  15.3 1.6 %copy-start.1 = (bf16[16,256,256]{2,1,0:T(8,128)(2,1)S(1)}, bf16[16,256,256]{2,1,0:T(8,128)(2,1)}, u32[]{:S(2)}) copy-start(bf16[16,256,256]{2,1,0:T(8,128)(2,1)} %refs_2_.4) | copy-start | bytes 6291460
  16.8 16.3 %copy-start.3 = (bf16[16,256,128]{2,1,0:T(8,128)(2,1)S(1)}, bf16[16,256,128]{2,1,0:T(8,128)(2,1)}, u32[]{:S(2)}) copy-start(bf16[16,256,128]{2,1,0:T(8,128)(2,1)} %hid_ref.5) | copy-start | bytes 3145732
  16.8 16.3 %copy-start.4 = (bf16[16,256,128]{2,1,0:T(8,128)(2,1)S(1)}, bf16[16,256,128]{2,1,0:T(8,128)(2,1)}, u32[]{:S(2)}) copy-start(bf16[16,256,128]{2,1,0:T(8,128)(2,1)} %grad_ref.3) | copy-start | bytes 3145732
  33.3 6.7 %copy-start.2 = (bf16[16,256,256]{2,1,0:T(8,128)(2,1)S(1)}, bf16[16,256,256]{2,1,0:T(8,128)(2,1)}, u32[]{:S(2)}) copy-start(bf16[16,256,256]{2,1,0:T(8,128)(2,1)} %refs_2_.4) | copy-start | bytes 6291460
  33.3 28.4 %collective-permute-start.2 = (bf16[6,272,128]{2,1,0:T(8,128)(2,1)S(1)}, bf16[6,272,128]{2,1,0:T(8,128)(2,1)S(1)}, u32[]{:S(2)}, u32[]{:S(2)}) collective-permute-start(bf16[6,272,128]{2,1,0:T(8,128)(2,1)S(1)} %get-tuple-element.37), channel_id=1, source_target_pairs={{0,8},{8,16},{16,24},{24,32},{32,40},{40,48},{48,56},{56,64},{64,7... | collective-permute-start | bytes 1253384 | tf_op jit(solution)/shard_map/ppermute | solution.py:25
  35.3 26.3 %collective-permute-start.3 = (bf16[6,272,128]{2,1,0:T(8,128)(2,1)S(1)}, bf16[6,272,128]{2,1,0:T(8,128)(2,1)S(1)}, u32[]{:S(2)}, u32[]{:S(2)}) collective-permute-start(bf16[6,272,128]{2,1,0:T(8,128)(2,1)S(1)} %get-tuple-element.38), channel_id=1, source_target_pairs={{8,0},{16,8},{24,16},{32,24},{40,32},{48,40},{56,48},{64,56},{72,6... | collective-permute-start | bytes 1253384 | tf_op jit(solution)/shard_map/ppermute | solution.py:25
  44.4 13.9 %copy-start.6 = (bf16[3,3,256,256]{3,2,1,0:T(8,128)(2,1)S(1)}, bf16[3,3,256,256]{3,2,1,0:T(8,128)(2,1)}, u32[]{:S(2)}) copy-start(bf16[3,3,256,256]{3,2,1,0:T(8,128)(2,1)} %param.13) | copy-start | bytes 3538948
  44.4 13.9 %copy-start.7 = (bf16[3,3,256,128]{3,2,1,0:T(8,128)(2,1)S(1)}, bf16[3,3,256,128]{3,2,1,0:T(8,128)(2,1)}, u32[]{:S(2)}) copy-start(bf16[3,3,256,128]{3,2,1,0:T(8,128)(2,1)} %param.14) | copy-start | bytes 1769476
  46.8 14.8 %collective-permute-start.5 = (bf16[4,272,128]{2,1,0:T(8,128)(2,1)S(1)}, bf16[4,272,128]{2,1,0:T(8,128)(2,1)S(1)}, u32[]{:S(2)}, u32[]{:S(2)}) collective-permute-start(bf16[4,272,128]{2,1,0:T(8,128)(2,1)S(1)} %get-tuple-element.46), channel_id=1, source_target_pairs={{0,8},{8,16},{16,24},{24,32},{32,40},{40,48},{48,56},{56,64},{64,7... | collective-permute-start | bytes 835592 | tf_op jit(solution)/shard_map/ppermute | solution.py:25
  48.7 12.9 %collective-permute-start.6 = (bf16[4,272,128]{2,1,0:T(8,128)(2,1)S(1)}, bf16[4,272,128]{2,1,0:T(8,128)(2,1)S(1)}, u32[]{:S(2)}, u32[]{:S(2)}) collective-permute-start(bf16[4,272,128]{2,1,0:T(8,128)(2,1)S(1)} %get-tuple-element.47), channel_id=1, source_target_pairs={{8,0},{16,8},{24,16},{32,24},{40,32},{48,40},{56,48},{64,56},{72,6... | collective-permute-start | bytes 835592 | tf_op jit(solution)/shard_map/ppermute | solution.py:25
  53.3 42.4 %collective-permute-start.8 = (bf16[16,128,256]{2,1,0:T(8,128)(2,1)S(1)}, bf16[16,128,256]{2,1,0:T(8,128)(2,1)S(1)}, u32[]{:S(2)}, u32[]{:S(2)}) collective-permute-start(bf16[16,128,256]{2,1,0:T(8,128)(2,1)S(1)} %slice.7), channel_id=1, source_target_pairs={{1,0},{2,1},{3,2},{4,3},{5,4},{6,5},{7,6},{9,8},{10,9},{11,10},{12... | collective-permute-start | bytes 3145736 | tf_op jit(solution)/shard_map/ppermute | solution.py:25
  85.6 10.0 %collective-permute-start.7 = (bf16[16,16,128]{2,1,0:T(8,128)(2,1)S(1)}, bf16[16,16,128]{2,1,0:T(8,128)(2,1)S(1)}, u32[]{:S(2)}, u32[]{:S(2)}) collective-permute-start(bf16[16,16,128]{2,1,0:T(8,128)(2,1)S(1)} %get-tuple-element.60), channel_id=1, source_target_pairs={{1,0},{2,1},{3,2},{4,3},{5,4},{6,5},{7,6},{9,8},{10,9},{11,10},{12... | collective-permute-start | bytes 196616 | tf_op jit(solution)/shard_map/ppermute | solution.py:25

commit v8 on v5

--- a/solution.py
+++ b/solution.py
@@ -13,6 +13,7 @@
 F32 = jnp.float32
 BF16 = jnp.bfloat16
 ROWS = 4
+GRAD_ROWS = 8
 SMALL_VMEM = 16 * 1024 * 1024
 GRU_VMEM = 36 * 1024 * 1024
 GATES_VMEM = 12 * 1024 * 1024
@@ -101,6 +102,12 @@
         last_ref[r] = jnp.concatenate([upper, lower], axis=0).astype(BF16)
 
 
+def join_columns(buf, row, own_row, edge_row):
+    own = own_row.shape[0]
+    buf[row, :own] = own_row
+    buf[row, own:] = edge_row
+
+
 def rim_kernel(
     hid_first_ref,
     grad_first_ref,
@@ -114,21 +121,19 @@
     pad_ref,
 ):
     rows = right_ref.shape[0]
-    own = hid_first_ref.shape[1]
-    chan = (right_ref.shape[2] - 3 * B) // 2
+    chan = left_ref.shape[2]
     pad_ref[...] = jnp.zeros_like(pad_ref)
     last = iota(pad_ref.shape, 0) >= EDGE - HALO
     for r in range(rows):
         pad_ref[:HALO] = right_ref[r, :, 2 * chan : 2 * chan + 2 * B].astype(F32)
         edge_ref[r] = jnp.where(last, left_ref[r].astype(F32), pad_ref[...]).astype(BF16)
     for r in range(HALO):
-        for out, hid, grad, row in (
-            (first_ref, hid_first_ref, grad_first_ref, r),
-            (last_ref, hid_last_ref, grad_last_ref, rows - HALO + r),
-        ):
-            out[r, :own, :B] = hid[r]
-            out[r, :own, B:] = grad[r]
-            out[r, own:] = edge_ref[row]
+        join_columns(first_ref, r, hid_first_ref[r], edge_ref[r, :, :B])
+        join_columns(last_ref, r, hid_last_ref[r], edge_ref[rows - HALO + r, :, :B])
+    for r in range(HALO // 2):
+        join_columns(first_ref, HALO + r, grad_first_ref[r], edge_ref[r, :, B:])
+        row = HALO - HALO // 2 + r
+        join_columns(last_ref, HALO + r, grad_last_ref[row], edge_ref[rows - HALO + row, :, B:])
 
 
 def taps_matrix(weight_ref, pad_ref):
@@ -256,12 +261,6 @@
 CHUNK = 4
 
 
-def join_columns(buf, row, own_row, edge_row):
-    own = own_row.shape[0]
-    buf[row, :own] = own_row
-    buf[row, own:] = edge_row
-
-
 def gates_hidden_kernel(
     hid_ref,
     edge_ref,
@@ -347,8 +346,7 @@
         if n < 0 or n >= rows:
             hg = hgt_ref[row] if n < 0 else hgb_ref[n - rows]
             mot = mott_ref[row] if n < 0 else motl_ref[n - rows]
-            h_ref[row] = hg[:, :B]
-            g_ref[row] = hg[:, B:]
+            h_ref[row] = hg
         else:
             mot = mota_ref[n] if n < half else motb_ref[n - half]
             join_columns(h_ref, row, hid_ref[n], edge_ref[n, :, :B])
@@ -356,6 +354,10 @@
         store3(m3_ref, row, mot.astype(F32))
         if row <= known[0] or row >= known[-1]:
             store3(u3_ref, row, h_ref[row].astype(F32))
+
+    for n in range(HALO // 2):
+        g_ref[HALO - HALO // 2 + n] = hgt_ref[HALO + n]
+        g_ref[HALO + rows + n] = hgb_ref[HALO + n]
 
     def gate(row, value):
         value = jax.nn.sigmoid(value)
@@ -569,7 +571,7 @@
     )
     before = [shift(features[:half], "cols", 1), shift(second, "cols", 1)]
 
-    rim = shape((HALO, wide, 2 * B), BF16)
+    rim = shape((HALO + HALO // 2, wide, B), BF16)
     edge_shape = shape((rows, EDGE, 2 * B), BF16)
     first_rim, last_rim, edge = pl.pallas_call(
         rim_kernel,
@@ -711,25 +713,27 @@
     )(*operands)
     next_grad = shift(tap_grad, "cols", -1)
 
+    gsize = GRAD_ROWS
+    gsteps = rows // gsize
     feat_shape = shape((rows, cols, chan), BF16)
     near_shape = shape((rows, B, B), BF16)
-    mid = steps // 2
+    mid = gsteps // 2
     grad_left, grad_first, near = pl.pallas_call(
         lambda *refs: grads_kernel(*args, *refs),
-        grid=(steps,),
+        grid=(gsteps,),
         in_specs=[
-            by_rows(pre_grad, size),
-            by_rows(feat_left, size),
-            by_rows(feat_right, size),
-            pl.BlockSpec((size, B, chan), lambda i: (jnp.minimum(i, mid - 1), 0, 0)),
-            pl.BlockSpec((size, B, chan), lambda i: (jnp.maximum(i - mid, 0), 0, 0)),
+            by_rows(pre_grad, gsize),
+            by_rows(feat_left, gsize),
+            by_rows(feat_right, gsize),
+            pl.BlockSpec((gsize, B, chan), lambda i: (jnp.minimum(i, mid - 1), 0, 0)),
+            pl.BlockSpec((gsize, B, chan), lambda i: (jnp.maximum(i - mid, 0), 0, 0)),
             whole(disparity),
             whole(mw16),
         ],
         out_specs=[
-            by_rows(feat_shape, size),
-            block((size, B, chan), 0, 0, 0),
-            by_rows(near_shape, size),
+            by_rows(feat_shape, gsize),
+            block((gsize, B, chan), 0, 0, 0),
+            by_rows(near_shape, gsize),
         ],
         out_shape=(feat_shape, feat_shape, near_shape),
         scratch_shapes=[pltpu.VMEM((B, B), BF16)],
@@ -739,15 +743,15 @@
     )(pre_grad, feat_left, feat_right, before[0], before[1], disparity, mw16)
     grad_right = pl.pallas_call(
         lambda *refs: last_kernel(*args, *refs),
-        grid=(steps,),
+        grid=(gsteps,),
         in_specs=[
-            by_rows(near, size),
-            by_rows(next_grad, size),
-            block((size, B, chan), 0, 1, 0),
-            by_rows(next_left, size),
+            by_rows(near, gsize),
+            by_rows(next_grad, gsize),
+            block((gsize, B, chan), 0, 1, 0),
+            by_rows(next_left, gsize),
             anywhere,
         ],
-        out_specs=block((size, B, chan), 0, 1, 0),
+        out_specs=block((gsize, B, chan), 0, 1, 0),
         out_shape=feat_shape,
         input_output_aliases={4: 0},
         compiler_params=params,

time: 97.1 us -> 91.5 us (0.942)
  the two profiles are of different devices: /device:TPU:49 before, /device:TPU:120 now
where the time goes in v8:
time: 91.5 us; the launch traced here: 91 us
  Pallas kernels  47.4 us (52%)
  starting transfers between devices  33.7 us (37%)
  waiting for transfers between devices  8.8 us (10%)
    ppermute x10, starting transfers between devices, shift(): return lax.ppermute(array, axis, pairs)  33.7 us
    pallas_call x1, Pallas kernels, per_device(): pl.pallas_call(gru_kernel, in_specs=[vmem] * len(operands), out_specs=[vm...  24 us
    ppermute x10, waiting for transfers between devices, shift(): return lax.ppermute(array, axis, pairs)  8.8 us
    pallas_call x1, Pallas kernels, per_device(): pl.pallas_call(lambda *refs: grads_kernel(*args, *refs), grid=(gsteps,),...  6.35 us
    pallas_call x2, Pallas kernels, left_lookup(): pl.pallas_call(lambda *refs: left_corr_kernel(*args, start, rim_step, *re...  4.85 us
    pallas_call x1, Pallas kernels, per_device(): pl.pallas_call(lambda *refs: right_corr_kernel(*args, *refs), grid=(steps...  4.76 us
    pallas_call x1, Pallas kernels, per_device(): pl.pallas_call(gates_hidden_kernel, in_specs=[vmem] * len(hid_operands),...  3.38 us
    pallas_call x1, Pallas kernels, per_device(): pl.pallas_call(pack_small_kernel, grid=(1,), in_specs=[block((rows, 8, ch...  2.04 us
  transfers between devices with their start and end apart: 10, of which 4 were waited for; matrix products, arithmetic and copies ran while one was open for 0% of the time, Pallas kernels for 48%

profile of v8, /device:TPU:120, one launch (start us, length us, event | category | flops | bytes accessed | tf_op | source)
XLA Modules:
  0.0 91.0 jit_solution(17553093705948402507)
XLA Ops:
  0.6 0.0 copy-start.1
  0.6 2.0 %pack_small.1 = (bf16[16,4,896]{2,1,0:T(4,128)(2,1)}, bf16[16,16,256]{2,1,0:T(8,128)(2,1)}) custom-call(bf16[16,256,256]{2,1,0:T(8,128)(2,1)} %refs_2_.5, bf16[16,256,256]{2,1,0:T(8,128)(2,1)} %refs_2_.4, bf16[16,256,128]{2,1,0:T(8,128)(2,1)} %hid_ref.5, bf16[16,256,128]{2,1,0:T(8,128)(2,1)} %grad_ref.3, bf16[16,256,256]{2,1,0:T(8,128)(2,1)} %refs_2_.4, ...), custom_call_target="tpu_custom_call" | custom-call | flops 65536 | bytes 262144 | tf_op jit(solution)/shard_map/pack_small/pallas_call | solution.py:536
  2.7 0.0 copy-start.2
  2.7 0.0 copy-start.3
  2.7 5.1 %collective-permute-start.1 = (bf16[16,16,256]{2,1,0:T(8,128)(2,1)}, bf16[16,16,256]{2,1,0:T(8,128)(2,1)S(1)}, u32[]{:S(2)}, u32[]{:S(2)}) collective-permute-start(bf16[16,16,256]{2,1,0:T(8,128)(2,1)} %get-tuple-element.32), channel_id=1, source_target_pairs={{0,1},{1,2},{2,3},{3,4},{4,5},{5,6},{6,7},{8,9},{9,10},{10,11},{11... | collective-permute-start | bytes 393224 | tf_op jit(solution)/shard_map/ppermute | solution.py:26
  7.7 3.3 %collective-permute-start = (bf16[16,4,896]{2,1,0:T(4,128)(2,1)}, bf16[16,4,896]{2,1,0:T(4,128)(2,1)S(1)}, u32[]{:S(2)}, u32[]{:S(2)}) collective-permute-start(bf16[16,4,896]{2,1,0:T(4,128)(2,1)} %get-tuple-element.31), channel_id=1, source_target_pairs={{1,0},{2,1},{3,2},{4,3},{5,4},{6,5},{7,6},{9,8},{10,9},{11,10},{12... | collective-permute-start | bytes 344072 | tf_op jit(solution)/shard_map/ppermute | solution.py:26
  11.1 0.0 copy-done.1
  11.1 0.1 fusion
  11.1 4.0 %collective-permute-start.4 = (bf16[8,128,256]{2,1,0:T(8,128)(2,1)S(1)}, bf16[8,128,256]{2,1,0:T(8,128)(2,1)S(1)}, u32[]{:S(2)}, u32[]{:S(2)}) collective-permute-start(bf16[8,128,256]{2,1,0:T(8,128)(2,1)S(1)} %get-tuple-element.59), channel_id=1, source_target_pairs={{0,1},{1,2},{2,3},{3,4},{4,5},{5,6},{6,7},{8,9},{9,10},{10,11},{11... | collective-permute-start | bytes 1572872 | tf_op jit(solution)/shard_map/ppermute | solution.py:26
  15.2 0.9 %collective-permute-done.right_ref.refs_3_ = bf16[16,4,896]{2,1,0:T(4,128)(2,1)S(1)} collective-permute-done((bf16[16,4,896]{2,1,0:T(4,128)(2,1)}, bf16[16,4,896]{2,1,0:T(4,128)(2,1)S(1)}, u32[]{:S(2)}, u32[]{:S(2)}) %collective-permute-start) | collective-permute-done | bytes 114720 | tf_op jit(solution)/shard_map/ppermute | solution.py:26
  16.1 0.0 collective-permute-done.1.left_ref.refs_3_
  16.1 0.0 copy-start
  16.1 2.0 %collective-permute-start.5 = (bf16[8,128,256]{2,1,0:T(8,128)(2,1)S(1)}, bf16[8,128,256]{2,1,0:T(8,128)(2,1)S(1)}, u32[]{:S(2)}, u32[]{:S(2)}) collective-permute-start(bf16[8,128,256]{2,1,0:T(8,128)(2,1)S(1)} %get-tuple-element.40), channel_id=1, source_target_pairs={{0,1},{1,2},{2,3},{3,4},{4,5},{5,6},{6,7},{8,9},{9,10},{10,11},{11... | collective-permute-start | bytes 1572872 | tf_op jit(solution)/shard_map/ppermute | solution.py:26
  18.2 0.0 copy-done.2
  18.2 0.0 copy-done.3
  18.2 0.1 rims.1
  18.4 0.0 copy-start.7
  18.4 0.0 copy-start.4
  18.4 2.1 %collective-permute-start.2 = (bf16[6,272,128]{2,1,0:T(8,128)(2,1)S(1)}, bf16[6,272,128]{2,1,0:T(8,128)(2,1)S(1)}, u32[]{:S(2)}, u32[]{:S(2)}) collective-permute-start(bf16[6,272,128]{2,1,0:T(8,128)(2,1)S(1)} %get-tuple-element.35), channel_id=1, source_target_pairs={{0,8},{8,16},{16,24},{24,32},{32,40},{40,48},{48,56},{56,64},{64,7... | collective-permute-start | bytes 1253384 | tf_op jit(solution)/shard_map/ppermute | solution.py:26
  20.4 4.5 %collective-permute-start.3 = (bf16[6,272,128]{2,1,0:T(8,128)(2,1)S(1)}, bf16[6,272,128]{2,1,0:T(8,128)(2,1)S(1)}, u32[]{:S(2)}, u32[]{:S(2)}) collective-permute-start(bf16[6,272,128]{2,1,0:T(8,128)(2,1)S(1)} %get-tuple-element.36), channel_id=1, source_target_pairs={{8,0},{16,8},{24,16},{32,24},{40,32},{48,40},{56,48},{64,56},{72,6... | collective-permute-start | bytes 1253384 | tf_op jit(solution)/shard_map/ppermute | solution.py:26
  25.0 0.0 copy-done
  25.0 0.1 slice.14
  25.1 0.0 copy-done.7
  25.1 0.0 copy-done.4
  25.1 4.8 %corr_right.1 = (bf16[16,144,128]{2,1,0:T(8,128)(2,1)S(1)}, f32[16,128,128]{2,1,0:T(8,128)S(1)}) custom-call(bf16[16,256,256]{2,1,0:T(8,128)(2,1)S(1)} %copy-done, bf16[16,256,256]{2,1,0:T(8,128)(2,1)S(1)} %copy-done.1, s32[16,256]{1,0:T(8,128)S(1)} %copy-done.4, bf16[16,4,896]{2,1,0:T(4,128)(2,1)S(1)} %collective-permute-done.right_ref.refs_3_, ...), custom_call_target="tpu_custom_call" | custom-call | flops 268435456 | bytes 6291456 | tf_op jit(solution)/shard_map/corr_right/pallas_call | solution.py:600
  29.9 0.4 collective-permute-done.4.refs_2_.refs_3_
  30.3 2.4 %corr_left.2 = (bf16[8,272,128]{2,1,0:T(8,128)(2,1)S(1)}, f32[8,128,128]{2,1,0:T(8,128)S(1)}, bf16[4,272,128]{2,1,0:T(8,128)(2,1)S(1)}) custom-call(bf16[16,256,256]{2,1,0:T(8,128)(2,1)S(1)} %copy-done, bf16[16,256,256]{2,1,0:T(8,128)(2,1)S(1)} %copy-done.1, bf16[8,128,256]{2,1,0:T(8,128)(2,1)S(1)} %collective-permute-done.4.refs_2_.refs_3_, ...), custom_call_target="tpu_custom_call" | custom-call | flops 134217728 | bytes 3145728 | tf_op jit(solution)/shard_map/corr_left/pallas_call | solution.py:625
  32.7 0.0 copy-start.5
  32.8 0.0 copy-start.6
  32.8 2.1 %collective-permute-start.7 = (bf16[4,272,128]{2,1,0:T(8,128)(2,1)S(1)}, bf16[4,272,128]{2,1,0:T(8,128)(2,1)S(1)}, u32[]{:S(2)}, u32[]{:S(2)}) collective-permute-start(bf16[4,272,128]{2,1,0:T(8,128)(2,1)S(1)} %get-tuple-element.43), channel_id=1, source_target_pairs={{8,0},{16,8},{24,16},{32,24},{40,32},{48,40},{56,48},{64,56},{72,6... | collective-permute-start | bytes 835592 | tf_op jit(solution)/shard_map/ppermute | solution.py:26
  34.8 6.7 %collective-permute-done.5.refs_2_.refs_4_ = bf16[8,128,256]{2,1,0:T(8,128)(2,1)S(1)} collective-permute-done((bf16[8,128,256]{2,1,0:T(8,128)(2,1)S(1)}, bf16[8,128,256]{2,1,0:T(8,128)(2,1)S(1)}, u32[]{:S(2)}, u32[]{:S(2)}) %collective-permute-start.5) | collective-permute-done | bytes 524320 | tf_op jit(solution)/shard_map/ppermute | solution.py:26
  41.5 2.4 %corr_left.3 = (bf16[8,272,128]{2,1,0:T(8,128)(2,1)S(1)}, f32[8,128,128]{2,1,0:T(8,128)S(1)}, bf16[4,272,128]{2,1,0:T(8,128)(2,1)S(1)}) custom-call(bf16[16,256,256]{2,1,0:T(8,128)(2,1)S(1)} %copy-done, bf16[16,256,256]{2,1,0:T(8,128)(2,1)S(1)} %copy-done.1, bf16[8,128,256]{2,1,0:T(8,128)(2,1)S(1)} %collective-permute-done.5.refs_2_.refs_4_, ...), custom_call_target="tpu_custom_call" | custom-call | flops 134217728 | bytes 3145728 | tf_op jit(solution)/shard_map/corr_left/pallas_call | solution.py:625
  44.0 1.9 %collective-permute-start.6 = (bf16[4,272,128]{2,1,0:T(8,128)(2,1)S(1)}, bf16[4,272,128]{2,1,0:T(8,128)(2,1)S(1)}, u32[]{:S(2)}, u32[]{:S(2)}) collective-permute-start(bf16[4,272,128]{2,1,0:T(8,128)(2,1)S(1)} %get-tuple-element.42), channel_id=1, source_target_pairs={{0,8},{8,16},{16,24},{24,32},{32,40},{40,48},{48,56},{56,64},{64,7... | collective-permute-start | bytes 835592 | tf_op jit(solution)/shard_map/ppermute | solution.py:26
  45.9 0.0 copy-done.5
  45.9 0.0 copy-done.6
  45.9 3.4 %gates_hidden.1 = (f32[14,272,256]{2,1,0:T(8,128)S(1)}, bf16[1152,256]{1,0:T(8,128)(2,1)S(1)}, bf16[3072,256]{1,0:T(8,128)(2,1)S(1)}, bf16[256,1152]{1,0:T(8,128)(2,1)S(1)}, bf16[256,3072]{1,0:T(8,128)(2,1)S(1)}) custom-call(bf16[16,256,128]{2,1,0:T(8,128)(2,1)S(1)} %copy-done.2, bf16[16,16,256]{2,1,0:T(8,128)(2,1)S(1)} %get-tuple-element.37.edge_ref, ...), custom_call_target="tpu_custom_call" | custom-call | flops 3529506816 | bytes 16777216 | tf_op jit(solution)/shard_map/gates_hidden/pallas_call | solution.py:664
  49.3 3.2 %collective-permute-start.9 = (bf16[16,128,256]{2,1,0:T(8,128)(2,1)S(1)}, bf16[16,128,256]{2,1,0:T(8,128)(2,1)S(1)}, u32[]{:S(2)}, u32[]{:S(2)}) collective-permute-start(bf16[16,128,256]{2,1,0:T(8,128)(2,1)S(1)} %slice.14), channel_id=1, source_target_pairs={{1,0},{2,1},{3,2},{4,3},{5,4},{6,5},{7,6},{9,8},{10,9},{11,10},{12... | collective-permute-start | bytes 3145736 | tf_op jit(solution)/shard_map/ppermute | solution.py:26
  52.5 0.0 collective-permute-done.2.hgt_ref
  52.5 0.0 collective-permute-done.3.hgb_ref
  52.5 0.0 collective-permute-done.7.motl_ref
  52.5 0.7 collective-permute-done.6.mott_ref
  53.2 24.0 %gru.1 = (bf16[16,256,128]{2,1,0:T(8,128)(2,1)}, bf16[16,256,128]{2,1,0:T(8,128)(2,1)S(1)}, bf16[16,16,128]{2,1,0:T(8,128)(2,1)S(1)}) custom-call(bf16[16,256,128]{2,1,0:T(8,128)(2,1)S(1)} %copy-done.2, bf16[16,256,128]{2,1,0:T(8,128)(2,1)S(1)} %copy-done.3, bf16[6,272,128]{2,1,0:T(8,128)(2,1)S(1)} %collective-permute-done.2.hgt_ref, ...), custom_call_target="tpu_custom_call" | custom-call | flops 15686696960 | bytes 16777216 | tf_op jit(solution)/shard_map/gru/pallas_call | solution.py:702
  77.1 5.6 %collective-permute-start.8 = (bf16[16,16,128]{2,1,0:T(8,128)(2,1)S(1)}, bf16[16,16,128]{2,1,0:T(8,128)(2,1)S(1)}, u32[]{:S(2)}, u32[]{:S(2)}) collective-permute-start(bf16[16,16,128]{2,1,0:T(8,128)(2,1)S(1)} %get-tuple-element.56), channel_id=1, source_target_pairs={{1,0},{2,1},{3,2},{4,3},{5,4},{6,5},{7,6},{9,8},{10,9},{11,10},{12... | collective-permute-start | bytes 196616 | tf_op jit(solution)/shard_map/ppermute | solution.py:26
  82.7 6.3 %grads.1 = (bf16[16,256,256]{2,1,0:T(8,128)(2,1)}, bf16[16,256,256]{2,1,0:T(8,128)(2,1)}, bf16[16,128,128]{2,1,0:T(8,128)(2,1)S(1)}) custom-call(bf16[16,256,128]{2,1,0:T(8,128)(2,1)S(1)} %get-tuple-element.53.refs_0_, bf16[16,256,256]{2,1,0:T(8,128)(2,1)S(1)} %copy-done, bf16[16,256,256]{2,1,0:T(8,128)(2,1)S(1)} %copy-done.1, ...), custom_call_target="tpu_custom_call" | custom-call | flops 1073741824 | bytes 12582912 | tf_op jit(solution)/shard_map/grads/pallas_call | solution.py:721
  89.1 0.0 collective-permute-done.8.refs_1_
  89.1 0.0 collective-permute-done.9.refs_3_
  89.1 2.0 %grad_right.1 = bf16[16,256,256]{2,1,0:T(8,128)(2,1)} custom-call(bf16[16,128,128]{2,1,0:T(8,128)(2,1)S(1)} %get-tuple-element.55.refs_0_, bf16[16,16,128]{2,1,0:T(8,128)(2,1)S(1)} %collective-permute-done.8.refs_1_, bf16[16,256,256]{2,1,0:T(8,128)(2,1)S(1)} %copy-done, ...), custom_call_target="tpu_custom_call", output_to_operand_aliasing={{}: (4, {})} | custom-call | flops 268435456 | bytes 4194304 | tf_op jit(solution)/shard_map/grad_right/pallas_call | solution.py:744
  (1 shorter events, 0.0 us)
Async XLA Ops:
  0.6 10.4 %copy-start.1 = (bf16[16,256,256]{2,1,0:T(8,128)(2,1)S(1)}, bf16[16,256,256]{2,1,0:T(8,128)(2,1)}, u32[]{:S(2)}) copy-start(bf16[16,256,256]{2,1,0:T(8,128)(2,1)} %refs_2_.4) | copy-start | bytes 6291460
  2.7 15.5 %copy-start.2 = (bf16[16,256,128]{2,1,0:T(8,128)(2,1)S(1)}, bf16[16,256,128]{2,1,0:T(8,128)(2,1)}, u32[]{:S(2)}) copy-start(bf16[16,256,128]{2,1,0:T(8,128)(2,1)} %hid_ref.5) | copy-start | bytes 3145732
  2.7 15.5 %copy-start.3 = (bf16[16,256,128]{2,1,0:T(8,128)(2,1)S(1)}, bf16[16,256,128]{2,1,0:T(8,128)(2,1)}, u32[]{:S(2)}) copy-start(bf16[16,256,128]{2,1,0:T(8,128)(2,1)} %grad_ref.3) | copy-start | bytes 3145732
  2.7 13.5 %collective-permute-start.1 = (bf16[16,16,256]{2,1,0:T(8,128)(2,1)}, bf16[16,16,256]{2,1,0:T(8,128)(2,1)S(1)}, u32[]{:S(2)}, u32[]{:S(2)}) collective-permute-start(bf16[16,16,256]{2,1,0:T(8,128)(2,1)} %get-tuple-element.32), channel_id=1, source_target_pairs={{0,1},{1,2},{2,3},{3,4},{4,5},{5,6},{6,7},{8,9},{9,10},{10,11},{11... | collective-permute-start | bytes 393224 | tf_op jit(solution)/shard_map/ppermute | solution.py:26
  7.7 8.4 %collective-permute-start = (bf16[16,4,896]{2,1,0:T(4,128)(2,1)}, bf16[16,4,896]{2,1,0:T(4,128)(2,1)S(1)}, u32[]{:S(2)}, u32[]{:S(2)}) collective-permute-start(bf16[16,4,896]{2,1,0:T(4,128)(2,1)} %get-tuple-element.31), channel_id=1, source_target_pairs={{1,0},{2,1},{3,2},{4,3},{5,4},{6,5},{7,6},{9,8},{10,9},{11,10},{12... | collective-permute-start | bytes 344072 | tf_op jit(solution)/shard_map/ppermute | solution.py:26
  11.1 19.2 %collective-permute-start.4 = (bf16[8,128,256]{2,1,0:T(8,128)(2,1)S(1)}, bf16[8,128,256]{2,1,0:T(8,128)(2,1)S(1)}, u32[]{:S(2)}, u32[]{:S(2)}) collective-permute-start(bf16[8,128,256]{2,1,0:T(8,128)(2,1)S(1)} %get-tuple-element.59), channel_id=1, source_target_pairs={{0,1},{1,2},{2,3},{3,4},{4,5},{5,6},{6,7},{8,9},{9,10},{10,11},{11... | collective-permute-start | bytes 1572872 | tf_op jit(solution)/shard_map/ppermute | solution.py:26
  16.1 8.8 %copy-start = (bf16[16,256,256]{2,1,0:T(8,128)(2,1)S(1)}, bf16[16,256,256]{2,1,0:T(8,128)(2,1)}, u32[]{:S(2)}) copy-start(bf16[16,256,256]{2,1,0:T(8,128)(2,1)} %refs_2_.5) | copy-start | bytes 6291460
  16.1 25.4 %collective-permute-start.5 = (bf16[8,128,256]{2,1,0:T(8,128)(2,1)S(1)}, bf16[8,128,256]{2,1,0:T(8,128)(2,1)S(1)}, u32[]{:S(2)}, u32[]{:S(2)}) collective-permute-start(bf16[8,128,256]{2,1,0:T(8,128)(2,1)S(1)} %get-tuple-element.40), channel_id=1, source_target_pairs={{0,1},{1,2},{2,3},{3,4},{4,5},{5,6},{6,7},{8,9},{9,10},{10,11},{11... | collective-permute-start | bytes 1572872 | tf_op jit(solution)/shard_map/ppermute | solution.py:26
  18.4 6.7 %copy-start.7 = (bf16[9,128]{1,0:T(8,128)(2,1)S(1)}, bf16[9,128]{1,0:T(8,128)(2,1)}, u32[]{:S(2)}) copy-start(bf16[9,128]{1,0:T(8,128)(2,1)} %param.12) | copy-start | bytes 6916
  18.4 6.7 %copy-start.4 = (s32[16,256]{1,0:T(8,128)S(1)}, s32[16,256]{1,0:T(8,128)}, u32[]{:S(2)}) copy-start(s32[16,256]{1,0:T(8,128)} %refs_5_.1) | copy-start | bytes 49156
  18.4 34.1 %collective-permute-start.2 = (bf16[6,272,128]{2,1,0:T(8,128)(2,1)S(1)}, bf16[6,272,128]{2,1,0:T(8,128)(2,1)S(1)}, u32[]{:S(2)}, u32[]{:S(2)}) collective-permute-start(bf16[6,272,128]{2,1,0:T(8,128)(2,1)S(1)} %get-tuple-element.35), channel_id=1, source_target_pairs={{0,8},{8,16},{16,24},{24,32},{32,40},{40,48},{48,56},{56,64},{64,7... | collective-permute-start | bytes 1253384 | tf_op jit(solution)/shard_map/ppermute | solution.py:26
  20.4 32.1 %collective-permute-start.3 = (bf16[6,272,128]{2,1,0:T(8,128)(2,1)S(1)}, bf16[6,272,128]{2,1,0:T(8,128)(2,1)S(1)}, u32[]{:S(2)}, u32[]{:S(2)}) collective-permute-start(bf16[6,272,128]{2,1,0:T(8,128)(2,1)S(1)} %get-tuple-element.36), channel_id=1, source_target_pairs={{8,0},{16,8},{24,16},{32,24},{40,32},{48,40},{56,48},{64,56},{72,6... | collective-permute-start | bytes 1253384 | tf_op jit(solution)/shard_map/ppermute | solution.py:26
  32.7 13.2 %copy-start.5 = (bf16[3,3,256,256]{3,2,1,0:T(8,128)(2,1)S(1)}, bf16[3,3,256,256]{3,2,1,0:T(8,128)(2,1)}, u32[]{:S(2)}) copy-start(bf16[3,3,256,256]{3,2,1,0:T(8,128)(2,1)} %param.13) | copy-start | bytes 3538948
  32.8 13.2 %copy-start.6 = (bf16[3,3,256,128]{3,2,1,0:T(8,128)(2,1)S(1)}, bf16[3,3,256,128]{3,2,1,0:T(8,128)(2,1)}, u32[]{:S(2)}) copy-start(bf16[3,3,256,128]{3,2,1,0:T(8,128)(2,1)} %param.14) | copy-start | bytes 1769476
  32.8 19.7 %collective-permute-start.7 = (bf16[4,272,128]{2,1,0:T(8,128)(2,1)S(1)}, bf16[4,272,128]{2,1,0:T(8,128)(2,1)S(1)}, u32[]{:S(2)}, u32[]{:S(2)}) collective-permute-start(bf16[4,272,128]{2,1,0:T(8,128)(2,1)S(1)} %get-tuple-element.43), channel_id=1, source_target_pairs={{8,0},{16,8},{24,16},{32,24},{40,32},{48,40},{56,48},{64,56},{72,6... | collective-permute-start | bytes 835592 | tf_op jit(solution)/shard_map/ppermute | solution.py:26
  44.0 9.2 %collective-permute-start.6 = (bf16[4,272,128]{2,1,0:T(8,128)(2,1)S(1)}, bf16[4,272,128]{2,1,0:T(8,128)(2,1)S(1)}, u32[]{:S(2)}, u32[]{:S(2)}) collective-permute-start(bf16[4,272,128]{2,1,0:T(8,128)(2,1)S(1)} %get-tuple-element.42), channel_id=1, source_target_pairs={{0,8},{8,16},{16,24},{24,32},{32,40},{40,48},{48,56},{56,64},{64,7... | collective-permute-start | bytes 835592 | tf_op jit(solution)/shard_map/ppermute | solution.py:26
  49.3 39.8 %collective-permute-start.9 = (bf16[16,128,256]{2,1,0:T(8,128)(2,1)S(1)}, bf16[16,128,256]{2,1,0:T(8,128)(2,1)S(1)}, u32[]{:S(2)}, u32[]{:S(2)}) collective-permute-start(bf16[16,128,256]{2,1,0:T(8,128)(2,1)S(1)} %slice.14), channel_id=1, source_target_pairs={{1,0},{2,1},{3,2},{4,3},{5,4},{6,5},{7,6},{9,8},{10,9},{11,10},{12... | collective-permute-start | bytes 3145736 | tf_op jit(solution)/shard_map/ppermute | solution.py:26
  77.1 11.9 %collective-permute-start.8 = (bf16[16,16,128]{2,1,0:T(8,128)(2,1)S(1)}, bf16[16,16,128]{2,1,0:T(8,128)(2,1)S(1)}, u32[]{:S(2)}, u32[]{:S(2)}) collective-permute-start(bf16[16,16,128]{2,1,0:T(8,128)(2,1)S(1)} %get-tuple-element.56), channel_id=1, source_target_pairs={{1,0},{2,1},{3,2},{4,3},{5,4},{6,5},{7,6},{9,8},{10,9},{11,10},{12... | collective-permute-start | bytes 196616 | tf_op jit(solution)/shard_map/ppermute | solution.py:26

commit v9 on v8

--- a/solution.py
+++ b/solution.py
@@ -184,7 +184,7 @@
     radius,
     scale,
     start,
-    rim_step,
+    rim_at,
     left_ref,
     own_ref,
     before_ref,
@@ -199,8 +199,7 @@
     mw_ref,
 ):
     rows, _, chan = own_ref.shape
-    step = pl.program_id(0)
-    first = start + step * rows
+    first = start
     pad_ref[...] = jnp.zeros_like(pad_ref)
     weight = taps_matrix(weight_ref, mw_ref)
     last = iota((EDGE, chan), 0) >= EDGE - HALO
@@ -225,9 +224,7 @@
         right_edge = mot_right_ref[r, B:].astype(F32)
         mot_ref[r, 2 * B :] = jnp.where(upper, right_edge, mot[B:]).astype(BF16)
 
-    @pl.when(step == rim_step)
-    def _():
-        rim_ref[...] = mot_ref[...]
+    rim_ref[...] = mot_ref[rim_at : rim_at + HALO]
 
 
 def shifted(value):
@@ -615,28 +612,28 @@
         name="corr_right",
     )(feat_left, feat_right, disparity, from_right, mw16)
 
-    def left_lookup(start, before, rim_step):
-        at = start // size
+    def left_lookup(start, before, rim_at):
+        at = start // half
         shapes = (
             shape((half, wide, B), BF16),
             shape((half, B, B), F32),
             shape((HALO, wide, B), BF16),
         )
         return pl.pallas_call(
-            lambda *refs: left_corr_kernel(*args, start, rim_step, *refs),
-            grid=(half // size,),
+            lambda *refs: left_corr_kernel(*args, start, rim_at, *refs),
+            grid=(1,),
             in_specs=[
-                block((size, B, chan), at, 0, 0),
-                block((size, B, chan), at, 0, 0),
-                by_rows(before, size),
-                block((size, EDGE, chan), at, 0, 0),
+                block((half, B, chan), at, 0, 0),
+                block((half, B, chan), at, 0, 0),
+                by_rows(before, half),
+                block((half, EDGE, chan), at, 0, 0),
                 whole(disparity),
-                block((size, B + EDGE, B), at, 0, 0),
+                block((half, B + EDGE, B), at, 0, 0),
                 whole(mw16),
             ],
-            out_specs=[by_rows(s, size) for s in shapes[:2]] + [whole(shapes[2])],
+            out_specs=[by_rows(s, half) for s in shapes[:2]] + [whole(shapes[2])],
             out_shape=shapes,
-            scratch_shapes=pads,
+            scratch_shapes=[pltpu.VMEM((half, B, chan), BF16), pads[1]],
             compiler_params=params,
             cost_estimate=cost(rows * B * 2 * B * chan, 3 << 20),
             name="corr_left",
@@ -644,7 +641,7 @@
 
     mot_a, pre_a, rim_a = left_lookup(0, before[0], 0)
     mot_low = shift(rim_a, "rows", -1)
-    mot_b, pre_b, rim_b = left_lookup(half, before[1], half // size - 1)
+    mot_b, pre_b, rim_b = left_lookup(half, before[1], half - HALO)
     mot_top = shift(rim_b, "rows", 1)
     first_left, _ = lax.optimization_barrier((feat_left[:, :B], mot_b))
     next_left = shift(first_left, "cols", -1)

time: 91.5 us -> 91.8 us (level)
  transfers between devices with their start and end apart: 10 -> 10, of which waited for: 4 -> 4; matrix products, arithmetic and copies ran while one was open for 0% -> 0% of each run, Pallas kernels for 48% -> 47%
where the time goes in v9:
time: 91.8 us; the launch traced here: 90.8 us
  Pallas kernels  47 us (51%)
  starting transfers between devices  33.5 us (36%)
  waiting for transfers between devices  9.21 us (10%)
    ppermute x10, starting transfers between devices, shift(): return lax.ppermute(array, axis, pairs)  33.5 us
    pallas_call x1, Pallas kernels, per_device(): pl.pallas_call(gru_kernel, in_specs=[vmem] * len(operands), out_specs=[vm...  24 us
    ppermute x10, waiting for transfers between devices, shift(): return lax.ppermute(array, axis, pairs)  9.21 us
    pallas_call x1, Pallas kernels, per_device(): pl.pallas_call(lambda *refs: grads_kernel(*args, *refs), grid=(gsteps,),...  6.34 us
    pallas_call x1, Pallas kernels, per_device(): pl.pallas_call(lambda *refs: right_corr_kernel(*args, *refs), grid=(steps...  4.76 us
    pallas_call x2, Pallas kernels, left_lookup(): pl.pallas_call(lambda *refs: left_corr_kernel(*args, start, rim_at, *refs...  4.44 us
    pallas_call x1, Pallas kernels, per_device(): pl.pallas_call(gates_hidden_kernel, in_specs=[vmem] * len(hid_operands),...  3.38 us
    pallas_call x1, Pallas kernels, per_device(): pl.pallas_call(pack_small_kernel, grid=(1,), in_specs=[block((rows, 8, ch...  2.04 us
  transfers between devices with their start and end apart: 10, of which 4 were waited for; matrix products, arithmetic and copies ran while one was open for 0% of the time, Pallas kernels for 47%

profile of v9, /device:TPU:120, one launch (start us, length us, event | category | flops | bytes accessed | tf_op | source)
XLA Modules:
  0.0 90.8 jit_solution(1333456716181738985)
XLA Ops:
  0.6 0.0 copy-start.1
  0.6 2.0 %pack_small.1 = (bf16[16,4,896]{2,1,0:T(4,128)(2,1)}, bf16[16,16,256]{2,1,0:T(8,128)(2,1)}) custom-call(bf16[16,256,256]{2,1,0:T(8,128)(2,1)} %refs_2_.5, bf16[16,256,256]{2,1,0:T(8,128)(2,1)} %refs_2_.4, bf16[16,256,128]{2,1,0:T(8,128)(2,1)} %hid_ref.5, bf16[16,256,128]{2,1,0:T(8,128)(2,1)} %grad_ref.3, bf16[16,256,256]{2,1,0:T(8,128)(2,1)} %refs_2_.4, ...), custom_call_target="tpu_custom_call" | custom-call | flops 65536 | bytes 262144 | tf_op jit(solution)/shard_map/pack_small/pallas_call | solution.py:533
  2.7 0.0 copy-start.2
  2.7 0.0 copy-start.3
  2.7 5.1 %collective-permute-start.1 = (bf16[16,16,256]{2,1,0:T(8,128)(2,1)}, bf16[16,16,256]{2,1,0:T(8,128)(2,1)S(1)}, u32[]{:S(2)}, u32[]{:S(2)}) collective-permute-start(bf16[16,16,256]{2,1,0:T(8,128)(2,1)} %get-tuple-element.32), channel_id=1, source_target_pairs={{0,1},{1,2},{2,3},{3,4},{4,5},{5,6},{6,7},{8,9},{9,10},{10,11},{11... | collective-permute-start | bytes 393224 | tf_op jit(solution)/shard_map/ppermute | solution.py:26
  7.7 3.3 %collective-permute-start = (bf16[16,4,896]{2,1,0:T(4,128)(2,1)}, bf16[16,4,896]{2,1,0:T(4,128)(2,1)S(1)}, u32[]{:S(2)}, u32[]{:S(2)}) collective-permute-start(bf16[16,4,896]{2,1,0:T(4,128)(2,1)} %get-tuple-element.31), channel_id=1, source_target_pairs={{1,0},{2,1},{3,2},{4,3},{5,4},{6,5},{7,6},{9,8},{10,9},{11,10},{12... | collective-permute-start | bytes 344072 | tf_op jit(solution)/shard_map/ppermute | solution.py:26
  11.1 0.0 copy-done.1
  11.1 0.1 fusion
  11.1 4.0 %collective-permute-start.4 = (bf16[8,128,256]{2,1,0:T(8,128)(2,1)S(1)}, bf16[8,128,256]{2,1,0:T(8,128)(2,1)S(1)}, u32[]{:S(2)}, u32[]{:S(2)}) collective-permute-start(bf16[8,128,256]{2,1,0:T(8,128)(2,1)S(1)} %get-tuple-element.59), channel_id=1, source_target_pairs={{0,1},{1,2},{2,3},{3,4},{4,5},{5,6},{6,7},{8,9},{9,10},{10,11},{11... | collective-permute-start | bytes 1572872 | tf_op jit(solution)/shard_map/ppermute | solution.py:26
  15.2 0.9 %collective-permute-done.right_ref.refs_3_ = bf16[16,4,896]{2,1,0:T(4,128)(2,1)S(1)} collective-permute-done((bf16[16,4,896]{2,1,0:T(4,128)(2,1)}, bf16[16,4,896]{2,1,0:T(4,128)(2,1)S(1)}, u32[]{:S(2)}, u32[]{:S(2)}) %collective-permute-start) | collective-permute-done | bytes 114720 | tf_op jit(solution)/shard_map/ppermute | solution.py:26
  16.1 0.0 collective-permute-done.1.left_ref.refs_3_
  16.1 0.0 copy-start
  16.1 2.0 %collective-permute-start.5 = (bf16[8,128,256]{2,1,0:T(8,128)(2,1)S(1)}, bf16[8,128,256]{2,1,0:T(8,128)(2,1)S(1)}, u32[]{:S(2)}, u32[]{:S(2)}) collective-permute-start(bf16[8,128,256]{2,1,0:T(8,128)(2,1)S(1)} %get-tuple-element.40), channel_id=1, source_target_pairs={{0,1},{1,2},{2,3},{3,4},{4,5},{5,6},{6,7},{8,9},{9,10},{10,11},{11... | collective-permute-start | bytes 1572872 | tf_op jit(solution)/shard_map/ppermute | solution.py:26
  18.2 0.0 copy-done.2
  18.2 0.0 copy-done.3
  18.2 0.1 rims.1
  18.4 0.0 copy-start.7
  18.4 0.0 copy-start.4
  18.4 2.1 %collective-permute-start.2 = (bf16[6,272,128]{2,1,0:T(8,128)(2,1)S(1)}, bf16[6,272,128]{2,1,0:T(8,128)(2,1)S(1)}, u32[]{:S(2)}, u32[]{:S(2)}) collective-permute-start(bf16[6,272,128]{2,1,0:T(8,128)(2,1)S(1)} %get-tuple-element.35), channel_id=1, source_target_pairs={{0,8},{8,16},{16,24},{24,32},{32,40},{40,48},{48,56},{56,64},{64,7... | collective-permute-start | bytes 1253384 | tf_op jit(solution)/shard_map/ppermute | solution.py:26
  20.4 4.5 %collective-permute-start.3 = (bf16[6,272,128]{2,1,0:T(8,128)(2,1)S(1)}, bf16[6,272,128]{2,1,0:T(8,128)(2,1)S(1)}, u32[]{:S(2)}, u32[]{:S(2)}) collective-permute-start(bf16[6,272,128]{2,1,0:T(8,128)(2,1)S(1)} %get-tuple-element.36), channel_id=1, source_target_pairs={{8,0},{16,8},{24,16},{32,24},{40,32},{48,40},{56,48},{64,56},{72,6... | collective-permute-start | bytes 1253384 | tf_op jit(solution)/shard_map/ppermute | solution.py:26
  25.0 0.0 copy-done
  25.0 0.1 slice.14
  25.1 0.0 copy-done.7
  25.1 0.0 copy-done.4
  25.1 4.8 %corr_right.1 = (bf16[16,144,128]{2,1,0:T(8,128)(2,1)S(1)}, f32[16,128,128]{2,1,0:T(8,128)S(1)}) custom-call(bf16[16,256,256]{2,1,0:T(8,128)(2,1)S(1)} %copy-done, bf16[16,256,256]{2,1,0:T(8,128)(2,1)S(1)} %copy-done.1, s32[16,256]{1,0:T(8,128)S(1)} %copy-done.4, bf16[16,4,896]{2,1,0:T(4,128)(2,1)S(1)} %collective-permute-done.right_ref.refs_3_, ...), custom_call_target="tpu_custom_call" | custom-call | flops 268435456 | bytes 6291456 | tf_op jit(solution)/shard_map/corr_right/pallas_call | solution.py:597
  29.9 0.4 collective-permute-done.4.refs_2_.refs_3_
  30.3 2.2 %corr_left.2 = (bf16[8,272,128]{2,1,0:T(8,128)(2,1)S(1)}, f32[8,128,128]{2,1,0:T(8,128)S(1)}, bf16[4,272,128]{2,1,0:T(8,128)(2,1)S(1)}) custom-call(bf16[16,256,256]{2,1,0:T(8,128)(2,1)S(1)} %copy-done, bf16[16,256,256]{2,1,0:T(8,128)(2,1)S(1)} %copy-done.1, bf16[8,128,256]{2,1,0:T(8,128)(2,1)S(1)} %collective-permute-done.4.refs_2_.refs_3_, ...), custom_call_target="tpu_custom_call" | custom-call | flops 134217728 | bytes 3145728 | tf_op jit(solution)/shard_map/corr_left/pallas_call | solution.py:622
  32.5 0.0 copy-start.5
  32.5 0.0 copy-start.6
  32.6 2.1 %collective-permute-start.7 = (bf16[4,272,128]{2,1,0:T(8,128)(2,1)S(1)}, bf16[4,272,128]{2,1,0:T(8,128)(2,1)S(1)}, u32[]{:S(2)}, u32[]{:S(2)}) collective-permute-start(bf16[4,272,128]{2,1,0:T(8,128)(2,1)S(1)} %get-tuple-element.43), channel_id=1, source_target_pairs={{8,0},{16,8},{24,16},{32,24},{40,32},{48,40},{56,48},{64,56},{72,6... | collective-permute-start | bytes 835592 | tf_op jit(solution)/shard_map/ppermute | solution.py:26
  34.6 6.9 %collective-permute-done.5.refs_2_.refs_4_ = bf16[8,128,256]{2,1,0:T(8,128)(2,1)S(1)} collective-permute-done((bf16[8,128,256]{2,1,0:T(8,128)(2,1)S(1)}, bf16[8,128,256]{2,1,0:T(8,128)(2,1)S(1)}, u32[]{:S(2)}, u32[]{:S(2)}) %collective-permute-start.5) | collective-permute-done | bytes 524320 | tf_op jit(solution)/shard_map/ppermute | solution.py:26
  41.5 2.2 %corr_left.3 = (bf16[8,272,128]{2,1,0:T(8,128)(2,1)S(1)}, f32[8,128,128]{2,1,0:T(8,128)S(1)}, bf16[4,272,128]{2,1,0:T(8,128)(2,1)S(1)}) custom-call(bf16[16,256,256]{2,1,0:T(8,128)(2,1)S(1)} %copy-done, bf16[16,256,256]{2,1,0:T(8,128)(2,1)S(1)} %copy-done.1, bf16[8,128,256]{2,1,0:T(8,128)(2,1)S(1)} %collective-permute-done.5.refs_2_.refs_4_, ...), custom_call_target="tpu_custom_call" | custom-call | flops 134217728 | bytes 3145728 | tf_op jit(solution)/shard_map/corr_left/pallas_call | solution.py:622
  43.8 1.9 %collective-permute-start.6 = (bf16[4,272,128]{2,1,0:T(8,128)(2,1)S(1)}, bf16[4,272,128]{2,1,0:T(8,128)(2,1)S(1)}, u32[]{:S(2)}, u32[]{:S(2)}) collective-permute-start(bf16[4,272,128]{2,1,0:T(8,128)(2,1)S(1)} %get-tuple-element.42), channel_id=1, source_target_pairs={{0,8},{8,16},{16,24},{24,32},{32,40},{40,48},{48,56},{56,64},{64,7... | collective-permute-start | bytes 835592 | tf_op jit(solution)/shard_map/ppermute | solution.py:26
  45.7 0.0 copy-done.5
  45.7 0.0 copy-done.6
  45.7 3.4 %gates_hidden.1 = (f32[14,272,256]{2,1,0:T(8,128)S(1)}, bf16[1152,256]{1,0:T(8,128)(2,1)S(1)}, bf16[3072,256]{1,0:T(8,128)(2,1)S(1)}, bf16[256,1152]{1,0:T(8,128)(2,1)S(1)}, bf16[256,3072]{1,0:T(8,128)(2,1)S(1)}) custom-call(bf16[16,256,128]{2,1,0:T(8,128)(2,1)S(1)} %copy-done.2, bf16[16,16,256]{2,1,0:T(8,128)(2,1)S(1)} %get-tuple-element.37.edge_ref, ...), custom_call_target="tpu_custom_call" | custom-call | flops 3529506816 | bytes 16777216 | tf_op jit(solution)/shard_map/gates_hidden/pallas_call | solution.py:661
  49.1 3.2 %collective-permute-start.9 = (bf16[16,128,256]{2,1,0:T(8,128)(2,1)S(1)}, bf16[16,128,256]{2,1,0:T(8,128)(2,1)S(1)}, u32[]{:S(2)}, u32[]{:S(2)}) collective-permute-start(bf16[16,128,256]{2,1,0:T(8,128)(2,1)S(1)} %slice.14), channel_id=1, source_target_pairs={{1,0},{2,1},{3,2},{4,3},{5,4},{6,5},{7,6},{9,8},{10,9},{11,10},{12... | collective-permute-start | bytes 3145736 | tf_op jit(solution)/shard_map/ppermute | solution.py:26
  52.3 0.0 collective-permute-done.2.hgt_ref
  52.3 0.0 collective-permute-done.3.hgb_ref
  52.3 0.0 collective-permute-done.7.motl_ref
  52.3 0.9 collective-permute-done.6.mott_ref
  53.2 24.0 %gru.1 = (bf16[16,256,128]{2,1,0:T(8,128)(2,1)}, bf16[16,256,128]{2,1,0:T(8,128)(2,1)S(1)}, bf16[16,16,128]{2,1,0:T(8,128)(2,1)S(1)}) custom-call(bf16[16,256,128]{2,1,0:T(8,128)(2,1)S(1)} %copy-done.2, bf16[16,256,128]{2,1,0:T(8,128)(2,1)S(1)} %copy-done.3, bf16[6,272,128]{2,1,0:T(8,128)(2,1)S(1)} %collective-permute-done.2.hgt_ref, ...), custom_call_target="tpu_custom_call" | custom-call | flops 15686696960 | bytes 16777216 | tf_op jit(solution)/shard_map/gru/pallas_call | solution.py:699
  77.1 5.4 %collective-permute-start.8 = (bf16[16,16,128]{2,1,0:T(8,128)(2,1)S(1)}, bf16[16,16,128]{2,1,0:T(8,128)(2,1)S(1)}, u32[]{:S(2)}, u32[]{:S(2)}) collective-permute-start(bf16[16,16,128]{2,1,0:T(8,128)(2,1)S(1)} %get-tuple-element.56), channel_id=1, source_target_pairs={{1,0},{2,1},{3,2},{4,3},{5,4},{6,5},{7,6},{9,8},{10,9},{11,10},{12... | collective-permute-start | bytes 196616 | tf_op jit(solution)/shard_map/ppermute | solution.py:26
  82.5 6.3 %grads.1 = (bf16[16,256,256]{2,1,0:T(8,128)(2,1)}, bf16[16,256,256]{2,1,0:T(8,128)(2,1)}, bf16[16,128,128]{2,1,0:T(8,128)(2,1)S(1)}) custom-call(bf16[16,256,128]{2,1,0:T(8,128)(2,1)S(1)} %get-tuple-element.53.refs_0_, bf16[16,256,256]{2,1,0:T(8,128)(2,1)S(1)} %copy-done, bf16[16,256,256]{2,1,0:T(8,128)(2,1)S(1)} %copy-done.1, ...), custom_call_target="tpu_custom_call" | custom-call | flops 1073741824 | bytes 12582912 | tf_op jit(solution)/shard_map/grads/pallas_call | solution.py:718
  88.9 0.0 collective-permute-done.8.refs_1_
  88.9 0.0 collective-permute-done.9.refs_3_
  88.9 2.0 %grad_right.1 = bf16[16,256,256]{2,1,0:T(8,128)(2,1)} custom-call(bf16[16,128,128]{2,1,0:T(8,128)(2,1)S(1)} %get-tuple-element.55.refs_0_, bf16[16,16,128]{2,1,0:T(8,128)(2,1)S(1)} %collective-permute-done.8.refs_1_, bf16[16,256,256]{2,1,0:T(8,128)(2,1)S(1)} %copy-done, ...), custom_call_target="tpu_custom_call", output_to_operand_aliasing={{}: (4, {})} | custom-call | flops 268435456 | bytes 4194304 | tf_op jit(solution)/shard_map/grad_right/pallas_call | solution.py:741
  (1 shorter events, 0.0 us)
Async XLA Ops:
  0.6 10.4 %copy-start.1 = (bf16[16,256,256]{2,1,0:T(8,128)(2,1)S(1)}, bf16[16,256,256]{2,1,0:T(8,128)(2,1)}, u32[]{:S(2)}) copy-start(bf16[16,256,256]{2,1,0:T(8,128)(2,1)} %refs_2_.4) | copy-start | bytes 6291460
  2.7 15.5 %copy-start.2 = (bf16[16,256,128]{2,1,0:T(8,128)(2,1)S(1)}, bf16[16,256,128]{2,1,0:T(8,128)(2,1)}, u32[]{:S(2)}) copy-start(bf16[16,256,128]{2,1,0:T(8,128)(2,1)} %hid_ref.5) | copy-start | bytes 3145732
  2.7 15.5 %copy-start.3 = (bf16[16,256,128]{2,1,0:T(8,128)(2,1)S(1)}, bf16[16,256,128]{2,1,0:T(8,128)(2,1)}, u32[]{:S(2)}) copy-start(bf16[16,256,128]{2,1,0:T(8,128)(2,1)} %grad_ref.3) | copy-start | bytes 3145732
  2.7 13.5 %collective-permute-start.1 = (bf16[16,16,256]{2,1,0:T(8,128)(2,1)}, bf16[16,16,256]{2,1,0:T(8,128)(2,1)S(1)}, u32[]{:S(2)}, u32[]{:S(2)}) collective-permute-start(bf16[16,16,256]{2,1,0:T(8,128)(2,1)} %get-tuple-element.32), channel_id=1, source_target_pairs={{0,1},{1,2},{2,3},{3,4},{4,5},{5,6},{6,7},{8,9},{9,10},{10,11},{11... | collective-permute-start | bytes 393224 | tf_op jit(solution)/shard_map/ppermute | solution.py:26
  7.7 8.4 %collective-permute-start = (bf16[16,4,896]{2,1,0:T(4,128)(2,1)}, bf16[16,4,896]{2,1,0:T(4,128)(2,1)S(1)}, u32[]{:S(2)}, u32[]{:S(2)}) collective-permute-start(bf16[16,4,896]{2,1,0:T(4,128)(2,1)} %get-tuple-element.31), channel_id=1, source_target_pairs={{1,0},{2,1},{3,2},{4,3},{5,4},{6,5},{7,6},{9,8},{10,9},{11,10},{12... | collective-permute-start | bytes 344072 | tf_op jit(solution)/shard_map/ppermute | solution.py:26
  11.1 19.2 %collective-permute-start.4 = (bf16[8,128,256]{2,1,0:T(8,128)(2,1)S(1)}, bf16[8,128,256]{2,1,0:T(8,128)(2,1)S(1)}, u32[]{:S(2)}, u32[]{:S(2)}) collective-permute-start(bf16[8,128,256]{2,1,0:T(8,128)(2,1)S(1)} %get-tuple-element.59), channel_id=1, source_target_pairs={{0,1},{1,2},{2,3},{3,4},{4,5},{5,6},{6,7},{8,9},{9,10},{10,11},{11... | collective-permute-start | bytes 1572872 | tf_op jit(solution)/shard_map/ppermute | solution.py:26
  16.1 8.8 %copy-start = (bf16[16,256,256]{2,1,0:T(8,128)(2,1)S(1)}, bf16[16,256,256]{2,1,0:T(8,128)(2,1)}, u32[]{:S(2)}) copy-start(bf16[16,256,256]{2,1,0:T(8,128)(2,1)} %refs_2_.5) | copy-start | bytes 6291460
  16.1 25.4 %collective-permute-start.5 = (bf16[8,128,256]{2,1,0:T(8,128)(2,1)S(1)}, bf16[8,128,256]{2,1,0:T(8,128)(2,1)S(1)}, u32[]{:S(2)}, u32[]{:S(2)}) collective-permute-start(bf16[8,128,256]{2,1,0:T(8,128)(2,1)S(1)} %get-tuple-element.40), channel_id=1, source_target_pairs={{0,1},{1,2},{2,3},{3,4},{4,5},{5,6},{6,7},{8,9},{9,10},{10,11},{11... | collective-permute-start | bytes 1572872 | tf_op jit(solution)/shard_map/ppermute | solution.py:26
  18.4 6.7 %copy-start.7 = (bf16[9,128]{1,0:T(8,128)(2,1)S(1)}, bf16[9,128]{1,0:T(8,128)(2,1)}, u32[]{:S(2)}) copy-start(bf16[9,128]{1,0:T(8,128)(2,1)} %param.12) | copy-start | bytes 6916
  18.4 6.7 %copy-start.4 = (s32[16,256]{1,0:T(8,128)S(1)}, s32[16,256]{1,0:T(8,128)}, u32[]{:S(2)}) copy-start(s32[16,256]{1,0:T(8,128)} %refs_5_.1) | copy-start | bytes 49156
  18.4 33.9 %collective-permute-start.2 = (bf16[6,272,128]{2,1,0:T(8,128)(2,1)S(1)}, bf16[6,272,128]{2,1,0:T(8,128)(2,1)S(1)}, u32[]{:S(2)}, u32[]{:S(2)}) collective-permute-start(bf16[6,272,128]{2,1,0:T(8,128)(2,1)S(1)} %get-tuple-element.35), channel_id=1, source_target_pairs={{0,8},{8,16},{16,24},{24,32},{32,40},{40,48},{48,56},{56,64},{64,7... | collective-permute-start | bytes 1253384 | tf_op jit(solution)/shard_map/ppermute | solution.py:26
  20.4 31.9 %collective-permute-start.3 = (bf16[6,272,128]{2,1,0:T(8,128)(2,1)S(1)}, bf16[6,272,128]{2,1,0:T(8,128)(2,1)S(1)}, u32[]{:S(2)}, u32[]{:S(2)}) collective-permute-start(bf16[6,272,128]{2,1,0:T(8,128)(2,1)S(1)} %get-tuple-element.36), channel_id=1, source_target_pairs={{8,0},{16,8},{24,16},{32,24},{40,32},{48,40},{56,48},{64,56},{72,6... | collective-permute-start | bytes 1253384 | tf_op jit(solution)/shard_map/ppermute | solution.py:26
  32.5 13.2 %copy-start.5 = (bf16[3,3,256,256]{3,2,1,0:T(8,128)(2,1)S(1)}, bf16[3,3,256,256]{3,2,1,0:T(8,128)(2,1)}, u32[]{:S(2)}) copy-start(bf16[3,3,256,256]{3,2,1,0:T(8,128)(2,1)} %param.13) | copy-start | bytes 3538948
  32.5 13.2 %copy-start.6 = (bf16[3,3,256,128]{3,2,1,0:T(8,128)(2,1)S(1)}, bf16[3,3,256,128]{3,2,1,0:T(8,128)(2,1)}, u32[]{:S(2)}) copy-start(bf16[3,3,256,128]{3,2,1,0:T(8,128)(2,1)} %param.14) | copy-start | bytes 1769476
  32.6 19.7 %collective-permute-start.7 = (bf16[4,272,128]{2,1,0:T(8,128)(2,1)S(1)}, bf16[4,272,128]{2,1,0:T(8,128)(2,1)S(1)}, u32[]{:S(2)}, u32[]{:S(2)}) collective-permute-start(bf16[4,272,128]{2,1,0:T(8,128)(2,1)S(1)} %get-tuple-element.43), channel_id=1, source_target_pairs={{8,0},{16,8},{24,16},{32,24},{40,32},{48,40},{56,48},{64,56},{72,6... | collective-permute-start | bytes 835592 | tf_op jit(solution)/shard_map/ppermute | solution.py:26
  43.8 9.4 %collective-permute-start.6 = (bf16[4,272,128]{2,1,0:T(8,128)(2,1)S(1)}, bf16[4,272,128]{2,1,0:T(8,128)(2,1)S(1)}, u32[]{:S(2)}, u32[]{:S(2)}) collective-permute-start(bf16[4,272,128]{2,1,0:T(8,128)(2,1)S(1)} %get-tuple-element.42), channel_id=1, source_target_pairs={{0,8},{8,16},{16,24},{24,32},{32,40},{40,48},{48,56},{56,64},{64,7... | collective-permute-start | bytes 835592 | tf_op jit(solution)/shard_map/ppermute | solution.py:26
  49.1 39.8 %collective-permute-start.9 = (bf16[16,128,256]{2,1,0:T(8,128)(2,1)S(1)}, bf16[16,128,256]{2,1,0:T(8,128)(2,1)S(1)}, u32[]{:S(2)}, u32[]{:S(2)}) collective-permute-start(bf16[16,128,256]{2,1,0:T(8,128)(2,1)S(1)} %slice.14), channel_id=1, source_target_pairs={{1,0},{2,1},{3,2},{4,3},{5,4},{6,5},{7,6},{9,8},{10,9},{11,10},{12... | collective-permute-start | bytes 3145736 | tf_op jit(solution)/shard_map/ppermute | solution.py:26
  77.1 11.7 %collective-permute-start.8 = (bf16[16,16,128]{2,1,0:T(8,128)(2,1)S(1)}, bf16[16,16,128]{2,1,0:T(8,128)(2,1)S(1)}, u32[]{:S(2)}, u32[]{:S(2)}) collective-permute-start(bf16[16,16,128]{2,1,0:T(8,128)(2,1)S(1)} %get-tuple-element.56), channel_id=1, source_target_pairs={{1,0},{2,1},{3,2},{4,3},{5,4},{6,5},{7,6},{9,8},{10,9},{11,10},{12... | collective-permute-start | bytes 196616 | tf_op jit(solution)/shard_map/ppermute | solution.py:26
